TPU v7x, 128 devices: a whole 4x4x4 slice. The times are simulated.
128 devices in a mesh: slab: 8 (over y, x_hi), brick: 16 (over x_lo, z, core).
Axes of the slice: x: 4 (x_hi: 2, x_lo: 2; x = x_hi * 2 + x_lo), y: 4, z: 4, core: 2. Of those that a mesh axis runs over, the one named last changes fastest.
Arguments:
- k_coeffs: float32 [16, 32, 16, 128], P('slab', 'brick'), may hold values from -0.3 to 0.4
- v_basis: float32 [32768, 128], P(('slab', 'brick')), may hold values from -4 to 4
Outputs:
- basis_x: float32 [16, 32, 16, 128], P('slab', 'brick')
- coupling: float32 [128, 128], replicated
- basis_v: float32 [32768, 128], P(('slab', 'brick'))
All inputs are finite; a program needn't handle non-finite values.
Results may differ from a plain program's by a relative error of at most 0.0001.
Values sent between devices are 32-bit elements; how exact they have to be, the bound alone decides.
No kernel may reach another device: no remote copies, remote signals or barrier semaphores. Data moves between devices by JAX's collectives and lax.ppermute only.
A program may use at most 64 MiB of HBM per device.

v0:
```python
import functools
import math

import jax
import jax.numpy as jnp
from jax import lax
from jax.experimental import pallas as pl
from jax.experimental.pallas import tpu as pltpu
from jax.sharding import PartitionSpec as P

NVX = 32


CFL = 0.9
VMAX = 6.0
COLLIDE = 0.3
RHO_MIN = 0.25
TEMP_MIN = 0.25
PRECISE = lax.Precision.HIGHEST
FINE = lax.Precision.HIGH
SPACING = 2.0 * VMAX / NVX
WEIGHT_V = SPACING**3
PANEL = 16


def contract(left, right, left_dim, right_dim, precision=PRECISE):
    return lax.dot_general(
        left, right, (((left_dim,), (right_dim,)), ((), ())), precision=precision
    )


def exchange(array, axis):
    return lax.all_to_all(array, axis, 0, 0, tiled=True)


def to_all(array, axis):
    copies = lax.axis_size(axis)
    return exchange(jnp.broadcast_to(array[None], (copies,) + array.shape), axis)


def velocities(indices):
    coords = jnp.stack([indices // (NVX * NVX), indices // NVX % NVX, indices % NVX])
    return -VMAX + (coords.astype(jnp.float32) + 0.5) * SPACING


def cell_state(moments):
    density = jnp.maximum(moments[0], RHO_MIN)
    drift = [moments[axis_id] / density for axis_id in (1, 2, 3)]
    square = drift[0] * drift[0] + drift[1] * drift[1] + drift[2] * drift[2]
    temper = jnp.maximum((moments[4] / density - square) / 3.0, TEMP_MIN)
    return density, drift, temper


def sum_over_devices(array):
    slabs, bricks = lax.axis_size("slab"), lax.axis_size("brick")
    devices = slabs * bricks

    def from_peer(values, mask):
        pairs = [(i, i ^ mask) for i in range(devices)]
        return lax.ppermute(values, ("slab", "brick"), pairs)

    step = 1
    array = array + from_peer(array, step)
    step = 2
    while step < devices:
        if step * 4 <= devices:
            one, two, three = (from_peer(array, step * k) for k in (1, 2, 3))
            array = (array + one) + (two + three)
            step *= 4
        else:
            array = array + from_peer(array, step)
            step *= 2
    return array


def three_parts(array):
    high = array.astype(jnp.bfloat16).astype(jnp.float32)
    rest = array - high
    middle = rest.astype(jnp.bfloat16).astype(jnp.float32)
    return high, middle, rest - middle


def two_parts(array):
    high = array.astype(jnp.bfloat16)
    return high, (array - high.astype(jnp.float32)).astype(jnp.bfloat16)


def factor_into(gram, work_ref, upper_ref, inverse_ref):
    size = gram.shape[0]
    rows = lax.broadcasted_iota(jnp.int32, (size, size), 0)
    cols = lax.broadcasted_iota(jnp.int32, (size, size), 1)
    work_ref[:, :size] = gram
    work_ref[:, size:] = jnp.where(rows == cols, 1.0, 0.0)
    panel_row = lax.broadcasted_iota(jnp.int32, (PANEL, size), 0)
    panel_col = lax.broadcasted_iota(jnp.int32, (PANEL, size), 1)
    for start in range(0, size, PANEL):
        stop = start + PANEL
        panel = work_ref[start:stop, :]
        spread = [
            jnp.broadcast_to(panel[:, start + t : start + t + 1], (PANEL, size))
            for t in range(PANEL)
        ]
        pivots = jnp.zeros((PANEL, size), jnp.float32)
        for t in range(PANEL):
            pivot = jnp.broadcast_to(spread[t][t : t + 1, :], (PANEL, size))
            pivots = jnp.where(panel_row == t, pivot, pivots)
            if t == PANEL - 1:
                break
            ratio = jnp.where(panel_row > t, spread[t] * (1.0 / pivot), 0.0)
            for u in range(t + 1, PANEL):
                spread[u] = spread[u] - ratio * jnp.broadcast_to(
                    spread[u][t : t + 1, :], (PANEL, size)
                )
            panel = panel - jnp.concatenate([ratio, ratio], axis=1) * jnp.broadcast_to(
                panel[t : t + 1, :], (PANEL, 2 * size)
            )
        scale = lax.rsqrt(pivots)
        panel = panel * jnp.concatenate([scale, scale], axis=1)
        left = jnp.where(panel_col >= panel_row + start, panel[:, :size], 0.0)
        right = panel[:, size:]
        upper_ref[start:stop, :] = left
        inverse_ref[start:stop, :] = right
        if stop < size:
            high, middle, low = three_parts(jnp.concatenate([left, right], axis=1))
            lhs = [high, high, middle, middle, high, low]
            rhs = [high, middle, high, middle, low, high]
            update = lax.dot_general(
                jnp.concatenate([part[:, :size] for part in lhs], axis=0).astype(jnp.bfloat16),
                jnp.concatenate(rhs, axis=0).astype(jnp.bfloat16),
                (((0,), (0,)), ((), ())),
                preferred_element_type=jnp.float32,
            )
            work_ref[stop:, :] = work_ref[stop:, :] - update[stop:, :]


def transport_kernel(nodes_ref, columns_ref, speeds_ref, out_ref):
    groups, rows, rank = nodes_ref.shape
    bricks = out_ref.shape[0]
    factors = [jnp.broadcast_to(columns_ref[:, i : i + 1], (rows, rank)) for i in range(4)]
    sums = [jnp.zeros((rank, rank), jnp.float32) for _ in range(6)]
    for group in range(groups):
        nodes = nodes_ref[group]
        weighted = jnp.concatenate([nodes] + [nodes * factor for factor in factors], axis=1)
        high, low = two_parts(weighted)
        node_high, node_low = high[:, :rank], low[:, :rank]
        product = lax.dot_general(
            jnp.concatenate([node_high, node_high, node_low], axis=0),
            jnp.concatenate([high, low, high], axis=0),
            (((0,), (0,)), ((), ())),
            preferred_element_type=jnp.float32,
        )
        plain = product[:, :rank]
        speed = jnp.broadcast_to(speeds_ref[group : group + 1, :], (rank, rank))
        sums[0] = sums[0] + jnp.maximum(speed, 0.0) * plain
        sums[1] = sums[1] + jnp.minimum(speed, 0.0) * plain
        for i in range(4):
            sums[2 + i] = sums[2 + i] + product[:, (i + 1) * rank : (i + 2) * rank]
    height = rank // bricks
    for i in range(6):
        out_ref[:, i * height : (i + 1) * height, :] = (sums[i] * WEIGHT_V).reshape(
            bricks, height, rank
        )


def advance_kernel(parts_ref, steps_ref, cells_ref, payload_ref, advanced_ref, *, time_step):
    cells, rank = cells_ref.shape
    bricks = parts_ref.shape[0]
    height = rank // bricks
    maxwell_proj = parts_ref[0, :cells, :]
    for i in range(1, bricks):
        maxwell_proj = maxwell_proj + parts_ref[i, :cells, :]
    maxwell_proj = maxwell_proj * WEIGHT_V
    flux = jnp.zeros((cells, rank), jnp.float32)
    for i in range(6):
        block = parts_ref[:, cells + i * height : cells + (i + 1) * height, :].reshape(rank, rank)
        flux = flux + contract(steps_ref[i], block, 1, 0)
    own = cells_ref[...]
    advanced = own - time_step * flux + COLLIDE * (maxwell_proj - own)
    advanced_ref[...] = advanced
    payload_ref[:, :cells, :] = jnp.broadcast_to(advanced[None], (bricks, cells, rank))
    projected = contract(advanced, maxwell_proj, 0, 0)
    payload_ref[:, cells:, :] = projected.reshape(bricks, height, rank)


def middle_kernel(
    pieces_ref,
    transport_ref,
    basis_ref,
    back_ref,
    advanced_ref,
    speeds_ref,
    basis_x_ref,
    velocity_ref,
    gram_ref,
    work_ref,
    upper_ref,
    inverse_ref,
    *,
    lengths,
    time_step,
    weight_x,
):
    bricks, _, rank = pieces_ref.shape
    rows = basis_ref.shape[0]
    height = rank // bricks

    def piece(ref, i):
        return ref[:, i * height : (i + 1) * height, :].reshape(rank, rank)

    factor_into(piece(pieces_ref, 0) * weight_x, work_ref, upper_ref, inverse_ref)
    upper, inverse = upper_ref[...], inverse_ref[...]
    basis_x_ref[...] = contract(advanced_ref[...], inverse, 1, 1)
    change = jnp.zeros((rank, rank), jnp.float32)
    turned = []
    for i in range(3):
        shift = piece(pieces_ref, 1 + i) * weight_x
        straight = contract(inverse, shift, 1, 0)
        crossed = contract(inverse, shift, 1, 1)
        if i == 0:
            straight, crossed = crossed, straight
        turned.append(contract(straight, inverse, 1, 1))
        change = change + lengths[i] * (
            contract(upper - straight, piece(transport_ref, 2 * i), 1, 0)
            + contract(crossed - upper, piece(transport_ref, 2 * i + 1), 1, 0)
        )
    projected = contract(inverse, piece(pieces_ref, 4) * weight_x, 1, 0)
    middle = upper + time_step * change - COLLIDE * (projected - upper)
    now = contract(basis_ref[...], middle, 1, 1)
    drift_sum = jnp.zeros((rows, rank), jnp.float32)
    for i in range(3):
        speed = jnp.broadcast_to(speeds_ref[:, i : i + 1], (rows, rank)) * lengths[i]
        minus = contract(now, turned[i], 1, 1)
        plus = contract(now, turned[i], 1, 0)
        drift_sum = drift_sum + jnp.maximum(speed, 0.0) * (now - minus)
        drift_sum = drift_sum + jnp.minimum(speed, 0.0) * (plus - now)
    back_proj = contract(back_ref[...] * weight_x, inverse, 1, 1)
    updated = now - time_step * drift_sum + COLLIDE * (back_proj - now)
    velocity_ref[...] = updated
    gram_ref[...] = contract(updated, updated, 0, 0) * WEIGHT_V


def last_kernel(gram_ref, velocity_ref, coupling_ref, basis_ref, work_ref, upper_ref, inverse_ref):
    factor_into(gram_ref[...], work_ref, upper_ref, inverse_ref)
    coupling_ref[...] = upper_ref[...].T
    basis_ref[...] = contract(velocity_ref[...], inverse_ref[...], 1, 1)


def f32(*shape):
    return jax.ShapeDtypeStruct(shape, jnp.float32)


def factor_scratch(rank):
    shapes = ((rank, 2 * rank), (rank, rank), (rank, rank))
    return [pltpu.VMEM(shape, jnp.float32) for shape in shapes]


def local(k_coeffs, v_basis):
    cells_x, cells_y, cells_z, rank = k_coeffs.shape
    cells = cells_x * cells_y * cells_z
    slabs, bricks = lax.axis_size("slab"), lax.axis_size("brick")
    devices = slabs * bricks
    slab, brick = lax.axis_index("slab"), lax.axis_index("brick")
    lengths = (cells_x * slabs, cells_y * bricks, cells_z)
    time_step = CFL / (VMAX * sum(lengths))
    weight_x = 1.0 / (lengths[0] * lengths[1] * lengths[2])
    rows = v_basis.shape[0]
    slab_cells = cells * bricks
    half = slab_cells // cells_x
    height = rank // bricks
    up = [(i, (i + 1) % slabs) for i in range(slabs)]
    down = [(i, (i - 1) % slabs) for i in range(slabs)]
    own_cells = k_coeffs.reshape(cells, rank)

    own_ids = (slab * bricks + brick) * rows + jnp.arange(rows, dtype=jnp.int32)
    own_velocity = velocities(own_ids)
    ones = jnp.ones_like(own_velocity[0])
    weights = jnp.stack(
        [ones, own_velocity[0], own_velocity[1], own_velocity[2]]
        + [jnp.sum(own_velocity * own_velocity, axis=0)]
        + [jnp.zeros_like(ones)] * 3
    )
    vectors_part = contract(weights, v_basis, 1, 0) * WEIGHT_V
    vectors_all = exchange(
        jnp.broadcast_to(vectors_part[None], (devices, 8, rank)), ("slab", "brick")
    )
    nodes = to_all(v_basis, "slab")
    k_slab = to_all(own_cells, "brick")
    vectors = jnp.sum(vectors_all, axis=0)
    k_below = lax.ppermute(k_coeffs[-1:], "slab", up)
    k_above = lax.ppermute(k_coeffs[:1], "slab", down)

    across = velocities(brick * rows + jnp.arange(rows, dtype=jnp.int32))
    columns = [f(across[i]) for i in (1, 2) for f in (lambda v: jnp.maximum(v, 0.0), lambda v: jnp.minimum(v, 0.0))]
    columns = jnp.stack(columns + [jnp.zeros_like(ones)] * 4, axis=1)
    owner = jnp.arange(slabs, dtype=jnp.int32) * bricks + brick
    first_velocity = velocities(owner * rows)[0]
    transport_part = pl.pallas_call(
        transport_kernel, out_shape=f32(bricks, 6 * height, rank), name="transport"
    )(nodes, columns, jnp.broadcast_to(first_velocity[:, None], (slabs, rank)))
    transport_slice = jnp.sum(exchange(transport_part, "brick"), axis=0)

    k_flat = k_slab.reshape(slab_cells, rank)
    moments = contract(vectors, k_flat, 1, 1)
    density, drift, temper = cell_state([moments[i : i + 1] for i in range(5)])
    distance = (across[1][:, None] - drift[1]) ** 2 + (across[2][:, None] - drift[2]) ** 2
    plane = jnp.exp(distance * (-0.5 / temper))
    moments = contract(k_flat, vectors, 1, 1)
    density, drift, temper = cell_state([moments[:, i : i + 1] for i in range(5)])
    amplitude = density * (2.0 * math.pi * temper) ** (-1.5)
    line = amplitude * jnp.exp((first_velocity[None, :] - drift[0]) ** 2 * (-0.5 / temper))

    node_columns = jnp.concatenate([nodes[i] for i in range(slabs)], axis=1)
    planes = contract(plane, node_columns, 0, 0, FINE)
    mproj_part = sum(
        line[:, i : i + 1] * planes[:, i * rank : (i + 1) * rank] for i in range(slabs)
    )
    second = exchange(
        jnp.concatenate(
            [
                mproj_part.reshape(bricks, cells, rank),
                jnp.broadcast_to(transport_slice[None], (bricks, 6 * height, rank)),
            ],
            axis=1,
        ),
        "brick",
    )

    slab_grid = k_slab.reshape(bricks, cells_x, cells_y, cells_z, rank)
    left = lax.dynamic_index_in_dim(slab_grid, (brick - 1) % bricks, 0, keepdims=False)
    right = lax.dynamic_index_in_dim(slab_grid, (brick + 1) % bricks, 0, keepdims=False)
    lower = [
        jnp.concatenate([k_below, k_coeffs[:-1]], axis=0),
        jnp.concatenate([left[:, -1:], k_coeffs[:, :-1]], axis=1),
        jnp.roll(k_coeffs, 1, axis=2),
    ]
    upper = [
        jnp.concatenate([k_coeffs[1:], k_above], axis=0),
        jnp.concatenate([k_coeffs[:, 1:], right[:, :1]], axis=1),
        jnp.roll(k_coeffs, -1, axis=2),
    ]
    steps = []
    for axis_id in range(3):
        steps.append(((k_coeffs - lower[axis_id]) * lengths[axis_id]).reshape(cells, rank))
        steps.append(((upper[axis_id] - k_coeffs) * lengths[axis_id]).reshape(cells, rank))
    payload, advanced = pl.pallas_call(
        functools.partial(advance_kernel, time_step=time_step),
        out_shape=(f32(bricks, cells + height, rank), f32(cells, rank)),
        name="advance",
    )(second, jnp.stack(steps), own_cells)
    third = exchange(payload, "brick")

    slab_advanced = third[:, :cells]
    projected_rows = jnp.sum(third[:, cells:], axis=0)
    adv_grid = slab_advanced.reshape(bricks, cells_x, cells_y, cells_z, rank)
    planes_x = [adv_grid[:, i].reshape(half, rank) for i in range(cells_x)]
    choose = brick * height + jnp.arange(height, dtype=jnp.int32)
    choose = (choose[:, None] == jnp.arange(rank, dtype=jnp.int32)[None]).astype(jnp.float32)
    chosen = contract(choose, planes_x[-1], 1, 1)
    chosen_below = lax.ppermute(chosen, "slab", up)
    before = jnp.concatenate([adv_grid[-1:, :, -1:], adv_grid[:-1, :, -1:]], axis=0)
    shift_y = jnp.concatenate([before, adv_grid[:, :, :-1]], axis=2).reshape(slab_cells, rank)
    shift_z = jnp.roll(adv_grid, 1, axis=3).reshape(slab_cells, rank)
    adv_flat = slab_advanced.reshape(slab_cells, rank)

    def own_rows(left_side, right_side):
        whole = contract(left_side, right_side, 0, 0)
        return lax.dynamic_slice_in_dim(whole, brick * height, height, 0)

    crossing = contract(chosen_below, planes_x[0], 1, 0)
    for i in range(1, cells_x):
        crossing = crossing + own_rows(planes_x[i - 1], planes_x[i])
    pieces = jnp.concatenate(
        [
            own_rows(adv_flat, adv_flat),
            crossing,
            own_rows(adv_flat, shift_y),
            own_rows(adv_flat, shift_z),
            projected_rows,
        ],
        axis=0,
    )
    reduced = to_all(jnp.sum(to_all(pieces, "slab"), axis=0), "brick")

    scaled = jnp.concatenate([line[:, i : i + 1] * adv_flat for i in range(slabs)], axis=1)
    back = contract(plane, scaled, 1, 0, FINE)
    fourth = exchange(
        jnp.stack([back[:, i * rank : (i + 1) * rank] for i in range(slabs)]), "slab"
    )
    back_own = jnp.sum(fourth, axis=0)

    speeds = jnp.stack(list(own_velocity) + [jnp.zeros_like(ones)] * 5, axis=1)
    basis_new, velocity_new, gram_part = pl.pallas_call(
        functools.partial(
            middle_kernel, lengths=lengths, time_step=time_step, weight_x=weight_x
        ),
        out_shape=(f32(cells, rank), f32(rows, rank), f32(rank, rank)),
        scratch_shapes=factor_scratch(rank),
        name="middle",
    )(reduced, second[:, cells:], v_basis, back_own, advanced, speeds)
    gram_v = sum_over_devices(gram_part)
    coupling, vbasis_new = pl.pallas_call(
        last_kernel,
        out_shape=(f32(rank, rank), f32(rows, rank)),
        scratch_shapes=factor_scratch(rank),
        name="last",
    )(gram_v, velocity_new)
    return (basis_new.reshape(cells_x, cells_y, cells_z, rank), coupling, vbasis_new)


def solution(mesh):
    placed = (P("slab", "brick", None, None), P(("slab", "brick"), None))
    return jax.shard_map(
        local,
        mesh=mesh,
        in_specs=placed,
        out_specs=(P("slab", "brick", None, None), P(), P(("slab", "brick"), None)),
        check_vma=False,
    )
```

profile of v0, /device:TPU:0, one launch (start us, length us, event | category | flops | bytes accessed | tf_op | source)
XLA Modules:
  0.0 225.9 jit_solution(10687515209004978324)
XLA Ops:
  0.6 1.6 broadcast_in_dim.18
  2.3 6.4 %all-to-all-start.1 = ((f32[16,64,128]{2,1,0:T(8,128)}), f32[16,64,128]{2,1,0:T(8,128)S(1)}, u32[]{:S(2)}, u32[]{:S(2)}) async-start(f32[16,64,128]{2,1,0:T(8,128)} %broadcast_in_dim.18), calls=%async_computation.1 | async-start | bytes 1048576 | tf_op jit(solution)/shard_map/all_to_all | solution.py:33
  8.7 0.7 fusion.78
  9.5 5.2 %collective-permute-start.1 = (f32[1,2,16,128]{3,2,1,0:T(8,128)S(1)}, f32[1,2,16,128]{3,2,1,0:T(8,128)S(1)}, u32[]{:S(2)}, u32[]{:S(2)}) collective-permute-start(f32[1,2,16,128]{3,2,1,0:T(8,128)S(1)} %get-tuple-element.42), channel_id=1, source_target_pairs={{0,112},{16,0},{32,16},{48,32},{64,48},{80,64},{96,80},{112,96},{1... | collective-permute-start | bytes 49160 | tf_op jit(solution)/shard_map/ppermute | solution.py:290
  15.7 0.8 copy.20.columns_ref
  17.2 1.1 convolution_multiply_fusion
  18.3 1.6 all-to-all-done.1
  19.9 0.8 broadcast_in_dim.16
  20.8 8.8 %all-to-all-start = ((f32[128,8,128]{2,1,0:T(8,128)}), f32[128,8,128]{2,1,0:T(8,128)S(1)}, u32[]{:S(2)}, u32[]{:S(2)}) async-start(f32[128,8,128]{2,1,0:T(8,128)} %broadcast_in_dim.16), calls=%async_computation | async-start | bytes 1048576 | tf_op jit(solution)/shard_map/all_to_all | solution.py:33
  29.6 0.8 fusion.75
  30.5 12.8 %all-to-all-done = f32[128,8,128]{2,1,0:T(8,128)S(1)} async-done(((f32[128,8,128]{2,1,0:T(8,128)}), f32[128,8,128]{2,1,0:T(8,128)S(1)}, u32[]{:S(2)}, u32[]{:S(2)}) %all-to-all-start) | async-done | bytes 524320 | tf_op jit(solution)/shard_map/all_to_all | solution.py:33
  43.3 1.0 broadcast_in_dim.19
  44.3 3.6 %all-to-all-start.2 = ((f32[8,256,128]{2,1,0:T(8,128)}), f32[8,256,128]{2,1,0:T(8,128)S(1)}, u32[]{:S(2)}, u32[]{:S(2)}) async-start(f32[8,256,128]{2,1,0:T(8,128)} %broadcast_in_dim.19), calls=%async_computation.2 | async-start | bytes 2097152 | tf_op jit(solution)/shard_map/all_to_all | solution.py:33
  48.8 16.0 %all-to-all-done.2.nodes_ref = f32[8,256,128]{2,1,0:T(8,128)S(1)} async-done(((f32[8,256,128]{2,1,0:T(8,128)}), f32[8,256,128]{2,1,0:T(8,128)S(1)}, u32[]{:S(2)}, u32[]{:S(2)}) %all-to-all-start.2) | async-done | bytes 1048608 | tf_op jit(solution)/shard_map/all_to_all | solution.py:33
  64.8 0.7 broadcast_in_dim.20.speeds_ref
  65.8 3.8 %transport.1 = f32[16,48,128]{2,1,0:T(8,128)} custom-call(f32[8,256,128]{2,1,0:T(8,128)} %copy-done, f32[256,8]{1,0:T(8,128)} %copy.20.columns_ref, f32[8,128]{1,0:T(8,128)} %broadcast_in_dim.20.speeds_ref), custom_call_target="tpu_custom_call" | custom-call | tf_op jit(solution)/shard_map/transport/pallas_call | solution.py:297
  69.6 3.6 %all-to-all-start.3 = ((f32[16,48,128]{2,1,0:T(8,128)}), f32[16,48,128]{2,1,0:T(8,128)S(1)}, u32[]{:S(2)}, u32[]{:S(2)}) async-start(f32[16,48,128]{2,1,0:T(8,128)} %transport.1), calls=%async_computation.3 | async-start | bytes 786432 | tf_op jit(solution)/shard_map/all_to_all | solution.py:33
  73.1 0.9 fusion.37
  74.1 0.9 fusion.36
  75.0 0.9 fusion.35
  75.9 0.9 fusion.34
  76.8 0.9 fusion.33
  77.7 0.9 fusion.32
  78.7 0.9 fusion.31
  79.6 0.9 fusion.30
  80.5 2.2 fusion.2
  82.7 1.4 fusion.3
  84.2 1.0 pad_maximum_fusion
  85.2 5.7 %all-to-all-start.4 = ((f32[16,112,128]{2,1,0:T(8,128)}), f32[16,112,128]{2,1,0:T(8,128)S(1)}, u32[]{:S(2)}, u32[]{:S(2)}) async-start(f32[16,112,128]{2,1,0:T(8,128)} %pad_maximum_fusion), calls=%async_computation.4 | async-start | bytes 1835008 | tf_op jit(solution)/shard_map/all_to_all | solution.py:33
  91.0 15.0 %all-to-all-done.4.parts_ref = f32[16,112,128]{2,1,0:T(8,128)S(1)} async-done(((f32[16,112,128]{2,1,0:T(8,128)}), f32[16,112,128]{2,1,0:T(8,128)S(1)}, u32[]{:S(2)}, u32[]{:S(2)}) %all-to-all-start.4) | async-done | bytes 917536 | tf_op jit(solution)/shard_map/all_to_all | solution.py:33
  106.1 0.9 copy-done.1
  107.0 2.9 %advance.1 = (f32[16,72,128]{2,1,0:T(8,128)}, f32[64,128]{1,0:T(8,128)}) custom-call(f32[16,112,128]{2,1,0:T(8,128)} %copy-done.1, f32[6,64,128]{2,1,0:T(8,128)} %copy-done.5, f32[64,128]{1,0:T(8,128)} %bitcast.174), custom_call_target="tpu_custom_call" | custom-call | tf_op jit(solution)/shard_map/advance/pallas_call | solution.py:345
  109.9 3.6 %all-to-all-start.5 = ((f32[16,72,128]{2,1,0:T(8,128)}), f32[16,72,128]{2,1,0:T(8,128)S(1)}, u32[]{:S(2)}, u32[]{:S(2)}) async-start(f32[16,72,128]{2,1,0:T(8,128)} %get-tuple-element.10), calls=%async_computation.5 | async-start | bytes 1179648 | tf_op jit(solution)/shard_map/all_to_all | solution.py:33
  113.5 11.6 %all-to-all-done.5 = f32[16,72,128]{2,1,0:T(8,128)S(1)} async-done(((f32[16,72,128]{2,1,0:T(8,128)}), f32[16,72,128]{2,1,0:T(8,128)S(1)}, u32[]{:S(2)}, u32[]{:S(2)}) %all-to-all-start.5) | async-done | bytes 589856 | tf_op jit(solution)/shard_map/all_to_all | solution.py:33
  126.1 1.1 collective-permute-start.2
  127.5 1.0 fusion.82
  128.6 1.0 fusion.83
  131.0 2.4 %fusion.1 = f32[256,1024]{1,0:T(8,128)S(1)} fusion(f32[1024,1024]{1,0:T(8,128)S(1)} %multiply_dynamic-update-slice_fusion, f32[1024]{0:T(1024)S(1)} %bitcast.201, f32[1024]{0:T(1024)S(1)} %bitcast.205, f32[256]{0:T(256)S(1)} %bitcast.212, f32[1024]{0:T(1024)S(1)} %bitcast.203, f32[256]{0:T(256)S(1)} %bitcast.210), kind=kOutput, calls=%fused_computation.6 | convolution fusion | flops 1612185600 | bytes 5257216 | tf_op jit(solution)/shard_map/dot_general | solution.py:27
  138.2 1.0 convolution_bitcast_fusion
  140.2 6.0 %all-to-all-start.6 = ((f32[8,40,128]{2,1,0:T(8,128)}), f32[8,40,128]{2,1,0:T(8,128)S(1)}, u32[]{:S(2)}, u32[]{:S(2)}) async-start(f32[8,40,128]{2,1,0:T(8,128)} %broadcast_in_dim.22), calls=%async_computation.6 | async-start | bytes 327680 | tf_op jit(solution)/shard_map/all_to_all | solution.py:33
  146.8 7.7 %all-to-all-done.6 = f32[8,40,128]{2,1,0:T(8,128)S(1)} async-done(((f32[8,40,128]{2,1,0:T(8,128)}), f32[8,40,128]{2,1,0:T(8,128)S(1)}, u32[]{:S(2)}, u32[]{:S(2)}) %all-to-all-start.6) | async-done | bytes 163872 | tf_op jit(solution)/shard_map/all_to_all | solution.py:33
  154.5 3.6 %all-to-all-start.8 = ((f32[8,256,128]{2,1,0:T(8,128)}), f32[8,256,128]{2,1,0:T(8,128)S(1)}, u32[]{:S(2)}, u32[]{:S(2)}) async-start(f32[8,256,128]{2,1,0:T(8,128)} %fusion.22), calls=%async_computation.8 | async-start | bytes 2097152 | tf_op jit(solution)/shard_map/all_to_all | solution.py:33
  158.1 15.2 %all-to-all-done.8 = f32[8,256,128]{2,1,0:T(8,128)S(1)} async-done(((f32[8,256,128]{2,1,0:T(8,128)}), f32[8,256,128]{2,1,0:T(8,128)S(1)}, u32[]{:S(2)}, u32[]{:S(2)}) %all-to-all-start.8) | async-done | bytes 1048608 | tf_op jit(solution)/shard_map/all_to_all | solution.py:33
  173.3 0.8 broadcast_in_dim.23
  174.0 3.8 %all-to-all-start.7 = ((f32[16,40,128]{2,1,0:T(8,128)}), f32[16,40,128]{2,1,0:T(8,128)S(1)}, u32[]{:S(2)}, u32[]{:S(2)}) async-start(f32[16,40,128]{2,1,0:T(8,128)} %broadcast_in_dim.23), calls=%async_computation.7 | async-start | bytes 655360 | tf_op jit(solution)/shard_map/all_to_all | solution.py:33
  177.9 0.8 copy.23.speeds_ref
  178.6 1.8 slice.340.transport_ref
  181.1 5.2 %all-to-all-done.7.pieces_ref = f32[16,40,128]{2,1,0:T(8,128)S(1)} async-done(((f32[16,40,128]{2,1,0:T(8,128)}), f32[16,40,128]{2,1,0:T(8,128)S(1)}, u32[]{:S(2)}, u32[]{:S(2)}) %all-to-all-start.7) | async-done | bytes 327712 | tf_op jit(solution)/shard_map/all_to_all | solution.py:33
  187.0 8.8 %middle.1 = (f32[64,128]{1,0:T(8,128)}, f32[256,128]{1,0:T(8,128)}, f32[128,128]{1,0:T(8,128)}) custom-call(f32[16,40,128]{2,1,0:T(8,128)} %copy-done.3, f32[16,48,128]{2,1,0:T(8,128)} %slice.340.transport_ref, f32[256,128]{1,0:T(8,128)} %basis_ref.1, f32[256,128]{1,0:T(8,128)} %reduce_sum.59.back_ref, f32[64,128]{1,0:T(8,128)} %get-tuple-element.11.advanced_ref, ...), custom_call_target="tpu_custom_call" | custom-call | tf_op jit(solution)/shard_map/middle/pallas_call | solution.py:392
  195.8 1.5 collective-permute-done.3
  197.3 0.8 add.345
  198.7 1.7 collective-permute-start.6
  200.4 1.3 collective-permute-start.4
  201.7 2.6 %collective-permute-done.5 = f32[128,128]{1,0:T(8,128)S(1)} collective-permute-done((f32[128,128]{1,0:T(8,128)S(1)}, f32[128,128]{1,0:T(8,128)S(1)}, u32[]{:S(2)}, u32[]{:S(2)}) %collective-permute-start.5) | collective-permute-done | bytes 65568 | tf_op jit(solution)/shard_map/ppermute | solution.py:60
  204.3 1.0 collective-permute-done.6
  205.3 1.5 collective-permute-start.8
  206.8 1.9 collective-permute-start.9
  208.9 2.4 %collective-permute-done.8 = f32[128,128]{1,0:T(8,128)S(1)} collective-permute-done((f32[128,128]{1,0:T(8,128)S(1)}, f32[128,128]{1,0:T(8,128)S(1)}, u32[]{:S(2)}, u32[]{:S(2)}) %collective-permute-start.8) | collective-permute-done | bytes 65568 | tf_op jit(solution)/shard_map/ppermute | solution.py:60
  211.2 1.1 collective-permute-done.9
  213.0 0.9 collective-permute-start.11
  213.9 1.7 collective-permute-start.12
  215.6 0.9 collective-permute-start.10
  216.5 2.5 %collective-permute-done.11 = f32[128,128]{1,0:T(8,128)S(1)} collective-permute-done((f32[128,128]{1,0:T(8,128)S(1)}, f32[128,128]{1,0:T(8,128)S(1)}, u32[]{:S(2)}, u32[]{:S(2)}) %collective-permute-start.11) | collective-permute-done | bytes 65568 | tf_op jit(solution)/shard_map/ppermute | solution.py:60
  220.5 5.4 %last.1 = (f32[128,128]{1,0:T(8,128)}, f32[256,128]{1,0:T(8,128)}) custom-call(f32[128,128]{1,0:T(8,128)} %add_add_fusion.gram_ref, f32[256,128]{1,0:T(8,128)} %get-tuple-element.14.velocity_ref), custom_call_target="tpu_custom_call" | custom-call | tf_op jit(solution)/shard_map/last/pallas_call | solution.py:401
  (102 shorter events, 16.3 us)
Async XLA Ops:
  0.6 42.7 %copy-start.4 = (f32[256,128]{1,0:T(8,128)S(1)}, f32[256,128]{1,0:T(8,128)}, u32[]{:S(2)}) copy-start(f32[256,128]{1,0:T(8,128)} %basis_ref.1) | copy-start | bytes 393220
  2.3 17.7 %all-to-all-start.1 = ((f32[16,64,128]{2,1,0:T(8,128)}), f32[16,64,128]{2,1,0:T(8,128)S(1)}, u32[]{:S(2)}, u32[]{:S(2)}) async-start(f32[16,64,128]{2,1,0:T(8,128)} %broadcast_in_dim.18), calls=%async_computation.1 | async-start | bytes 1048576 | tf_op jit(solution)/shard_map/all_to_all | solution.py:33
  9.5 81.4 %collective-permute-start.1 = (f32[1,2,16,128]{3,2,1,0:T(8,128)S(1)}, f32[1,2,16,128]{3,2,1,0:T(8,128)S(1)}, u32[]{:S(2)}, u32[]{:S(2)}) collective-permute-start(f32[1,2,16,128]{3,2,1,0:T(8,128)S(1)} %get-tuple-element.42), channel_id=1, source_target_pairs={{0,112},{16,0},{32,16},{48,32},{64,48},{80,64},{96,80},{112,96},{1... | collective-permute-start | bytes 49160 | tf_op jit(solution)/shard_map/ppermute | solution.py:290
  14.6 76.3 %collective-permute-start = (f32[1,2,16,128]{3,2,1,0:T(8,128)S(1)}, f32[1,2,16,128]{3,2,1,0:T(8,128)S(1)}, u32[]{:S(2)}, u32[]{:S(2)}) collective-permute-start(f32[1,2,16,128]{3,2,1,0:T(8,128)S(1)} %get-tuple-element.41), channel_id=1, source_target_pairs={{0,16},{16,32},{32,48},{48,64},{64,80},{80,96},{96,112},{112,0},{1... | collective-permute-start | bytes 49160 | tf_op jit(solution)/shard_map/ppermute | solution.py:289
  20.8 22.5 %all-to-all-start = ((f32[128,8,128]{2,1,0:T(8,128)}), f32[128,8,128]{2,1,0:T(8,128)S(1)}, u32[]{:S(2)}, u32[]{:S(2)}) async-start(f32[128,8,128]{2,1,0:T(8,128)} %broadcast_in_dim.16), calls=%async_computation | async-start | bytes 1048576 | tf_op jit(solution)/shard_map/all_to_all | solution.py:33
  44.3 20.5 %all-to-all-start.2 = ((f32[8,256,128]{2,1,0:T(8,128)}), f32[8,256,128]{2,1,0:T(8,128)S(1)}, u32[]{:S(2)}, u32[]{:S(2)}) async-start(f32[8,256,128]{2,1,0:T(8,128)} %broadcast_in_dim.19), calls=%async_computation.2 | async-start | bytes 2097152 | tf_op jit(solution)/shard_map/all_to_all | solution.py:33
  64.8 1.0 copy-start
  69.6 14.5 %all-to-all-start.3 = ((f32[16,48,128]{2,1,0:T(8,128)}), f32[16,48,128]{2,1,0:T(8,128)S(1)}, u32[]{:S(2)}, u32[]{:S(2)}) async-start(f32[16,48,128]{2,1,0:T(8,128)} %transport.1), calls=%async_computation.3 | async-start | bytes 786432 | tf_op jit(solution)/shard_map/all_to_all | solution.py:33
  82.7 8.2 %copy-start.2 = (f32[2,2,16,128]{3,2,1,0:T(8,128)S(1)}, f32[2,2,16,128]{3,2,1,0:T(8,128)}, u32[]{:S(2)}) copy-start(f32[2,2,16,128]{3,2,1,0:T(8,128)} %param.2) | copy-start | bytes 98308
  85.2 20.8 %all-to-all-start.4 = ((f32[16,112,128]{2,1,0:T(8,128)}), f32[16,112,128]{2,1,0:T(8,128)S(1)}, u32[]{:S(2)}, u32[]{:S(2)}) async-start(f32[16,112,128]{2,1,0:T(8,128)} %pad_maximum_fusion), calls=%async_computation.4 | async-start | bytes 1835008 | tf_op jit(solution)/shard_map/all_to_all | solution.py:33
  91.0 15.0 %copy-start.5 = (f32[6,64,128]{2,1,0:T(8,128)}, f32[6,64,128]{2,1,0:T(8,128)S(1)}, u32[]{:S(2)}) copy-start(f32[6,64,128]{2,1,0:T(8,128)S(1)} %constant_dynamic-update-slice_fusion.steps_ref) | copy-start | bytes 589828
  106.0 0.9 copy-start.1
  109.9 15.2 %all-to-all-start.5 = ((f32[16,72,128]{2,1,0:T(8,128)}), f32[16,72,128]{2,1,0:T(8,128)S(1)}, u32[]{:S(2)}, u32[]{:S(2)}) async-start(f32[16,72,128]{2,1,0:T(8,128)} %get-tuple-element.10), calls=%async_computation.5 | async-start | bytes 1179648 | tf_op jit(solution)/shard_map/all_to_all | solution.py:33
  126.1 13.1 %collective-permute-start.2 = (f32[8,512]{1,0:T(8,128)S(1)}, f32[8,512]{1,0:T(8,128)S(1)}, u32[]{:S(2)}, u32[]{:S(2)}) collective-permute-start(f32[8,512]{1,0:T(8,128)S(1)} %fusion.58), channel_id=1, source_target_pairs={{0,16},{16,32},{32,48},{48,64},{64,80},{80,96},{96,112},{112,0},{1... | collective-permute-start | bytes 49160 | tf_op jit(solution)/shard_map/ppermute | solution.py:359
  140.2 14.3 %all-to-all-start.6 = ((f32[8,40,128]{2,1,0:T(8,128)}), f32[8,40,128]{2,1,0:T(8,128)S(1)}, u32[]{:S(2)}, u32[]{:S(2)}) async-start(f32[8,40,128]{2,1,0:T(8,128)} %broadcast_in_dim.22), calls=%async_computation.6 | async-start | bytes 327680 | tf_op jit(solution)/shard_map/all_to_all | solution.py:33
  154.5 18.8 %all-to-all-start.8 = ((f32[8,256,128]{2,1,0:T(8,128)}), f32[8,256,128]{2,1,0:T(8,128)S(1)}, u32[]{:S(2)}, u32[]{:S(2)}) async-start(f32[8,256,128]{2,1,0:T(8,128)} %fusion.22), calls=%async_computation.8 | async-start | bytes 2097152 | tf_op jit(solution)/shard_map/all_to_all | solution.py:33
  174.0 12.3 %all-to-all-start.7 = ((f32[16,40,128]{2,1,0:T(8,128)}), f32[16,40,128]{2,1,0:T(8,128)S(1)}, u32[]{:S(2)}, u32[]{:S(2)}) async-start(f32[16,40,128]{2,1,0:T(8,128)} %broadcast_in_dim.23), calls=%async_computation.7 | async-start | bytes 655360 | tf_op jit(solution)/shard_map/all_to_all | solution.py:33
  186.3 0.7 copy-start.3
  195.8 1.5 collective-permute-start.3
  198.1 6.1 %collective-permute-start.5 = (f32[128,128]{1,0:T(8,128)S(1)}, f32[128,128]{1,0:T(8,128)S(1)}, u32[]{:S(2)}, u32[]{:S(2)}) collective-permute-start(f32[128,128]{1,0:T(8,128)S(1)} %add.345), channel_id=1, source_target_pairs={{0,4},{1,5},{2,6},{3,7},{4,0},{5,1},{6,2},{7,3},{8,12},{9,13},{10,... | collective-permute-start | bytes 196616 | tf_op jit(solution)/shard_map/ppermute | solution.py:60
  198.7 6.6 %collective-permute-start.6 = (f32[128,128]{1,0:T(8,128)S(1)}, f32[128,128]{1,0:T(8,128)S(1)}, u32[]{:S(2)}, u32[]{:S(2)}) collective-permute-start(f32[128,128]{1,0:T(8,128)S(1)} %add.345), channel_id=1, source_target_pairs={{0,6},{1,7},{2,4},{3,5},{4,2},{5,3},{6,0},{7,1},{8,14},{9,15},{10,... | collective-permute-start | bytes 196616 | tf_op jit(solution)/shard_map/ppermute | solution.py:60
  200.4 4.9 %collective-permute-start.4 = (f32[128,128]{1,0:T(8,128)S(1)}, f32[128,128]{1,0:T(8,128)S(1)}, u32[]{:S(2)}, u32[]{:S(2)}) collective-permute-start(f32[128,128]{1,0:T(8,128)S(1)} %add.345), channel_id=1, source_target_pairs={{0,2},{1,3},{2,0},{3,1},{4,6},{5,7},{6,4},{7,5},{8,10},{9,11},{10,... | collective-permute-start | bytes 196616 | tf_op jit(solution)/shard_map/ppermute | solution.py:60
  205.3 6.0 %collective-permute-start.8 = (f32[128,128]{1,0:T(8,128)S(1)}, f32[128,128]{1,0:T(8,128)S(1)}, u32[]{:S(2)}, u32[]{:S(2)}) collective-permute-start(f32[128,128]{1,0:T(8,128)S(1)} %add_add_fusion.2), channel_id=1, source_target_pairs={{0,16},{1,17},{2,18},{3,19},{4,20},{5,21},{6,22},{7,23},{8,24},{9,... | collective-permute-start | bytes 196616 | tf_op jit(solution)/shard_map/ppermute | solution.py:60
  206.8 5.6 %collective-permute-start.9 = (f32[128,128]{1,0:T(8,128)S(1)}, f32[128,128]{1,0:T(8,128)S(1)}, u32[]{:S(2)}, u32[]{:S(2)}) collective-permute-start(f32[128,128]{1,0:T(8,128)S(1)} %add_add_fusion.2), channel_id=1, source_target_pairs={{0,24},{1,25},{2,26},{3,27},{4,28},{5,29},{6,30},{7,31},{8,16},{9,... | collective-permute-start | bytes 196616 | tf_op jit(solution)/shard_map/ppermute | solution.py:60
  208.7 4.3 %collective-permute-start.7 = (f32[128,128]{1,0:T(8,128)S(1)}, f32[128,128]{1,0:T(8,128)S(1)}, u32[]{:S(2)}, u32[]{:S(2)}) collective-permute-start(f32[128,128]{1,0:T(8,128)S(1)} %add_add_fusion.2), channel_id=1, source_target_pairs={{0,8},{1,9},{2,10},{3,11},{4,12},{5,13},{6,14},{7,15},{8,0},{9,1},... | collective-permute-start | bytes 196616 | tf_op jit(solution)/shard_map/ppermute | solution.py:60
  213.0 6.0 %collective-permute-start.11 = (f32[128,128]{1,0:T(8,128)S(1)}, f32[128,128]{1,0:T(8,128)S(1)}, u32[]{:S(2)}, u32[]{:S(2)}) collective-permute-start(f32[128,128]{1,0:T(8,128)S(1)} %add_add_fusion.1), channel_id=1, source_target_pairs={{0,64},{1,65},{2,66},{3,67},{4,68},{5,69},{6,70},{7,71},{8,72},{9,... | collective-permute-start | bytes 196616 | tf_op jit(solution)/shard_map/ppermute | solution.py:60
  213.9 5.8 %collective-permute-start.12 = (f32[128,128]{1,0:T(8,128)S(1)}, f32[128,128]{1,0:T(8,128)S(1)}, u32[]{:S(2)}, u32[]{:S(2)}) collective-permute-start(f32[128,128]{1,0:T(8,128)S(1)} %add_add_fusion.1), channel_id=1, source_target_pairs={{0,96},{1,97},{2,98},{3,99},{4,100},{5,101},{6,102},{7,103},{8,104... | collective-permute-start | bytes 196616 | tf_op jit(solution)/shard_map/ppermute | solution.py:60
  215.6 4.3 %collective-permute-start.10 = (f32[128,128]{1,0:T(8,128)S(1)}, f32[128,128]{1,0:T(8,128)S(1)}, u32[]{:S(2)}, u32[]{:S(2)}) collective-permute-start(f32[128,128]{1,0:T(8,128)S(1)} %add_add_fusion.1), channel_id=1, source_target_pairs={{0,32},{1,33},{2,34},{3,35},{4,36},{5,37},{6,38},{7,39},{8,40},{9,... | collective-permute-start | bytes 196616 | tf_op jit(solution)/shard_map/ppermute | solution.py:60
where the time goes:
time: 227 us; the launch traced here: 226 us
  waiting for transfers between devices  97.5 us (43%)
  starting transfers between devices  61.9 us (27%)
  local copies, waits for them, and re-layouts  27.1 us (12%)
  Pallas kernels  20.9 us (9%)
  matrix products  10.3 us (5%)
  other arithmetic  6.94 us (3%)
    all_to_all x9, waiting for transfers between devices, exchange(): return lax.all_to_all(array, axis, 0, 0, tiled=True)  85.1 us
    all_to_all x9, starting transfers between devices, exchange(): return lax.all_to_all(array, axis, 0, 0, tiled=True)  44.9 us
    unnamed x34, local copies, waits for them, and re-layouts  13.1 us
    ppermute x10, waiting for transfers between devices, from_peer(): return lax.ppermute(values, ('slab', 'brick'), pairs)  12.5 us
    ppermute x10, starting transfers between devices, from_peer(): return lax.ppermute(values, ('slab', 'brick'), pairs)  10.7 us
    dot_general x10, matrix products, contract(): lax.dot_general(left, right, (((left_dim,), (right_dim,)), ((), ())), pre...  10.3 us
    pallas_call x1, Pallas kernels, local(): pl.pallas_call(functools.partial(middle_kernel, lengths=lengths, time_ste...  8.78 us
    pallas_call x1, Pallas kernels, local(): pl.pallas_call(last_kernel, out_shape=(f32(rank, rank), f32(rows, rank)),...  5.44 us
  transfers between devices with their start and end apart: 22, of which 17 were waited for; matrix products, arithmetic and copies ran while one was open for 16% of the time, Pallas kernels for 2%

commit v1 on v0

--- a/solution.py
+++ b/solution.py
@@ -51,26 +51,33 @@
     return density, drift, temper
 
 
-def sum_over_devices(array):
-    slabs, bricks = lax.axis_size("slab"), lax.axis_size("brick")
-    devices = slabs * bricks
-
-    def from_peer(values, mask):
-        pairs = [(i, i ^ mask) for i in range(devices)]
-        return lax.ppermute(values, ("slab", "brick"), pairs)
-
-    step = 1
-    array = array + from_peer(array, step)
-    step = 2
-    while step < devices:
-        if step * 4 <= devices:
-            one, two, three = (from_peer(array, step * k) for k in (1, 2, 3))
-            array = (array + one) + (two + three)
-            step *= 4
-        else:
-            array = array + from_peer(array, step)
-            step *= 2
+def from_peer(values, axis, mask):
+    return lax.ppermute(values, axis, [(i, i ^ mask) for i in range(lax.axis_size(axis))])
+
+
+def sum_over(array, axis, groups):
+    for masks in groups:
+        parts = [array] + [from_peer(array, axis, mask) for mask in masks]
+        array = sum_pairs(parts)
     return array
+
+
+def sum_pairs(parts):
+    if len(parts) == 1:
+        return parts[0]
+    half = len(parts) // 2
+    return sum_pairs(parts[:half]) + sum_pairs(parts[half:])
+
+
+def gather_relative(array, axis, groups):
+    array = array[None]
+    for masks in groups:
+        array = jnp.concatenate([array] + [from_peer(array, axis, mask) for mask in masks], axis=0)
+    return array
+
+
+BRICK_GROUPS = ((1,), (2, 4, 6), (8,))
+SLAB_GROUPS = ((1,), (2, 4, 6))
 
 
 def three_parts(array):
@@ -133,11 +140,12 @@
             work_ref[stop:, :] = work_ref[stop:, :] - update[stop:, :]
 
 
-def transport_kernel(nodes_ref, columns_ref, speeds_ref, out_ref):
+def transport_kernel(nodes_ref, columns_ref, speeds_ref, weights_ref, out_ref, vectors_ref):
     groups, rows, rank = nodes_ref.shape
     bricks = out_ref.shape[0]
     factors = [jnp.broadcast_to(columns_ref[:, i : i + 1], (rows, rank)) for i in range(4)]
     sums = [jnp.zeros((rank, rank), jnp.float32) for _ in range(6)]
+    vectors = jnp.zeros(vectors_ref.shape, jnp.float32)
     for group in range(groups):
         nodes = nodes_ref[group]
         weighted = jnp.concatenate([nodes] + [nodes * factor for factor in factors], axis=1)
@@ -149,17 +157,81 @@
             (((0,), (0,)), ((), ())),
             preferred_element_type=jnp.float32,
         )
+        vectors = vectors + contract(weights_ref[group], nodes, 1, 0)
         plain = product[:, :rank]
         speed = jnp.broadcast_to(speeds_ref[group : group + 1, :], (rank, rank))
         sums[0] = sums[0] + jnp.maximum(speed, 0.0) * plain
         sums[1] = sums[1] + jnp.minimum(speed, 0.0) * plain
         for i in range(4):
             sums[2 + i] = sums[2 + i] + product[:, (i + 1) * rank : (i + 2) * rank]
+    vectors_ref[...] = vectors * WEIGHT_V
     height = rank // bricks
     for i in range(6):
         out_ref[:, i * height : (i + 1) * height, :] = (sums[i] * WEIGHT_V).reshape(
             bricks, height, rank
         )
+
+
+def maxwell_kernel(
+    brick_ref, cells_ref, vectors_ref, nodes_ref, first_ref, across_ref, part_ref, line_ref, state_ref
+):
+    bricks, cells, rank = cells_ref.shape
+    groups, rows, _ = nodes_ref.shape
+    total = bricks * cells
+    brick = brick_ref[0]
+    k_flat = jnp.concatenate([cells_ref[i ^ brick] for i in range(bricks)], axis=0)
+    moments = contract(vectors_ref[...], k_flat, 1, 1)
+    density, drift, temper = cell_state([moments[i : i + 1] for i in range(5)])
+    slope = -0.5 / temper
+    amplitude = density * jnp.exp(-1.5 * jnp.log(2.0 * math.pi * temper))
+    first = jnp.broadcast_to(first_ref[:, :1], (groups, total))
+    line = amplitude * jnp.exp((first - drift[0]) ** 2 * slope)
+    state = jnp.concatenate([drift[1], drift[2], slope] + [amplitude] * 5, axis=0)
+    state_ref[...] = state
+    both = jnp.concatenate([line, state], axis=0).T
+    line_cols = both[:, :groups]
+    line_ref[...] = line_cols
+    distance = (across_ref[0:1, :] - both[:, groups : groups + 1]) ** 2
+    distance = distance + (across_ref[1:2, :] - both[:, groups + 1 : groups + 2]) ** 2
+    high, low = two_parts(jnp.exp(distance * both[:, groups + 2 : groups + 3]))
+    lhs = jnp.concatenate([high, high, low], axis=1)
+    result = jnp.zeros((total, rank), jnp.float32)
+    for group in range(0, groups, 2):
+        node_high, node_low = two_parts(
+            jnp.concatenate([nodes_ref[group], nodes_ref[group + 1]], axis=1)
+        )
+        product = lax.dot_general(
+            lhs,
+            jnp.concatenate([node_high, node_low, node_high], axis=0),
+            (((1,), (0,)), ((), ())),
+            preferred_element_type=jnp.float32,
+        )
+        result = result + line_cols[:, group : group + 1] * product[:, :rank]
+        result = result + line_cols[:, group + 1 : group + 2] * product[:, rank:]
+    part_ref[...] = result.reshape(bricks, cells, rank)
+
+
+def back_kernel(parts_ref, line_ref, state_ref, across_ref, out_ref):
+    bricks, _, rank = parts_ref.shape
+    groups, rows, _ = out_ref.shape
+    total = line_ref.shape[0]
+    cells = total // bricks
+    advanced = parts_ref[:, :cells, :].reshape(total, rank)
+    distance = (across_ref[:, 0:1] - state_ref[0:1, :]) ** 2
+    distance = distance + (across_ref[:, 1:2] - state_ref[1:2, :]) ** 2
+    high, low = two_parts(jnp.exp(distance * state_ref[2:3, :]))
+    lhs = jnp.concatenate([high, high, low], axis=1)
+    for group in range(0, groups, 2):
+        scaled = [line_ref[:, i : i + 1] * advanced for i in (group, group + 1)]
+        part_high, part_low = two_parts(jnp.concatenate(scaled, axis=1))
+        product = lax.dot_general(
+            lhs,
+            jnp.concatenate([part_high, part_low, part_high], axis=0),
+            (((1,), (0,)), ((), ())),
+            preferred_element_type=jnp.float32,
+        )
+        out_ref[group] = product[:, :rank]
+        out_ref[group + 1] = product[:, rank:]
 
 
 def advance_kernel(parts_ref, steps_ref, cells_ref, payload_ref, advanced_ref, *, time_step):
@@ -183,6 +255,7 @@
 
 
 def middle_kernel(
+    brick_ref,
     pieces_ref,
     transport_ref,
     basis_ref,
@@ -203,9 +276,15 @@
     bricks, _, rank = pieces_ref.shape
     rows = basis_ref.shape[0]
     height = rank // bricks
+    cells = advanced_ref.shape[0]
+    brick = brick_ref[0]
 
     def piece(ref, i):
-        return ref[:, i * height : (i + 1) * height, :].reshape(rank, rank)
+        if ref is transport_ref:
+            start = cells + i * height
+            return ref[:, start : start + height, :].reshape(rank, rank)
+        rows_of = [ref[j ^ brick, i * height : (i + 1) * height, :] for j in range(bricks)]
+        return jnp.concatenate(rows_of, axis=0)
 
     factor_into(piece(pieces_ref, 0) * weight_x, work_ref, upper_ref, inverse_ref)
     upper, inverse = upper_ref[...], inverse_ref[...]
@@ -233,7 +312,10 @@
         plus = contract(now, turned[i], 1, 0)
         drift_sum = drift_sum + jnp.maximum(speed, 0.0) * (now - minus)
         drift_sum = drift_sum + jnp.minimum(speed, 0.0) * (plus - now)
-    back_proj = contract(back_ref[...] * weight_x, inverse, 1, 1)
+    back = back_ref[0]
+    for i in range(1, back_ref.shape[0]):
+        back = back + back_ref[i]
+    back_proj = contract(back * weight_x, inverse, 1, 1)
     updated = now - time_step * drift_sum + COLLIDE * (back_proj - now)
     velocity_ref[...] = updated
     gram_ref[...] = contract(updated, updated, 0, 0) * WEIGHT_V
@@ -274,18 +356,16 @@
     own_ids = (slab * bricks + brick) * rows + jnp.arange(rows, dtype=jnp.int32)
     own_velocity = velocities(own_ids)
     ones = jnp.ones_like(own_velocity[0])
+    slab_owner = jnp.arange(slabs, dtype=jnp.int32)[:, None] * bricks + brick
+    slab_velocity = velocities(slab_owner * rows + jnp.arange(rows, dtype=jnp.int32)[None])
     weights = jnp.stack(
-        [ones, own_velocity[0], own_velocity[1], own_velocity[2]]
-        + [jnp.sum(own_velocity * own_velocity, axis=0)]
-        + [jnp.zeros_like(ones)] * 3
-    )
-    vectors_part = contract(weights, v_basis, 1, 0) * WEIGHT_V
-    vectors_all = exchange(
-        jnp.broadcast_to(vectors_part[None], (devices, 8, rank)), ("slab", "brick")
+        [jnp.ones_like(slab_velocity[0]), slab_velocity[0], slab_velocity[1], slab_velocity[2]]
+        + [jnp.sum(slab_velocity * slab_velocity, axis=0)]
+        + [jnp.zeros_like(slab_velocity[0])] * 3,
+        axis=1,
     )
     nodes = to_all(v_basis, "slab")
-    k_slab = to_all(own_cells, "brick")
-    vectors = jnp.sum(vectors_all, axis=0)
+    k_slab = gather_relative(own_cells, "brick", BRICK_GROUPS)
     k_below = lax.ppermute(k_coeffs[-1:], "slab", up)
     k_above = lax.ppermute(k_coeffs[:1], "slab", down)
 
@@ -294,40 +374,37 @@
     columns = jnp.stack(columns + [jnp.zeros_like(ones)] * 4, axis=1)
     owner = jnp.arange(slabs, dtype=jnp.int32) * bricks + brick
     first_velocity = velocities(owner * rows)[0]
-    transport_part = pl.pallas_call(
-        transport_kernel, out_shape=f32(bricks, 6 * height, rank), name="transport"
-    )(nodes, columns, jnp.broadcast_to(first_velocity[:, None], (slabs, rank)))
+    first_speeds = jnp.broadcast_to(first_velocity[:, None], (slabs, rank))
+    transport_part, vectors_part = pl.pallas_call(
+        transport_kernel,
+        out_shape=(f32(bricks, 6 * height, rank), f32(8, rank)),
+        name="transport",
+    )(nodes, columns, first_speeds, weights)
+    vectors = sum_over(vectors_part, "brick", BRICK_GROUPS)
     transport_slice = jnp.sum(exchange(transport_part, "brick"), axis=0)
 
-    k_flat = k_slab.reshape(slab_cells, rank)
-    moments = contract(vectors, k_flat, 1, 1)
-    density, drift, temper = cell_state([moments[i : i + 1] for i in range(5)])
-    distance = (across[1][:, None] - drift[1]) ** 2 + (across[2][:, None] - drift[2]) ** 2
-    plane = jnp.exp(distance * (-0.5 / temper))
-    moments = contract(k_flat, vectors, 1, 1)
-    density, drift, temper = cell_state([moments[:, i : i + 1] for i in range(5)])
-    amplitude = density * (2.0 * math.pi * temper) ** (-1.5)
-    line = amplitude * jnp.exp((first_velocity[None, :] - drift[0]) ** 2 * (-0.5 / temper))
-
-    node_columns = jnp.concatenate([nodes[i] for i in range(slabs)], axis=1)
-    planes = contract(plane, node_columns, 0, 0, FINE)
-    mproj_part = sum(
-        line[:, i : i + 1] * planes[:, i * rank : (i + 1) * rank] for i in range(slabs)
-    )
+    brick_id = brick.astype(jnp.int32)[None]
+    vector_specs = [pl.BlockSpec(memory_space=pltpu.SMEM)]
+    whole = pl.BlockSpec(memory_space=pltpu.VMEM)
+    mproj_part, line, state = pl.pallas_call(
+        maxwell_kernel,
+        out_shape=(f32(bricks, cells, rank), f32(slab_cells, slabs), f32(8, slab_cells)),
+        in_specs=vector_specs + [whole] * 5,
+        name="maxwell",
+    )(brick_id, k_slab, vectors, nodes, first_speeds, across[1:])
     second = exchange(
         jnp.concatenate(
-            [
-                mproj_part.reshape(bricks, cells, rank),
-                jnp.broadcast_to(transport_slice[None], (bricks, 6 * height, rank)),
-            ],
+            [mproj_part, jnp.broadcast_to(transport_slice[None], (bricks, 6 * height, rank))],
             axis=1,
         ),
         "brick",
     )
 
     slab_grid = k_slab.reshape(bricks, cells_x, cells_y, cells_z, rank)
-    left = lax.dynamic_index_in_dim(slab_grid, (brick - 1) % bricks, 0, keepdims=False)
-    right = lax.dynamic_index_in_dim(slab_grid, (brick + 1) % bricks, 0, keepdims=False)
+    left = ((brick - 1) % bricks) ^ brick
+    right = ((brick + 1) % bricks) ^ brick
+    left = lax.dynamic_index_in_dim(slab_grid, left, 0, keepdims=False)
+    right = lax.dynamic_index_in_dim(slab_grid, right, 0, keepdims=False)
     lower = [
         jnp.concatenate([k_below, k_coeffs[:-1]], axis=0),
         jnp.concatenate([left[:, -1:], k_coeffs[:, :-1]], axis=1),
@@ -379,14 +456,13 @@
         ],
         axis=0,
     )
-    reduced = to_all(jnp.sum(to_all(pieces, "slab"), axis=0), "brick")
-
-    scaled = jnp.concatenate([line[:, i : i + 1] * adv_flat for i in range(slabs)], axis=1)
-    back = contract(plane, scaled, 1, 0, FINE)
-    fourth = exchange(
-        jnp.stack([back[:, i * rank : (i + 1) * rank] for i in range(slabs)]), "slab"
-    )
-    back_own = jnp.sum(fourth, axis=0)
+    pieces = sum_over(pieces, "slab", SLAB_GROUPS)
+    reduced = gather_relative(pieces, "brick", BRICK_GROUPS)
+
+    back = pl.pallas_call(back_kernel, out_shape=f32(slabs, rows, rank), name="back")(
+        third, line, state, across[1:].T
+    )
+    fourth = exchange(back, "slab")
 
     speeds = jnp.stack(list(own_velocity) + [jnp.zeros_like(ones)] * 5, axis=1)
     basis_new, velocity_new, gram_part = pl.pallas_call(
@@ -394,10 +470,11 @@
             middle_kernel, lengths=lengths, time_step=time_step, weight_x=weight_x
         ),
         out_shape=(f32(cells, rank), f32(rows, rank), f32(rank, rank)),
+        in_specs=vector_specs + [whole] * 6,
         scratch_shapes=factor_scratch(rank),
         name="middle",
-    )(reduced, second[:, cells:], v_basis, back_own, advanced, speeds)
-    gram_v = sum_over_devices(gram_part)
+    )(brick_id, reduced, second, v_basis, fourth, advanced, speeds)
+    gram_v = sum_over(sum_over(gram_part, "brick", BRICK_GROUPS), "slab", SLAB_GROUPS)
     coupling, vbasis_new = pl.pallas_call(
         last_kernel,
         out_shape=(f32(rank, rank), f32(rows, rank)),

time: 227 us -> 192 us (0.85)
  waiting for transfers between devices: 97.5 us -> 74.6 us
  local copies, waits for them, and re-layouts: 27.1 us -> 11.5 us
  Pallas kernels: 20.9 us -> 31.9 us
  matrix products: 10.3 us -> 4.12 us
  other arithmetic: 6.94 us -> 4.11 us
    all_to_all x9 -> x5, waiting for transfers between devices: 85.1 us -> 29.5 us  [exchange(): return lax.all_to_all(array, axis, 0, 0, tiled=True)]
    ppermute x10 -> x28, waiting for transfers between devices: 12.5 us -> 39.6 us  [from_peer(): lax.ppermute(values, axis, [(i, i ^ mask) for i in range(lax.axis_size(ax...]
    ppermute x10 -> x28, starting transfers between devices: 10.7 us -> 33.9 us  [from_peer(): lax.ppermute(values, axis, [(i, i ^ mask) for i in range(lax.axis_size(ax...]
    all_to_all x9 -> x5, starting transfers between devices: 44.9 us -> 22.5 us  [exchange(): return lax.all_to_all(array, axis, 0, 0, tiled=True)]
    pallas_call x1 -> x3, Pallas kernels: 3.8 us -> 14.4 us  [the longest x1 5.02 us: local(): pl.pallas_call(maxwell_kernel, out_shape=(f32(bricks, cells, rank), f32(s...]
    unnamed x34 -> x41, local copies, waits for them, and re-layouts: 13.1 us -> 3.35 us
    dot_general x10 -> x6, matrix products: 10.3 us -> 4.12 us  [contract(): lax.dot_general(left, right, (((left_dim,), (right_dim,)), ((), ())), pre...]
    ppermute x1, waiting for transfers between devices: 0.01 us -> 5.46 us  [local(): chosen_below = lax.ppermute(chosen, 'slab', up)]
  transfers between devices with their start and end apart: 22 -> 36, of which waited for: 17 -> 21; matrix products, arithmetic and copies ran while one was open for 16% -> 6% of each run, Pallas kernels for 2% -> 8%
where the time goes in v1:
time: 192 us; the launch traced here: 190 us
  waiting for transfers between devices  74.6 us (39%)
  starting transfers between devices  63 us (33%)
  Pallas kernels  31.9 us (17%)
  local copies, waits for them, and re-layouts  11.5 us (6%)
  matrix products  4.12 us (2%)
  other arithmetic  4.11 us (2%)
    ppermute x28, waiting for transfers between devices, from_peer(): lax.ppermute(values, axis, [(i, i ^ mask) for i in range(lax.axis_size(ax...  39.6 us
    ppermute x28, starting transfers between devices, from_peer(): lax.ppermute(values, axis, [(i, i ^ mask) for i in range(lax.axis_size(ax...  33.9 us
    all_to_all x5, waiting for transfers between devices, exchange(): return lax.all_to_all(array, axis, 0, 0, tiled=True)  29.5 us
    all_to_all x5, starting transfers between devices, exchange(): return lax.all_to_all(array, axis, 0, 0, tiled=True)  22.5 us
    pallas_call x1, Pallas kernels, local(): pl.pallas_call(functools.partial(middle_kernel, lengths=lengths, time_ste...  9.19 us
    ppermute x1, waiting for transfers between devices, local(): chosen_below = lax.ppermute(chosen, 'slab', up)  5.46 us
    pallas_call x1, Pallas kernels, local(): pl.pallas_call(last_kernel, out_shape=(f32(rank, rank), f32(rows, rank)),...  5.44 us
    pallas_call x1, Pallas kernels, local(): pl.pallas_call(maxwell_kernel, out_shape=(f32(bricks, cells, rank), f32(s...  5.02 us
  transfers between devices with their start and end apart: 36, of which 21 were waited for; matrix products, arithmetic and copies ran while one was open for 6% of the time, Pallas kernels for 8%

profile of v1, /device:TPU:0, one launch (start us, length us, event | category | flops | bytes accessed | tf_op | source)
XLA Modules:
  0.0 190.4 jit_solution(18344574356349792328)
XLA Ops:
  0.6 0.8 fusion.39
  1.4 3.1 %collective-permute-start.10 = (f32[1,2,16,128]{3,2,1,0:T(8,128)S(1)}, f32[1,2,16,128]{3,2,1,0:T(8,128)S(1)}, u32[]{:S(2)}, u32[]{:S(2)}) collective-permute-start(f32[1,2,16,128]{3,2,1,0:T(8,128)S(1)} %get-tuple-element.68), channel_id=1, source_target_pairs={{0,16},{16,32},{32,48},{48,64},{64,80},{80,96},{96,112},{112,0},{1... | collective-permute-start | bytes 49160 | tf_op jit(solution)/shard_map/ppermute | solution.py:369
  4.5 2.5 %collective-permute-start.11 = (f32[1,2,16,128]{3,2,1,0:T(8,128)S(1)}, f32[1,2,16,128]{3,2,1,0:T(8,128)S(1)}, u32[]{:S(2)}, u32[]{:S(2)}) collective-permute-start(f32[1,2,16,128]{3,2,1,0:T(8,128)S(1)} %get-tuple-element.69), channel_id=1, source_target_pairs={{0,112},{16,0},{32,16},{48,32},{64,48},{80,64},{96,80},{112,96},{1... | collective-permute-start | bytes 49160 | tf_op jit(solution)/shard_map/ppermute | solution.py:370
  7.1 2.0 %broadcast_in_dim.13 = f32[8,256,128]{2,1,0:T(8,128)} broadcast(f32[256,128]{1,0:T(8,128)} %basis_ref.1), dimensions={1,2} | broadcast | bytes 1179648 | tf_op jit(solution)/shard_map/broadcast_in_dim | solution.py:38
  9.0 4.9 %all-to-all-start = ((f32[8,256,128]{2,1,0:T(8,128)}), f32[8,256,128]{2,1,0:T(8,128)S(1)}, u32[]{:S(2)}, u32[]{:S(2)}) async-start(f32[8,256,128]{2,1,0:T(8,128)} %broadcast_in_dim.13), calls=%async_computation | async-start | bytes 2097152 | tf_op jit(solution)/shard_map/all_to_all | solution.py:33
  14.6 0.8 slice_bitcast_fusion.4
  15.8 0.8 copy.31.columns_ref
  17.2 0.7 stack.52.weights_ref
  18.0 4.1 %collective-permute-start.3 = (f32[2,64,128]{2,1,0:T(8,128)S(1)}, f32[2,64,128]{2,1,0:T(8,128)S(1)}, u32[]{:S(2)}, u32[]{:S(2)}) collective-permute-start(f32[2,64,128]{2,1,0:T(8,128)S(1)} %pad_maximum_fusion.3), channel_id=1, source_target_pairs={{0,6},{1,7},{2,4},{3,5},{4,2},{5,3},{6,0},{7,1},{8,14},{9,15},{10,... | collective-permute-start | bytes 196616 | tf_op jit(solution)/shard_map/ppermute | solution.py:55
  22.1 0.9 collective-permute-start.1
  23.0 3.6 %collective-permute-done.1 = f32[2,64,128]{2,1,0:T(8,128)S(1)} collective-permute-done((f32[2,64,128]{2,1,0:T(8,128)S(1)}, f32[2,64,128]{2,1,0:T(8,128)S(1)}, u32[]{:S(2)}, u32[]{:S(2)}) %collective-permute-start.1) | collective-permute-done | bytes 65568 | tf_op jit(solution)/shard_map/ppermute | solution.py:55
  26.7 1.5 collective-permute-done.2
  28.3 0.7 collective-permute-start.4
  29.0 2.9 %all-to-all-done.nodes_ref = f32[8,256,128]{2,1,0:T(8,128)S(1)} async-done(((f32[8,256,128]{2,1,0:T(8,128)}), f32[8,256,128]{2,1,0:T(8,128)S(1)}, u32[]{:S(2)}, u32[]{:S(2)}) %all-to-all-start) | async-done | bytes 1048608 | tf_op jit(solution)/shard_map/all_to_all | solution.py:33
  31.9 0.7 broadcast_in_dim.15.speeds_ref.first_ref
  32.9 4.4 %transport.1 = (f32[16,48,128]{2,1,0:T(8,128)}, f32[8,128]{1,0:T(8,128)}) custom-call(f32[8,256,128]{2,1,0:T(8,128)} %copy-done, f32[256,8]{1,0:T(8,128)} %copy.31.columns_ref, f32[8,128]{1,0:T(8,128)} %broadcast_in_dim.15.speeds_ref.first_ref, f32[8,8,256]{2,1,0:T(8,128)} %stack.52.weights_ref), custom_call_target="tpu_custom_call" | custom-call | tf_op jit(solution)/shard_map/transport/pallas_call | solution.py:378
  37.3 6.1 %all-to-all-start.1 = ((f32[16,48,128]{2,1,0:T(8,128)}), f32[16,48,128]{2,1,0:T(8,128)S(1)}, u32[]{:S(2)}, u32[]{:S(2)}) async-start(f32[16,48,128]{2,1,0:T(8,128)} %get-tuple-element.17), calls=%async_computation.1 | async-start | bytes 786432 | tf_op jit(solution)/shard_map/all_to_all | solution.py:33
  43.5 3.2 %collective-permute-start.8 = (f32[8,128]{1,0:T(8,128)S(1)}, f32[8,128]{1,0:T(8,128)S(1)}, u32[]{:S(2)}, u32[]{:S(2)}) collective-permute-start(f32[8,128]{1,0:T(8,128)S(1)} %add.407), channel_id=1, source_target_pairs={{0,6},{1,7},{2,4},{3,5},{4,2},{5,3},{6,0},{7,1},{8,14},{9,15},{10,... | collective-permute-start | bytes 12296 | tf_op jit(solution)/shard_map/ppermute | solution.py:55
  46.7 0.9 collective-permute-start.7
  47.7 3.7 %collective-permute-done.8 = f32[8,128]{1,0:T(8,128)S(1)} collective-permute-done((f32[8,128]{1,0:T(8,128)S(1)}, f32[8,128]{1,0:T(8,128)S(1)}, u32[]{:S(2)}, u32[]{:S(2)}) %collective-permute-start.8) | collective-permute-done | bytes 4128 | tf_op jit(solution)/shard_map/ppermute | solution.py:55
  51.9 2.1 %collective-permute-start.9 = (f32[8,128]{1,0:T(8,128)S(1)}, f32[8,128]{1,0:T(8,128)S(1)}, u32[]{:S(2)}, u32[]{:S(2)}) collective-permute-start(f32[8,128]{1,0:T(8,128)S(1)} %add_add_fusion.2), channel_id=1, source_target_pairs={{0,8},{1,9},{2,10},{3,11},{4,12},{5,13},{6,14},{7,15},{8,0},{9,1},... | collective-permute-start | bytes 12296 | tf_op jit(solution)/shard_map/ppermute | solution.py:55
  54.0 1.6 collective-permute-done.9
  56.2 5.0 %maxwell.1 = (f32[16,64,128]{2,1,0:T(8,128)}, f32[1024,8]{1,0:T(8,128)}, f32[8,1024]{1,0:T(8,128)}) custom-call(s32[1]{0:T(128)} %bitcast.brick_ref, f32[16,64,128]{2,1,0:T(8,128)} %copy-done.5, f32[8,128]{1,0:T(8,128)} %add.411.vectors_ref, f32[8,256,128]{2,1,0:T(8,128)} %copy-done, f32[8,128]{1,0:T(8,128)} %broadcast_in_dim.15.speeds_ref.first_ref, ...), custom_call_target="tpu_custom_call" | custom-call | tf_op jit(solution)/shard_map/maxwell/pallas_call | solution.py:389
  61.3 1.0 copy-done.6
  62.3 1.0 pad_maximum_fusion
  63.3 4.2 %all-to-all-start.2 = ((f32[16,112,128]{2,1,0:T(8,128)}), f32[16,112,128]{2,1,0:T(8,128)S(1)}, u32[]{:S(2)}, u32[]{:S(2)}) async-start(f32[16,112,128]{2,1,0:T(8,128)} %pad_maximum_fusion), calls=%async_computation.2 | async-start | bytes 1835008 | tf_op jit(solution)/shard_map/all_to_all | solution.py:33
  67.6 15.0 %all-to-all-done.2.parts_ref.transport_ref = f32[16,112,128]{2,1,0:T(8,128)S(1)} async-done(((f32[16,112,128]{2,1,0:T(8,128)}), f32[16,112,128]{2,1,0:T(8,128)S(1)}, u32[]{:S(2)}, u32[]{:S(2)}) %all-to-all-start.2) | async-done | bytes 917536 | tf_op jit(solution)/shard_map/all_to_all | solution.py:33
  82.6 0.9 copy-done.2
  83.6 2.9 %advance.1 = (f32[16,72,128]{2,1,0:T(8,128)}, f32[64,128]{1,0:T(8,128)}) custom-call(f32[16,112,128]{2,1,0:T(8,128)} %copy-done.2, f32[6,64,128]{2,1,0:T(8,128)} %copy-done.8, f32[64,128]{1,0:T(8,128)} %bitcast.82), custom_call_target="tpu_custom_call" | custom-call | tf_op jit(solution)/shard_map/advance/pallas_call | solution.py:422
  86.5 3.8 %all-to-all-start.3 = ((f32[16,72,128]{2,1,0:T(8,128)}), f32[16,72,128]{2,1,0:T(8,128)S(1)}, u32[]{:S(2)}, u32[]{:S(2)}) async-start(f32[16,72,128]{2,1,0:T(8,128)} %get-tuple-element.18), calls=%async_computation.3 | async-start | bytes 1179648 | tf_op jit(solution)/shard_map/all_to_all | solution.py:33
  90.3 11.4 %all-to-all-done.3.parts_ref = f32[16,72,128]{2,1,0:T(8,128)S(1)} async-done(((f32[16,72,128]{2,1,0:T(8,128)}), f32[16,72,128]{2,1,0:T(8,128)S(1)}, u32[]{:S(2)}, u32[]{:S(2)}) %all-to-all-start.3) | async-done | bytes 589856 | tf_op jit(solution)/shard_map/all_to_all | solution.py:33
  102.5 1.0 fusion.40
  103.6 1.0 fusion.41
  104.9 0.9 collective-permute-start.12
  105.8 1.0 convolution_bitcast_fusion
  106.8 5.5 %collective-permute-done.12 = f32[8,512]{1,0:T(8,128)S(1)} collective-permute-done((f32[8,512]{1,0:T(8,128)S(1)}, f32[8,512]{1,0:T(8,128)S(1)}, u32[]{:S(2)}, u32[]{:S(2)}) %collective-permute-start.12) | collective-permute-done | bytes 16416 | tf_op jit(solution)/shard_map/ppermute | solution.py:436
  112.6 5.2 %collective-permute-done.13 = f32[40,128]{1,0:T(8,128)S(1)} collective-permute-done((f32[40,128]{1,0:T(8,128)S(1)}, f32[40,128]{1,0:T(8,128)S(1)}, u32[]{:S(2)}, u32[]{:S(2)}) %collective-permute-start.13) | collective-permute-done | bytes 20512 | tf_op jit(solution)/shard_map/ppermute | solution.py:55
  118.1 0.7 collective-permute-start.15
  118.8 3.2 %collective-permute-start.14 = (f32[40,128]{1,0:T(8,128)S(1)}, f32[40,128]{1,0:T(8,128)S(1)}, u32[]{:S(2)}, u32[]{:S(2)}) collective-permute-start(f32[40,128]{1,0:T(8,128)S(1)} %add.421), channel_id=1, source_target_pairs={{0,32},{16,48},{32,0},{48,16},{64,96},{80,112},{96,64},{112,80},{1... | collective-permute-start | bytes 61448 | tf_op jit(solution)/shard_map/ppermute | solution.py:55
  122.1 4.9 %back.1 = f32[8,256,128]{2,1,0:T(8,128)} custom-call(f32[16,72,128]{2,1,0:T(8,128)} %copy-done.1, f32[1024,8]{1,0:T(8,128)} %get-tuple-element.19.line_ref, f32[8,1024]{1,0:T(8,128)} %get-tuple-element.20.state_ref, f32[256,2]{1,0:T(8,128)} %get-tuple-element.42.across_ref), custom_call_target="tpu_custom_call" | custom-call | tf_op jit(solution)/shard_map/back/pallas_call | solution.py:462
  127.1 3.6 %all-to-all-start.4 = ((f32[8,256,128]{2,1,0:T(8,128)}), f32[8,256,128]{2,1,0:T(8,128)S(1)}, u32[]{:S(2)}, u32[]{:S(2)}) async-start(f32[8,256,128]{2,1,0:T(8,128)} %back.1), calls=%async_computation.4 | async-start | bytes 2097152 | tf_op jit(solution)/shard_map/all_to_all | solution.py:33
  130.8 1.2 collective-permute-done.17
  132.0 0.9 collective-permute-start.20
  132.9 3.2 %collective-permute-start.18 = (f32[2,40,128]{2,1,0:T(8,128)S(1)}, f32[2,40,128]{2,1,0:T(8,128)S(1)}, u32[]{:S(2)}, u32[]{:S(2)}) collective-permute-start(f32[2,40,128]{2,1,0:T(8,128)S(1)} %pad_maximum_fusion.4), channel_id=1, source_target_pairs={{0,2},{1,3},{2,0},{3,1},{4,6},{5,7},{6,4},{7,5},{8,10},{9,11},{10,... | collective-permute-start | bytes 122888 | tf_op jit(solution)/shard_map/ppermute | solution.py:55
  136.1 2.4 %collective-permute-done.18 = f32[2,40,128]{2,1,0:T(8,128)S(1)} collective-permute-done((f32[2,40,128]{2,1,0:T(8,128)S(1)}, f32[2,40,128]{2,1,0:T(8,128)S(1)}, u32[]{:S(2)}, u32[]{:S(2)}) %collective-permute-start.18) | collective-permute-done | bytes 40992 | tf_op jit(solution)/shard_map/ppermute | solution.py:55
  138.5 0.8 collective-permute-start.21
  139.7 0.8 copy.36.speeds_ref
  140.5 3.7 %collective-permute-done.21 = f32[8,40,128]{2,1,0:T(8,128)S(1)} collective-permute-done((f32[8,40,128]{2,1,0:T(8,128)S(1)}, f32[8,40,128]{2,1,0:T(8,128)S(1)}, u32[]{:S(2)}, u32[]{:S(2)}) %collective-permute-start.21) | collective-permute-done | bytes 163872 | tf_op jit(solution)/shard_map/ppermute | solution.py:55
  145.4 9.2 %middle.1 = (f32[64,128]{1,0:T(8,128)}, f32[256,128]{1,0:T(8,128)}, f32[128,128]{1,0:T(8,128)}) custom-call(s32[1]{0:T(128)} %bitcast.brick_ref, f32[16,40,128]{2,1,0:T(8,128)} %copy-done.7, f32[16,112,128]{2,1,0:T(8,128)} %copy-done.2, f32[256,128]{1,0:T(8,128)} %basis_ref.1, f32[8,256,128]{2,1,0:T(8,128)} %copy-done.3, ...), custom_call_target="tpu_custom_call" | custom-call | tf_op jit(solution)/shard_map/middle/pallas_call | solution.py:468
  154.6 1.5 collective-permute-done.22
  156.1 0.9 add.432
  156.9 2.1 %collective-permute-start.25 = (f32[128,128]{1,0:T(8,128)S(1)}, f32[128,128]{1,0:T(8,128)S(1)}, u32[]{:S(2)}, u32[]{:S(2)}) collective-permute-start(f32[128,128]{1,0:T(8,128)S(1)} %add.432), channel_id=1, source_target_pairs={{0,6},{1,7},{2,4},{3,5},{4,2},{5,3},{6,0},{7,1},{8,14},{9,15},{10,... | collective-permute-start | bytes 196616 | tf_op jit(solution)/shard_map/ppermute | solution.py:55
  159.0 1.5 collective-permute-start.24
  161.1 1.4 collective-permute-done.25
  162.5 2.7 %collective-permute-done.24 = f32[128,128]{1,0:T(8,128)S(1)} collective-permute-done((f32[128,128]{1,0:T(8,128)S(1)}, f32[128,128]{1,0:T(8,128)S(1)}, u32[]{:S(2)}, u32[]{:S(2)}) %collective-permute-start.24) | collective-permute-done | bytes 65568 | tf_op jit(solution)/shard_map/ppermute | solution.py:55
  165.1 0.7 collective-permute-start.26
  165.9 3.6 %collective-permute-done.26 = f32[128,128]{1,0:T(8,128)S(1)} collective-permute-done((f32[128,128]{1,0:T(8,128)S(1)}, f32[128,128]{1,0:T(8,128)S(1)}, u32[]{:S(2)}, u32[]{:S(2)}) %collective-permute-start.26) | collective-permute-done | bytes 65568 | tf_op jit(solution)/shard_map/ppermute | solution.py:55
  169.5 3.7 %collective-permute-start.27 = (f32[128,128]{1,0:T(8,128)S(1)}, f32[128,128]{1,0:T(8,128)S(1)}, u32[]{:S(2)}, u32[]{:S(2)}) collective-permute-start(f32[128,128]{1,0:T(8,128)S(1)} %add.436), channel_id=1, source_target_pairs={{0,16},{16,0},{32,48},{48,32},{64,80},{80,64},{96,112},{112,96},{1... | collective-permute-start | bytes 196616 | tf_op jit(solution)/shard_map/ppermute | solution.py:55
  173.2 2.2 %collective-permute-done.27 = f32[128,128]{1,0:T(8,128)S(1)} collective-permute-done((f32[128,128]{1,0:T(8,128)S(1)}, f32[128,128]{1,0:T(8,128)S(1)}, u32[]{:S(2)}, u32[]{:S(2)}) %collective-permute-start.27) | collective-permute-done | bytes 65568 | tf_op jit(solution)/shard_map/ppermute | solution.py:55
  175.4 3.2 %collective-permute-start.30 = (f32[128,128]{1,0:T(8,128)S(1)}, f32[128,128]{1,0:T(8,128)S(1)}, u32[]{:S(2)}, u32[]{:S(2)}) collective-permute-start(f32[128,128]{1,0:T(8,128)S(1)} %add.437), channel_id=1, source_target_pairs={{0,96},{16,112},{32,64},{48,80},{64,32},{80,48},{96,0},{112,16},{1... | collective-permute-start | bytes 196616 | tf_op jit(solution)/shard_map/ppermute | solution.py:55
  178.6 0.8 collective-permute-start.29
  179.6 1.4 collective-permute-done.30
  181.0 3.4 %collective-permute-done.29 = f32[128,128]{1,0:T(8,128)S(1)} collective-permute-done((f32[128,128]{1,0:T(8,128)S(1)}, f32[128,128]{1,0:T(8,128)S(1)}, u32[]{:S(2)}, u32[]{:S(2)}) %collective-permute-start.29) | collective-permute-done | bytes 65568 | tf_op jit(solution)/shard_map/ppermute | solution.py:55
  185.0 5.4 %last.1 = (f32[128,128]{1,0:T(8,128)}, f32[256,128]{1,0:T(8,128)}) custom-call(f32[128,128]{1,0:T(8,128)} %add_add_fusion.gram_ref, f32[256,128]{1,0:T(8,128)} %get-tuple-element.24.velocity_ref), custom_call_target="tpu_custom_call" | custom-call | tf_op jit(solution)/shard_map/last/pallas_call | solution.py:478
  (135 shorter events, 8.4 us)
Async XLA Ops:
  0.6 6.4 %copy-start.4 = (f32[2,2,16,128]{3,2,1,0:T(8,128)S(1)}, f32[2,2,16,128]{3,2,1,0:T(8,128)}, u32[]{:S(2)}) copy-start(f32[2,2,16,128]{3,2,1,0:T(8,128)} %param.2) | copy-start | bytes 98308
  1.4 66.0 %collective-permute-start.10 = (f32[1,2,16,128]{3,2,1,0:T(8,128)S(1)}, f32[1,2,16,128]{3,2,1,0:T(8,128)S(1)}, u32[]{:S(2)}, u32[]{:S(2)}) collective-permute-start(f32[1,2,16,128]{3,2,1,0:T(8,128)S(1)} %get-tuple-element.68), channel_id=1, source_target_pairs={{0,16},{16,32},{32,48},{48,64},{64,80},{80,96},{96,112},{112,0},{1... | collective-permute-start | bytes 49160 | tf_op jit(solution)/shard_map/ppermute | solution.py:369
  4.5 62.9 %collective-permute-start.11 = (f32[1,2,16,128]{3,2,1,0:T(8,128)S(1)}, f32[1,2,16,128]{3,2,1,0:T(8,128)S(1)}, u32[]{:S(2)}, u32[]{:S(2)}) collective-permute-start(f32[1,2,16,128]{3,2,1,0:T(8,128)S(1)} %get-tuple-element.69), channel_id=1, source_target_pairs={{0,112},{16,0},{32,16},{48,32},{64,48},{80,64},{96,80},{112,96},{1... | collective-permute-start | bytes 49160 | tf_op jit(solution)/shard_map/ppermute | solution.py:370
  7.1 10.9 %collective-permute-start = (f32[1,64,128]{2,1,0:T(8,128)S(1)}, f32[1,64,128]{2,1,0:T(8,128)S(1)}, u32[]{:S(2)}, u32[]{:S(2)}) collective-permute-start(f32[1,64,128]{2,1,0:T(8,128)S(1)} %bitcast.83), channel_id=1, source_target_pairs={{0,1},{1,0},{2,3},{3,2},{4,5},{5,4},{6,7},{7,6},{8,9},{9,8},{10,11... | collective-permute-start | bytes 98312 | tf_op jit(solution)/shard_map/ppermute | solution.py:55
  9.0 22.8 %all-to-all-start = ((f32[8,256,128]{2,1,0:T(8,128)}), f32[8,256,128]{2,1,0:T(8,128)S(1)}, u32[]{:S(2)}, u32[]{:S(2)}) async-start(f32[8,256,128]{2,1,0:T(8,128)} %broadcast_in_dim.13), calls=%async_computation | async-start | bytes 2097152 | tf_op jit(solution)/shard_map/all_to_all | solution.py:33
  18.0 10.3 %collective-permute-start.3 = (f32[2,64,128]{2,1,0:T(8,128)S(1)}, f32[2,64,128]{2,1,0:T(8,128)S(1)}, u32[]{:S(2)}, u32[]{:S(2)}) collective-permute-start(f32[2,64,128]{2,1,0:T(8,128)S(1)} %pad_maximum_fusion.3), channel_id=1, source_target_pairs={{0,6},{1,7},{2,4},{3,5},{4,2},{5,3},{6,0},{7,1},{8,14},{9,15},{10,... | collective-permute-start | bytes 196616 | tf_op jit(solution)/shard_map/ppermute | solution.py:55
  22.1 6.2 %collective-permute-start.2 = (f32[2,64,128]{2,1,0:T(8,128)S(1)}, f32[2,64,128]{2,1,0:T(8,128)S(1)}, u32[]{:S(2)}, u32[]{:S(2)}) collective-permute-start(f32[2,64,128]{2,1,0:T(8,128)S(1)} %pad_maximum_fusion.3), channel_id=1, source_target_pairs={{0,4},{1,5},{2,6},{3,7},{4,0},{5,1},{6,2},{7,3},{8,12},{9,13},{10,... | collective-permute-start | bytes 196616 | tf_op jit(solution)/shard_map/ppermute | solution.py:55
  22.1 4.6 %collective-permute-start.1 = (f32[2,64,128]{2,1,0:T(8,128)S(1)}, f32[2,64,128]{2,1,0:T(8,128)S(1)}, u32[]{:S(2)}, u32[]{:S(2)}) collective-permute-start(f32[2,64,128]{2,1,0:T(8,128)S(1)} %pad_maximum_fusion.3), channel_id=1, source_target_pairs={{0,2},{1,3},{2,0},{3,1},{4,6},{5,7},{6,4},{7,5},{8,10},{9,11},{10,... | collective-permute-start | bytes 196616 | tf_op jit(solution)/shard_map/ppermute | solution.py:55
  28.3 9.0 %collective-permute-start.4 = (f32[8,64,128]{2,1,0:T(8,128)S(1)}, f32[8,64,128]{2,1,0:T(8,128)S(1)}, u32[]{:S(2)}, u32[]{:S(2)}) collective-permute-start(f32[8,64,128]{2,1,0:T(8,128)S(1)} %get-tuple-element.44), channel_id=1, source_target_pairs={{0,8},{1,9},{2,10},{3,11},{4,12},{5,13},{6,14},{7,15},{8,0},{9,1},... | collective-permute-start | bytes 786440 | tf_op jit(solution)/shard_map/ppermute | solution.py:55
  31.9 1.0 copy-start
  37.3 6.2 %collective-permute-start.5 = (f32[8,128]{1,0:T(8,128)}, f32[8,128]{1,0:T(8,128)S(1)}, u32[]{:S(2)}, u32[]{:S(2)}) collective-permute-start(f32[8,128]{1,0:T(8,128)} %get-tuple-element.15), channel_id=1, source_target_pairs={{0,1},{1,0},{2,3},{3,2},{4,5},{5,4},{6,7},{7,6},{8,9},{9,8},{10,11... | collective-permute-start | bytes 12296 | tf_op jit(solution)/shard_map/ppermute | solution.py:55
  37.3 6.2 %copy-start.9 = (f32[8,128]{1,0:T(8,128)S(1)}, f32[8,128]{1,0:T(8,128)}, u32[]{:S(2)}) copy-start(f32[8,128]{1,0:T(8,128)} %get-tuple-element.15) | copy-start | bytes 12292
  37.3 23.9 %all-to-all-start.1 = ((f32[16,48,128]{2,1,0:T(8,128)}), f32[16,48,128]{2,1,0:T(8,128)S(1)}, u32[]{:S(2)}, u32[]{:S(2)}) async-start(f32[16,48,128]{2,1,0:T(8,128)} %get-tuple-element.17), calls=%async_computation.1 | async-start | bytes 786432 | tf_op jit(solution)/shard_map/all_to_all | solution.py:33
  43.5 7.9 %collective-permute-start.8 = (f32[8,128]{1,0:T(8,128)S(1)}, f32[8,128]{1,0:T(8,128)S(1)}, u32[]{:S(2)}, u32[]{:S(2)}) collective-permute-start(f32[8,128]{1,0:T(8,128)S(1)} %add.407), channel_id=1, source_target_pairs={{0,6},{1,7},{2,4},{3,5},{4,2},{5,3},{6,0},{7,1},{8,14},{9,15},{10,... | collective-permute-start | bytes 12296 | tf_op jit(solution)/shard_map/ppermute | solution.py:55
  46.7 5.2 %collective-permute-start.7 = (f32[8,128]{1,0:T(8,128)S(1)}, f32[8,128]{1,0:T(8,128)S(1)}, u32[]{:S(2)}, u32[]{:S(2)}) collective-permute-start(f32[8,128]{1,0:T(8,128)S(1)} %add.407), channel_id=1, source_target_pairs={{0,4},{1,5},{2,6},{3,7},{4,0},{5,1},{6,2},{7,3},{8,12},{9,13},{10,... | collective-permute-start | bytes 12296 | tf_op jit(solution)/shard_map/ppermute | solution.py:55
  47.6 4.3 %collective-permute-start.6 = (f32[8,128]{1,0:T(8,128)S(1)}, f32[8,128]{1,0:T(8,128)S(1)}, u32[]{:S(2)}, u32[]{:S(2)}) collective-permute-start(f32[8,128]{1,0:T(8,128)S(1)} %add.407), channel_id=1, source_target_pairs={{0,2},{1,3},{2,0},{3,1},{4,6},{5,7},{6,4},{7,5},{8,10},{9,11},{10,... | collective-permute-start | bytes 12296 | tf_op jit(solution)/shard_map/ppermute | solution.py:55
  47.7 8.5 %copy-start.5 = (f32[16,64,128]{2,1,0:T(8,128)}, f32[16,64,128]{2,1,0:T(8,128)S(1)}, u32[]{:S(2)}) copy-start(f32[16,64,128]{2,1,0:T(8,128)S(1)} %constant_dynamic-update-slice_fusion.5.cells_ref) | copy-start | bytes 1572868
  51.9 3.7 %collective-permute-start.9 = (f32[8,128]{1,0:T(8,128)S(1)}, f32[8,128]{1,0:T(8,128)S(1)}, u32[]{:S(2)}, u32[]{:S(2)}) collective-permute-start(f32[8,128]{1,0:T(8,128)S(1)} %add_add_fusion.2), channel_id=1, source_target_pairs={{0,8},{1,9},{2,10},{3,11},{4,12},{5,13},{6,14},{7,15},{8,0},{9,1},... | collective-permute-start | bytes 12296 | tf_op jit(solution)/shard_map/ppermute | solution.py:55
  61.2 1.0 copy-start.6
  63.3 19.3 %all-to-all-start.2 = ((f32[16,112,128]{2,1,0:T(8,128)}), f32[16,112,128]{2,1,0:T(8,128)S(1)}, u32[]{:S(2)}, u32[]{:S(2)}) async-start(f32[16,112,128]{2,1,0:T(8,128)} %pad_maximum_fusion), calls=%async_computation.2 | async-start | bytes 1835008 | tf_op jit(solution)/shard_map/all_to_all | solution.py:33
  67.6 15.0 %copy-start.8 = (f32[6,64,128]{2,1,0:T(8,128)}, f32[6,64,128]{2,1,0:T(8,128)S(1)}, u32[]{:S(2)}) copy-start(f32[6,64,128]{2,1,0:T(8,128)S(1)} %constant_dynamic-update-slice_fusion.17.steps_ref) | copy-start | bytes 589828
  82.6 0.9 copy-start.2
  86.5 15.2 %all-to-all-start.3 = ((f32[16,72,128]{2,1,0:T(8,128)}), f32[16,72,128]{2,1,0:T(8,128)S(1)}, u32[]{:S(2)}, u32[]{:S(2)}) async-start(f32[16,72,128]{2,1,0:T(8,128)} %get-tuple-element.18), calls=%async_computation.3 | async-start | bytes 1179648 | tf_op jit(solution)/shard_map/all_to_all | solution.py:33
  101.6 4.1 %copy-start.1 = (f32[16,72,128]{2,1,0:T(8,128)}, f32[16,72,128]{2,1,0:T(8,128)S(1)}, u32[]{:S(2)}) copy-start(f32[16,72,128]{2,1,0:T(8,128)S(1)} %all-to-all-done.3.parts_ref) | copy-start | bytes 1769476
  104.9 7.4 %collective-permute-start.12 = (f32[8,512]{1,0:T(8,128)S(1)}, f32[8,512]{1,0:T(8,128)S(1)}, u32[]{:S(2)}, u32[]{:S(2)}) collective-permute-start(f32[8,512]{1,0:T(8,128)S(1)} %fusion.19), channel_id=1, source_target_pairs={{0,16},{16,32},{32,48},{48,64},{64,80},{80,96},{96,112},{112,0},{1... | collective-permute-start | bytes 49160 | tf_op jit(solution)/shard_map/ppermute | solution.py:436
  112.5 5.4 %collective-permute-start.13 = (f32[40,128]{1,0:T(8,128)S(1)}, f32[40,128]{1,0:T(8,128)S(1)}, u32[]{:S(2)}, u32[]{:S(2)}) collective-permute-start(f32[40,128]{1,0:T(8,128)S(1)} %constant_dynamic-update-slice_fusion.23), channel_id=1, source_target_pairs={{0,16},{16,0},{32,48},{48,32},{64,80},{80,64},{96,112},{112,96},{1... | collective-permute-start | bytes 61448 | tf_op jit(solution)/shard_map/ppermute | solution.py:55
  117.9 12.7 %collective-permute-start.16 = (f32[40,128]{1,0:T(8,128)S(1)}, f32[40,128]{1,0:T(8,128)S(1)}, u32[]{:S(2)}, u32[]{:S(2)}) collective-permute-start(f32[40,128]{1,0:T(8,128)S(1)} %add.421), channel_id=1, source_target_pairs={{0,96},{16,112},{32,64},{48,80},{64,32},{80,48},{96,0},{112,16},{1... | collective-permute-start | bytes 61448 | tf_op jit(solution)/shard_map/ppermute | solution.py:55
  118.1 12.5 %collective-permute-start.15 = (f32[40,128]{1,0:T(8,128)S(1)}, f32[40,128]{1,0:T(8,128)S(1)}, u32[]{:S(2)}, u32[]{:S(2)}) collective-permute-start(f32[40,128]{1,0:T(8,128)S(1)} %add.421), channel_id=1, source_target_pairs={{0,64},{16,80},{32,96},{48,112},{64,0},{80,16},{96,32},{112,48},{1... | collective-permute-start | bytes 61448 | tf_op jit(solution)/shard_map/ppermute | solution.py:55
  118.8 11.8 %collective-permute-start.14 = (f32[40,128]{1,0:T(8,128)S(1)}, f32[40,128]{1,0:T(8,128)S(1)}, u32[]{:S(2)}, u32[]{:S(2)}) collective-permute-start(f32[40,128]{1,0:T(8,128)S(1)} %add.421), channel_id=1, source_target_pairs={{0,32},{16,48},{32,0},{48,16},{64,96},{80,112},{96,64},{112,80},{1... | collective-permute-start | bytes 61448 | tf_op jit(solution)/shard_map/ppermute | solution.py:55
  127.1 17.4 %all-to-all-start.4 = ((f32[8,256,128]{2,1,0:T(8,128)}), f32[8,256,128]{2,1,0:T(8,128)S(1)}, u32[]{:S(2)}, u32[]{:S(2)}) async-start(f32[8,256,128]{2,1,0:T(8,128)} %back.1), calls=%async_computation.4 | async-start | bytes 2097152 | tf_op jit(solution)/shard_map/all_to_all | solution.py:33
  130.7 1.3 collective-permute-start.17
  132.0 6.5 %collective-permute-start.20 = (f32[2,40,128]{2,1,0:T(8,128)S(1)}, f32[2,40,128]{2,1,0:T(8,128)S(1)}, u32[]{:S(2)}, u32[]{:S(2)}) collective-permute-start(f32[2,40,128]{2,1,0:T(8,128)S(1)} %pad_maximum_fusion.4), channel_id=1, source_target_pairs={{0,6},{1,7},{2,4},{3,5},{4,2},{5,3},{6,0},{7,1},{8,14},{9,15},{10,... | collective-permute-start | bytes 122888 | tf_op jit(solution)/shard_map/ppermute | solution.py:55
  132.9 5.6 %collective-permute-start.19 = (f32[2,40,128]{2,1,0:T(8,128)S(1)}, f32[2,40,128]{2,1,0:T(8,128)S(1)}, u32[]{:S(2)}, u32[]{:S(2)}) collective-permute-start(f32[2,40,128]{2,1,0:T(8,128)S(1)} %pad_maximum_fusion.4), channel_id=1, source_target_pairs={{0,4},{1,5},{2,6},{3,7},{4,0},{5,1},{6,2},{7,3},{8,12},{9,13},{10,... | collective-permute-start | bytes 122888 | tf_op jit(solution)/shard_map/ppermute | solution.py:55
  132.9 5.6 %collective-permute-start.18 = (f32[2,40,128]{2,1,0:T(8,128)S(1)}, f32[2,40,128]{2,1,0:T(8,128)S(1)}, u32[]{:S(2)}, u32[]{:S(2)}) collective-permute-start(f32[2,40,128]{2,1,0:T(8,128)S(1)} %pad_maximum_fusion.4), channel_id=1, source_target_pairs={{0,2},{1,3},{2,0},{3,1},{4,6},{5,7},{6,4},{7,5},{8,10},{9,11},{10,... | collective-permute-start | bytes 122888 | tf_op jit(solution)/shard_map/ppermute | solution.py:55
  138.5 5.6 %collective-permute-start.21 = (f32[8,40,128]{2,1,0:T(8,128)S(1)}, f32[8,40,128]{2,1,0:T(8,128)S(1)}, u32[]{:S(2)}, u32[]{:S(2)}) collective-permute-start(f32[8,40,128]{2,1,0:T(8,128)S(1)} %get-tuple-element.50), channel_id=1, source_target_pairs={{0,8},{1,9},{2,10},{3,11},{4,12},{5,13},{6,14},{7,15},{8,0},{9,1},... | collective-permute-start | bytes 491528 | tf_op jit(solution)/shard_map/ppermute | solution.py:55
  144.2 0.7 copy-start.7
  144.4 1.0 copy-start.3
  154.6 1.5 collective-permute-start.22
  156.9 5.5 %collective-permute-start.25 = (f32[128,128]{1,0:T(8,128)S(1)}, f32[128,128]{1,0:T(8,128)S(1)}, u32[]{:S(2)}, u32[]{:S(2)}) collective-permute-start(f32[128,128]{1,0:T(8,128)S(1)} %add.432), channel_id=1, source_target_pairs={{0,6},{1,7},{2,4},{3,5},{4,2},{5,3},{6,0},{7,1},{8,14},{9,15},{10,... | collective-permute-start | bytes 196616 | tf_op jit(solution)/shard_map/ppermute | solution.py:55
  159.0 6.1 %collective-permute-start.24 = (f32[128,128]{1,0:T(8,128)S(1)}, f32[128,128]{1,0:T(8,128)S(1)}, u32[]{:S(2)}, u32[]{:S(2)}) collective-permute-start(f32[128,128]{1,0:T(8,128)S(1)} %add.432), channel_id=1, source_target_pairs={{0,4},{1,5},{2,6},{3,7},{4,0},{5,1},{6,2},{7,3},{8,12},{9,13},{10,... | collective-permute-start | bytes 196616 | tf_op jit(solution)/shard_map/ppermute | solution.py:55
  160.5 4.6 %collective-permute-start.23 = (f32[128,128]{1,0:T(8,128)S(1)}, f32[128,128]{1,0:T(8,128)S(1)}, u32[]{:S(2)}, u32[]{:S(2)}) collective-permute-start(f32[128,128]{1,0:T(8,128)S(1)} %add.432), channel_id=1, source_target_pairs={{0,2},{1,3},{2,0},{3,1},{4,6},{5,7},{6,4},{7,5},{8,10},{9,11},{10,... | collective-permute-start | bytes 196616 | tf_op jit(solution)/shard_map/ppermute | solution.py:55
  165.1 4.3 %collective-permute-start.26 = (f32[128,128]{1,0:T(8,128)S(1)}, f32[128,128]{1,0:T(8,128)S(1)}, u32[]{:S(2)}, u32[]{:S(2)}) collective-permute-start(f32[128,128]{1,0:T(8,128)S(1)} %add_add_fusion.1), channel_id=1, source_target_pairs={{0,8},{1,9},{2,10},{3,11},{4,12},{5,13},{6,14},{7,15},{8,0},{9,1},... | collective-permute-start | bytes 196616 | tf_op jit(solution)/shard_map/ppermute | solution.py:55
  169.5 5.9 %collective-permute-start.27 = (f32[128,128]{1,0:T(8,128)S(1)}, f32[128,128]{1,0:T(8,128)S(1)}, u32[]{:S(2)}, u32[]{:S(2)}) collective-permute-start(f32[128,128]{1,0:T(8,128)S(1)} %add.436), channel_id=1, source_target_pairs={{0,16},{16,0},{32,48},{48,32},{64,80},{80,64},{96,112},{112,96},{1... | collective-permute-start | bytes 196616 | tf_op jit(solution)/shard_map/ppermute | solution.py:55
  175.4 5.6 %collective-permute-start.30 = (f32[128,128]{1,0:T(8,128)S(1)}, f32[128,128]{1,0:T(8,128)S(1)}, u32[]{:S(2)}, u32[]{:S(2)}) collective-permute-start(f32[128,128]{1,0:T(8,128)S(1)} %add.437), channel_id=1, source_target_pairs={{0,96},{16,112},{32,64},{48,80},{64,32},{80,48},{96,0},{112,16},{1... | collective-permute-start | bytes 196616 | tf_op jit(solution)/shard_map/ppermute | solution.py:55
  178.6 5.8 %collective-permute-start.29 = (f32[128,128]{1,0:T(8,128)S(1)}, f32[128,128]{1,0:T(8,128)S(1)}, u32[]{:S(2)}, u32[]{:S(2)}) collective-permute-start(f32[128,128]{1,0:T(8,128)S(1)} %add.437), channel_id=1, source_target_pairs={{0,64},{16,80},{32,96},{48,112},{64,0},{80,16},{96,32},{112,48},{1... | collective-permute-start | bytes 196616 | tf_op jit(solution)/shard_map/ppermute | solution.py:55
  179.4 4.9 %collective-permute-start.28 = (f32[128,128]{1,0:T(8,128)S(1)}, f32[128,128]{1,0:T(8,128)S(1)}, u32[]{:S(2)}, u32[]{:S(2)}) collective-permute-start(f32[128,128]{1,0:T(8,128)S(1)} %add.437), channel_id=1, source_target_pairs={{0,32},{16,48},{32,0},{48,16},{64,96},{80,112},{96,64},{112,80},{1... | collective-permute-start | bytes 196616 | tf_op jit(solution)/shard_map/ppermute | solution.py:55

commit v2 on v1

--- a/solution.py
+++ b/solution.py
@@ -52,7 +52,8 @@
 
 
 def from_peer(values, axis, mask):
-    return lax.ppermute(values, axis, [(i, i ^ mask) for i in range(lax.axis_size(axis))])
+    peers = lax.axis_size(axis)
+    return lax.ppermute(values, axis, [(i, i ^ mask) for i in range(peers)])
 
 
 def sum_over(array, axis, groups):
@@ -78,6 +79,7 @@
 
 BRICK_GROUPS = ((1,), (2, 4, 6), (8,))
 SLAB_GROUPS = ((1,), (2, 4, 6))
+ALL_GROUPS = ((1,), (2, 4, 6), (8, 16, 24), (32, 64, 96))
 
 
 def three_parts(array):
@@ -140,12 +142,12 @@
             work_ref[stop:, :] = work_ref[stop:, :] - update[stop:, :]
 
 
-def transport_kernel(nodes_ref, columns_ref, speeds_ref, weights_ref, out_ref, vectors_ref):
+def transport_kernel(nodes_ref, columns_ref, speeds_ref, weights_ref, out_ref):
     groups, rows, rank = nodes_ref.shape
     bricks = out_ref.shape[0]
     factors = [jnp.broadcast_to(columns_ref[:, i : i + 1], (rows, rank)) for i in range(4)]
     sums = [jnp.zeros((rank, rank), jnp.float32) for _ in range(6)]
-    vectors = jnp.zeros(vectors_ref.shape, jnp.float32)
+    vectors = jnp.zeros((8, rank), jnp.float32)
     for group in range(groups):
         nodes = nodes_ref[group]
         weighted = jnp.concatenate([nodes] + [nodes * factor for factor in factors], axis=1)
@@ -164,23 +166,29 @@
         sums[1] = sums[1] + jnp.minimum(speed, 0.0) * plain
         for i in range(4):
             sums[2 + i] = sums[2 + i] + product[:, (i + 1) * rank : (i + 2) * rank]
-    vectors_ref[...] = vectors * WEIGHT_V
+    out_ref[:, :8, :] = jnp.broadcast_to((vectors * WEIGHT_V)[None], (bricks, 8, rank))
     height = rank // bricks
     for i in range(6):
-        out_ref[:, i * height : (i + 1) * height, :] = (sums[i] * WEIGHT_V).reshape(
+        start = 8 + i * height
+        out_ref[:, start : start + height, :] = (sums[i] * WEIGHT_V).reshape(
             bricks, height, rank
         )
 
 
 def maxwell_kernel(
-    brick_ref, cells_ref, vectors_ref, nodes_ref, first_ref, across_ref, part_ref, line_ref, state_ref
+    brick_ref, cells_ref, integrals_ref, nodes_ref, first_ref, across_ref, part_ref, line_ref, state_ref
 ):
     bricks, cells, rank = cells_ref.shape
     groups, rows, _ = nodes_ref.shape
     total = bricks * cells
     brick = brick_ref[0]
     k_flat = jnp.concatenate([cells_ref[i ^ brick] for i in range(bricks)], axis=0)
-    moments = contract(vectors_ref[...], k_flat, 1, 1)
+    integrals = integrals_ref[0]
+    for i in range(1, bricks):
+        integrals = integrals + integrals_ref[i]
+    height = integrals.shape[0] - 8
+    part_ref[:, cells:, :] = jnp.broadcast_to(integrals[8:][None], (bricks, height, rank))
+    moments = contract(integrals[:8], k_flat, 1, 1)
     density, drift, temper = cell_state([moments[i : i + 1] for i in range(5)])
     slope = -0.5 / temper
     amplitude = density * jnp.exp(-1.5 * jnp.log(2.0 * math.pi * temper))
@@ -208,7 +216,7 @@
         )
         result = result + line_cols[:, group : group + 1] * product[:, :rank]
         result = result + line_cols[:, group + 1 : group + 2] * product[:, rank:]
-    part_ref[...] = result.reshape(bricks, cells, rank)
+    part_ref[:, :cells, :] = result.reshape(bricks, cells, rank)
 
 
 def back_kernel(parts_ref, line_ref, state_ref, across_ref, out_ref):
@@ -366,8 +374,9 @@
     )
     nodes = to_all(v_basis, "slab")
     k_slab = gather_relative(own_cells, "brick", BRICK_GROUPS)
-    k_below = lax.ppermute(k_coeffs[-1:], "slab", up)
-    k_above = lax.ppermute(k_coeffs[:1], "slab", down)
+    k_edges, k_slab = lax.optimization_barrier((k_coeffs, k_slab))
+    k_below = lax.ppermute(k_edges[-1:], "slab", up)
+    k_above = lax.ppermute(k_edges[:1], "slab", down)
 
     across = velocities(brick * rows + jnp.arange(rows, dtype=jnp.int32))
     columns = [f(across[i]) for i in (1, 2) for f in (lambda v: jnp.maximum(v, 0.0), lambda v: jnp.minimum(v, 0.0))]
@@ -375,30 +384,25 @@
     owner = jnp.arange(slabs, dtype=jnp.int32) * bricks + brick
     first_velocity = velocities(owner * rows)[0]
     first_speeds = jnp.broadcast_to(first_velocity[:, None], (slabs, rank))
-    transport_part, vectors_part = pl.pallas_call(
-        transport_kernel,
-        out_shape=(f32(bricks, 6 * height, rank), f32(8, rank)),
-        name="transport",
+    transport_part = pl.pallas_call(
+        transport_kernel, out_shape=f32(bricks, 8 + 6 * height, rank), name="transport"
     )(nodes, columns, first_speeds, weights)
-    vectors = sum_over(vectors_part, "brick", BRICK_GROUPS)
-    transport_slice = jnp.sum(exchange(transport_part, "brick"), axis=0)
+    integrals = exchange(transport_part, "brick")
 
     brick_id = brick.astype(jnp.int32)[None]
     vector_specs = [pl.BlockSpec(memory_space=pltpu.SMEM)]
     whole = pl.BlockSpec(memory_space=pltpu.VMEM)
-    mproj_part, line, state = pl.pallas_call(
+    payload, line, state = pl.pallas_call(
         maxwell_kernel,
-        out_shape=(f32(bricks, cells, rank), f32(slab_cells, slabs), f32(8, slab_cells)),
+        out_shape=(
+            f32(bricks, cells + 6 * height, rank),
+            f32(slab_cells, slabs),
+            f32(8, slab_cells),
+        ),
         in_specs=vector_specs + [whole] * 5,
         name="maxwell",
-    )(brick_id, k_slab, vectors, nodes, first_speeds, across[1:])
-    second = exchange(
-        jnp.concatenate(
-            [mproj_part, jnp.broadcast_to(transport_slice[None], (bricks, 6 * height, rank))],
-            axis=1,
-        ),
-        "brick",
-    )
+    )(brick_id, k_slab, integrals, nodes, first_speeds, across[1:])
+    second = exchange(payload, "brick")
 
     slab_grid = k_slab.reshape(bricks, cells_x, cells_y, cells_z, rank)
     left = ((brick - 1) % bricks) ^ brick
@@ -434,6 +438,14 @@
     choose = (choose[:, None] == jnp.arange(rank, dtype=jnp.int32)[None]).astype(jnp.float32)
     chosen = contract(choose, planes_x[-1], 1, 1)
     chosen_below = lax.ppermute(chosen, "slab", up)
+    back = pl.pallas_call(back_kernel, out_shape=f32(slabs, rows, rank), name="back")(
+        third, line, state, across[1:].T
+    )
+    back, slab_advanced = lax.optimization_barrier((back, slab_advanced))
+    fourth = exchange(back, "slab")
+
+    adv_grid = slab_advanced.reshape(bricks, cells_x, cells_y, cells_z, rank)
+    planes_x = [adv_grid[:, i].reshape(half, rank) for i in range(cells_x)]
     before = jnp.concatenate([adv_grid[-1:, :, -1:], adv_grid[:-1, :, -1:]], axis=0)
     shift_y = jnp.concatenate([before, adv_grid[:, :, :-1]], axis=2).reshape(slab_cells, rank)
     shift_z = jnp.roll(adv_grid, 1, axis=3).reshape(slab_cells, rank)
@@ -459,11 +471,6 @@
     pieces = sum_over(pieces, "slab", SLAB_GROUPS)
     reduced = gather_relative(pieces, "brick", BRICK_GROUPS)
 
-    back = pl.pallas_call(back_kernel, out_shape=f32(slabs, rows, rank), name="back")(
-        third, line, state, across[1:].T
-    )
-    fourth = exchange(back, "slab")
-
     speeds = jnp.stack(list(own_velocity) + [jnp.zeros_like(ones)] * 5, axis=1)
     basis_new, velocity_new, gram_part = pl.pallas_call(
         functools.partial(
@@ -474,7 +481,7 @@
         scratch_shapes=factor_scratch(rank),
         name="middle",
     )(brick_id, reduced, second, v_basis, fourth, advanced, speeds)
-    gram_v = sum_over(sum_over(gram_part, "brick", BRICK_GROUPS), "slab", SLAB_GROUPS)
+    gram_v = sum_over(gram_part, ("slab", "brick"), ALL_GROUPS)
     coupling, vbasis_new = pl.pallas_call(
         last_kernel,
         out_shape=(f32(rank, rank), f32(rows, rank)),

time: 192 us -> 181 us (0.943)
  starting transfers between devices: 63 us -> 56 us
  waiting for transfers between devices: 74.6 us -> 72.4 us
    ppermute x30 -> x26, starting transfers between devices: 39.6 us -> 31.1 us  [the longest x24 27.5 us: from_peer(): return lax.ppermute(values, axis, [(i, i ^ mask) for i in range(peers)])]
    ppermute x30 -> x26, waiting for transfers between devices: 39.6 us -> 32.3 us  [the longest x24 32.3 us: from_peer(): return lax.ppermute(values, axis, [(i, i ^ mask) for i in range(peers)])]
    all_to_all x5, waiting for transfers between devices: 29.5 us -> 36.5 us  [exchange(): return lax.all_to_all(array, axis, 0, 0, tiled=True)]
  transfers between devices with their start and end apart: 36 -> 32, of which waited for: 21 -> 19; matrix products, arithmetic and copies ran while one was open for 6% -> 6% of each run, Pallas kernels for 8% -> 5%
where the time goes in v2:
time: 181 us; the launch traced here: 180 us
  waiting for transfers between devices  72.4 us (40%)
  starting transfers between devices  56 us (31%)
  Pallas kernels  32.1 us (18%)
  local copies, waits for them, and re-layouts  11.1 us (6%)
  matrix products  4.07 us (2%)
  other arithmetic  3.3 us (2%)
    all_to_all x5, waiting for transfers between devices, exchange(): return lax.all_to_all(array, axis, 0, 0, tiled=True)  36.5 us
    ppermute x24, waiting for transfers between devices, from_peer(): return lax.ppermute(values, axis, [(i, i ^ mask) for i in range(peers)])  32.3 us
    ppermute x24, starting transfers between devices, from_peer(): return lax.ppermute(values, axis, [(i, i ^ mask) for i in range(peers)])  27.5 us
    all_to_all x5, starting transfers between devices, exchange(): return lax.all_to_all(array, axis, 0, 0, tiled=True)  24.1 us
    pallas_call x1, Pallas kernels, local(): pl.pallas_call(functools.partial(middle_kernel, lengths=lengths, time_ste...  9.19 us
    pallas_call x1, Pallas kernels, local(): pl.pallas_call(last_kernel, out_shape=(f32(rank, rank), f32(rows, rank)),...  5.44 us
    pallas_call x1, Pallas kernels, local(): pl.pallas_call(maxwell_kernel, out_shape=(f32(bricks, cells + 6 * height,...  5.26 us
    pallas_call x1, Pallas kernels, local(): pl.pallas_call(back_kernel, out_shape=f32(slabs, rows, rank), name='back')  4.9 us
  transfers between devices with their start and end apart: 32, of which 19 were waited for; matrix products, arithmetic and copies ran while one was open for 6% of the time, Pallas kernels for 5%

profile of v2, /device:TPU:0, one launch (start us, length us, event | category | flops | bytes accessed | tf_op | source)
XLA Modules:
  0.0 180.2 jit_solution(6053908848535922811)
XLA Ops:
  0.7 1.9 %broadcast_in_dim.11 = f32[8,256,128]{2,1,0:T(8,128)} broadcast(f32[256,128]{1,0:T(8,128)} %basis_ref.1), dimensions={1,2} | broadcast | bytes 1179648 | tf_op jit(solution)/shard_map/broadcast_in_dim | solution.py:38
  2.7 7.1 %all-to-all-start = ((f32[8,256,128]{2,1,0:T(8,128)}), f32[8,256,128]{2,1,0:T(8,128)S(1)}, u32[]{:S(2)}, u32[]{:S(2)}) async-start(f32[8,256,128]{2,1,0:T(8,128)} %broadcast_in_dim.11), calls=%async_computation | async-start | bytes 2097152 | tf_op jit(solution)/shard_map/all_to_all | solution.py:33
  10.4 0.7 slice_bitcast_fusion.6
  11.2 4.1 %collective-permute-start.3 = (f32[2,64,128]{2,1,0:T(8,128)S(1)}, f32[2,64,128]{2,1,0:T(8,128)S(1)}, u32[]{:S(2)}, u32[]{:S(2)}) collective-permute-start(f32[2,64,128]{2,1,0:T(8,128)S(1)} %pad_maximum_fusion.2), channel_id=1, source_target_pairs={{0,6},{1,7},{2,4},{3,5},{4,2},{5,3},{6,0},{7,1},{8,14},{9,15},{10,... | collective-permute-start | bytes 196616 | tf_op jit(solution)/shard_map/ppermute | solution.py:56
  15.3 0.9 collective-permute-start.1
  16.3 3.6 %collective-permute-done.1 = f32[2,64,128]{2,1,0:T(8,128)S(1)} collective-permute-done((f32[2,64,128]{2,1,0:T(8,128)S(1)}, f32[2,64,128]{2,1,0:T(8,128)S(1)}, u32[]{:S(2)}, u32[]{:S(2)}) %collective-permute-start.1) | collective-permute-done | bytes 65568 | tf_op jit(solution)/shard_map/ppermute | solution.py:56
  20.0 1.5 collective-permute-done.2
  21.5 0.7 collective-permute-start.4
  22.6 0.8 copy.31.columns_ref
  23.4 0.7 copy.32.across_ref
  24.1 0.7 stack.52.weights_ref
  24.8 3.0 %all-to-all-done.nodes_ref = f32[8,256,128]{2,1,0:T(8,128)S(1)} async-done(((f32[8,256,128]{2,1,0:T(8,128)}), f32[8,256,128]{2,1,0:T(8,128)S(1)}, u32[]{:S(2)}, u32[]{:S(2)}) %all-to-all-start) | async-done | bytes 1048608 | tf_op jit(solution)/shard_map/all_to_all | solution.py:33
  27.8 0.7 broadcast_in_dim.26.speeds_ref.first_ref
  28.8 4.5 %transport.1 = f32[16,56,128]{2,1,0:T(8,128)} custom-call(f32[8,256,128]{2,1,0:T(8,128)} %copy-done, f32[256,8]{1,0:T(8,128)} %copy.31.columns_ref, f32[8,128]{1,0:T(8,128)} %broadcast_in_dim.26.speeds_ref.first_ref, f32[8,8,256]{2,1,0:T(8,128)} %stack.52.weights_ref), custom_call_target="tpu_custom_call" | custom-call | tf_op jit(solution)/shard_map/transport/pallas_call | solution.py:387
  33.2 6.0 %all-to-all-start.1 = ((f32[16,56,128]{2,1,0:T(8,128)}), f32[16,56,128]{2,1,0:T(8,128)S(1)}, u32[]{:S(2)}, u32[]{:S(2)}) async-start(f32[16,56,128]{2,1,0:T(8,128)} %transport.1), calls=%async_computation.1 | async-start | bytes 917504 | tf_op jit(solution)/shard_map/all_to_all | solution.py:33
  39.3 1.4 collective-permute-start.6
  40.7 2.2 %collective-permute-start.5 = (f32[1,2,16,128]{3,2,1,0:T(8,128)S(1)}, f32[1,2,16,128]{3,2,1,0:T(8,128)S(1)}, u32[]{:S(2)}, u32[]{:S(2)}) collective-permute-start(f32[1,2,16,128]{3,2,1,0:T(8,128)S(1)} %get-tuple-element.73), channel_id=1, source_target_pairs={{0,16},{16,32},{32,48},{48,64},{64,80},{80,96},{96,112},{112,0},{1... | collective-permute-start | bytes 49160 | tf_op jit(solution)/shard_map/ppermute | solution.py:378
  42.9 6.8 %all-to-all-done.1.integrals_ref = f32[16,56,128]{2,1,0:T(8,128)S(1)} async-done(((f32[16,56,128]{2,1,0:T(8,128)}), f32[16,56,128]{2,1,0:T(8,128)S(1)}, u32[]{:S(2)}, u32[]{:S(2)}) %all-to-all-start.1) | async-done | bytes 458784 | tf_op jit(solution)/shard_map/all_to_all | solution.py:33
  49.8 0.8 copy-done.5
  50.5 5.3 %maxwell.1 = (f32[16,112,128]{2,1,0:T(8,128)}, f32[1024,8]{1,0:T(8,128)}, f32[8,1024]{1,0:T(8,128)}) custom-call(s32[1]{0:T(128)} %bitcast.brick_ref, f32[16,64,128]{2,1,0:T(8,128)} %copy-done.6, f32[16,56,128]{2,1,0:T(8,128)} %copy-done.5, f32[8,256,128]{2,1,0:T(8,128)} %copy-done, f32[8,128]{1,0:T(8,128)} %broadcast_in_dim.26.speeds_ref.first_ref, ...), custom_call_target="tpu_custom_call" | custom-call | tf_op jit(solution)/shard_map/maxwell/pallas_call | solution.py:395
  55.8 3.6 %all-to-all-start.2 = ((f32[16,112,128]{2,1,0:T(8,128)}), f32[16,112,128]{2,1,0:T(8,128)S(1)}, u32[]{:S(2)}, u32[]{:S(2)}) async-start(f32[16,112,128]{2,1,0:T(8,128)} %get-tuple-element.18), calls=%async_computation.2 | async-start | bytes 1835008 | tf_op jit(solution)/shard_map/all_to_all | solution.py:33
  59.6 15.0 %all-to-all-done.2.parts_ref.transport_ref = f32[16,112,128]{2,1,0:T(8,128)S(1)} async-done(((f32[16,112,128]{2,1,0:T(8,128)}), f32[16,112,128]{2,1,0:T(8,128)S(1)}, u32[]{:S(2)}, u32[]{:S(2)}) %all-to-all-start.2) | async-done | bytes 917536 | tf_op jit(solution)/shard_map/all_to_all | solution.py:33
  74.6 0.9 copy-done.1
  75.5 2.9 %advance.1 = (f32[16,72,128]{2,1,0:T(8,128)}, f32[64,128]{1,0:T(8,128)}) custom-call(f32[16,112,128]{2,1,0:T(8,128)} %copy-done.1, f32[6,64,128]{2,1,0:T(8,128)} %copy-done.8, f32[64,128]{1,0:T(8,128)} %bitcast.80), custom_call_target="tpu_custom_call" | custom-call | tf_op jit(solution)/shard_map/advance/pallas_call | solution.py:426
  78.4 3.8 %all-to-all-start.3 = ((f32[16,72,128]{2,1,0:T(8,128)}), f32[16,72,128]{2,1,0:T(8,128)S(1)}, u32[]{:S(2)}, u32[]{:S(2)}) async-start(f32[16,72,128]{2,1,0:T(8,128)} %get-tuple-element.20), calls=%async_computation.3 | async-start | bytes 1179648 | tf_op jit(solution)/shard_map/all_to_all | solution.py:33
  82.2 11.4 %all-to-all-done.3.parts_ref = f32[16,72,128]{2,1,0:T(8,128)S(1)} async-done(((f32[16,72,128]{2,1,0:T(8,128)}), f32[16,72,128]{2,1,0:T(8,128)S(1)}, u32[]{:S(2)}, u32[]{:S(2)}) %all-to-all-start.3) | async-done | bytes 589856 | tf_op jit(solution)/shard_map/all_to_all | solution.py:33
  93.6 0.8 copy-done.2
  94.4 4.9 %back.1 = f32[8,256,128]{2,1,0:T(8,128)} custom-call(f32[16,72,128]{2,1,0:T(8,128)} %copy-done.2, f32[1024,8]{1,0:T(8,128)} %get-tuple-element.21.line_ref, f32[8,1024]{1,0:T(8,128)} %get-tuple-element.22.state_ref, f32[256,2]{1,0:T(8,128)} %get-tuple-element.44.across_ref), custom_call_target="tpu_custom_call" | custom-call | tf_op jit(solution)/shard_map/back/pallas_call | solution.py:441
  99.3 0.6 convolution_bitcast_fusion.1
  99.9 1.0 convolution_bitcast_fusion
  101.3 0.8 collective-permute-start.7
  102.1 1.0 fusion.37
  103.2 1.0 fusion.38
  104.2 0.9 slice_reduce_fusion.3
  105.1 3.6 %collective-permute-done.7 = f32[8,512]{1,0:T(8,128)S(1)} collective-permute-done((f32[8,512]{1,0:T(8,128)S(1)}, f32[8,512]{1,0:T(8,128)S(1)}, u32[]{:S(2)}, u32[]{:S(2)}) %collective-permute-start.7) | collective-permute-done | bytes 16416 | tf_op jit(solution)/shard_map/ppermute | solution.py:440
  109.0 5.2 %collective-permute-done.8 = f32[40,128]{1,0:T(8,128)S(1)} collective-permute-done((f32[40,128]{1,0:T(8,128)S(1)}, f32[40,128]{1,0:T(8,128)S(1)}, u32[]{:S(2)}, u32[]{:S(2)}) %collective-permute-start.8) | collective-permute-done | bytes 20512 | tf_op jit(solution)/shard_map/ppermute | solution.py:56
  114.4 0.7 collective-permute-start.10
  115.1 3.2 %collective-permute-start.9 = (f32[40,128]{1,0:T(8,128)S(1)}, f32[40,128]{1,0:T(8,128)S(1)}, u32[]{:S(2)}, u32[]{:S(2)}) collective-permute-start(f32[40,128]{1,0:T(8,128)S(1)} %add.404), channel_id=1, source_target_pairs={{0,32},{16,48},{32,0},{48,16},{64,96},{80,112},{96,64},{112,80},{1... | collective-permute-start | bytes 61448 | tf_op jit(solution)/shard_map/ppermute | solution.py:56
  118.5 3.6 %all-to-all-start.4 = ((f32[8,256,128]{2,1,0:T(8,128)}), f32[8,256,128]{2,1,0:T(8,128)S(1)}, u32[]{:S(2)}, u32[]{:S(2)}) async-start(f32[8,256,128]{2,1,0:T(8,128)} %back.1), calls=%async_computation.4 | async-start | bytes 2097152 | tf_op jit(solution)/shard_map/all_to_all | solution.py:33
  122.3 1.2 collective-permute-done.12
  123.4 0.9 collective-permute-start.15
  124.3 3.2 %collective-permute-start.13 = (f32[2,40,128]{2,1,0:T(8,128)S(1)}, f32[2,40,128]{2,1,0:T(8,128)S(1)}, u32[]{:S(2)}, u32[]{:S(2)}) collective-permute-start(f32[2,40,128]{2,1,0:T(8,128)S(1)} %pad_maximum_fusion.3), channel_id=1, source_target_pairs={{0,2},{1,3},{2,0},{3,1},{4,6},{5,7},{6,4},{7,5},{8,10},{9,11},{10,... | collective-permute-start | bytes 122888 | tf_op jit(solution)/shard_map/ppermute | solution.py:56
  127.5 2.4 %collective-permute-done.13 = f32[2,40,128]{2,1,0:T(8,128)S(1)} collective-permute-done((f32[2,40,128]{2,1,0:T(8,128)S(1)}, f32[2,40,128]{2,1,0:T(8,128)S(1)}, u32[]{:S(2)}, u32[]{:S(2)}) %collective-permute-start.13) | collective-permute-done | bytes 40992 | tf_op jit(solution)/shard_map/ppermute | solution.py:56
  130.0 0.8 collective-permute-start.16
  131.1 0.8 copy.36.speeds_ref
  131.9 3.7 %collective-permute-done.16 = f32[8,40,128]{2,1,0:T(8,128)S(1)} collective-permute-done((f32[8,40,128]{2,1,0:T(8,128)S(1)}, f32[8,40,128]{2,1,0:T(8,128)S(1)}, u32[]{:S(2)}, u32[]{:S(2)}) %collective-permute-start.16) | collective-permute-done | bytes 163872 | tf_op jit(solution)/shard_map/ppermute | solution.py:56
  136.9 9.2 %middle.1 = (f32[64,128]{1,0:T(8,128)}, f32[256,128]{1,0:T(8,128)}, f32[128,128]{1,0:T(8,128)}) custom-call(s32[1]{0:T(128)} %bitcast.brick_ref, f32[16,40,128]{2,1,0:T(8,128)} %copy-done.7, f32[16,112,128]{2,1,0:T(8,128)} %copy-done.1, f32[256,128]{1,0:T(8,128)} %basis_ref.1, f32[8,256,128]{2,1,0:T(8,128)} %copy-done.3, ...), custom_call_target="tpu_custom_call" | custom-call | tf_op jit(solution)/shard_map/middle/pallas_call | solution.py:475
  146.1 1.5 collective-permute-done.17
  147.5 0.9 add.415
  148.4 2.1 %collective-permute-start.20 = (f32[128,128]{1,0:T(8,128)S(1)}, f32[128,128]{1,0:T(8,128)S(1)}, u32[]{:S(2)}, u32[]{:S(2)}) collective-permute-start(f32[128,128]{1,0:T(8,128)S(1)} %add.415), channel_id=1, source_target_pairs={{0,6},{1,7},{2,4},{3,5},{4,2},{5,3},{6,0},{7,1},{8,14},{9,15},{10,... | collective-permute-start | bytes 196616 | tf_op jit(solution)/shard_map/ppermute | solution.py:56
  150.5 1.5 collective-permute-start.19
  151.9 0.6 collective-permute-start.18
  152.5 1.4 collective-permute-done.20
  153.9 2.7 %collective-permute-done.19 = f32[128,128]{1,0:T(8,128)S(1)} collective-permute-done((f32[128,128]{1,0:T(8,128)S(1)}, f32[128,128]{1,0:T(8,128)S(1)}, u32[]{:S(2)}, u32[]{:S(2)}) %collective-permute-start.19) | collective-permute-done | bytes 65568 | tf_op jit(solution)/shard_map/ppermute | solution.py:56
  156.6 3.1 %collective-permute-start.23 = (f32[128,128]{1,0:T(8,128)S(1)}, f32[128,128]{1,0:T(8,128)S(1)}, u32[]{:S(2)}, u32[]{:S(2)}) collective-permute-start(f32[128,128]{1,0:T(8,128)S(1)} %add_add_fusion.2), channel_id=1, source_target_pairs={{0,24},{1,25},{2,26},{3,27},{4,28},{5,29},{6,30},{7,31},{8,16},{9,... | collective-permute-start | bytes 196616 | tf_op jit(solution)/shard_map/ppermute | solution.py:56
  160.2 0.6 collective-permute-start.21
  160.8 1.4 collective-permute-done.23
  162.2 3.3 %collective-permute-done.22 = f32[128,128]{1,0:T(8,128)S(1)} collective-permute-done((f32[128,128]{1,0:T(8,128)S(1)}, f32[128,128]{1,0:T(8,128)S(1)}, u32[]{:S(2)}, u32[]{:S(2)}) %collective-permute-start.22) | collective-permute-done | bytes 65568 | tf_op jit(solution)/shard_map/ppermute | solution.py:56
  165.5 2.8 %collective-permute-start.26 = (f32[128,128]{1,0:T(8,128)S(1)}, f32[128,128]{1,0:T(8,128)S(1)}, u32[]{:S(2)}, u32[]{:S(2)}) collective-permute-start(f32[128,128]{1,0:T(8,128)S(1)} %add_add_fusion.1), channel_id=1, source_target_pairs={{0,96},{1,97},{2,98},{3,99},{4,100},{5,101},{6,102},{7,103},{8,104... | collective-permute-start | bytes 196616 | tf_op jit(solution)/shard_map/ppermute | solution.py:56
  168.3 0.8 collective-permute-start.25
  169.7 1.4 collective-permute-done.26
  171.1 3.0 %collective-permute-done.25 = f32[128,128]{1,0:T(8,128)S(1)} collective-permute-done((f32[128,128]{1,0:T(8,128)S(1)}, f32[128,128]{1,0:T(8,128)S(1)}, u32[]{:S(2)}, u32[]{:S(2)}) %collective-permute-start.25) | collective-permute-done | bytes 65568 | tf_op jit(solution)/shard_map/ppermute | solution.py:56
  174.1 0.7 add_add_fusion.gram_ref
  174.8 5.4 %last.1 = (f32[128,128]{1,0:T(8,128)}, f32[256,128]{1,0:T(8,128)}) custom-call(f32[128,128]{1,0:T(8,128)} %add_add_fusion.gram_ref, f32[256,128]{1,0:T(8,128)} %get-tuple-element.28.velocity_ref), custom_call_target="tpu_custom_call" | custom-call | tf_op jit(solution)/shard_map/last/pallas_call | solution.py:485
  (114 shorter events, 5.3 us)
Async XLA Ops:
  0.6 10.6 %collective-permute-start = (f32[1,64,128]{2,1,0:T(8,128)}, f32[1,64,128]{2,1,0:T(8,128)S(1)}, u32[]{:S(2)}, u32[]{:S(2)}) collective-permute-start(f32[1,64,128]{2,1,0:T(8,128)} %bitcast.79), channel_id=1, source_target_pairs={{0,1},{1,0},{2,3},{3,2},{4,5},{5,4},{6,7},{7,6},{8,9},{9,8},{10,11... | collective-permute-start | bytes 98312 | tf_op jit(solution)/shard_map/ppermute | solution.py:56
  2.7 7.2 %copy-start.4 = (f32[2,2,16,128]{3,2,1,0:T(8,128)S(1)}, f32[2,2,16,128]{3,2,1,0:T(8,128)}, u32[]{:S(2)}) copy-start(f32[2,2,16,128]{3,2,1,0:T(8,128)} %param.2) | copy-start | bytes 98308
  2.7 25.2 %all-to-all-start = ((f32[8,256,128]{2,1,0:T(8,128)}), f32[8,256,128]{2,1,0:T(8,128)S(1)}, u32[]{:S(2)}, u32[]{:S(2)}) async-start(f32[8,256,128]{2,1,0:T(8,128)} %broadcast_in_dim.11), calls=%async_computation | async-start | bytes 2097152 | tf_op jit(solution)/shard_map/all_to_all | solution.py:33
  11.2 10.3 %collective-permute-start.3 = (f32[2,64,128]{2,1,0:T(8,128)S(1)}, f32[2,64,128]{2,1,0:T(8,128)S(1)}, u32[]{:S(2)}, u32[]{:S(2)}) collective-permute-start(f32[2,64,128]{2,1,0:T(8,128)S(1)} %pad_maximum_fusion.2), channel_id=1, source_target_pairs={{0,6},{1,7},{2,4},{3,5},{4,2},{5,3},{6,0},{7,1},{8,14},{9,15},{10,... | collective-permute-start | bytes 196616 | tf_op jit(solution)/shard_map/ppermute | solution.py:56
  15.3 6.1 %collective-permute-start.2 = (f32[2,64,128]{2,1,0:T(8,128)S(1)}, f32[2,64,128]{2,1,0:T(8,128)S(1)}, u32[]{:S(2)}, u32[]{:S(2)}) collective-permute-start(f32[2,64,128]{2,1,0:T(8,128)S(1)} %pad_maximum_fusion.2), channel_id=1, source_target_pairs={{0,4},{1,5},{2,6},{3,7},{4,0},{5,1},{6,2},{7,3},{8,12},{9,13},{10,... | collective-permute-start | bytes 196616 | tf_op jit(solution)/shard_map/ppermute | solution.py:56
  15.3 4.6 %collective-permute-start.1 = (f32[2,64,128]{2,1,0:T(8,128)S(1)}, f32[2,64,128]{2,1,0:T(8,128)S(1)}, u32[]{:S(2)}, u32[]{:S(2)}) collective-permute-start(f32[2,64,128]{2,1,0:T(8,128)S(1)} %pad_maximum_fusion.2), channel_id=1, source_target_pairs={{0,2},{1,3},{2,0},{3,1},{4,6},{5,7},{6,4},{7,5},{8,10},{9,11},{10,... | collective-permute-start | bytes 196616 | tf_op jit(solution)/shard_map/ppermute | solution.py:56
  21.5 17.7 %collective-permute-start.4 = (f32[8,64,128]{2,1,0:T(8,128)S(1)}, f32[8,64,128]{2,1,0:T(8,128)S(1)}, u32[]{:S(2)}, u32[]{:S(2)}) collective-permute-start(f32[8,64,128]{2,1,0:T(8,128)S(1)} %get-tuple-element.46), channel_id=1, source_target_pairs={{0,8},{1,9},{2,10},{3,11},{4,12},{5,13},{6,14},{7,15},{8,0},{9,1},... | collective-permute-start | bytes 786440 | tf_op jit(solution)/shard_map/ppermute | solution.py:56
  27.8 1.0 copy-start
  33.2 16.5 %all-to-all-start.1 = ((f32[16,56,128]{2,1,0:T(8,128)}), f32[16,56,128]{2,1,0:T(8,128)S(1)}, u32[]{:S(2)}, u32[]{:S(2)}) async-start(f32[16,56,128]{2,1,0:T(8,128)} %transport.1), calls=%async_computation.1 | async-start | bytes 917504 | tf_op jit(solution)/shard_map/all_to_all | solution.py:33
  39.3 10.5 %copy-start.6 = (f32[16,64,128]{2,1,0:T(8,128)}, f32[16,64,128]{2,1,0:T(8,128)S(1)}, u32[]{:S(2)}) copy-start(f32[16,64,128]{2,1,0:T(8,128)S(1)} %constant_dynamic-update-slice_fusion.5.cells_ref) | copy-start | bytes 1572868
  39.3 20.1 %collective-permute-start.6 = (f32[1,2,16,128]{3,2,1,0:T(8,128)S(1)}, f32[1,2,16,128]{3,2,1,0:T(8,128)S(1)}, u32[]{:S(2)}, u32[]{:S(2)}) collective-permute-start(f32[1,2,16,128]{3,2,1,0:T(8,128)S(1)} %get-tuple-element.72), channel_id=1, source_target_pairs={{0,112},{16,0},{32,16},{48,32},{64,48},{80,64},{96,80},{112,96},{1... | collective-permute-start | bytes 49160 | tf_op jit(solution)/shard_map/ppermute | solution.py:379
  40.7 18.7 %collective-permute-start.5 = (f32[1,2,16,128]{3,2,1,0:T(8,128)S(1)}, f32[1,2,16,128]{3,2,1,0:T(8,128)S(1)}, u32[]{:S(2)}, u32[]{:S(2)}) collective-permute-start(f32[1,2,16,128]{3,2,1,0:T(8,128)S(1)} %get-tuple-element.73), channel_id=1, source_target_pairs={{0,16},{16,32},{32,48},{48,64},{64,80},{80,96},{96,112},{112,0},{1... | collective-permute-start | bytes 49160 | tf_op jit(solution)/shard_map/ppermute | solution.py:378
  49.8 0.8 copy-start.5
  55.8 18.8 %all-to-all-start.2 = ((f32[16,112,128]{2,1,0:T(8,128)}), f32[16,112,128]{2,1,0:T(8,128)S(1)}, u32[]{:S(2)}, u32[]{:S(2)}) async-start(f32[16,112,128]{2,1,0:T(8,128)} %get-tuple-element.18), calls=%async_computation.2 | async-start | bytes 1835008 | tf_op jit(solution)/shard_map/all_to_all | solution.py:33
  59.6 15.0 %copy-start.8 = (f32[6,64,128]{2,1,0:T(8,128)}, f32[6,64,128]{2,1,0:T(8,128)S(1)}, u32[]{:S(2)}) copy-start(f32[6,64,128]{2,1,0:T(8,128)S(1)} %constant_dynamic-update-slice_fusion.11.steps_ref) | copy-start | bytes 589828
  74.6 0.9 copy-start.1
  78.4 15.2 %all-to-all-start.3 = ((f32[16,72,128]{2,1,0:T(8,128)}), f32[16,72,128]{2,1,0:T(8,128)S(1)}, u32[]{:S(2)}, u32[]{:S(2)}) async-start(f32[16,72,128]{2,1,0:T(8,128)} %get-tuple-element.20), calls=%async_computation.3 | async-start | bytes 1179648 | tf_op jit(solution)/shard_map/all_to_all | solution.py:33
  93.6 0.8 copy-start.2
  101.3 7.4 %collective-permute-start.7 = (f32[8,512]{1,0:T(8,128)S(1)}, f32[8,512]{1,0:T(8,128)S(1)}, u32[]{:S(2)}, u32[]{:S(2)}) collective-permute-start(f32[8,512]{1,0:T(8,128)S(1)} %fusion.18), channel_id=1, source_target_pairs={{0,16},{16,32},{32,48},{48,64},{64,80},{80,96},{96,112},{112,0},{1... | collective-permute-start | bytes 49160 | tf_op jit(solution)/shard_map/ppermute | solution.py:440
  108.9 5.4 %collective-permute-start.8 = (f32[40,128]{1,0:T(8,128)S(1)}, f32[40,128]{1,0:T(8,128)S(1)}, u32[]{:S(2)}, u32[]{:S(2)}) collective-permute-start(f32[40,128]{1,0:T(8,128)S(1)} %constant_dynamic-update-slice_fusion.17), channel_id=1, source_target_pairs={{0,16},{16,0},{32,48},{48,32},{64,80},{80,64},{96,112},{112,96},{1... | collective-permute-start | bytes 61448 | tf_op jit(solution)/shard_map/ppermute | solution.py:56
  114.3 7.8 %collective-permute-start.11 = (f32[40,128]{1,0:T(8,128)S(1)}, f32[40,128]{1,0:T(8,128)S(1)}, u32[]{:S(2)}, u32[]{:S(2)}) collective-permute-start(f32[40,128]{1,0:T(8,128)S(1)} %add.404), channel_id=1, source_target_pairs={{0,96},{16,112},{32,64},{48,80},{64,32},{80,48},{96,0},{112,16},{1... | collective-permute-start | bytes 61448 | tf_op jit(solution)/shard_map/ppermute | solution.py:56
  114.4 7.7 %collective-permute-start.10 = (f32[40,128]{1,0:T(8,128)S(1)}, f32[40,128]{1,0:T(8,128)S(1)}, u32[]{:S(2)}, u32[]{:S(2)}) collective-permute-start(f32[40,128]{1,0:T(8,128)S(1)} %add.404), channel_id=1, source_target_pairs={{0,64},{16,80},{32,96},{48,112},{64,0},{80,16},{96,32},{112,48},{1... | collective-permute-start | bytes 61448 | tf_op jit(solution)/shard_map/ppermute | solution.py:56
  115.1 7.0 %collective-permute-start.9 = (f32[40,128]{1,0:T(8,128)S(1)}, f32[40,128]{1,0:T(8,128)S(1)}, u32[]{:S(2)}, u32[]{:S(2)}) collective-permute-start(f32[40,128]{1,0:T(8,128)S(1)} %add.404), channel_id=1, source_target_pairs={{0,32},{16,48},{32,0},{48,16},{64,96},{80,112},{96,64},{112,80},{1... | collective-permute-start | bytes 61448 | tf_op jit(solution)/shard_map/ppermute | solution.py:56
  118.5 17.4 %all-to-all-start.4 = ((f32[8,256,128]{2,1,0:T(8,128)}), f32[8,256,128]{2,1,0:T(8,128)S(1)}, u32[]{:S(2)}, u32[]{:S(2)}) async-start(f32[8,256,128]{2,1,0:T(8,128)} %back.1), calls=%async_computation.4 | async-start | bytes 2097152 | tf_op jit(solution)/shard_map/all_to_all | solution.py:33
  122.1 1.3 collective-permute-start.12
  123.4 6.5 %collective-permute-start.15 = (f32[2,40,128]{2,1,0:T(8,128)S(1)}, f32[2,40,128]{2,1,0:T(8,128)S(1)}, u32[]{:S(2)}, u32[]{:S(2)}) collective-permute-start(f32[2,40,128]{2,1,0:T(8,128)S(1)} %pad_maximum_fusion.3), channel_id=1, source_target_pairs={{0,6},{1,7},{2,4},{3,5},{4,2},{5,3},{6,0},{7,1},{8,14},{9,15},{10,... | collective-permute-start | bytes 122888 | tf_op jit(solution)/shard_map/ppermute | solution.py:56
  124.3 5.6 %collective-permute-start.14 = (f32[2,40,128]{2,1,0:T(8,128)S(1)}, f32[2,40,128]{2,1,0:T(8,128)S(1)}, u32[]{:S(2)}, u32[]{:S(2)}) collective-permute-start(f32[2,40,128]{2,1,0:T(8,128)S(1)} %pad_maximum_fusion.3), channel_id=1, source_target_pairs={{0,4},{1,5},{2,6},{3,7},{4,0},{5,1},{6,2},{7,3},{8,12},{9,13},{10,... | collective-permute-start | bytes 122888 | tf_op jit(solution)/shard_map/ppermute | solution.py:56
  124.3 5.6 %collective-permute-start.13 = (f32[2,40,128]{2,1,0:T(8,128)S(1)}, f32[2,40,128]{2,1,0:T(8,128)S(1)}, u32[]{:S(2)}, u32[]{:S(2)}) collective-permute-start(f32[2,40,128]{2,1,0:T(8,128)S(1)} %pad_maximum_fusion.3), channel_id=1, source_target_pairs={{0,2},{1,3},{2,0},{3,1},{4,6},{5,7},{6,4},{7,5},{8,10},{9,11},{10,... | collective-permute-start | bytes 122888 | tf_op jit(solution)/shard_map/ppermute | solution.py:56
  130.0 5.6 %collective-permute-start.16 = (f32[8,40,128]{2,1,0:T(8,128)S(1)}, f32[8,40,128]{2,1,0:T(8,128)S(1)}, u32[]{:S(2)}, u32[]{:S(2)}) collective-permute-start(f32[8,40,128]{2,1,0:T(8,128)S(1)} %get-tuple-element.52), channel_id=1, source_target_pairs={{0,8},{1,9},{2,10},{3,11},{4,12},{5,13},{6,14},{7,15},{8,0},{9,1},... | collective-permute-start | bytes 491528 | tf_op jit(solution)/shard_map/ppermute | solution.py:56
  135.6 0.7 copy-start.7
  135.9 1.0 copy-start.3
  146.0 1.5 collective-permute-start.17
  148.4 5.5 %collective-permute-start.20 = (f32[128,128]{1,0:T(8,128)S(1)}, f32[128,128]{1,0:T(8,128)S(1)}, u32[]{:S(2)}, u32[]{:S(2)}) collective-permute-start(f32[128,128]{1,0:T(8,128)S(1)} %add.415), channel_id=1, source_target_pairs={{0,6},{1,7},{2,4},{3,5},{4,2},{5,3},{6,0},{7,1},{8,14},{9,15},{10,... | collective-permute-start | bytes 196616 | tf_op jit(solution)/shard_map/ppermute | solution.py:56
  150.5 6.1 %collective-permute-start.19 = (f32[128,128]{1,0:T(8,128)S(1)}, f32[128,128]{1,0:T(8,128)S(1)}, u32[]{:S(2)}, u32[]{:S(2)}) collective-permute-start(f32[128,128]{1,0:T(8,128)S(1)} %add.415), channel_id=1, source_target_pairs={{0,4},{1,5},{2,6},{3,7},{4,0},{5,1},{6,2},{7,3},{8,12},{9,13},{10,... | collective-permute-start | bytes 196616 | tf_op jit(solution)/shard_map/ppermute | solution.py:56
  151.9 4.6 %collective-permute-start.18 = (f32[128,128]{1,0:T(8,128)S(1)}, f32[128,128]{1,0:T(8,128)S(1)}, u32[]{:S(2)}, u32[]{:S(2)}) collective-permute-start(f32[128,128]{1,0:T(8,128)S(1)} %add.415), channel_id=1, source_target_pairs={{0,2},{1,3},{2,0},{3,1},{4,6},{5,7},{6,4},{7,5},{8,10},{9,11},{10,... | collective-permute-start | bytes 196616 | tf_op jit(solution)/shard_map/ppermute | solution.py:56
  156.6 5.6 %collective-permute-start.23 = (f32[128,128]{1,0:T(8,128)S(1)}, f32[128,128]{1,0:T(8,128)S(1)}, u32[]{:S(2)}, u32[]{:S(2)}) collective-permute-start(f32[128,128]{1,0:T(8,128)S(1)} %add_add_fusion.2), channel_id=1, source_target_pairs={{0,24},{1,25},{2,26},{3,27},{4,28},{5,29},{6,30},{7,31},{8,16},{9,... | collective-permute-start | bytes 196616 | tf_op jit(solution)/shard_map/ppermute | solution.py:56
  159.7 5.8 %collective-permute-start.22 = (f32[128,128]{1,0:T(8,128)S(1)}, f32[128,128]{1,0:T(8,128)S(1)}, u32[]{:S(2)}, u32[]{:S(2)}) collective-permute-start(f32[128,128]{1,0:T(8,128)S(1)} %add_add_fusion.2), channel_id=1, source_target_pairs={{0,16},{1,17},{2,18},{3,19},{4,20},{5,21},{6,22},{7,23},{8,24},{9,... | collective-permute-start | bytes 196616 | tf_op jit(solution)/shard_map/ppermute | solution.py:56
  160.2 5.3 %collective-permute-start.21 = (f32[128,128]{1,0:T(8,128)S(1)}, f32[128,128]{1,0:T(8,128)S(1)}, u32[]{:S(2)}, u32[]{:S(2)}) collective-permute-start(f32[128,128]{1,0:T(8,128)S(1)} %add_add_fusion.2), channel_id=1, source_target_pairs={{0,8},{1,9},{2,10},{3,11},{4,12},{5,13},{6,14},{7,15},{8,0},{9,1},... | collective-permute-start | bytes 196616 | tf_op jit(solution)/shard_map/ppermute | solution.py:56
  165.5 5.6 %collective-permute-start.26 = (f32[128,128]{1,0:T(8,128)S(1)}, f32[128,128]{1,0:T(8,128)S(1)}, u32[]{:S(2)}, u32[]{:S(2)}) collective-permute-start(f32[128,128]{1,0:T(8,128)S(1)} %add_add_fusion.1), channel_id=1, source_target_pairs={{0,96},{1,97},{2,98},{3,99},{4,100},{5,101},{6,102},{7,103},{8,104... | collective-permute-start | bytes 196616 | tf_op jit(solution)/shard_map/ppermute | solution.py:56
  168.3 5.8 %collective-permute-start.25 = (f32[128,128]{1,0:T(8,128)S(1)}, f32[128,128]{1,0:T(8,128)S(1)}, u32[]{:S(2)}, u32[]{:S(2)}) collective-permute-start(f32[128,128]{1,0:T(8,128)S(1)} %add_add_fusion.1), channel_id=1, source_target_pairs={{0,64},{1,65},{2,66},{3,67},{4,68},{5,69},{6,70},{7,71},{8,72},{9,... | collective-permute-start | bytes 196616 | tf_op jit(solution)/shard_map/ppermute | solution.py:56
  169.2 4.9 %collective-permute-start.24 = (f32[128,128]{1,0:T(8,128)S(1)}, f32[128,128]{1,0:T(8,128)S(1)}, u32[]{:S(2)}, u32[]{:S(2)}) collective-permute-start(f32[128,128]{1,0:T(8,128)S(1)} %add_add_fusion.1), channel_id=1, source_target_pairs={{0,32},{1,33},{2,34},{3,35},{4,36},{5,37},{6,38},{7,39},{8,40},{9,... | collective-permute-start | bytes 196616 | tf_op jit(solution)/shard_map/ppermute | solution.py:56

commit v3 on v2

--- a/solution.py
+++ b/solution.py
@@ -52,7 +52,8 @@
 
 
 def from_peer(values, axis, mask):
-    peers = lax.axis_size(axis)
+    axes = axis if isinstance(axis, tuple) else (axis,)
+    peers = math.prod(lax.axis_size(name) for name in axes)
     return lax.ppermute(values, axis, [(i, i ^ mask) for i in range(peers)])
 
 
@@ -71,14 +72,16 @@
 
 
 def gather_relative(array, axis, groups):
-    array = array[None]
+    return gather_more(array[None], axis, groups)
+
+
+def gather_more(array, axis, groups):
     for masks in groups:
         array = jnp.concatenate([array] + [from_peer(array, axis, mask) for mask in masks], axis=0)
     return array
 
 
 BRICK_GROUPS = ((1,), (2, 4, 6), (8,))
-SLAB_GROUPS = ((1,), (2, 4, 6))
 ALL_GROUPS = ((1,), (2, 4, 6), (8, 16, 24), (32, 64, 96))
 
 
@@ -285,13 +288,14 @@
     rows = basis_ref.shape[0]
     height = rank // bricks
     cells = advanced_ref.shape[0]
-    brick = brick_ref[0]
+    masks = [j ^ brick_ref[0] for j in range(bricks)]
+    slots = [((m >> 1) & 3) * 4 + (m & 1) * 2 + (m >> 3) for m in masks]
 
     def piece(ref, i):
         if ref is transport_ref:
             start = cells + i * height
             return ref[:, start : start + height, :].reshape(rank, rank)
-        rows_of = [ref[j ^ brick, i * height : (i + 1) * height, :] for j in range(bricks)]
+        rows_of = [ref[slot, i * height : (i + 1) * height, :] for slot in slots]
         return jnp.concatenate(rows_of, axis=0)
 
     factor_into(piece(pieces_ref, 0) * weight_x, work_ref, upper_ref, inverse_ref)
@@ -438,12 +442,6 @@
     choose = (choose[:, None] == jnp.arange(rank, dtype=jnp.int32)[None]).astype(jnp.float32)
     chosen = contract(choose, planes_x[-1], 1, 1)
     chosen_below = lax.ppermute(chosen, "slab", up)
-    back = pl.pallas_call(back_kernel, out_shape=f32(slabs, rows, rank), name="back")(
-        third, line, state, across[1:].T
-    )
-    back, slab_advanced = lax.optimization_barrier((back, slab_advanced))
-    fourth = exchange(back, "slab")
-
     adv_grid = slab_advanced.reshape(bricks, cells_x, cells_y, cells_z, rank)
     planes_x = [adv_grid[:, i].reshape(half, rank) for i in range(cells_x)]
     before = jnp.concatenate([adv_grid[-1:, :, -1:], adv_grid[:-1, :, -1:]], axis=0)
@@ -468,8 +466,17 @@
         ],
         axis=0,
     )
-    pieces = sum_over(pieces, "slab", SLAB_GROUPS)
-    reduced = gather_relative(pieces, "brick", BRICK_GROUPS)
+    pieces, third_after = lax.optimization_barrier((pieces, third))
+    back = pl.pallas_call(back_kernel, out_shape=f32(slabs, rows, rank), name="back")(
+        third_after, line, state, across[1:].T
+    )
+    fourth = exchange(back, "slab")
+
+    both = ("slab", "brick")
+    lower_x, upper_x, cross_x = (from_peer(pieces, both, mask) for mask in (8, 16, 24))
+    reduced = jnp.stack([pieces + upper_x, lower_x + cross_x])
+    reduced = sum_over(reduced, both, ((32, 64, 96),))
+    reduced = gather_more(reduced, both, ((1,), (2, 4, 6)))
 
     speeds = jnp.stack(list(own_velocity) + [jnp.zeros_like(ones)] * 5, axis=1)
     basis_new, velocity_new, gram_part = pl.pallas_call(

time: 181 us -> 178 us (0.983)
  waiting for transfers between devices: 72.4 us -> 67 us
  starting transfers between devices: 56 us -> 59.5 us
    ppermute x24 -> x25, waiting for transfers between devices: 32.3 us -> 24.2 us  [from_peer(): return lax.ppermute(values, axis, [(i, i ^ mask) for i in range(peers)])]
    all_to_all x5, waiting for transfers between devices: 36.5 us -> 39.4 us  [exchange(): return lax.all_to_all(array, axis, 0, 0, tiled=True)]
    ppermute x24 -> x25, starting transfers between devices: 27.5 us -> 29.9 us  [from_peer(): return lax.ppermute(values, axis, [(i, i ^ mask) for i in range(peers)])]
    unnamed x34 -> x33, local copies, waits for them, and re-layouts: 3.79 us -> 3.04 us
  transfers between devices with their start and end apart: 32 -> 33, of which waited for: 19 -> 23; matrix products, arithmetic and copies ran while one was open for 6% -> 6% of each run, Pallas kernels for 5% -> 8%
where the time goes in v3:
time: 178 us; the launch traced here: 177 us
  waiting for transfers between devices  67 us (38%)
  starting transfers between devices  59.5 us (33%)
  Pallas kernels  32.1 us (18%)
  local copies, waits for them, and re-layouts  10.3 us (6%)
  matrix products  4.12 us (2%)
  other arithmetic  2.46 us (1%)
    all_to_all x5, waiting for transfers between devices, exchange(): return lax.all_to_all(array, axis, 0, 0, tiled=True)  39.4 us
    ppermute x25, starting transfers between devices, from_peer(): return lax.ppermute(values, axis, [(i, i ^ mask) for i in range(peers)])  29.9 us
    all_to_all x5, starting transfers between devices, exchange(): return lax.all_to_all(array, axis, 0, 0, tiled=True)  25.1 us
    ppermute x25, waiting for transfers between devices, from_peer(): return lax.ppermute(values, axis, [(i, i ^ mask) for i in range(peers)])  24.2 us
    pallas_call x1, Pallas kernels, local(): pl.pallas_call(functools.partial(middle_kernel, lengths=lengths, time_ste...  9.19 us
    pallas_call x1, Pallas kernels, local(): pl.pallas_call(last_kernel, out_shape=(f32(rank, rank), f32(rows, rank)),...  5.44 us
    pallas_call x1, Pallas kernels, local(): pl.pallas_call(maxwell_kernel, out_shape=(f32(bricks, cells + 6 * height,...  5.25 us
    pallas_call x1, Pallas kernels, local(): pl.pallas_call(back_kernel, out_shape=f32(slabs, rows, rank), name='back')  4.89 us
  transfers between devices with their start and end apart: 33, of which 23 were waited for; matrix products, arithmetic and copies ran while one was open for 6% of the time, Pallas kernels for 8%

profile of v3, /device:TPU:0, one launch (start us, length us, event | category | flops | bytes accessed | tf_op | source)
XLA Modules:
  0.0 176.7 jit_solution(1907187250740163442)
XLA Ops:
  0.7 1.9 %broadcast_in_dim.9 = f32[8,256,128]{2,1,0:T(8,128)} broadcast(f32[256,128]{1,0:T(8,128)} %basis_ref.1), dimensions={1,2} | broadcast | bytes 1179648 | tf_op jit(solution)/shard_map/broadcast_in_dim | solution.py:38
  2.7 7.1 %all-to-all-start = ((f32[8,256,128]{2,1,0:T(8,128)}), f32[8,256,128]{2,1,0:T(8,128)S(1)}, u32[]{:S(2)}, u32[]{:S(2)}) async-start(f32[8,256,128]{2,1,0:T(8,128)} %broadcast_in_dim.9), calls=%async_computation | async-start | bytes 2097152 | tf_op jit(solution)/shard_map/all_to_all | solution.py:33
  10.5 0.8 slice_bitcast_fusion.4
  11.2 2.0 %collective-permute-start.1 = (f32[2,64,128]{2,1,0:T(8,128)S(1)}, f32[2,64,128]{2,1,0:T(8,128)S(1)}, u32[]{:S(2)}, u32[]{:S(2)}) collective-permute-start(f32[2,64,128]{2,1,0:T(8,128)S(1)} %pad_maximum_fusion.3), channel_id=1, source_target_pairs={{0,2},{1,3},{2,0},{3,1},{4,6},{5,7},{6,4},{7,5},{8,10},{9,11},{10,... | collective-permute-start | bytes 196616 | tf_op jit(solution)/shard_map/ppermute | solution.py:57
  13.2 3.6 %collective-permute-start.2 = (f32[2,64,128]{2,1,0:T(8,128)S(1)}, f32[2,64,128]{2,1,0:T(8,128)S(1)}, u32[]{:S(2)}, u32[]{:S(2)}) collective-permute-start(f32[2,64,128]{2,1,0:T(8,128)S(1)} %pad_maximum_fusion.3), channel_id=1, source_target_pairs={{0,4},{1,5},{2,6},{3,7},{4,0},{5,1},{6,2},{7,3},{8,12},{9,13},{10,... | collective-permute-start | bytes 196616 | tf_op jit(solution)/shard_map/ppermute | solution.py:57
  16.9 3.6 %collective-permute-done.2 = f32[2,64,128]{2,1,0:T(8,128)S(1)} collective-permute-done((f32[2,64,128]{2,1,0:T(8,128)S(1)}, f32[2,64,128]{2,1,0:T(8,128)S(1)}, u32[]{:S(2)}, u32[]{:S(2)}) %collective-permute-start.2) | collective-permute-done | bytes 65568 | tf_op jit(solution)/shard_map/ppermute | solution.py:57
  20.4 1.9 %collective-permute-done.3 = f32[2,64,128]{2,1,0:T(8,128)S(1)} collective-permute-done((f32[2,64,128]{2,1,0:T(8,128)S(1)}, f32[2,64,128]{2,1,0:T(8,128)S(1)}, u32[]{:S(2)}, u32[]{:S(2)}) %collective-permute-start.3) | collective-permute-done | bytes 65568 | tf_op jit(solution)/shard_map/ppermute | solution.py:57
  22.3 0.7 collective-permute-start.4
  23.4 0.8 copy.31.columns_ref
  24.2 0.7 copy.32.across_ref
  24.9 0.7 stack.61.weights_ref
  25.6 2.1 %all-to-all-done.nodes_ref = f32[8,256,128]{2,1,0:T(8,128)S(1)} async-done(((f32[8,256,128]{2,1,0:T(8,128)}), f32[8,256,128]{2,1,0:T(8,128)S(1)}, u32[]{:S(2)}, u32[]{:S(2)}) %all-to-all-start) | async-done | bytes 1048608 | tf_op jit(solution)/shard_map/all_to_all | solution.py:33
  27.7 0.7 broadcast_in_dim.11.speeds_ref.first_ref
  28.7 4.5 %transport.1 = f32[16,56,128]{2,1,0:T(8,128)} custom-call(f32[8,256,128]{2,1,0:T(8,128)} %copy-done, f32[256,8]{1,0:T(8,128)} %copy.31.columns_ref, f32[8,128]{1,0:T(8,128)} %broadcast_in_dim.11.speeds_ref.first_ref, f32[8,8,256]{2,1,0:T(8,128)} %stack.61.weights_ref), custom_call_target="tpu_custom_call" | custom-call | tf_op jit(solution)/shard_map/transport/pallas_call | solution.py:391
  33.1 6.1 %all-to-all-start.1 = ((f32[16,56,128]{2,1,0:T(8,128)}), f32[16,56,128]{2,1,0:T(8,128)S(1)}, u32[]{:S(2)}, u32[]{:S(2)}) async-start(f32[16,56,128]{2,1,0:T(8,128)} %transport.1), calls=%async_computation.1 | async-start | bytes 917504 | tf_op jit(solution)/shard_map/all_to_all | solution.py:33
  39.3 1.6 collective-permute-start.6
  40.9 2.0 %collective-permute-start.5 = (f32[1,2,16,128]{3,2,1,0:T(8,128)S(1)}, f32[1,2,16,128]{3,2,1,0:T(8,128)S(1)}, u32[]{:S(2)}, u32[]{:S(2)}) collective-permute-start(f32[1,2,16,128]{3,2,1,0:T(8,128)S(1)} %get-tuple-element.69), channel_id=1, source_target_pairs={{0,16},{16,32},{32,48},{48,64},{64,80},{80,96},{96,112},{112,0},{1... | collective-permute-start | bytes 49160 | tf_op jit(solution)/shard_map/ppermute | solution.py:382
  42.9 6.8 %all-to-all-done.1.integrals_ref = f32[16,56,128]{2,1,0:T(8,128)S(1)} async-done(((f32[16,56,128]{2,1,0:T(8,128)}), f32[16,56,128]{2,1,0:T(8,128)S(1)}, u32[]{:S(2)}, u32[]{:S(2)}) %all-to-all-start.1) | async-done | bytes 458784 | tf_op jit(solution)/shard_map/all_to_all | solution.py:33
  49.8 0.8 copy-done.5
  50.5 5.3 %maxwell.1 = (f32[16,112,128]{2,1,0:T(8,128)}, f32[1024,8]{1,0:T(8,128)}, f32[8,1024]{1,0:T(8,128)}) custom-call(s32[1]{0:T(128)} %bitcast.brick_ref, f32[16,64,128]{2,1,0:T(8,128)} %copy-done.6, f32[16,56,128]{2,1,0:T(8,128)} %copy-done.5, f32[8,256,128]{2,1,0:T(8,128)} %copy-done, f32[8,128]{1,0:T(8,128)} %broadcast_in_dim.11.speeds_ref.first_ref, ...), custom_call_target="tpu_custom_call" | custom-call | tf_op jit(solution)/shard_map/maxwell/pallas_call | solution.py:399
  55.8 3.6 %all-to-all-start.2 = ((f32[16,112,128]{2,1,0:T(8,128)}), f32[16,112,128]{2,1,0:T(8,128)S(1)}, u32[]{:S(2)}, u32[]{:S(2)}) async-start(f32[16,112,128]{2,1,0:T(8,128)} %get-tuple-element.18), calls=%async_computation.2 | async-start | bytes 1835008 | tf_op jit(solution)/shard_map/all_to_all | solution.py:33
  59.6 15.0 %all-to-all-done.2.parts_ref.transport_ref = f32[16,112,128]{2,1,0:T(8,128)S(1)} async-done(((f32[16,112,128]{2,1,0:T(8,128)}), f32[16,112,128]{2,1,0:T(8,128)S(1)}, u32[]{:S(2)}, u32[]{:S(2)}) %all-to-all-start.2) | async-done | bytes 917536 | tf_op jit(solution)/shard_map/all_to_all | solution.py:33
  74.6 0.9 copy-done.2
  75.5 2.9 %advance.1 = (f32[16,72,128]{2,1,0:T(8,128)}, f32[64,128]{1,0:T(8,128)}) custom-call(f32[16,112,128]{2,1,0:T(8,128)} %copy-done.2, f32[6,64,128]{2,1,0:T(8,128)} %copy-done.8, f32[64,128]{1,0:T(8,128)} %bitcast.78), custom_call_target="tpu_custom_call" | custom-call | tf_op jit(solution)/shard_map/advance/pallas_call | solution.py:430
  78.4 3.6 %all-to-all-start.3 = ((f32[16,72,128]{2,1,0:T(8,128)}), f32[16,72,128]{2,1,0:T(8,128)S(1)}, u32[]{:S(2)}, u32[]{:S(2)}) async-start(f32[16,72,128]{2,1,0:T(8,128)} %get-tuple-element.20), calls=%async_computation.3 | async-start | bytes 1179648 | tf_op jit(solution)/shard_map/all_to_all | solution.py:33
  82.0 11.5 %all-to-all-done.3.parts_ref = f32[16,72,128]{2,1,0:T(8,128)S(1)} async-done(((f32[16,72,128]{2,1,0:T(8,128)}), f32[16,72,128]{2,1,0:T(8,128)S(1)}, u32[]{:S(2)}, u32[]{:S(2)}) %all-to-all-start.3) | async-done | bytes 589856 | tf_op jit(solution)/shard_map/all_to_all | solution.py:33
  94.6 0.9 collective-permute-start.7
  95.5 1.0 fusion.41
  96.7 1.0 fusion.42
  97.7 1.0 convolution_bitcast_fusion
  98.7 3.4 %collective-permute-done.7 = f32[8,512]{1,0:T(8,128)S(1)} collective-permute-done((f32[8,512]{1,0:T(8,128)S(1)}, f32[8,512]{1,0:T(8,128)S(1)}, u32[]{:S(2)}, u32[]{:S(2)}) %collective-permute-start.7) | collective-permute-done | bytes 16416 | tf_op jit(solution)/shard_map/ppermute | solution.py:444
  103.2 3.6 %collective-permute-start.10 = (f32[40,128]{1,0:T(8,128)S(1)}, f32[40,128]{1,0:T(8,128)S(1)}, u32[]{:S(2)}, u32[]{:S(2)}) collective-permute-start(f32[40,128]{1,0:T(8,128)S(1)} %constant_dynamic-update-slice_fusion.17), channel_id=1, source_target_pairs={{0,24},{1,25},{2,26},{3,27},{4,28},{5,29},{6,30},{7,31},{8,16},{9,... | collective-permute-start | bytes 61448 | tf_op jit(solution)/shard_map/ppermute | solution.py:57
  106.8 1.0 collective-permute-done.8
  107.8 0.8 collective-permute-done.10
  108.6 1.4 collective-permute-start.12
  110.0 0.7 collective-permute-start.13
  110.6 1.5 collective-permute-start.11
  112.1 4.9 %back.1 = f32[8,256,128]{2,1,0:T(8,128)} custom-call(f32[16,72,128]{2,1,0:T(8,128)} %copy-done.1, f32[1024,8]{1,0:T(8,128)} %get-tuple-element.23.line_ref, f32[8,1024]{1,0:T(8,128)} %get-tuple-element.24.state_ref, f32[256,2]{1,0:T(8,128)} %get-tuple-element.46.across_ref), custom_call_target="tpu_custom_call" | custom-call | tf_op jit(solution)/shard_map/back/pallas_call | solution.py:470
  117.0 4.6 %all-to-all-start.4 = ((f32[8,256,128]{2,1,0:T(8,128)}), f32[8,256,128]{2,1,0:T(8,128)S(1)}, u32[]{:S(2)}, u32[]{:S(2)}) async-start(f32[8,256,128]{2,1,0:T(8,128)} %back.1), calls=%async_computation.4 | async-start | bytes 2097152 | tf_op jit(solution)/shard_map/all_to_all | solution.py:33
  122.1 0.8 copy.36.speeds_ref
  123.0 2.4 %collective-permute-start.16 = (f32[4,40,128]{2,1,0:T(8,128)S(1)}, f32[4,40,128]{2,1,0:T(8,128)S(1)}, u32[]{:S(2)}, u32[]{:S(2)}) collective-permute-start(f32[4,40,128]{2,1,0:T(8,128)S(1)} %pad_maximum_fusion.2), channel_id=1, source_target_pairs={{0,4},{1,5},{2,6},{3,7},{4,0},{5,1},{6,2},{7,3},{8,12},{9,13},{10,... | collective-permute-start | bytes 245768 | tf_op jit(solution)/shard_map/ppermute | solution.py:57
  125.4 2.3 %collective-permute-start.17 = (f32[4,40,128]{2,1,0:T(8,128)S(1)}, f32[4,40,128]{2,1,0:T(8,128)S(1)}, u32[]{:S(2)}, u32[]{:S(2)}) collective-permute-start(f32[4,40,128]{2,1,0:T(8,128)S(1)} %pad_maximum_fusion.2), channel_id=1, source_target_pairs={{0,6},{1,7},{2,4},{3,5},{4,2},{5,3},{6,0},{7,1},{8,14},{9,15},{10,... | collective-permute-start | bytes 245768 | tf_op jit(solution)/shard_map/ppermute | solution.py:57
  128.3 1.7 collective-permute-done.16
  130.0 1.7 collective-permute-done.17
  131.7 4.0 %all-to-all-done.4.back_ref = f32[8,256,128]{2,1,0:T(8,128)S(1)} async-done(((f32[8,256,128]{2,1,0:T(8,128)}), f32[8,256,128]{2,1,0:T(8,128)S(1)}, u32[]{:S(2)}, u32[]{:S(2)}) %all-to-all-start.4) | async-done | bytes 1048608 | tf_op jit(solution)/shard_map/all_to_all | solution.py:33
  135.7 1.0 copy-done.3
  136.6 9.2 %middle.1 = (f32[64,128]{1,0:T(8,128)}, f32[256,128]{1,0:T(8,128)}, f32[128,128]{1,0:T(8,128)}) custom-call(s32[1]{0:T(128)} %bitcast.brick_ref, f32[16,40,128]{2,1,0:T(8,128)} %copy-done.7, f32[16,112,128]{2,1,0:T(8,128)} %copy-done.2, f32[256,128]{1,0:T(8,128)} %basis_ref.1, f32[8,256,128]{2,1,0:T(8,128)} %copy-done.3, ...), custom_call_target="tpu_custom_call" | custom-call | tf_op jit(solution)/shard_map/middle/pallas_call | solution.py:482
  145.8 1.5 collective-permute-done.18
  147.3 0.9 add.419
  148.1 1.5 collective-permute-start.20
  149.6 1.3 collective-permute-start.21
  150.9 0.8 collective-permute-start.19
  151.7 2.4 %collective-permute-done.20 = f32[128,128]{1,0:T(8,128)S(1)} collective-permute-done((f32[128,128]{1,0:T(8,128)S(1)}, f32[128,128]{1,0:T(8,128)S(1)}, u32[]{:S(2)}, u32[]{:S(2)}) %collective-permute-start.20) | collective-permute-done | bytes 65568 | tf_op jit(solution)/shard_map/ppermute | solution.py:57
  154.0 1.3 collective-permute-done.21
  155.4 0.9 collective-permute-start.23
  156.3 2.8 %collective-permute-start.24 = (f32[128,128]{1,0:T(8,128)S(1)}, f32[128,128]{1,0:T(8,128)S(1)}, u32[]{:S(2)}, u32[]{:S(2)}) collective-permute-start(f32[128,128]{1,0:T(8,128)S(1)} %add_add_fusion.2), channel_id=1, source_target_pairs={{0,24},{1,25},{2,26},{3,27},{4,28},{5,29},{6,30},{7,31},{8,16},{9,... | collective-permute-start | bytes 196616 | tf_op jit(solution)/shard_map/ppermute | solution.py:57
  159.2 2.6 %collective-permute-done.23 = f32[128,128]{1,0:T(8,128)S(1)} collective-permute-done((f32[128,128]{1,0:T(8,128)S(1)}, f32[128,128]{1,0:T(8,128)S(1)}, u32[]{:S(2)}, u32[]{:S(2)}) %collective-permute-start.23) | collective-permute-done | bytes 65568 | tf_op jit(solution)/shard_map/ppermute | solution.py:57
  162.1 1.3 collective-permute-done.22
  163.5 1.0 collective-permute-start.26
  164.4 2.0 %collective-permute-start.27 = (f32[128,128]{1,0:T(8,128)S(1)}, f32[128,128]{1,0:T(8,128)S(1)}, u32[]{:S(2)}, u32[]{:S(2)}) collective-permute-start(f32[128,128]{1,0:T(8,128)S(1)} %add_add_fusion.1), channel_id=1, source_target_pairs={{0,96},{1,97},{2,98},{3,99},{4,100},{5,101},{6,102},{7,103},{8,104... | collective-permute-start | bytes 196616 | tf_op jit(solution)/shard_map/ppermute | solution.py:57
  167.0 2.3 %collective-permute-done.26 = f32[128,128]{1,0:T(8,128)S(1)} collective-permute-done((f32[128,128]{1,0:T(8,128)S(1)}, f32[128,128]{1,0:T(8,128)S(1)}, u32[]{:S(2)}, u32[]{:S(2)}) %collective-permute-start.26) | collective-permute-done | bytes 65568 | tf_op jit(solution)/shard_map/ppermute | solution.py:57
  169.3 0.7 collective-permute-done.27
  170.0 0.7 collective-permute-done.25
  171.3 5.4 %last.1 = (f32[128,128]{1,0:T(8,128)}, f32[256,128]{1,0:T(8,128)}) custom-call(f32[128,128]{1,0:T(8,128)} %add_add_fusion.gram_ref, f32[256,128]{1,0:T(8,128)} %get-tuple-element.28.velocity_ref), custom_call_target="tpu_custom_call" | custom-call | tf_op jit(solution)/shard_map/last/pallas_call | solution.py:492
  (115 shorter events, 6.5 us)
Async XLA Ops:
  0.6 10.6 %collective-permute-start = (f32[1,64,128]{2,1,0:T(8,128)}, f32[1,64,128]{2,1,0:T(8,128)S(1)}, u32[]{:S(2)}, u32[]{:S(2)}) collective-permute-start(f32[1,64,128]{2,1,0:T(8,128)} %bitcast.77), channel_id=1, source_target_pairs={{0,1},{1,0},{2,3},{3,2},{4,5},{5,4},{6,7},{7,6},{8,9},{9,8},{10,11... | collective-permute-start | bytes 98312 | tf_op jit(solution)/shard_map/ppermute | solution.py:57
  2.7 7.2 %copy-start.4 = (f32[2,2,16,128]{3,2,1,0:T(8,128)S(1)}, f32[2,2,16,128]{3,2,1,0:T(8,128)}, u32[]{:S(2)}) copy-start(f32[2,2,16,128]{3,2,1,0:T(8,128)} %param.2) | copy-start | bytes 98308
  2.7 25.0 %all-to-all-start = ((f32[8,256,128]{2,1,0:T(8,128)}), f32[8,256,128]{2,1,0:T(8,128)S(1)}, u32[]{:S(2)}, u32[]{:S(2)}) async-start(f32[8,256,128]{2,1,0:T(8,128)} %broadcast_in_dim.9), calls=%async_computation | async-start | bytes 2097152 | tf_op jit(solution)/shard_map/all_to_all | solution.py:33
  11.2 5.6 %collective-permute-start.1 = (f32[2,64,128]{2,1,0:T(8,128)S(1)}, f32[2,64,128]{2,1,0:T(8,128)S(1)}, u32[]{:S(2)}, u32[]{:S(2)}) collective-permute-start(f32[2,64,128]{2,1,0:T(8,128)S(1)} %pad_maximum_fusion.3), channel_id=1, source_target_pairs={{0,2},{1,3},{2,0},{3,1},{4,6},{5,7},{6,4},{7,5},{8,10},{9,11},{10,... | collective-permute-start | bytes 196616 | tf_op jit(solution)/shard_map/ppermute | solution.py:57
  13.2 7.2 %collective-permute-start.2 = (f32[2,64,128]{2,1,0:T(8,128)S(1)}, f32[2,64,128]{2,1,0:T(8,128)S(1)}, u32[]{:S(2)}, u32[]{:S(2)}) collective-permute-start(f32[2,64,128]{2,1,0:T(8,128)S(1)} %pad_maximum_fusion.3), channel_id=1, source_target_pairs={{0,4},{1,5},{2,6},{3,7},{4,0},{5,1},{6,2},{7,3},{8,12},{9,13},{10,... | collective-permute-start | bytes 196616 | tf_op jit(solution)/shard_map/ppermute | solution.py:57
  16.8 5.5 %collective-permute-start.3 = (f32[2,64,128]{2,1,0:T(8,128)S(1)}, f32[2,64,128]{2,1,0:T(8,128)S(1)}, u32[]{:S(2)}, u32[]{:S(2)}) collective-permute-start(f32[2,64,128]{2,1,0:T(8,128)S(1)} %pad_maximum_fusion.3), channel_id=1, source_target_pairs={{0,6},{1,7},{2,4},{3,5},{4,2},{5,3},{6,0},{7,1},{8,14},{9,15},{10,... | collective-permute-start | bytes 196616 | tf_op jit(solution)/shard_map/ppermute | solution.py:57
  22.3 17.0 %collective-permute-start.4 = (f32[8,64,128]{2,1,0:T(8,128)S(1)}, f32[8,64,128]{2,1,0:T(8,128)S(1)}, u32[]{:S(2)}, u32[]{:S(2)}) collective-permute-start(f32[8,64,128]{2,1,0:T(8,128)S(1)} %get-tuple-element.48), channel_id=1, source_target_pairs={{0,8},{1,9},{2,10},{3,11},{4,12},{5,13},{6,14},{7,15},{8,0},{9,1},... | collective-permute-start | bytes 786440 | tf_op jit(solution)/shard_map/ppermute | solution.py:57
  27.7 1.0 copy-start
  33.1 16.6 %all-to-all-start.1 = ((f32[16,56,128]{2,1,0:T(8,128)}), f32[16,56,128]{2,1,0:T(8,128)S(1)}, u32[]{:S(2)}, u32[]{:S(2)}) async-start(f32[16,56,128]{2,1,0:T(8,128)} %transport.1), calls=%async_computation.1 | async-start | bytes 917504 | tf_op jit(solution)/shard_map/all_to_all | solution.py:33
  39.3 10.5 %copy-start.6 = (f32[16,64,128]{2,1,0:T(8,128)}, f32[16,64,128]{2,1,0:T(8,128)S(1)}, u32[]{:S(2)}) copy-start(f32[16,64,128]{2,1,0:T(8,128)S(1)} %constant_dynamic-update-slice_fusion.5.cells_ref) | copy-start | bytes 1572868
  39.3 20.1 %collective-permute-start.6 = (f32[1,2,16,128]{3,2,1,0:T(8,128)S(1)}, f32[1,2,16,128]{3,2,1,0:T(8,128)S(1)}, u32[]{:S(2)}, u32[]{:S(2)}) collective-permute-start(f32[1,2,16,128]{3,2,1,0:T(8,128)S(1)} %get-tuple-element.68), channel_id=1, source_target_pairs={{0,112},{16,0},{32,16},{48,32},{64,48},{80,64},{96,80},{112,96},{1... | collective-permute-start | bytes 49160 | tf_op jit(solution)/shard_map/ppermute | solution.py:383
  40.9 18.5 %collective-permute-start.5 = (f32[1,2,16,128]{3,2,1,0:T(8,128)S(1)}, f32[1,2,16,128]{3,2,1,0:T(8,128)S(1)}, u32[]{:S(2)}, u32[]{:S(2)}) collective-permute-start(f32[1,2,16,128]{3,2,1,0:T(8,128)S(1)} %get-tuple-element.69), channel_id=1, source_target_pairs={{0,16},{16,32},{32,48},{48,64},{64,80},{80,96},{96,112},{112,0},{1... | collective-permute-start | bytes 49160 | tf_op jit(solution)/shard_map/ppermute | solution.py:382
  49.8 0.8 copy-start.5
  55.8 18.8 %all-to-all-start.2 = ((f32[16,112,128]{2,1,0:T(8,128)}), f32[16,112,128]{2,1,0:T(8,128)S(1)}, u32[]{:S(2)}, u32[]{:S(2)}) async-start(f32[16,112,128]{2,1,0:T(8,128)} %get-tuple-element.18), calls=%async_computation.2 | async-start | bytes 1835008 | tf_op jit(solution)/shard_map/all_to_all | solution.py:33
  59.6 15.0 %copy-start.8 = (f32[6,64,128]{2,1,0:T(8,128)}, f32[6,64,128]{2,1,0:T(8,128)S(1)}, u32[]{:S(2)}) copy-start(f32[6,64,128]{2,1,0:T(8,128)S(1)} %constant_dynamic-update-slice_fusion.11.steps_ref) | copy-start | bytes 589828
  74.6 0.9 copy-start.2
  78.4 15.2 %all-to-all-start.3 = ((f32[16,72,128]{2,1,0:T(8,128)}), f32[16,72,128]{2,1,0:T(8,128)S(1)}, u32[]{:S(2)}, u32[]{:S(2)}) async-start(f32[16,72,128]{2,1,0:T(8,128)} %get-tuple-element.20), calls=%async_computation.3 | async-start | bytes 1179648 | tf_op jit(solution)/shard_map/all_to_all | solution.py:33
  93.6 5.1 %copy-start.1 = (f32[16,72,128]{2,1,0:T(8,128)}, f32[16,72,128]{2,1,0:T(8,128)S(1)}, u32[]{:S(2)}) copy-start(f32[16,72,128]{2,1,0:T(8,128)S(1)} %all-to-all-done.3.parts_ref) | copy-start | bytes 1769476
  94.6 7.5 %collective-permute-start.7 = (f32[8,512]{1,0:T(8,128)S(1)}, f32[8,512]{1,0:T(8,128)S(1)}, u32[]{:S(2)}, u32[]{:S(2)}) collective-permute-start(f32[8,512]{1,0:T(8,128)S(1)} %fusion.19), channel_id=1, source_target_pairs={{0,16},{16,32},{32,48},{48,64},{64,80},{80,96},{96,112},{112,0},{1... | collective-permute-start | bytes 49160 | tf_op jit(solution)/shard_map/ppermute | solution.py:444
  102.4 5.4 %collective-permute-start.8 = (f32[40,128]{1,0:T(8,128)S(1)}, f32[40,128]{1,0:T(8,128)S(1)}, u32[]{:S(2)}, u32[]{:S(2)}) collective-permute-start(f32[40,128]{1,0:T(8,128)S(1)} %constant_dynamic-update-slice_fusion.17), channel_id=1, source_target_pairs={{0,16},{1,17},{2,18},{3,19},{4,20},{5,21},{6,22},{7,23},{8,24},{9,... | collective-permute-start | bytes 61448 | tf_op jit(solution)/shard_map/ppermute | solution.py:57
  102.6 5.1 %collective-permute-start.9 = (f32[40,128]{1,0:T(8,128)S(1)}, f32[40,128]{1,0:T(8,128)S(1)}, u32[]{:S(2)}, u32[]{:S(2)}) collective-permute-start(f32[40,128]{1,0:T(8,128)S(1)} %constant_dynamic-update-slice_fusion.17), channel_id=1, source_target_pairs={{0,8},{1,9},{2,10},{3,11},{4,12},{5,13},{6,14},{7,15},{8,0},{9,1},... | collective-permute-start | bytes 61448 | tf_op jit(solution)/shard_map/ppermute | solution.py:57
  103.2 5.3 %collective-permute-start.10 = (f32[40,128]{1,0:T(8,128)S(1)}, f32[40,128]{1,0:T(8,128)S(1)}, u32[]{:S(2)}, u32[]{:S(2)}) collective-permute-start(f32[40,128]{1,0:T(8,128)S(1)} %constant_dynamic-update-slice_fusion.17), channel_id=1, source_target_pairs={{0,24},{1,25},{2,26},{3,27},{4,28},{5,29},{6,30},{7,31},{8,16},{9,... | collective-permute-start | bytes 61448 | tf_op jit(solution)/shard_map/ppermute | solution.py:57
  108.6 13.1 %collective-permute-start.12 = (f32[2,40,128]{2,1,0:T(8,128)S(1)}, f32[2,40,128]{2,1,0:T(8,128)S(1)}, u32[]{:S(2)}, u32[]{:S(2)}) collective-permute-start(f32[2,40,128]{2,1,0:T(8,128)S(1)} %pad_maximum_fusion.4), channel_id=1, source_target_pairs={{0,64},{1,65},{2,66},{3,67},{4,68},{5,69},{6,70},{7,71},{8,72},{9,... | collective-permute-start | bytes 122888 | tf_op jit(solution)/shard_map/ppermute | solution.py:57
  110.0 11.7 %collective-permute-start.13 = (f32[2,40,128]{2,1,0:T(8,128)S(1)}, f32[2,40,128]{2,1,0:T(8,128)S(1)}, u32[]{:S(2)}, u32[]{:S(2)}) collective-permute-start(f32[2,40,128]{2,1,0:T(8,128)S(1)} %pad_maximum_fusion.4), channel_id=1, source_target_pairs={{0,96},{1,97},{2,98},{3,99},{4,100},{5,101},{6,102},{7,103},{8,104... | collective-permute-start | bytes 122888 | tf_op jit(solution)/shard_map/ppermute | solution.py:57
  110.6 11.0 %collective-permute-start.11 = (f32[2,40,128]{2,1,0:T(8,128)S(1)}, f32[2,40,128]{2,1,0:T(8,128)S(1)}, u32[]{:S(2)}, u32[]{:S(2)}) collective-permute-start(f32[2,40,128]{2,1,0:T(8,128)S(1)} %pad_maximum_fusion.4), channel_id=1, source_target_pairs={{0,32},{1,33},{2,34},{3,35},{4,36},{5,37},{6,38},{7,39},{8,40},{9,... | collective-permute-start | bytes 122888 | tf_op jit(solution)/shard_map/ppermute | solution.py:57
  117.0 18.6 %all-to-all-start.4 = ((f32[8,256,128]{2,1,0:T(8,128)}), f32[8,256,128]{2,1,0:T(8,128)S(1)}, u32[]{:S(2)}, u32[]{:S(2)}) async-start(f32[8,256,128]{2,1,0:T(8,128)} %back.1), calls=%async_computation.4 | async-start | bytes 2097152 | tf_op jit(solution)/shard_map/all_to_all | solution.py:33
  121.7 1.3 collective-permute-start.14
  123.0 5.3 %collective-permute-start.15 = (f32[4,40,128]{2,1,0:T(8,128)S(1)}, f32[4,40,128]{2,1,0:T(8,128)S(1)}, u32[]{:S(2)}, u32[]{:S(2)}) collective-permute-start(f32[4,40,128]{2,1,0:T(8,128)S(1)} %pad_maximum_fusion.2), channel_id=1, source_target_pairs={{0,2},{1,3},{2,0},{3,1},{4,6},{5,7},{6,4},{7,5},{8,10},{9,11},{10,... | collective-permute-start | bytes 245768 | tf_op jit(solution)/shard_map/ppermute | solution.py:57
  123.0 7.0 %collective-permute-start.16 = (f32[4,40,128]{2,1,0:T(8,128)S(1)}, f32[4,40,128]{2,1,0:T(8,128)S(1)}, u32[]{:S(2)}, u32[]{:S(2)}) collective-permute-start(f32[4,40,128]{2,1,0:T(8,128)S(1)} %pad_maximum_fusion.2), channel_id=1, source_target_pairs={{0,4},{1,5},{2,6},{3,7},{4,0},{5,1},{6,2},{7,3},{8,12},{9,13},{10,... | collective-permute-start | bytes 245768 | tf_op jit(solution)/shard_map/ppermute | solution.py:57
  125.4 6.3 %collective-permute-start.17 = (f32[4,40,128]{2,1,0:T(8,128)S(1)}, f32[4,40,128]{2,1,0:T(8,128)S(1)}, u32[]{:S(2)}, u32[]{:S(2)}) collective-permute-start(f32[4,40,128]{2,1,0:T(8,128)S(1)} %pad_maximum_fusion.2), channel_id=1, source_target_pairs={{0,6},{1,7},{2,4},{3,5},{4,2},{5,3},{6,0},{7,1},{8,14},{9,15},{10,... | collective-permute-start | bytes 245768 | tf_op jit(solution)/shard_map/ppermute | solution.py:57
  131.7 4.0 %copy-start.7 = (f32[16,40,128]{2,1,0:T(8,128)}, f32[16,40,128]{2,1,0:T(8,128)S(1)}, u32[]{:S(2)}) copy-start(f32[16,40,128]{2,1,0:T(8,128)S(1)} %constant_dynamic-update-slice_fusion.21.pieces_ref) | copy-start | bytes 983044
  135.7 1.0 copy-start.3
  145.8 1.5 collective-permute-start.18
  148.1 5.9 %collective-permute-start.20 = (f32[128,128]{1,0:T(8,128)S(1)}, f32[128,128]{1,0:T(8,128)S(1)}, u32[]{:S(2)}, u32[]{:S(2)}) collective-permute-start(f32[128,128]{1,0:T(8,128)S(1)} %add.419), channel_id=1, source_target_pairs={{0,4},{1,5},{2,6},{3,7},{4,0},{5,1},{6,2},{7,3},{8,12},{9,13},{10,... | collective-permute-start | bytes 196616 | tf_op jit(solution)/shard_map/ppermute | solution.py:57
  149.6 5.8 %collective-permute-start.21 = (f32[128,128]{1,0:T(8,128)S(1)}, f32[128,128]{1,0:T(8,128)S(1)}, u32[]{:S(2)}, u32[]{:S(2)}) collective-permute-start(f32[128,128]{1,0:T(8,128)S(1)} %add.419), channel_id=1, source_target_pairs={{0,6},{1,7},{2,4},{3,5},{4,2},{5,3},{6,0},{7,1},{8,14},{9,15},{10,... | collective-permute-start | bytes 196616 | tf_op jit(solution)/shard_map/ppermute | solution.py:57
  150.9 4.5 %collective-permute-start.19 = (f32[128,128]{1,0:T(8,128)S(1)}, f32[128,128]{1,0:T(8,128)S(1)}, u32[]{:S(2)}, u32[]{:S(2)}) collective-permute-start(f32[128,128]{1,0:T(8,128)S(1)} %add.419), channel_id=1, source_target_pairs={{0,2},{1,3},{2,0},{3,1},{4,6},{5,7},{6,4},{7,5},{8,10},{9,11},{10,... | collective-permute-start | bytes 196616 | tf_op jit(solution)/shard_map/ppermute | solution.py:57
  155.4 6.4 %collective-permute-start.23 = (f32[128,128]{1,0:T(8,128)S(1)}, f32[128,128]{1,0:T(8,128)S(1)}, u32[]{:S(2)}, u32[]{:S(2)}) collective-permute-start(f32[128,128]{1,0:T(8,128)S(1)} %add_add_fusion.2), channel_id=1, source_target_pairs={{0,16},{1,17},{2,18},{3,19},{4,20},{5,21},{6,22},{7,23},{8,24},{9,... | collective-permute-start | bytes 196616 | tf_op jit(solution)/shard_map/ppermute | solution.py:57
  156.3 5.8 %collective-permute-start.24 = (f32[128,128]{1,0:T(8,128)S(1)}, f32[128,128]{1,0:T(8,128)S(1)}, u32[]{:S(2)}, u32[]{:S(2)}) collective-permute-start(f32[128,128]{1,0:T(8,128)S(1)} %add_add_fusion.2), channel_id=1, source_target_pairs={{0,24},{1,25},{2,26},{3,27},{4,28},{5,29},{6,30},{7,31},{8,16},{9,... | collective-permute-start | bytes 196616 | tf_op jit(solution)/shard_map/ppermute | solution.py:57
  159.2 4.3 %collective-permute-start.22 = (f32[128,128]{1,0:T(8,128)S(1)}, f32[128,128]{1,0:T(8,128)S(1)}, u32[]{:S(2)}, u32[]{:S(2)}) collective-permute-start(f32[128,128]{1,0:T(8,128)S(1)} %add_add_fusion.2), channel_id=1, source_target_pairs={{0,8},{1,9},{2,10},{3,11},{4,12},{5,13},{6,14},{7,15},{8,0},{9,1},... | collective-permute-start | bytes 196616 | tf_op jit(solution)/shard_map/ppermute | solution.py:57
  163.5 5.9 %collective-permute-start.26 = (f32[128,128]{1,0:T(8,128)S(1)}, f32[128,128]{1,0:T(8,128)S(1)}, u32[]{:S(2)}, u32[]{:S(2)}) collective-permute-start(f32[128,128]{1,0:T(8,128)S(1)} %add_add_fusion.1), channel_id=1, source_target_pairs={{0,64},{1,65},{2,66},{3,67},{4,68},{5,69},{6,70},{7,71},{8,72},{9,... | collective-permute-start | bytes 196616 | tf_op jit(solution)/shard_map/ppermute | solution.py:57
  164.4 5.6 %collective-permute-start.27 = (f32[128,128]{1,0:T(8,128)S(1)}, f32[128,128]{1,0:T(8,128)S(1)}, u32[]{:S(2)}, u32[]{:S(2)}) collective-permute-start(f32[128,128]{1,0:T(8,128)S(1)} %add_add_fusion.1), channel_id=1, source_target_pairs={{0,96},{1,97},{2,98},{3,99},{4,100},{5,101},{6,102},{7,103},{8,104... | collective-permute-start | bytes 196616 | tf_op jit(solution)/shard_map/ppermute | solution.py:57
  166.4 4.3 %collective-permute-start.25 = (f32[128,128]{1,0:T(8,128)S(1)}, f32[128,128]{1,0:T(8,128)S(1)}, u32[]{:S(2)}, u32[]{:S(2)}) collective-permute-start(f32[128,128]{1,0:T(8,128)S(1)} %add_add_fusion.1), channel_id=1, source_target_pairs={{0,32},{1,33},{2,34},{3,35},{4,36},{5,37},{6,38},{7,39},{8,40},{9,... | collective-permute-start | bytes 196616 | tf_op jit(solution)/shard_map/ppermute | solution.py:57

commit v4 on v3

--- a/solution.py
+++ b/solution.py
@@ -21,6 +21,7 @@
 SPACING = 2.0 * VMAX / NVX
 WEIGHT_V = SPACING**3
 PANEL = 16
+VMEM_BYTES = 24 * 2**20
 
 
 def contract(left, right, left_dim, right_dim, precision=PRECISE):
@@ -389,7 +390,7 @@
     first_velocity = velocities(owner * rows)[0]
     first_speeds = jnp.broadcast_to(first_velocity[:, None], (slabs, rank))
     transport_part = pl.pallas_call(
-        transport_kernel, out_shape=f32(bricks, 8 + 6 * height, rank), name="transport"
+        transport_kernel, out_shape=f32(bricks, 8 + 6 * height, rank), name="transport", compiler_params=pltpu.CompilerParams(vmem_limit_bytes=VMEM_BYTES)
     )(nodes, columns, first_speeds, weights)
     integrals = exchange(transport_part, "brick")
 
@@ -404,7 +405,7 @@
             f32(8, slab_cells),
         ),
         in_specs=vector_specs + [whole] * 5,
-        name="maxwell",
+        name="maxwell", compiler_params=pltpu.CompilerParams(vmem_limit_bytes=VMEM_BYTES),
     )(brick_id, k_slab, integrals, nodes, first_speeds, across[1:])
     second = exchange(payload, "brick")
 
@@ -430,7 +431,7 @@
     payload, advanced = pl.pallas_call(
         functools.partial(advance_kernel, time_step=time_step),
         out_shape=(f32(bricks, cells + height, rank), f32(cells, rank)),
-        name="advance",
+        name="advance", compiler_params=pltpu.CompilerParams(vmem_limit_bytes=VMEM_BYTES),
     )(second, jnp.stack(steps), own_cells)
     third = exchange(payload, "brick")
 
@@ -467,7 +468,7 @@
         axis=0,
     )
     pieces, third_after = lax.optimization_barrier((pieces, third))
-    back = pl.pallas_call(back_kernel, out_shape=f32(slabs, rows, rank), name="back")(
+    back = pl.pallas_call(back_kernel, out_shape=f32(slabs, rows, rank), name="back", compiler_params=pltpu.CompilerParams(vmem_limit_bytes=VMEM_BYTES))(
         third_after, line, state, across[1:].T
     )
     fourth = exchange(back, "slab")
@@ -486,14 +487,14 @@
         out_shape=(f32(cells, rank), f32(rows, rank), f32(rank, rank)),
         in_specs=vector_specs + [whole] * 6,
         scratch_shapes=factor_scratch(rank),
-        name="middle",
+        name="middle", compiler_params=pltpu.CompilerParams(vmem_limit_bytes=VMEM_BYTES),
     )(brick_id, reduced, second, v_basis, fourth, advanced, speeds)
     gram_v = sum_over(gram_part, ("slab", "brick"), ALL_GROUPS)
     coupling, vbasis_new = pl.pallas_call(
         last_kernel,
         out_shape=(f32(rank, rank), f32(rows, rank)),
         scratch_shapes=factor_scratch(rank),
-        name="last",
+        name="last", compiler_params=pltpu.CompilerParams(vmem_limit_bytes=VMEM_BYTES),
     )(gram_v, velocity_new)
     return (basis_new.reshape(cells_x, cells_y, cells_z, rank), coupling, vbasis_new)
 

time: 178 us -> 164 us (0.921)
  Pallas kernels: 32.1 us -> 23.9 us
  local copies, waits for them, and re-layouts: 10.3 us -> 3.57 us
  waiting for transfers between devices: 67 us -> 70.1 us
    unnamed x33 -> x19, local copies, waits for them, and re-layouts: 3.04 us -> 0.12 us
    all_to_all x5, waiting for transfers between devices: 39.4 us -> 42.2 us  [exchange(): return lax.all_to_all(array, axis, 0, 0, tiled=True)]
    pallas_call x1, Pallas kernels: 9.19 us -> 7.21 us  [local(): pl.pallas_call(functools.partial(middle_kernel, lengths=lengths, time_ste...]
  transfers between devices with their start and end apart: 33 -> 33, of which waited for: 23 -> 23; matrix products, arithmetic and copies ran while one was open for 6% -> 4% of each run, Pallas kernels for 8% -> 6%
where the time goes in v4:
time: 164 us; the launch traced here: 163 us
  waiting for transfers between devices  70.1 us (43%)
  starting transfers between devices  59.4 us (36%)
  Pallas kernels  23.9 us (15%)
  matrix products  4.07 us (2%)
  local copies, waits for them, and re-layouts  3.57 us (2%)
    all_to_all x5, waiting for transfers between devices, exchange(): return lax.all_to_all(array, axis, 0, 0, tiled=True)  42.2 us
    ppermute x25, starting transfers between devices, from_peer(): return lax.ppermute(values, axis, [(i, i ^ mask) for i in range(peers)])  29.9 us
    all_to_all x5, starting transfers between devices, exchange(): return lax.all_to_all(array, axis, 0, 0, tiled=True)  25.1 us
    ppermute x25, waiting for transfers between devices, from_peer(): return lax.ppermute(values, axis, [(i, i ^ mask) for i in range(peers)])  24.4 us
    pallas_call x1, Pallas kernels, local(): pl.pallas_call(functools.partial(middle_kernel, lengths=lengths, time_ste...  7.21 us
    pallas_call x1, Pallas kernels, local(): pl.pallas_call(last_kernel, out_shape=(f32(rank, rank), f32(rows, rank)),...  4.5 us
    dot_general x6, matrix products, contract(): lax.dot_general(left, right, (((left_dim,), (right_dim,)), ((), ())), pre...  4.07 us
    pallas_call x1, Pallas kernels, local(): pl.pallas_call(maxwell_kernel, out_shape=(f32(bricks, cells + 6 * height,...  3.74 us
  transfers between devices with their start and end apart: 33, of which 23 were waited for; matrix products, arithmetic and copies ran while one was open for 4% of the time, Pallas kernels for 6%

profile of v4, /device:TPU:0, one launch (start us, length us, event | category | flops | bytes accessed | tf_op | source)
XLA Modules:
  0.0 163.3 jit_solution(17070992425706250214)
XLA Ops:
  0.7 2.0 %broadcast_in_dim.9 = f32[8,256,128]{2,1,0:T(8,128)} broadcast(f32[256,128]{1,0:T(8,128)} %basis_ref.1), dimensions={1,2} | broadcast | bytes 1179648 | tf_op jit(solution)/shard_map/broadcast_in_dim | solution.py:39
  2.7 7.1 %all-to-all-start = ((f32[8,256,128]{2,1,0:T(8,128)}), f32[8,256,128]{2,1,0:T(8,128)S(1)}, u32[]{:S(2)}, u32[]{:S(2)}) async-start(f32[8,256,128]{2,1,0:T(8,128)} %broadcast_in_dim.9), calls=%async_computation | async-start | bytes 2097152 | tf_op jit(solution)/shard_map/all_to_all | solution.py:34
  10.6 2.0 %collective-permute-start.1 = (f32[2,64,128]{2,1,0:T(8,128)S(1)}, f32[2,64,128]{2,1,0:T(8,128)S(1)}, u32[]{:S(2)}, u32[]{:S(2)}) collective-permute-start(f32[2,64,128]{2,1,0:T(8,128)S(1)} %pad_maximum_fusion.3), channel_id=1, source_target_pairs={{0,2},{1,3},{2,0},{3,1},{4,6},{5,7},{6,4},{7,5},{8,10},{9,11},{10,... | collective-permute-start | bytes 196616 | tf_op jit(solution)/shard_map/ppermute | solution.py:58
  12.6 3.6 %collective-permute-start.2 = (f32[2,64,128]{2,1,0:T(8,128)S(1)}, f32[2,64,128]{2,1,0:T(8,128)S(1)}, u32[]{:S(2)}, u32[]{:S(2)}) collective-permute-start(f32[2,64,128]{2,1,0:T(8,128)S(1)} %pad_maximum_fusion.3), channel_id=1, source_target_pairs={{0,4},{1,5},{2,6},{3,7},{4,0},{5,1},{6,2},{7,3},{8,12},{9,13},{10,... | collective-permute-start | bytes 196616 | tf_op jit(solution)/shard_map/ppermute | solution.py:58
  16.2 3.6 %collective-permute-done.2 = f32[2,64,128]{2,1,0:T(8,128)S(1)} collective-permute-done((f32[2,64,128]{2,1,0:T(8,128)S(1)}, f32[2,64,128]{2,1,0:T(8,128)S(1)}, u32[]{:S(2)}, u32[]{:S(2)}) %collective-permute-start.2) | collective-permute-done | bytes 65568 | tf_op jit(solution)/shard_map/ppermute | solution.py:58
  19.8 1.9 %collective-permute-done.3 = f32[2,64,128]{2,1,0:T(8,128)S(1)} collective-permute-done((f32[2,64,128]{2,1,0:T(8,128)S(1)}, f32[2,64,128]{2,1,0:T(8,128)S(1)}, u32[]{:S(2)}, u32[]{:S(2)}) %collective-permute-start.3) | collective-permute-done | bytes 65568 | tf_op jit(solution)/shard_map/ppermute | solution.py:58
  21.7 0.7 collective-permute-start.4
  22.4 0.3 minimum_reduce_fusion
  23.1 4.6 %all-to-all-done.nodes_ref = f32[8,256,128]{2,1,0:T(8,128)S(1)} async-done(((f32[8,256,128]{2,1,0:T(8,128)}), f32[8,256,128]{2,1,0:T(8,128)S(1)}, u32[]{:S(2)}, u32[]{:S(2)}) %all-to-all-start) | async-done | bytes 1048608 | tf_op jit(solution)/shard_map/all_to_all | solution.py:34
  27.8 3.1 %transport.1 = f32[16,56,128]{2,1,0:T(8,128)} custom-call(f32[8,256,128]{2,1,0:T(8,128)S(1)} %all-to-all-done.nodes_ref, f32[256,8]{1,0:T(8,128)S(1)} %copy.31.columns_ref, f32[8,128]{1,0:T(8,128)S(1)} %broadcast_in_dim.11.speeds_ref.first_ref, f32[8,8,256]{2,1,0:T(8,128)S(1)} %stack.61.weights_ref), custom_call_target="tpu_custom_call" | custom-call | tf_op jit(solution)/shard_map/transport/pallas_call | solution.py:392
  30.9 6.1 %all-to-all-start.1 = ((f32[16,56,128]{2,1,0:T(8,128)}), f32[16,56,128]{2,1,0:T(8,128)S(1)}, u32[]{:S(2)}, u32[]{:S(2)}) async-start(f32[16,56,128]{2,1,0:T(8,128)} %transport.1), calls=%async_computation.1 | async-start | bytes 917504 | tf_op jit(solution)/shard_map/all_to_all | solution.py:34
  37.1 1.4 collective-permute-start.6
  38.6 2.2 %collective-permute-start.5 = (f32[1,2,16,128]{3,2,1,0:T(8,128)S(1)}, f32[1,2,16,128]{3,2,1,0:T(8,128)S(1)}, u32[]{:S(2)}, u32[]{:S(2)}) collective-permute-start(f32[1,2,16,128]{3,2,1,0:T(8,128)S(1)} %get-tuple-element.69), channel_id=1, source_target_pairs={{0,16},{16,32},{32,48},{48,64},{64,80},{80,96},{96,112},{112,0},{1... | collective-permute-start | bytes 49160 | tf_op jit(solution)/shard_map/ppermute | solution.py:383
  40.8 6.8 %all-to-all-done.1.integrals_ref = f32[16,56,128]{2,1,0:T(8,128)S(1)} async-done(((f32[16,56,128]{2,1,0:T(8,128)}), f32[16,56,128]{2,1,0:T(8,128)S(1)}, u32[]{:S(2)}, u32[]{:S(2)}) %all-to-all-start.1) | async-done | bytes 458784 | tf_op jit(solution)/shard_map/all_to_all | solution.py:34
  47.6 3.7 %maxwell.1 = (f32[16,112,128]{2,1,0:T(8,128)}, f32[1024,8]{1,0:T(8,128)S(1)}, f32[8,1024]{1,0:T(8,128)S(1)}) custom-call(s32[1]{0:T(128)} %bitcast.brick_ref, f32[16,64,128]{2,1,0:T(8,128)S(1)} %constant_dynamic-update-slice_fusion.5.cells_ref, f32[16,56,128]{2,1,0:T(8,128)S(1)} %all-to-all-done.1.integrals_ref, f32[8,256,128]{2,1,0:T(8,128)S(1)} %all-to-all-done.nodes_ref, ...), custom_call_target="tpu_custom_call" | custom-call | tf_op jit(solution)/shard_map/maxwell/pallas_call | solution.py:400
  51.3 3.6 %all-to-all-start.2 = ((f32[16,112,128]{2,1,0:T(8,128)}), f32[16,112,128]{2,1,0:T(8,128)S(1)}, u32[]{:S(2)}, u32[]{:S(2)}) async-start(f32[16,112,128]{2,1,0:T(8,128)} %get-tuple-element.18), calls=%async_computation.2 | async-start | bytes 1835008 | tf_op jit(solution)/shard_map/all_to_all | solution.py:34
  55.1 15.0 %all-to-all-done.2.parts_ref.transport_ref = f32[16,112,128]{2,1,0:T(8,128)S(1)} async-done(((f32[16,112,128]{2,1,0:T(8,128)}), f32[16,112,128]{2,1,0:T(8,128)S(1)}, u32[]{:S(2)}, u32[]{:S(2)}) %all-to-all-start.2) | async-done | bytes 917536 | tf_op jit(solution)/shard_map/all_to_all | solution.py:34
  70.1 1.6 advance.1
  71.7 3.6 %all-to-all-start.3 = ((f32[16,72,128]{2,1,0:T(8,128)}), f32[16,72,128]{2,1,0:T(8,128)S(1)}, u32[]{:S(2)}, u32[]{:S(2)}) async-start(f32[16,72,128]{2,1,0:T(8,128)} %get-tuple-element.20), calls=%async_computation.3 | async-start | bytes 1179648 | tf_op jit(solution)/shard_map/all_to_all | solution.py:34
  75.3 11.5 %all-to-all-done.3.parts_ref = f32[16,72,128]{2,1,0:T(8,128)S(1)} async-done(((f32[16,72,128]{2,1,0:T(8,128)}), f32[16,72,128]{2,1,0:T(8,128)S(1)}, u32[]{:S(2)}, u32[]{:S(2)}) %all-to-all-start.3) | async-done | bytes 589856 | tf_op jit(solution)/shard_map/all_to_all | solution.py:34
  87.0 0.6 convolution_bitcast_fusion.1
  87.7 0.2 fusion.19
  87.9 0.9 collective-permute-start.7
  88.8 1.0 fusion.41
  89.9 1.0 fusion.42
  90.9 1.0 convolution_bitcast_fusion
  92.0 3.4 %collective-permute-done.7 = f32[8,512]{1,0:T(8,128)S(1)} collective-permute-done((f32[8,512]{1,0:T(8,128)S(1)}, f32[8,512]{1,0:T(8,128)S(1)}, u32[]{:S(2)}, u32[]{:S(2)}) %collective-permute-start.7) | collective-permute-done | bytes 16416 | tf_op jit(solution)/shard_map/ppermute | solution.py:445
  95.4 0.2 fusion
  95.9 0.6 collective-permute-start.9
  96.5 3.6 %collective-permute-start.10 = (f32[40,128]{1,0:T(8,128)S(1)}, f32[40,128]{1,0:T(8,128)S(1)}, u32[]{:S(2)}, u32[]{:S(2)}) collective-permute-start(f32[40,128]{1,0:T(8,128)S(1)} %constant_dynamic-update-slice_fusion.17), channel_id=1, source_target_pairs={{0,24},{1,25},{2,26},{3,27},{4,28},{5,29},{6,30},{7,31},{8,16},{9,... | collective-permute-start | bytes 61448 | tf_op jit(solution)/shard_map/ppermute | solution.py:58
  100.1 1.0 collective-permute-done.8
  101.1 0.8 collective-permute-done.10
  101.9 1.3 collective-permute-start.12
  103.2 0.7 collective-permute-start.13
  103.9 1.5 collective-permute-start.11
  105.4 3.7 %back.1 = f32[8,256,128]{2,1,0:T(8,128)} custom-call(f32[16,72,128]{2,1,0:T(8,128)S(1)} %all-to-all-done.3.parts_ref, f32[1024,8]{1,0:T(8,128)S(1)} %get-tuple-element.23.line_ref, f32[8,1024]{1,0:T(8,128)S(1)} %get-tuple-element.24.state_ref, f32[256,2]{1,0:T(8,128)S(1)} %get-tuple-element.46.across_ref), custom_call_target="tpu_custom_call" | custom-call | tf_op jit(solution)/shard_map/back/pallas_call | solution.py:471
  109.1 4.6 %all-to-all-start.4 = ((f32[8,256,128]{2,1,0:T(8,128)}), f32[8,256,128]{2,1,0:T(8,128)S(1)}, u32[]{:S(2)}, u32[]{:S(2)}) async-start(f32[8,256,128]{2,1,0:T(8,128)} %back.1), calls=%async_computation.4 | async-start | bytes 2097152 | tf_op jit(solution)/shard_map/all_to_all | solution.py:34
  113.8 0.3 slice_reduce_fusion
  114.3 0.8 collective-permute-done.14
  115.1 2.4 %collective-permute-start.16 = (f32[4,40,128]{2,1,0:T(8,128)S(1)}, f32[4,40,128]{2,1,0:T(8,128)S(1)}, u32[]{:S(2)}, u32[]{:S(2)}) collective-permute-start(f32[4,40,128]{2,1,0:T(8,128)S(1)} %pad_maximum_fusion.2), channel_id=1, source_target_pairs={{0,4},{1,5},{2,6},{3,7},{4,0},{5,1},{6,2},{7,3},{8,12},{9,13},{10,... | collective-permute-start | bytes 245768 | tf_op jit(solution)/shard_map/ppermute | solution.py:58
  117.4 2.3 %collective-permute-start.17 = (f32[4,40,128]{2,1,0:T(8,128)S(1)}, f32[4,40,128]{2,1,0:T(8,128)S(1)}, u32[]{:S(2)}, u32[]{:S(2)}) collective-permute-start(f32[4,40,128]{2,1,0:T(8,128)S(1)} %pad_maximum_fusion.2), channel_id=1, source_target_pairs={{0,6},{1,7},{2,4},{3,5},{4,2},{5,3},{6,0},{7,1},{8,14},{9,15},{10,... | collective-permute-start | bytes 245768 | tf_op jit(solution)/shard_map/ppermute | solution.py:58
  119.8 0.6 collective-permute-done.15
  120.4 1.4 collective-permute-done.16
  121.8 1.7 %collective-permute-done.17 = f32[4,40,128]{2,1,0:T(8,128)S(1)} collective-permute-done((f32[4,40,128]{2,1,0:T(8,128)S(1)}, f32[4,40,128]{2,1,0:T(8,128)S(1)}, u32[]{:S(2)}, u32[]{:S(2)}) %collective-permute-start.17) | collective-permute-done | bytes 81952 | tf_op jit(solution)/shard_map/ppermute | solution.py:58
  123.4 4.3 %all-to-all-done.4.back_ref = f32[8,256,128]{2,1,0:T(8,128)S(1)} async-done(((f32[8,256,128]{2,1,0:T(8,128)}), f32[8,256,128]{2,1,0:T(8,128)S(1)}, u32[]{:S(2)}, u32[]{:S(2)}) %all-to-all-start.4) | async-done | bytes 1048608 | tf_op jit(solution)/shard_map/all_to_all | solution.py:34
  127.7 7.2 %middle.1 = (f32[64,128]{1,0:T(8,128)}, f32[256,128]{1,0:T(8,128)S(1)}, f32[128,128]{1,0:T(8,128)S(1)}) custom-call(s32[1]{0:T(128)} %bitcast.brick_ref, f32[16,40,128]{2,1,0:T(8,128)S(1)} %constant_dynamic-update-slice_fusion.21.pieces_ref, f32[16,112,128]{2,1,0:T(8,128)S(1)} %all-to-all-done.2.parts_ref.transport_ref, f32[256,128]{1,0:T(8,128)S(1)} %copy-done.1, ...), custom_call_target="tpu_custom_call" | custom-call | tf_op jit(solution)/shard_map/middle/pallas_call | solution.py:483
  134.9 1.3 collective-permute-done.18
  136.2 1.5 collective-permute-start.20
  137.7 1.3 collective-permute-start.21
  139.0 0.8 collective-permute-start.19
  139.8 2.4 %collective-permute-done.20 = f32[128,128]{1,0:T(8,128)S(1)} collective-permute-done((f32[128,128]{1,0:T(8,128)S(1)}, f32[128,128]{1,0:T(8,128)S(1)}, u32[]{:S(2)}, u32[]{:S(2)}) %collective-permute-start.20) | collective-permute-done | bytes 65568 | tf_op jit(solution)/shard_map/ppermute | solution.py:58
  142.1 1.3 collective-permute-done.21
  143.5 0.9 collective-permute-start.23
  144.4 2.8 %collective-permute-start.24 = (f32[128,128]{1,0:T(8,128)S(1)}, f32[128,128]{1,0:T(8,128)S(1)}, u32[]{:S(2)}, u32[]{:S(2)}) collective-permute-start(f32[128,128]{1,0:T(8,128)S(1)} %add_add_fusion.2), channel_id=1, source_target_pairs={{0,24},{1,25},{2,26},{3,27},{4,28},{5,29},{6,30},{7,31},{8,16},{9,... | collective-permute-start | bytes 196616 | tf_op jit(solution)/shard_map/ppermute | solution.py:58
  147.3 2.6 %collective-permute-done.23 = f32[128,128]{1,0:T(8,128)S(1)} collective-permute-done((f32[128,128]{1,0:T(8,128)S(1)}, f32[128,128]{1,0:T(8,128)S(1)}, u32[]{:S(2)}, u32[]{:S(2)}) %collective-permute-start.23) | collective-permute-done | bytes 65568 | tf_op jit(solution)/shard_map/ppermute | solution.py:58
  149.8 0.4 collective-permute-done.24
  150.2 1.3 collective-permute-done.22
  151.5 1.0 collective-permute-start.26
  152.5 2.0 %collective-permute-start.27 = (f32[128,128]{1,0:T(8,128)S(1)}, f32[128,128]{1,0:T(8,128)S(1)}, u32[]{:S(2)}, u32[]{:S(2)}) collective-permute-start(f32[128,128]{1,0:T(8,128)S(1)} %add_add_fusion.1), channel_id=1, source_target_pairs={{0,96},{1,97},{2,98},{3,99},{4,100},{5,101},{6,102},{7,103},{8,104... | collective-permute-start | bytes 196616 | tf_op jit(solution)/shard_map/ppermute | solution.py:58
  154.5 0.6 collective-permute-start.25
  155.1 2.3 %collective-permute-done.26 = f32[128,128]{1,0:T(8,128)S(1)} collective-permute-done((f32[128,128]{1,0:T(8,128)S(1)}, f32[128,128]{1,0:T(8,128)S(1)}, u32[]{:S(2)}, u32[]{:S(2)}) %collective-permute-start.26) | collective-permute-done | bytes 65568 | tf_op jit(solution)/shard_map/ppermute | solution.py:58
  157.4 0.7 collective-permute-done.27
  158.1 0.7 collective-permute-done.25
  158.8 4.5 %last.1 = (f32[128,128]{1,0:T(8,128)}, f32[256,128]{1,0:T(8,128)}) custom-call(f32[128,128]{1,0:T(8,128)S(1)} %add_add_fusion.gram_ref, f32[256,128]{1,0:T(8,128)S(1)} %get-tuple-element.28.velocity_ref), custom_call_target="tpu_custom_call" | custom-call | tf_op jit(solution)/shard_map/last/pallas_call | solution.py:493
  (101 shorter events, 2.3 us)
Async XLA Ops:
  0.6 10.0 %collective-permute-start = (f32[1,64,128]{2,1,0:T(8,128)}, f32[1,64,128]{2,1,0:T(8,128)S(1)}, u32[]{:S(2)}, u32[]{:S(2)}) collective-permute-start(f32[1,64,128]{2,1,0:T(8,128)} %bitcast.68), channel_id=1, source_target_pairs={{0,1},{1,0},{2,3},{3,2},{4,5},{5,4},{6,7},{7,6},{8,9},{9,8},{10,11... | collective-permute-start | bytes 98312 | tf_op jit(solution)/shard_map/ppermute | solution.py:58
  2.7 7.2 %copy-start = (f32[2,2,16,128]{3,2,1,0:T(8,128)S(1)}, f32[2,2,16,128]{3,2,1,0:T(8,128)}, u32[]{:S(2)}) copy-start(f32[2,2,16,128]{3,2,1,0:T(8,128)} %param.2) | copy-start | bytes 98308
  2.7 25.0 %all-to-all-start = ((f32[8,256,128]{2,1,0:T(8,128)}), f32[8,256,128]{2,1,0:T(8,128)S(1)}, u32[]{:S(2)}, u32[]{:S(2)}) async-start(f32[8,256,128]{2,1,0:T(8,128)} %broadcast_in_dim.9), calls=%async_computation | async-start | bytes 2097152 | tf_op jit(solution)/shard_map/all_to_all | solution.py:34
  10.6 5.6 %collective-permute-start.1 = (f32[2,64,128]{2,1,0:T(8,128)S(1)}, f32[2,64,128]{2,1,0:T(8,128)S(1)}, u32[]{:S(2)}, u32[]{:S(2)}) collective-permute-start(f32[2,64,128]{2,1,0:T(8,128)S(1)} %pad_maximum_fusion.3), channel_id=1, source_target_pairs={{0,2},{1,3},{2,0},{3,1},{4,6},{5,7},{6,4},{7,5},{8,10},{9,11},{10,... | collective-permute-start | bytes 196616 | tf_op jit(solution)/shard_map/ppermute | solution.py:58
  12.6 7.2 %collective-permute-start.2 = (f32[2,64,128]{2,1,0:T(8,128)S(1)}, f32[2,64,128]{2,1,0:T(8,128)S(1)}, u32[]{:S(2)}, u32[]{:S(2)}) collective-permute-start(f32[2,64,128]{2,1,0:T(8,128)S(1)} %pad_maximum_fusion.3), channel_id=1, source_target_pairs={{0,4},{1,5},{2,6},{3,7},{4,0},{5,1},{6,2},{7,3},{8,12},{9,13},{10,... | collective-permute-start | bytes 196616 | tf_op jit(solution)/shard_map/ppermute | solution.py:58
  16.2 5.5 %collective-permute-start.3 = (f32[2,64,128]{2,1,0:T(8,128)S(1)}, f32[2,64,128]{2,1,0:T(8,128)S(1)}, u32[]{:S(2)}, u32[]{:S(2)}) collective-permute-start(f32[2,64,128]{2,1,0:T(8,128)S(1)} %pad_maximum_fusion.3), channel_id=1, source_target_pairs={{0,6},{1,7},{2,4},{3,5},{4,2},{5,3},{6,0},{7,1},{8,14},{9,15},{10,... | collective-permute-start | bytes 196616 | tf_op jit(solution)/shard_map/ppermute | solution.py:58
  21.7 15.4 %collective-permute-start.4 = (f32[8,64,128]{2,1,0:T(8,128)S(1)}, f32[8,64,128]{2,1,0:T(8,128)S(1)}, u32[]{:S(2)}, u32[]{:S(2)}) collective-permute-start(f32[8,64,128]{2,1,0:T(8,128)S(1)} %get-tuple-element.48), channel_id=1, source_target_pairs={{0,8},{1,9},{2,10},{3,11},{4,12},{5,13},{6,14},{7,15},{8,0},{9,1},... | collective-permute-start | bytes 786440 | tf_op jit(solution)/shard_map/ppermute | solution.py:58
  30.9 16.6 %all-to-all-start.1 = ((f32[16,56,128]{2,1,0:T(8,128)}), f32[16,56,128]{2,1,0:T(8,128)S(1)}, u32[]{:S(2)}, u32[]{:S(2)}) async-start(f32[16,56,128]{2,1,0:T(8,128)} %transport.1), calls=%async_computation.1 | async-start | bytes 917504 | tf_op jit(solution)/shard_map/all_to_all | solution.py:34
  37.1 17.8 %collective-permute-start.6 = (f32[1,2,16,128]{3,2,1,0:T(8,128)S(1)}, f32[1,2,16,128]{3,2,1,0:T(8,128)S(1)}, u32[]{:S(2)}, u32[]{:S(2)}) collective-permute-start(f32[1,2,16,128]{3,2,1,0:T(8,128)S(1)} %get-tuple-element.68), channel_id=1, source_target_pairs={{0,112},{16,0},{32,16},{48,32},{64,48},{80,64},{96,80},{112,96},{1... | collective-permute-start | bytes 49160 | tf_op jit(solution)/shard_map/ppermute | solution.py:384
  38.6 16.4 %collective-permute-start.5 = (f32[1,2,16,128]{3,2,1,0:T(8,128)S(1)}, f32[1,2,16,128]{3,2,1,0:T(8,128)S(1)}, u32[]{:S(2)}, u32[]{:S(2)}) collective-permute-start(f32[1,2,16,128]{3,2,1,0:T(8,128)S(1)} %get-tuple-element.69), channel_id=1, source_target_pairs={{0,16},{16,32},{32,48},{48,64},{64,80},{80,96},{96,112},{112,0},{1... | collective-permute-start | bytes 49160 | tf_op jit(solution)/shard_map/ppermute | solution.py:383
  51.3 18.8 %all-to-all-start.2 = ((f32[16,112,128]{2,1,0:T(8,128)}), f32[16,112,128]{2,1,0:T(8,128)S(1)}, u32[]{:S(2)}, u32[]{:S(2)}) async-start(f32[16,112,128]{2,1,0:T(8,128)} %get-tuple-element.18), calls=%async_computation.2 | async-start | bytes 1835008 | tf_op jit(solution)/shard_map/all_to_all | solution.py:34
  71.7 15.2 %all-to-all-start.3 = ((f32[16,72,128]{2,1,0:T(8,128)}), f32[16,72,128]{2,1,0:T(8,128)S(1)}, u32[]{:S(2)}, u32[]{:S(2)}) async-start(f32[16,72,128]{2,1,0:T(8,128)} %get-tuple-element.20), calls=%async_computation.3 | async-start | bytes 1179648 | tf_op jit(solution)/shard_map/all_to_all | solution.py:34
  87.9 7.5 %collective-permute-start.7 = (f32[8,512]{1,0:T(8,128)S(1)}, f32[8,512]{1,0:T(8,128)S(1)}, u32[]{:S(2)}, u32[]{:S(2)}) collective-permute-start(f32[8,512]{1,0:T(8,128)S(1)} %fusion.19), channel_id=1, source_target_pairs={{0,16},{16,32},{32,48},{48,64},{64,80},{80,96},{96,112},{112,0},{1... | collective-permute-start | bytes 49160 | tf_op jit(solution)/shard_map/ppermute | solution.py:445
  95.7 5.4 %collective-permute-start.8 = (f32[40,128]{1,0:T(8,128)S(1)}, f32[40,128]{1,0:T(8,128)S(1)}, u32[]{:S(2)}, u32[]{:S(2)}) collective-permute-start(f32[40,128]{1,0:T(8,128)S(1)} %constant_dynamic-update-slice_fusion.17), channel_id=1, source_target_pairs={{0,16},{1,17},{2,18},{3,19},{4,20},{5,21},{6,22},{7,23},{8,24},{9,... | collective-permute-start | bytes 61448 | tf_op jit(solution)/shard_map/ppermute | solution.py:58
  95.9 5.1 %collective-permute-start.9 = (f32[40,128]{1,0:T(8,128)S(1)}, f32[40,128]{1,0:T(8,128)S(1)}, u32[]{:S(2)}, u32[]{:S(2)}) collective-permute-start(f32[40,128]{1,0:T(8,128)S(1)} %constant_dynamic-update-slice_fusion.17), channel_id=1, source_target_pairs={{0,8},{1,9},{2,10},{3,11},{4,12},{5,13},{6,14},{7,15},{8,0},{9,1},... | collective-permute-start | bytes 61448 | tf_op jit(solution)/shard_map/ppermute | solution.py:58
  96.5 5.3 %collective-permute-start.10 = (f32[40,128]{1,0:T(8,128)S(1)}, f32[40,128]{1,0:T(8,128)S(1)}, u32[]{:S(2)}, u32[]{:S(2)}) collective-permute-start(f32[40,128]{1,0:T(8,128)S(1)} %constant_dynamic-update-slice_fusion.17), channel_id=1, source_target_pairs={{0,24},{1,25},{2,26},{3,27},{4,28},{5,29},{6,30},{7,31},{8,16},{9,... | collective-permute-start | bytes 61448 | tf_op jit(solution)/shard_map/ppermute | solution.py:58
  101.9 11.8 %collective-permute-start.12 = (f32[2,40,128]{2,1,0:T(8,128)S(1)}, f32[2,40,128]{2,1,0:T(8,128)S(1)}, u32[]{:S(2)}, u32[]{:S(2)}) collective-permute-start(f32[2,40,128]{2,1,0:T(8,128)S(1)} %pad_maximum_fusion.4), channel_id=1, source_target_pairs={{0,64},{1,65},{2,66},{3,67},{4,68},{5,69},{6,70},{7,71},{8,72},{9,... | collective-permute-start | bytes 122888 | tf_op jit(solution)/shard_map/ppermute | solution.py:58
  103.2 10.5 %collective-permute-start.13 = (f32[2,40,128]{2,1,0:T(8,128)S(1)}, f32[2,40,128]{2,1,0:T(8,128)S(1)}, u32[]{:S(2)}, u32[]{:S(2)}) collective-permute-start(f32[2,40,128]{2,1,0:T(8,128)S(1)} %pad_maximum_fusion.4), channel_id=1, source_target_pairs={{0,96},{1,97},{2,98},{3,99},{4,100},{5,101},{6,102},{7,103},{8,104... | collective-permute-start | bytes 122888 | tf_op jit(solution)/shard_map/ppermute | solution.py:58
  103.9 9.8 %collective-permute-start.11 = (f32[2,40,128]{2,1,0:T(8,128)S(1)}, f32[2,40,128]{2,1,0:T(8,128)S(1)}, u32[]{:S(2)}, u32[]{:S(2)}) collective-permute-start(f32[2,40,128]{2,1,0:T(8,128)S(1)} %pad_maximum_fusion.4), channel_id=1, source_target_pairs={{0,32},{1,33},{2,34},{3,35},{4,36},{5,37},{6,38},{7,39},{8,40},{9,... | collective-permute-start | bytes 122888 | tf_op jit(solution)/shard_map/ppermute | solution.py:58
  109.1 18.6 %all-to-all-start.4 = ((f32[8,256,128]{2,1,0:T(8,128)}), f32[8,256,128]{2,1,0:T(8,128)S(1)}, u32[]{:S(2)}, u32[]{:S(2)}) async-start(f32[8,256,128]{2,1,0:T(8,128)} %back.1), calls=%async_computation.4 | async-start | bytes 2097152 | tf_op jit(solution)/shard_map/all_to_all | solution.py:34
  113.7 1.3 collective-permute-start.14
  115.1 5.3 %collective-permute-start.15 = (f32[4,40,128]{2,1,0:T(8,128)S(1)}, f32[4,40,128]{2,1,0:T(8,128)S(1)}, u32[]{:S(2)}, u32[]{:S(2)}) collective-permute-start(f32[4,40,128]{2,1,0:T(8,128)S(1)} %pad_maximum_fusion.2), channel_id=1, source_target_pairs={{0,2},{1,3},{2,0},{3,1},{4,6},{5,7},{6,4},{7,5},{8,10},{9,11},{10,... | collective-permute-start | bytes 245768 | tf_op jit(solution)/shard_map/ppermute | solution.py:58
  115.1 6.7 %collective-permute-start.16 = (f32[4,40,128]{2,1,0:T(8,128)S(1)}, f32[4,40,128]{2,1,0:T(8,128)S(1)}, u32[]{:S(2)}, u32[]{:S(2)}) collective-permute-start(f32[4,40,128]{2,1,0:T(8,128)S(1)} %pad_maximum_fusion.2), channel_id=1, source_target_pairs={{0,4},{1,5},{2,6},{3,7},{4,0},{5,1},{6,2},{7,3},{8,12},{9,13},{10,... | collective-permute-start | bytes 245768 | tf_op jit(solution)/shard_map/ppermute | solution.py:58
  117.4 6.0 %collective-permute-start.17 = (f32[4,40,128]{2,1,0:T(8,128)S(1)}, f32[4,40,128]{2,1,0:T(8,128)S(1)}, u32[]{:S(2)}, u32[]{:S(2)}) collective-permute-start(f32[4,40,128]{2,1,0:T(8,128)S(1)} %pad_maximum_fusion.2), channel_id=1, source_target_pairs={{0,6},{1,7},{2,4},{3,5},{4,2},{5,3},{6,0},{7,1},{8,14},{9,15},{10,... | collective-permute-start | bytes 245768 | tf_op jit(solution)/shard_map/ppermute | solution.py:58
  120.4 7.4 %copy-start.1 = (f32[256,128]{1,0:T(8,128)S(1)}, f32[256,128]{1,0:T(8,128)}, u32[]{:S(2)}) copy-start(f32[256,128]{1,0:T(8,128)} %basis_ref.1) | copy-start | bytes 393220
  134.9 1.3 collective-permute-start.18
  136.2 5.9 %collective-permute-start.20 = (f32[128,128]{1,0:T(8,128)S(1)}, f32[128,128]{1,0:T(8,128)S(1)}, u32[]{:S(2)}, u32[]{:S(2)}) collective-permute-start(f32[128,128]{1,0:T(8,128)S(1)} %add.419), channel_id=1, source_target_pairs={{0,4},{1,5},{2,6},{3,7},{4,0},{5,1},{6,2},{7,3},{8,12},{9,13},{10,... | collective-permute-start | bytes 196616 | tf_op jit(solution)/shard_map/ppermute | solution.py:58
  137.7 5.8 %collective-permute-start.21 = (f32[128,128]{1,0:T(8,128)S(1)}, f32[128,128]{1,0:T(8,128)S(1)}, u32[]{:S(2)}, u32[]{:S(2)}) collective-permute-start(f32[128,128]{1,0:T(8,128)S(1)} %add.419), channel_id=1, source_target_pairs={{0,6},{1,7},{2,4},{3,5},{4,2},{5,3},{6,0},{7,1},{8,14},{9,15},{10,... | collective-permute-start | bytes 196616 | tf_op jit(solution)/shard_map/ppermute | solution.py:58
  139.0 4.5 %collective-permute-start.19 = (f32[128,128]{1,0:T(8,128)S(1)}, f32[128,128]{1,0:T(8,128)S(1)}, u32[]{:S(2)}, u32[]{:S(2)}) collective-permute-start(f32[128,128]{1,0:T(8,128)S(1)} %add.419), channel_id=1, source_target_pairs={{0,2},{1,3},{2,0},{3,1},{4,6},{5,7},{6,4},{7,5},{8,10},{9,11},{10,... | collective-permute-start | bytes 196616 | tf_op jit(solution)/shard_map/ppermute | solution.py:58
  143.5 6.4 %collective-permute-start.23 = (f32[128,128]{1,0:T(8,128)S(1)}, f32[128,128]{1,0:T(8,128)S(1)}, u32[]{:S(2)}, u32[]{:S(2)}) collective-permute-start(f32[128,128]{1,0:T(8,128)S(1)} %add_add_fusion.2), channel_id=1, source_target_pairs={{0,16},{1,17},{2,18},{3,19},{4,20},{5,21},{6,22},{7,23},{8,24},{9,... | collective-permute-start | bytes 196616 | tf_op jit(solution)/shard_map/ppermute | solution.py:58
  144.4 5.8 %collective-permute-start.24 = (f32[128,128]{1,0:T(8,128)S(1)}, f32[128,128]{1,0:T(8,128)S(1)}, u32[]{:S(2)}, u32[]{:S(2)}) collective-permute-start(f32[128,128]{1,0:T(8,128)S(1)} %add_add_fusion.2), channel_id=1, source_target_pairs={{0,24},{1,25},{2,26},{3,27},{4,28},{5,29},{6,30},{7,31},{8,16},{9,... | collective-permute-start | bytes 196616 | tf_op jit(solution)/shard_map/ppermute | solution.py:58
  147.3 4.3 %collective-permute-start.22 = (f32[128,128]{1,0:T(8,128)S(1)}, f32[128,128]{1,0:T(8,128)S(1)}, u32[]{:S(2)}, u32[]{:S(2)}) collective-permute-start(f32[128,128]{1,0:T(8,128)S(1)} %add_add_fusion.2), channel_id=1, source_target_pairs={{0,8},{1,9},{2,10},{3,11},{4,12},{5,13},{6,14},{7,15},{8,0},{9,1},... | collective-permute-start | bytes 196616 | tf_op jit(solution)/shard_map/ppermute | solution.py:58
  151.5 5.9 %collective-permute-start.26 = (f32[128,128]{1,0:T(8,128)S(1)}, f32[128,128]{1,0:T(8,128)S(1)}, u32[]{:S(2)}, u32[]{:S(2)}) collective-permute-start(f32[128,128]{1,0:T(8,128)S(1)} %add_add_fusion.1), channel_id=1, source_target_pairs={{0,64},{1,65},{2,66},{3,67},{4,68},{5,69},{6,70},{7,71},{8,72},{9,... | collective-permute-start | bytes 196616 | tf_op jit(solution)/shard_map/ppermute | solution.py:58
  152.5 5.6 %collective-permute-start.27 = (f32[128,128]{1,0:T(8,128)S(1)}, f32[128,128]{1,0:T(8,128)S(1)}, u32[]{:S(2)}, u32[]{:S(2)}) collective-permute-start(f32[128,128]{1,0:T(8,128)S(1)} %add_add_fusion.1), channel_id=1, source_target_pairs={{0,96},{1,97},{2,98},{3,99},{4,100},{5,101},{6,102},{7,103},{8,104... | collective-permute-start | bytes 196616 | tf_op jit(solution)/shard_map/ppermute | solution.py:58
  154.5 4.3 %collective-permute-start.25 = (f32[128,128]{1,0:T(8,128)S(1)}, f32[128,128]{1,0:T(8,128)S(1)}, u32[]{:S(2)}, u32[]{:S(2)}) collective-permute-start(f32[128,128]{1,0:T(8,128)S(1)} %add_add_fusion.1), channel_id=1, source_target_pairs={{0,32},{1,33},{2,34},{3,35},{4,36},{5,37},{6,38},{7,39},{8,40},{9,... | collective-permute-start | bytes 196616 | tf_op jit(solution)/shard_map/ppermute | solution.py:58

commit v5 on v4

--- a/solution.py
+++ b/solution.py
@@ -146,6 +146,18 @@
             work_ref[stop:, :] = work_ref[stop:, :] - update[stop:, :]
 
 
+def contract_three(left, right, left_dim, right_dim):
+    left_high, left_low = two_parts(left)
+    right_high, right_low = two_parts(right)
+    dims = (((left_dim,), (right_dim,)), ((), ()))
+
+    def product(one, other):
+        return lax.dot_general(one, other, dims, preferred_element_type=jnp.float32)
+
+    small = product(left_high, right_low) + product(left_low, right_high)
+    return product(left_high, right_high) + small
+
+
 def transport_kernel(nodes_ref, columns_ref, speeds_ref, weights_ref, out_ref):
     groups, rows, rank = nodes_ref.shape
     bricks = out_ref.shape[0]
@@ -223,6 +235,47 @@
     part_ref[:, :cells, :] = result.reshape(bricks, cells, rank)
 
 
+def products_kernel(
+    brick_ref, parts_ref, pieces_ref, chosen_ref, work_ref, *, cells_x, cells_y, cells_z
+):
+    bricks, _, rank = parts_ref.shape
+    height = rank // bricks
+    cells = cells_x * cells_y * cells_z
+    total = bricks * cells
+    advanced = parts_ref[:, :cells, :].reshape(total, rank)
+    last_plane = parts_ref[:, cells - cells // cells_x : cells, :].reshape(-1, rank)
+    start = pl.multiple_of(brick_ref[0] * height, height)
+    chosen_row = lax.broadcasted_iota(jnp.int32, (height, rank), 0) + start
+    chosen_col = lax.broadcasted_iota(jnp.int32, (height, rank), 1)
+    chosen_ref[...] = contract(jnp.where(chosen_row == chosen_col, 1.0, 0.0), last_plane, 1, 1)
+    row = lax.broadcasted_iota(jnp.int32, (total, rank), 0)
+    plane = cells_y * cells_z
+
+    def shifted(amount):
+        return pltpu.roll(advanced, amount % total, 0)
+
+    along_x = jnp.where(row // plane % cells_x < cells_x - 1, shifted(-plane), 0.0)
+    wrap = cells - (cells_y - 1) * cells_z
+    along_y = jnp.where(row // cells_z % cells_y > 0, shifted(cells_z), shifted(wrap))
+    along_z = jnp.where(row % cells_z > 0, shifted(1), shifted(1 - cells_z))
+    left_high, left_low = two_parts(advanced)
+    high, low = two_parts(jnp.concatenate([along_x, along_y, along_z], axis=1))
+    work_ref[:, :rank] = contract(advanced, advanced, 0, 0)
+    work_ref[:, rank:] = lax.dot_general(
+        jnp.concatenate([left_high, left_high, left_low], axis=0),
+        jnp.concatenate([high, low, high], axis=0),
+        (((0,), (0,)), ((), ())),
+        preferred_element_type=jnp.float32,
+    )
+    own = work_ref[pl.ds(start, height), :]
+    for i in range(4):
+        pieces_ref[i * height : (i + 1) * height, :] = own[:, i * rank : (i + 1) * rank]
+    projected = parts_ref[0, cells:, :]
+    for i in range(1, bricks):
+        projected = projected + parts_ref[i, cells:, :]
+    pieces_ref[4 * height :, :] = projected
+
+
 def back_kernel(parts_ref, line_ref, state_ref, across_ref, out_ref):
     bricks, _, rank = parts_ref.shape
     groups, rows, _ = out_ref.shape
@@ -312,8 +365,8 @@
             straight, crossed = crossed, straight
         turned.append(contract(straight, inverse, 1, 1))
         change = change + lengths[i] * (
-            contract(upper - straight, piece(transport_ref, 2 * i), 1, 0)
-            + contract(crossed - upper, piece(transport_ref, 2 * i + 1), 1, 0)
+            contract_three(upper - straight, piece(transport_ref, 2 * i), 1, 0)
+            + contract_three(crossed - upper, piece(transport_ref, 2 * i + 1), 1, 0)
         )
     projected = contract(inverse, piece(pieces_ref, 4) * weight_x, 1, 0)
     middle = upper + time_step * change - COLLIDE * (projected - upper)
@@ -321,8 +374,8 @@
     drift_sum = jnp.zeros((rows, rank), jnp.float32)
     for i in range(3):
         speed = jnp.broadcast_to(speeds_ref[:, i : i + 1], (rows, rank)) * lengths[i]
-        minus = contract(now, turned[i], 1, 1)
-        plus = contract(now, turned[i], 1, 0)
+        minus = contract_three(now, turned[i], 1, 1)
+        plus = contract_three(now, turned[i], 1, 0)
         drift_sum = drift_sum + jnp.maximum(speed, 0.0) * (now - minus)
         drift_sum = drift_sum + jnp.minimum(speed, 0.0) * (plus - now)
     back = back_ref[0]
@@ -435,44 +488,27 @@
     )(second, jnp.stack(steps), own_cells)
     third = exchange(payload, "brick")
 
-    slab_advanced = third[:, :cells]
-    projected_rows = jnp.sum(third[:, cells:], axis=0)
-    adv_grid = slab_advanced.reshape(bricks, cells_x, cells_y, cells_z, rank)
-    planes_x = [adv_grid[:, i].reshape(half, rank) for i in range(cells_x)]
-    choose = brick * height + jnp.arange(height, dtype=jnp.int32)
-    choose = (choose[:, None] == jnp.arange(rank, dtype=jnp.int32)[None]).astype(jnp.float32)
-    chosen = contract(choose, planes_x[-1], 1, 1)
+    pieces, chosen = pl.pallas_call(
+        functools.partial(products_kernel, cells_x=cells_x, cells_y=cells_y, cells_z=cells_z),
+        out_shape=(f32(5 * height, rank), f32(height, half)),
+        in_specs=vector_specs + [whole],
+        scratch_shapes=[pltpu.VMEM((rank, 4 * rank), jnp.float32)],
+        name="products",
+        compiler_params=pltpu.CompilerParams(vmem_limit_bytes=VMEM_BYTES),
+    )(brick_id, third)
+    chosen, third_after = lax.optimization_barrier((chosen, third))
     chosen_below = lax.ppermute(chosen, "slab", up)
-    adv_grid = slab_advanced.reshape(bricks, cells_x, cells_y, cells_z, rank)
-    planes_x = [adv_grid[:, i].reshape(half, rank) for i in range(cells_x)]
-    before = jnp.concatenate([adv_grid[-1:, :, -1:], adv_grid[:-1, :, -1:]], axis=0)
-    shift_y = jnp.concatenate([before, adv_grid[:, :, :-1]], axis=2).reshape(slab_cells, rank)
-    shift_z = jnp.roll(adv_grid, 1, axis=3).reshape(slab_cells, rank)
-    adv_flat = slab_advanced.reshape(slab_cells, rank)
-
-    def own_rows(left_side, right_side):
-        whole = contract(left_side, right_side, 0, 0)
-        return lax.dynamic_slice_in_dim(whole, brick * height, height, 0)
-
-    crossing = contract(chosen_below, planes_x[0], 1, 0)
-    for i in range(1, cells_x):
-        crossing = crossing + own_rows(planes_x[i - 1], planes_x[i])
-    pieces = jnp.concatenate(
-        [
-            own_rows(adv_flat, adv_flat),
-            crossing,
-            own_rows(adv_flat, shift_y),
-            own_rows(adv_flat, shift_z),
-            projected_rows,
-        ],
-        axis=0,
-    )
-    pieces, third_after = lax.optimization_barrier((pieces, third))
+    first_plane = third[:, : cells // cells_x].reshape(half, rank)
+
     back = pl.pallas_call(back_kernel, out_shape=f32(slabs, rows, rank), name="back", compiler_params=pltpu.CompilerParams(vmem_limit_bytes=VMEM_BYTES))(
         third_after, line, state, across[1:].T
     )
+
+    pieces = pieces + jnp.pad(
+        contract(chosen_below, first_plane, 1, 0), ((height, 3 * height), (0, 0))
+    )
+    pieces, back = lax.optimization_barrier((pieces, back))
     fourth = exchange(back, "slab")
-
     both = ("slab", "brick")
     lower_x, upper_x, cross_x = (from_peer(pieces, both, mask) for mask in (8, 16, 24))
     reduced = jnp.stack([pieces + upper_x, lower_x + cross_x])

time: 164 us -> 160 us (0.976)
  matrix products: 4.07 us -> 0.22 us
    dot_general x6 -> x1, matrix products: 4.07 us -> 0.22 us  [contract(): lax.dot_general(left, right, (((left_dim,), (right_dim,)), ((), ())), pre...]
  transfers between devices with their start and end apart: 33 -> 33, of which waited for: 23 -> 23; matrix products, arithmetic and copies ran while one was open for 4% -> 3% of each run, Pallas kernels for 6% -> 7%
where the time goes in v5:
time: 160 us
  waiting for transfers between devices  69.8 us (44%)
  starting transfers between devices  59.5 us (37%)
  Pallas kernels  24.6 us (15%)
  local copies, waits for them, and re-layouts  3.4 us (2%)
    all_to_all x5, waiting for transfers between devices, exchange(): return lax.all_to_all(array, axis, 0, 0, tiled=True)  42.5 us
    ppermute x25, starting transfers between devices, from_peer(): return lax.ppermute(values, axis, [(i, i ^ mask) for i in range(peers)])  29.9 us
    all_to_all x5, starting transfers between devices, exchange(): return lax.all_to_all(array, axis, 0, 0, tiled=True)  25.1 us
    ppermute x25, waiting for transfers between devices, from_peer(): return lax.ppermute(values, axis, [(i, i ^ mask) for i in range(peers)])  24.4 us
    pallas_call x1, Pallas kernels, local(): pl.pallas_call(functools.partial(middle_kernel, lengths=lengths, time_ste...  6.69 us
    pallas_call x1, Pallas kernels, local(): pl.pallas_call(last_kernel, out_shape=(f32(rank, rank), f32(rows, rank)),...  4.49 us
    pallas_call x1, Pallas kernels, local(): pl.pallas_call(maxwell_kernel, out_shape=(f32(bricks, cells + 6 * height,...  3.73 us
    pallas_call x1, Pallas kernels, local(): pl.pallas_call(back_kernel, out_shape=f32(slabs, rows, rank), name='back'...  3.67 us
  transfers between devices with their start and end apart: 33, of which 23 were waited for; matrix products, arithmetic and copies ran while one was open for 3% of the time, Pallas kernels for 7%

profile of v5, /device:TPU:0, one launch (start us, length us, event | category | flops | bytes accessed | tf_op | source)
XLA Modules:
  0.0 159.6 jit_solution(5011921384434788907)
XLA Ops:
  0.7 2.0 %broadcast_in_dim.9 = f32[8,256,128]{2,1,0:T(8,128)} broadcast(f32[256,128]{1,0:T(8,128)} %basis_ref.1), dimensions={1,2} | broadcast | bytes 1179648 | tf_op jit(solution)/shard_map/broadcast_in_dim | solution.py:39
  2.7 7.1 %all-to-all-start = ((f32[8,256,128]{2,1,0:T(8,128)}), f32[8,256,128]{2,1,0:T(8,128)S(1)}, u32[]{:S(2)}, u32[]{:S(2)}) async-start(f32[8,256,128]{2,1,0:T(8,128)} %broadcast_in_dim.9), calls=%async_computation | async-start | bytes 2097152 | tf_op jit(solution)/shard_map/all_to_all | solution.py:34
  10.0 0.1 copy.24
  10.2 0.2 and_select_fusion.3
  10.6 2.0 %collective-permute-start.1 = (f32[2,64,128]{2,1,0:T(8,128)S(1)}, f32[2,64,128]{2,1,0:T(8,128)S(1)}, u32[]{:S(2)}, u32[]{:S(2)}) collective-permute-start(f32[2,64,128]{2,1,0:T(8,128)S(1)} %pad_maximum_fusion.1), channel_id=1, source_target_pairs={{0,2},{1,3},{2,0},{3,1},{4,6},{5,7},{6,4},{7,5},{8,10},{9,11},{10,... | collective-permute-start | bytes 196616 | tf_op jit(solution)/shard_map/ppermute | solution.py:58
  12.6 3.6 %collective-permute-start.2 = (f32[2,64,128]{2,1,0:T(8,128)S(1)}, f32[2,64,128]{2,1,0:T(8,128)S(1)}, u32[]{:S(2)}, u32[]{:S(2)}) collective-permute-start(f32[2,64,128]{2,1,0:T(8,128)S(1)} %pad_maximum_fusion.1), channel_id=1, source_target_pairs={{0,4},{1,5},{2,6},{3,7},{4,0},{5,1},{6,2},{7,3},{8,12},{9,13},{10,... | collective-permute-start | bytes 196616 | tf_op jit(solution)/shard_map/ppermute | solution.py:58
  16.2 3.6 %collective-permute-done.2 = f32[2,64,128]{2,1,0:T(8,128)S(1)} collective-permute-done((f32[2,64,128]{2,1,0:T(8,128)S(1)}, f32[2,64,128]{2,1,0:T(8,128)S(1)}, u32[]{:S(2)}, u32[]{:S(2)}) %collective-permute-start.2) | collective-permute-done | bytes 65568 | tf_op jit(solution)/shard_map/ppermute | solution.py:58
  19.8 1.9 %collective-permute-done.3 = f32[2,64,128]{2,1,0:T(8,128)S(1)} collective-permute-done((f32[2,64,128]{2,1,0:T(8,128)S(1)}, f32[2,64,128]{2,1,0:T(8,128)S(1)}, u32[]{:S(2)}, u32[]{:S(2)}) %collective-permute-start.3) | collective-permute-done | bytes 65568 | tf_op jit(solution)/shard_map/ppermute | solution.py:58
  21.7 0.7 collective-permute-start.4
  22.4 0.3 minimum_reduce_fusion
  23.1 4.6 %all-to-all-done.nodes_ref = f32[8,256,128]{2,1,0:T(8,128)S(1)} async-done(((f32[8,256,128]{2,1,0:T(8,128)}), f32[8,256,128]{2,1,0:T(8,128)S(1)}, u32[]{:S(2)}, u32[]{:S(2)}) %all-to-all-start) | async-done | bytes 1048608 | tf_op jit(solution)/shard_map/all_to_all | solution.py:34
  27.8 3.2 %transport.1 = f32[16,56,128]{2,1,0:T(8,128)} custom-call(f32[8,256,128]{2,1,0:T(8,128)S(1)} %all-to-all-done.nodes_ref, f32[256,8]{1,0:T(8,128)S(1)} %copy.25.columns_ref, f32[8,128]{1,0:T(8,128)S(1)} %broadcast_in_dim.21.speeds_ref.first_ref, f32[8,8,256]{2,1,0:T(8,128)S(1)} %stack.61.weights_ref), custom_call_target="tpu_custom_call" | custom-call | tf_op jit(solution)/shard_map/transport/pallas_call | solution.py:445
  31.0 6.1 %all-to-all-start.1 = ((f32[16,56,128]{2,1,0:T(8,128)}), f32[16,56,128]{2,1,0:T(8,128)S(1)}, u32[]{:S(2)}, u32[]{:S(2)}) async-start(f32[16,56,128]{2,1,0:T(8,128)} %transport.1), calls=%async_computation.1 | async-start | bytes 917504 | tf_op jit(solution)/shard_map/all_to_all | solution.py:34
  37.1 1.4 collective-permute-start.6
  38.6 2.2 %collective-permute-start.5 = (f32[1,2,16,128]{3,2,1,0:T(8,128)S(1)}, f32[1,2,16,128]{3,2,1,0:T(8,128)S(1)}, u32[]{:S(2)}, u32[]{:S(2)}) collective-permute-start(f32[1,2,16,128]{3,2,1,0:T(8,128)S(1)} %get-tuple-element.75), channel_id=1, source_target_pairs={{0,16},{16,32},{32,48},{48,64},{64,80},{80,96},{96,112},{112,0},{1... | collective-permute-start | bytes 49160 | tf_op jit(solution)/shard_map/ppermute | solution.py:436
  40.8 6.8 %all-to-all-done.1.integrals_ref = f32[16,56,128]{2,1,0:T(8,128)S(1)} async-done(((f32[16,56,128]{2,1,0:T(8,128)}), f32[16,56,128]{2,1,0:T(8,128)S(1)}, u32[]{:S(2)}, u32[]{:S(2)}) %all-to-all-start.1) | async-done | bytes 458784 | tf_op jit(solution)/shard_map/all_to_all | solution.py:34
  47.6 3.7 %maxwell.1 = (f32[16,112,128]{2,1,0:T(8,128)}, f32[1024,8]{1,0:T(8,128)S(1)}, f32[8,1024]{1,0:T(8,128)S(1)}) custom-call(s32[1]{0:T(128)} %bitcast.brick_ref, f32[16,64,128]{2,1,0:T(8,128)S(1)} %constant_dynamic-update-slice_fusion.5.cells_ref, f32[16,56,128]{2,1,0:T(8,128)S(1)} %all-to-all-done.1.integrals_ref, f32[8,256,128]{2,1,0:T(8,128)S(1)} %all-to-all-done.nodes_ref, ...), custom_call_target="tpu_custom_call" | custom-call | tf_op jit(solution)/shard_map/maxwell/pallas_call | solution.py:453
  51.3 3.6 %all-to-all-start.2 = ((f32[16,112,128]{2,1,0:T(8,128)}), f32[16,112,128]{2,1,0:T(8,128)S(1)}, u32[]{:S(2)}, u32[]{:S(2)}) async-start(f32[16,112,128]{2,1,0:T(8,128)} %get-tuple-element.22), calls=%async_computation.2 | async-start | bytes 1835008 | tf_op jit(solution)/shard_map/all_to_all | solution.py:34
  55.1 15.0 %all-to-all-done.2.parts_ref.transport_ref = f32[16,112,128]{2,1,0:T(8,128)S(1)} async-done(((f32[16,112,128]{2,1,0:T(8,128)}), f32[16,112,128]{2,1,0:T(8,128)S(1)}, u32[]{:S(2)}, u32[]{:S(2)}) %all-to-all-start.2) | async-done | bytes 917536 | tf_op jit(solution)/shard_map/all_to_all | solution.py:34
  70.1 1.6 %advance.1 = (f32[16,72,128]{2,1,0:T(8,128)}, f32[64,128]{1,0:T(8,128)S(1)}) custom-call(f32[16,112,128]{2,1,0:T(8,128)S(1)} %all-to-all-done.2.parts_ref.transport_ref, f32[6,64,128]{2,1,0:T(8,128)S(1)} %constant_dynamic-update-slice_fusion.11.steps_ref, f32[64,128]{1,0:T(8,128)S(1)} %bitcast.42), custom_call_target="tpu_custom_call" | custom-call | tf_op jit(solution)/shard_map/advance/pallas_call | solution.py:484
  71.7 3.6 %all-to-all-start.3 = ((f32[16,72,128]{2,1,0:T(8,128)}), f32[16,72,128]{2,1,0:T(8,128)S(1)}, u32[]{:S(2)}, u32[]{:S(2)}) async-start(f32[16,72,128]{2,1,0:T(8,128)} %get-tuple-element.24), calls=%async_computation.3 | async-start | bytes 1179648 | tf_op jit(solution)/shard_map/all_to_all | solution.py:34
  75.3 11.5 %all-to-all-done.3.parts_ref = f32[16,72,128]{2,1,0:T(8,128)S(1)} async-done(((f32[16,72,128]{2,1,0:T(8,128)}), f32[16,72,128]{2,1,0:T(8,128)S(1)}, u32[]{:S(2)}, u32[]{:S(2)}) %all-to-all-start.3) | async-done | bytes 589856 | tf_op jit(solution)/shard_map/all_to_all | solution.py:34
  86.9 1.2 products.1
  88.1 1.0 collective-permute-start.7
  89.1 3.7 %back.1 = f32[8,256,128]{2,1,0:T(8,128)} custom-call(f32[16,72,128]{2,1,0:T(8,128)S(1)} %all-to-all-done.3.parts_ref, f32[1024,8]{1,0:T(8,128)S(1)} %get-tuple-element.29.line_ref, f32[8,1024]{1,0:T(8,128)S(1)} %get-tuple-element.30.state_ref, f32[256,2]{1,0:T(8,128)S(1)} %get-tuple-element.52.across_ref), custom_call_target="tpu_custom_call" | custom-call | tf_op jit(solution)/shard_map/back/pallas_call | solution.py:503
  92.8 2.9 %collective-permute-done.7 = f32[8,512]{1,0:T(8,128)S(1)} collective-permute-done((f32[8,512]{1,0:T(8,128)S(1)}, f32[8,512]{1,0:T(8,128)S(1)}, u32[]{:S(2)}, u32[]{:S(2)}) %collective-permute-start.7) | collective-permute-done | bytes 16416 | tf_op jit(solution)/shard_map/ppermute | solution.py:500
  95.7 0.2 fusion.32
  96.0 0.1 copy.27
  96.2 0.6 collective-permute-start.9
  96.8 3.6 %collective-permute-start.10 = (f32[40,128]{1,0:T(8,128)S(1)}, f32[40,128]{1,0:T(8,128)S(1)}, u32[]{:S(2)}, u32[]{:S(2)}) collective-permute-start(f32[40,128]{1,0:T(8,128)S(1)} %pad_add_fusion), channel_id=1, source_target_pairs={{0,24},{1,25},{2,26},{3,27},{4,28},{5,29},{6,30},{7,31},{8,16},{9,... | collective-permute-start | bytes 61448 | tf_op jit(solution)/shard_map/ppermute | solution.py:58
  100.3 1.0 collective-permute-done.8
  101.3 0.8 collective-permute-done.10
  102.1 1.9 %collective-permute-start.12 = (f32[2,40,128]{2,1,0:T(8,128)S(1)}, f32[2,40,128]{2,1,0:T(8,128)S(1)}, u32[]{:S(2)}, u32[]{:S(2)}) collective-permute-start(f32[2,40,128]{2,1,0:T(8,128)S(1)} %pad_maximum_fusion.2), channel_id=1, source_target_pairs={{0,64},{1,65},{2,66},{3,67},{4,68},{5,69},{6,70},{7,71},{8,72},{9,... | collective-permute-start | bytes 122888 | tf_op jit(solution)/shard_map/ppermute | solution.py:58
  104.0 0.7 collective-permute-start.13
  104.7 1.0 collective-permute-start.11
  105.7 4.6 %all-to-all-start.4 = ((f32[8,256,128]{2,1,0:T(8,128)}), f32[8,256,128]{2,1,0:T(8,128)S(1)}, u32[]{:S(2)}, u32[]{:S(2)}) async-start(f32[8,256,128]{2,1,0:T(8,128)} %back.1), calls=%async_computation.4 | async-start | bytes 2097152 | tf_op jit(solution)/shard_map/all_to_all | solution.py:34
  110.4 0.3 slice_reduce_fusion
  110.7 0.1 copy.28.speeds_ref
  110.9 0.8 collective-permute-done.14
  111.6 2.4 %collective-permute-start.16 = (f32[4,40,128]{2,1,0:T(8,128)S(1)}, f32[4,40,128]{2,1,0:T(8,128)S(1)}, u32[]{:S(2)}, u32[]{:S(2)}) collective-permute-start(f32[4,40,128]{2,1,0:T(8,128)S(1)} %pad_maximum_fusion), channel_id=1, source_target_pairs={{0,4},{1,5},{2,6},{3,7},{4,0},{5,1},{6,2},{7,3},{8,12},{9,13},{10,... | collective-permute-start | bytes 245768 | tf_op jit(solution)/shard_map/ppermute | solution.py:58
  114.0 2.3 %collective-permute-start.17 = (f32[4,40,128]{2,1,0:T(8,128)S(1)}, f32[4,40,128]{2,1,0:T(8,128)S(1)}, u32[]{:S(2)}, u32[]{:S(2)}) collective-permute-start(f32[4,40,128]{2,1,0:T(8,128)S(1)} %pad_maximum_fusion), channel_id=1, source_target_pairs={{0,6},{1,7},{2,4},{3,5},{4,2},{5,3},{6,0},{7,1},{8,14},{9,15},{10,... | collective-permute-start | bytes 245768 | tf_op jit(solution)/shard_map/ppermute | solution.py:58
  116.3 0.6 collective-permute-done.15
  116.9 1.4 collective-permute-done.16
  118.4 1.7 %collective-permute-done.17 = f32[4,40,128]{2,1,0:T(8,128)S(1)} collective-permute-done((f32[4,40,128]{2,1,0:T(8,128)S(1)}, f32[4,40,128]{2,1,0:T(8,128)S(1)}, u32[]{:S(2)}, u32[]{:S(2)}) %collective-permute-start.17) | collective-permute-done | bytes 81952 | tf_op jit(solution)/shard_map/ppermute | solution.py:58
  120.0 4.6 %all-to-all-done.4.back_ref = f32[8,256,128]{2,1,0:T(8,128)S(1)} async-done(((f32[8,256,128]{2,1,0:T(8,128)}), f32[8,256,128]{2,1,0:T(8,128)S(1)}, u32[]{:S(2)}, u32[]{:S(2)}) %all-to-all-start.4) | async-done | bytes 1048608 | tf_op jit(solution)/shard_map/all_to_all | solution.py:34
  124.6 6.7 %middle.1 = (f32[64,128]{1,0:T(8,128)}, f32[256,128]{1,0:T(8,128)S(1)}, f32[128,128]{1,0:T(8,128)S(1)}) custom-call(s32[1]{0:T(128)} %bitcast.brick_ref, f32[16,40,128]{2,1,0:T(8,128)S(1)} %constant_dynamic-update-slice_fusion.17.pieces_ref, f32[16,112,128]{2,1,0:T(8,128)S(1)} %all-to-all-done.2.parts_ref.transport_ref, f32[256,128]{1,0:T(8,128)S(1)} %copy-done.1, ...), custom_call_target="tpu_custom_call" | custom-call | tf_op jit(solution)/shard_map/middle/pallas_call | solution.py:519
  131.3 1.3 collective-permute-done.18
  132.6 1.5 collective-permute-start.20
  134.1 1.3 collective-permute-start.21
  135.3 0.8 collective-permute-start.19
  136.1 2.4 %collective-permute-done.20 = f32[128,128]{1,0:T(8,128)S(1)} collective-permute-done((f32[128,128]{1,0:T(8,128)S(1)}, f32[128,128]{1,0:T(8,128)S(1)}, u32[]{:S(2)}, u32[]{:S(2)}) %collective-permute-start.20) | collective-permute-done | bytes 65568 | tf_op jit(solution)/shard_map/ppermute | solution.py:58
  138.5 1.3 collective-permute-done.21
  139.8 0.9 collective-permute-start.23
  140.8 2.6 %collective-permute-start.24 = (f32[128,128]{1,0:T(8,128)S(1)}, f32[128,128]{1,0:T(8,128)S(1)}, u32[]{:S(2)}, u32[]{:S(2)}) collective-permute-start(f32[128,128]{1,0:T(8,128)S(1)} %add_add_fusion.2), channel_id=1, source_target_pairs={{0,24},{1,25},{2,26},{3,27},{4,28},{5,29},{6,30},{7,31},{8,16},{9,... | collective-permute-start | bytes 196616 | tf_op jit(solution)/shard_map/ppermute | solution.py:58
  143.4 2.8 %collective-permute-done.23 = f32[128,128]{1,0:T(8,128)S(1)} collective-permute-done((f32[128,128]{1,0:T(8,128)S(1)}, f32[128,128]{1,0:T(8,128)S(1)}, u32[]{:S(2)}, u32[]{:S(2)}) %collective-permute-start.23) | collective-permute-done | bytes 65568 | tf_op jit(solution)/shard_map/ppermute | solution.py:58
  146.2 0.4 collective-permute-done.24
  146.6 1.0 collective-permute-done.22
  147.6 1.2 collective-permute-start.26
  148.8 2.0 %collective-permute-start.27 = (f32[128,128]{1,0:T(8,128)S(1)}, f32[128,128]{1,0:T(8,128)S(1)}, u32[]{:S(2)}, u32[]{:S(2)}) collective-permute-start(f32[128,128]{1,0:T(8,128)S(1)} %add_add_fusion.1), channel_id=1, source_target_pairs={{0,96},{1,97},{2,98},{3,99},{4,100},{5,101},{6,102},{7,103},{8,104... | collective-permute-start | bytes 196616 | tf_op jit(solution)/shard_map/ppermute | solution.py:58
  150.8 0.6 collective-permute-start.25
  151.4 2.3 %collective-permute-done.26 = f32[128,128]{1,0:T(8,128)S(1)} collective-permute-done((f32[128,128]{1,0:T(8,128)S(1)}, f32[128,128]{1,0:T(8,128)S(1)}, u32[]{:S(2)}, u32[]{:S(2)}) %collective-permute-start.26) | collective-permute-done | bytes 65568 | tf_op jit(solution)/shard_map/ppermute | solution.py:58
  153.7 0.7 collective-permute-done.27
  154.4 0.7 collective-permute-done.25
  155.1 4.5 %last.1 = (f32[128,128]{1,0:T(8,128)}, f32[256,128]{1,0:T(8,128)}) custom-call(f32[128,128]{1,0:T(8,128)S(1)} %add_add_fusion.gram_ref, f32[256,128]{1,0:T(8,128)S(1)} %get-tuple-element.36.velocity_ref), custom_call_target="tpu_custom_call" | custom-call | tf_op jit(solution)/shard_map/last/pallas_call | solution.py:529
  (86 shorter events, 1.5 us)
Async XLA Ops:
  0.6 10.0 %collective-permute-start = (f32[1,64,128]{2,1,0:T(8,128)}, f32[1,64,128]{2,1,0:T(8,128)S(1)}, u32[]{:S(2)}, u32[]{:S(2)}) collective-permute-start(f32[1,64,128]{2,1,0:T(8,128)} %bitcast.39), channel_id=1, source_target_pairs={{0,1},{1,0},{2,3},{3,2},{4,5},{5,4},{6,7},{7,6},{8,9},{9,8},{10,11... | collective-permute-start | bytes 98312 | tf_op jit(solution)/shard_map/ppermute | solution.py:58
  2.7 7.2 %copy-start = (f32[2,2,16,128]{3,2,1,0:T(8,128)S(1)}, f32[2,2,16,128]{3,2,1,0:T(8,128)}, u32[]{:S(2)}) copy-start(f32[2,2,16,128]{3,2,1,0:T(8,128)} %param.2) | copy-start | bytes 98308
  2.7 25.0 %all-to-all-start = ((f32[8,256,128]{2,1,0:T(8,128)}), f32[8,256,128]{2,1,0:T(8,128)S(1)}, u32[]{:S(2)}, u32[]{:S(2)}) async-start(f32[8,256,128]{2,1,0:T(8,128)} %broadcast_in_dim.9), calls=%async_computation | async-start | bytes 2097152 | tf_op jit(solution)/shard_map/all_to_all | solution.py:34
  10.6 5.6 %collective-permute-start.1 = (f32[2,64,128]{2,1,0:T(8,128)S(1)}, f32[2,64,128]{2,1,0:T(8,128)S(1)}, u32[]{:S(2)}, u32[]{:S(2)}) collective-permute-start(f32[2,64,128]{2,1,0:T(8,128)S(1)} %pad_maximum_fusion.1), channel_id=1, source_target_pairs={{0,2},{1,3},{2,0},{3,1},{4,6},{5,7},{6,4},{7,5},{8,10},{9,11},{10,... | collective-permute-start | bytes 196616 | tf_op jit(solution)/shard_map/ppermute | solution.py:58
  12.6 7.2 %collective-permute-start.2 = (f32[2,64,128]{2,1,0:T(8,128)S(1)}, f32[2,64,128]{2,1,0:T(8,128)S(1)}, u32[]{:S(2)}, u32[]{:S(2)}) collective-permute-start(f32[2,64,128]{2,1,0:T(8,128)S(1)} %pad_maximum_fusion.1), channel_id=1, source_target_pairs={{0,4},{1,5},{2,6},{3,7},{4,0},{5,1},{6,2},{7,3},{8,12},{9,13},{10,... | collective-permute-start | bytes 196616 | tf_op jit(solution)/shard_map/ppermute | solution.py:58
  16.2 5.5 %collective-permute-start.3 = (f32[2,64,128]{2,1,0:T(8,128)S(1)}, f32[2,64,128]{2,1,0:T(8,128)S(1)}, u32[]{:S(2)}, u32[]{:S(2)}) collective-permute-start(f32[2,64,128]{2,1,0:T(8,128)S(1)} %pad_maximum_fusion.1), channel_id=1, source_target_pairs={{0,6},{1,7},{2,4},{3,5},{4,2},{5,3},{6,0},{7,1},{8,14},{9,15},{10,... | collective-permute-start | bytes 196616 | tf_op jit(solution)/shard_map/ppermute | solution.py:58
  21.7 15.4 %collective-permute-start.4 = (f32[8,64,128]{2,1,0:T(8,128)S(1)}, f32[8,64,128]{2,1,0:T(8,128)S(1)}, u32[]{:S(2)}, u32[]{:S(2)}) collective-permute-start(f32[8,64,128]{2,1,0:T(8,128)S(1)} %get-tuple-element.54), channel_id=1, source_target_pairs={{0,8},{1,9},{2,10},{3,11},{4,12},{5,13},{6,14},{7,15},{8,0},{9,1},... | collective-permute-start | bytes 786440 | tf_op jit(solution)/shard_map/ppermute | solution.py:58
  31.0 16.6 %all-to-all-start.1 = ((f32[16,56,128]{2,1,0:T(8,128)}), f32[16,56,128]{2,1,0:T(8,128)S(1)}, u32[]{:S(2)}, u32[]{:S(2)}) async-start(f32[16,56,128]{2,1,0:T(8,128)} %transport.1), calls=%async_computation.1 | async-start | bytes 917504 | tf_op jit(solution)/shard_map/all_to_all | solution.py:34
  37.1 17.8 %collective-permute-start.6 = (f32[1,2,16,128]{3,2,1,0:T(8,128)S(1)}, f32[1,2,16,128]{3,2,1,0:T(8,128)S(1)}, u32[]{:S(2)}, u32[]{:S(2)}) collective-permute-start(f32[1,2,16,128]{3,2,1,0:T(8,128)S(1)} %get-tuple-element.74), channel_id=1, source_target_pairs={{0,112},{16,0},{32,16},{48,32},{64,48},{80,64},{96,80},{112,96},{1... | collective-permute-start | bytes 49160 | tf_op jit(solution)/shard_map/ppermute | solution.py:437
  38.6 16.4 %collective-permute-start.5 = (f32[1,2,16,128]{3,2,1,0:T(8,128)S(1)}, f32[1,2,16,128]{3,2,1,0:T(8,128)S(1)}, u32[]{:S(2)}, u32[]{:S(2)}) collective-permute-start(f32[1,2,16,128]{3,2,1,0:T(8,128)S(1)} %get-tuple-element.75), channel_id=1, source_target_pairs={{0,16},{16,32},{32,48},{48,64},{64,80},{80,96},{96,112},{112,0},{1... | collective-permute-start | bytes 49160 | tf_op jit(solution)/shard_map/ppermute | solution.py:436
  51.3 18.8 %all-to-all-start.2 = ((f32[16,112,128]{2,1,0:T(8,128)}), f32[16,112,128]{2,1,0:T(8,128)S(1)}, u32[]{:S(2)}, u32[]{:S(2)}) async-start(f32[16,112,128]{2,1,0:T(8,128)} %get-tuple-element.22), calls=%async_computation.2 | async-start | bytes 1835008 | tf_op jit(solution)/shard_map/all_to_all | solution.py:34
  71.7 15.2 %all-to-all-start.3 = ((f32[16,72,128]{2,1,0:T(8,128)}), f32[16,72,128]{2,1,0:T(8,128)S(1)}, u32[]{:S(2)}, u32[]{:S(2)}) async-start(f32[16,72,128]{2,1,0:T(8,128)} %get-tuple-element.24), calls=%async_computation.3 | async-start | bytes 1179648 | tf_op jit(solution)/shard_map/all_to_all | solution.py:34
  88.1 7.6 %collective-permute-start.7 = (f32[8,512]{1,0:T(8,128)S(1)}, f32[8,512]{1,0:T(8,128)S(1)}, u32[]{:S(2)}, u32[]{:S(2)}) collective-permute-start(f32[8,512]{1,0:T(8,128)S(1)} %get-tuple-element.27), channel_id=1, source_target_pairs={{0,16},{16,32},{32,48},{48,64},{64,80},{80,96},{96,112},{112,0},{1... | collective-permute-start | bytes 49160 | tf_op jit(solution)/shard_map/ppermute | solution.py:500
  95.9 5.4 %collective-permute-start.8 = (f32[40,128]{1,0:T(8,128)S(1)}, f32[40,128]{1,0:T(8,128)S(1)}, u32[]{:S(2)}, u32[]{:S(2)}) collective-permute-start(f32[40,128]{1,0:T(8,128)S(1)} %pad_add_fusion), channel_id=1, source_target_pairs={{0,16},{1,17},{2,18},{3,19},{4,20},{5,21},{6,22},{7,23},{8,24},{9,... | collective-permute-start | bytes 61448 | tf_op jit(solution)/shard_map/ppermute | solution.py:58
  96.2 5.1 %collective-permute-start.9 = (f32[40,128]{1,0:T(8,128)S(1)}, f32[40,128]{1,0:T(8,128)S(1)}, u32[]{:S(2)}, u32[]{:S(2)}) collective-permute-start(f32[40,128]{1,0:T(8,128)S(1)} %pad_add_fusion), channel_id=1, source_target_pairs={{0,8},{1,9},{2,10},{3,11},{4,12},{5,13},{6,14},{7,15},{8,0},{9,1},... | collective-permute-start | bytes 61448 | tf_op jit(solution)/shard_map/ppermute | solution.py:58
  96.8 5.3 %collective-permute-start.10 = (f32[40,128]{1,0:T(8,128)S(1)}, f32[40,128]{1,0:T(8,128)S(1)}, u32[]{:S(2)}, u32[]{:S(2)}) collective-permute-start(f32[40,128]{1,0:T(8,128)S(1)} %pad_add_fusion), channel_id=1, source_target_pairs={{0,24},{1,25},{2,26},{3,27},{4,28},{5,29},{6,30},{7,31},{8,16},{9,... | collective-permute-start | bytes 61448 | tf_op jit(solution)/shard_map/ppermute | solution.py:58
  102.1 8.2 %collective-permute-start.12 = (f32[2,40,128]{2,1,0:T(8,128)S(1)}, f32[2,40,128]{2,1,0:T(8,128)S(1)}, u32[]{:S(2)}, u32[]{:S(2)}) collective-permute-start(f32[2,40,128]{2,1,0:T(8,128)S(1)} %pad_maximum_fusion.2), channel_id=1, source_target_pairs={{0,64},{1,65},{2,66},{3,67},{4,68},{5,69},{6,70},{7,71},{8,72},{9,... | collective-permute-start | bytes 122888 | tf_op jit(solution)/shard_map/ppermute | solution.py:58
  104.0 6.3 %collective-permute-start.13 = (f32[2,40,128]{2,1,0:T(8,128)S(1)}, f32[2,40,128]{2,1,0:T(8,128)S(1)}, u32[]{:S(2)}, u32[]{:S(2)}) collective-permute-start(f32[2,40,128]{2,1,0:T(8,128)S(1)} %pad_maximum_fusion.2), channel_id=1, source_target_pairs={{0,96},{1,97},{2,98},{3,99},{4,100},{5,101},{6,102},{7,103},{8,104... | collective-permute-start | bytes 122888 | tf_op jit(solution)/shard_map/ppermute | solution.py:58
  104.7 5.6 %collective-permute-start.11 = (f32[2,40,128]{2,1,0:T(8,128)S(1)}, f32[2,40,128]{2,1,0:T(8,128)S(1)}, u32[]{:S(2)}, u32[]{:S(2)}) collective-permute-start(f32[2,40,128]{2,1,0:T(8,128)S(1)} %pad_maximum_fusion.2), channel_id=1, source_target_pairs={{0,32},{1,33},{2,34},{3,35},{4,36},{5,37},{6,38},{7,39},{8,40},{9,... | collective-permute-start | bytes 122888 | tf_op jit(solution)/shard_map/ppermute | solution.py:58
  105.7 18.9 %all-to-all-start.4 = ((f32[8,256,128]{2,1,0:T(8,128)}), f32[8,256,128]{2,1,0:T(8,128)S(1)}, u32[]{:S(2)}, u32[]{:S(2)}) async-start(f32[8,256,128]{2,1,0:T(8,128)} %back.1), calls=%async_computation.4 | async-start | bytes 2097152 | tf_op jit(solution)/shard_map/all_to_all | solution.py:34
  110.3 1.3 collective-permute-start.14
  111.6 5.3 %collective-permute-start.15 = (f32[4,40,128]{2,1,0:T(8,128)S(1)}, f32[4,40,128]{2,1,0:T(8,128)S(1)}, u32[]{:S(2)}, u32[]{:S(2)}) collective-permute-start(f32[4,40,128]{2,1,0:T(8,128)S(1)} %pad_maximum_fusion), channel_id=1, source_target_pairs={{0,2},{1,3},{2,0},{3,1},{4,6},{5,7},{6,4},{7,5},{8,10},{9,11},{10,... | collective-permute-start | bytes 245768 | tf_op jit(solution)/shard_map/ppermute | solution.py:58
  111.6 6.7 %collective-permute-start.16 = (f32[4,40,128]{2,1,0:T(8,128)S(1)}, f32[4,40,128]{2,1,0:T(8,128)S(1)}, u32[]{:S(2)}, u32[]{:S(2)}) collective-permute-start(f32[4,40,128]{2,1,0:T(8,128)S(1)} %pad_maximum_fusion), channel_id=1, source_target_pairs={{0,4},{1,5},{2,6},{3,7},{4,0},{5,1},{6,2},{7,3},{8,12},{9,13},{10,... | collective-permute-start | bytes 245768 | tf_op jit(solution)/shard_map/ppermute | solution.py:58
  114.0 6.0 %collective-permute-start.17 = (f32[4,40,128]{2,1,0:T(8,128)S(1)}, f32[4,40,128]{2,1,0:T(8,128)S(1)}, u32[]{:S(2)}, u32[]{:S(2)}) collective-permute-start(f32[4,40,128]{2,1,0:T(8,128)S(1)} %pad_maximum_fusion), channel_id=1, source_target_pairs={{0,6},{1,7},{2,4},{3,5},{4,2},{5,3},{6,0},{7,1},{8,14},{9,15},{10,... | collective-permute-start | bytes 245768 | tf_op jit(solution)/shard_map/ppermute | solution.py:58
  116.9 7.7 %copy-start.1 = (f32[256,128]{1,0:T(8,128)S(1)}, f32[256,128]{1,0:T(8,128)}, u32[]{:S(2)}) copy-start(f32[256,128]{1,0:T(8,128)} %basis_ref.1) | copy-start | bytes 393220
  131.3 1.3 collective-permute-start.18
  132.6 5.9 %collective-permute-start.20 = (f32[128,128]{1,0:T(8,128)S(1)}, f32[128,128]{1,0:T(8,128)S(1)}, u32[]{:S(2)}, u32[]{:S(2)}) collective-permute-start(f32[128,128]{1,0:T(8,128)S(1)} %add.402), channel_id=1, source_target_pairs={{0,4},{1,5},{2,6},{3,7},{4,0},{5,1},{6,2},{7,3},{8,12},{9,13},{10,... | collective-permute-start | bytes 196616 | tf_op jit(solution)/shard_map/ppermute | solution.py:58
  134.1 5.8 %collective-permute-start.21 = (f32[128,128]{1,0:T(8,128)S(1)}, f32[128,128]{1,0:T(8,128)S(1)}, u32[]{:S(2)}, u32[]{:S(2)}) collective-permute-start(f32[128,128]{1,0:T(8,128)S(1)} %add.402), channel_id=1, source_target_pairs={{0,6},{1,7},{2,4},{3,5},{4,2},{5,3},{6,0},{7,1},{8,14},{9,15},{10,... | collective-permute-start | bytes 196616 | tf_op jit(solution)/shard_map/ppermute | solution.py:58
  135.3 4.5 %collective-permute-start.19 = (f32[128,128]{1,0:T(8,128)S(1)}, f32[128,128]{1,0:T(8,128)S(1)}, u32[]{:S(2)}, u32[]{:S(2)}) collective-permute-start(f32[128,128]{1,0:T(8,128)S(1)} %add.402), channel_id=1, source_target_pairs={{0,2},{1,3},{2,0},{3,1},{4,6},{5,7},{6,4},{7,5},{8,10},{9,11},{10,... | collective-permute-start | bytes 196616 | tf_op jit(solution)/shard_map/ppermute | solution.py:58
  139.8 6.4 %collective-permute-start.23 = (f32[128,128]{1,0:T(8,128)S(1)}, f32[128,128]{1,0:T(8,128)S(1)}, u32[]{:S(2)}, u32[]{:S(2)}) collective-permute-start(f32[128,128]{1,0:T(8,128)S(1)} %add_add_fusion.2), channel_id=1, source_target_pairs={{0,16},{1,17},{2,18},{3,19},{4,20},{5,21},{6,22},{7,23},{8,24},{9,... | collective-permute-start | bytes 196616 | tf_op jit(solution)/shard_map/ppermute | solution.py:58
  140.8 5.8 %collective-permute-start.24 = (f32[128,128]{1,0:T(8,128)S(1)}, f32[128,128]{1,0:T(8,128)S(1)}, u32[]{:S(2)}, u32[]{:S(2)}) collective-permute-start(f32[128,128]{1,0:T(8,128)S(1)} %add_add_fusion.2), channel_id=1, source_target_pairs={{0,24},{1,25},{2,26},{3,27},{4,28},{5,29},{6,30},{7,31},{8,16},{9,... | collective-permute-start | bytes 196616 | tf_op jit(solution)/shard_map/ppermute | solution.py:58
  143.3 4.3 %collective-permute-start.22 = (f32[128,128]{1,0:T(8,128)S(1)}, f32[128,128]{1,0:T(8,128)S(1)}, u32[]{:S(2)}, u32[]{:S(2)}) collective-permute-start(f32[128,128]{1,0:T(8,128)S(1)} %add_add_fusion.2), channel_id=1, source_target_pairs={{0,8},{1,9},{2,10},{3,11},{4,12},{5,13},{6,14},{7,15},{8,0},{9,1},... | collective-permute-start | bytes 196616 | tf_op jit(solution)/shard_map/ppermute | solution.py:58
  147.6 6.1 %collective-permute-start.26 = (f32[128,128]{1,0:T(8,128)S(1)}, f32[128,128]{1,0:T(8,128)S(1)}, u32[]{:S(2)}, u32[]{:S(2)}) collective-permute-start(f32[128,128]{1,0:T(8,128)S(1)} %add_add_fusion.1), channel_id=1, source_target_pairs={{0,64},{1,65},{2,66},{3,67},{4,68},{5,69},{6,70},{7,71},{8,72},{9,... | collective-permute-start | bytes 196616 | tf_op jit(solution)/shard_map/ppermute | solution.py:58
  148.8 5.6 %collective-permute-start.27 = (f32[128,128]{1,0:T(8,128)S(1)}, f32[128,128]{1,0:T(8,128)S(1)}, u32[]{:S(2)}, u32[]{:S(2)}) collective-permute-start(f32[128,128]{1,0:T(8,128)S(1)} %add_add_fusion.1), channel_id=1, source_target_pairs={{0,96},{1,97},{2,98},{3,99},{4,100},{5,101},{6,102},{7,103},{8,104... | collective-permute-start | bytes 196616 | tf_op jit(solution)/shard_map/ppermute | solution.py:58
  150.8 4.3 %collective-permute-start.25 = (f32[128,128]{1,0:T(8,128)S(1)}, f32[128,128]{1,0:T(8,128)S(1)}, u32[]{:S(2)}, u32[]{:S(2)}) collective-permute-start(f32[128,128]{1,0:T(8,128)S(1)} %add_add_fusion.1), channel_id=1, source_target_pairs={{0,32},{1,33},{2,34},{3,35},{4,36},{5,37},{6,38},{7,39},{8,40},{9,... | collective-permute-start | bytes 196616 | tf_op jit(solution)/shard_map/ppermute | solution.py:58

commit v6 on v5

--- a/solution.py
+++ b/solution.py
@@ -158,6 +158,17 @@
     return product(left_high, right_high) + small
 
 
+def repeat_kernel(source_ref, out_ref, sems):
+    copies = [
+        pltpu.make_async_copy(source_ref, out_ref.at[i], sems.at[i])
+        for i in range(out_ref.shape[0])
+    ]
+    for copy in copies:
+        copy.start()
+    for copy in copies:
+        copy.wait()
+
+
 def transport_kernel(nodes_ref, columns_ref, speeds_ref, weights_ref, out_ref):
     groups, rows, rank = nodes_ref.shape
     bricks = out_ref.shape[0]
@@ -430,7 +441,17 @@
         + [jnp.zeros_like(slab_velocity[0])] * 3,
         axis=1,
     )
-    nodes = to_all(v_basis, "slab")
+    nodes = exchange(
+        pl.pallas_call(
+            repeat_kernel,
+            out_shape=f32(slabs, rows, rank),
+            in_specs=[pl.BlockSpec(memory_space=pl.ANY)],
+            out_specs=pl.BlockSpec(memory_space=pl.ANY),
+            scratch_shapes=[pltpu.SemaphoreType.DMA((slabs,))],
+            name="repeat",
+        )(v_basis),
+        "slab",
+    )
     k_slab = gather_relative(own_cells, "brick", BRICK_GROUPS)
     k_edges, k_slab = lax.optimization_barrier((k_coeffs, k_slab))
     k_below = lax.ppermute(k_edges[-1:], "slab", up)
@@ -513,7 +534,10 @@
     lower_x, upper_x, cross_x = (from_peer(pieces, both, mask) for mask in (8, 16, 24))
     reduced = jnp.stack([pieces + upper_x, lower_x + cross_x])
     reduced = sum_over(reduced, both, ((32, 64, 96),))
-    reduced = gather_more(reduced, both, ((1,), (2, 4, 6)))
+    reduced = gather_more(reduced, both, ((1,),))
+    later, fourth = lax.optimization_barrier((reduced, fourth))
+    peers_z = [from_peer(part, both, mask) for part, mask in ((reduced, 2), (later, 4), (reduced, 6))]
+    reduced = jnp.concatenate([reduced] + peers_z, axis=0)
 
     speeds = jnp.stack(list(own_velocity) + [jnp.zeros_like(ones)] * 5, axis=1)
     basis_new, velocity_new, gram_part = pl.pallas_call(

time: 160 us -> 196 us (1.23)
  Pallas kernels: 24.6 us -> 57.5 us
  waiting for transfers between devices: 69.8 us -> 73.9 us
  local copies, waits for them, and re-layouts: 3.4 us -> 1.44 us
    pallas_call x0 -> x1, Pallas kernels: none -> 32.9 us  [local(): pl.pallas_call(repeat_kernel, out_shape=f32(slabs, rows, rank), in_specs=...]
    ppermute x25, waiting for transfers between devices: 24.4 us -> 33 us  [from_peer(): return lax.ppermute(values, axis, [(i, i ^ mask) for i in range(peers)])]
    all_to_all x5, waiting for transfers between devices: 42.5 us -> 38 us  [exchange(): return lax.all_to_all(array, axis, 0, 0, tiled=True)]
    ppermute x25, starting transfers between devices: 29.9 us -> 32.1 us  [from_peer(): return lax.ppermute(values, axis, [(i, i ^ mask) for i in range(peers)])]
    broadcast_in_dim x1 -> x0, local copies, waits for them, and re-layouts: 1.96 us -> none  [to_all(): jnp.broadcast_to(array[None], (copies,) + array.shape)]
  transfers between devices with their start and end apart: 33 -> 33, of which waited for: 23 -> 21; matrix products, arithmetic and copies ran while one was open for 3% -> 1% of each run, Pallas kernels for 7% -> 22%
where the time goes in v6:
time: 196 us
  waiting for transfers between devices  73.9 us (38%)
  starting transfers between devices  60.6 us (31%)
  Pallas kernels  57.5 us (29%)
    all_to_all x5, waiting for transfers between devices, exchange(): return lax.all_to_all(array, axis, 0, 0, tiled=True)  38 us
    ppermute x25, waiting for transfers between devices, from_peer(): return lax.ppermute(values, axis, [(i, i ^ mask) for i in range(peers)])  33 us
    pallas_call x1, Pallas kernels, local(): pl.pallas_call(repeat_kernel, out_shape=f32(slabs, rows, rank), in_specs=...  32.9 us
    ppermute x25, starting transfers between devices, from_peer(): return lax.ppermute(values, axis, [(i, i ^ mask) for i in range(peers)])  32.1 us
    all_to_all x5, starting transfers between devices, exchange(): return lax.all_to_all(array, axis, 0, 0, tiled=True)  23.9 us
    pallas_call x1, Pallas kernels, local(): pl.pallas_call(functools.partial(middle_kernel, lengths=lengths, time_ste...  6.7 us
    pallas_call x1, Pallas kernels, local(): pl.pallas_call(last_kernel, out_shape=(f32(rank, rank), f32(rows, rank)),...  4.49 us
  transfers between devices with their start and end apart: 33, of which 21 were waited for; matrix products, arithmetic and copies ran while one was open for 1% of the time, Pallas kernels for 22%

profile of v6, /device:TPU:0, one launch (start us, length us, event | category | flops | bytes accessed | tf_op | source)
XLA Modules:
  0.0 195.9 jit_solution(12111113180831223408)
XLA Ops:
  0.6 0.1 collective-permute-start
  0.7 32.9 %repeat.1 = f32[8,256,128]{2,1,0:T(8,128)} custom-call(f32[256,128]{1,0:T(8,128)} %basis_ref.1), custom_call_target="tpu_custom_call" | custom-call | tf_op jit(solution)/shard_map/repeat/pallas_call | solution.py:445
  33.7 7.0 %all-to-all-start = ((f32[8,256,128]{2,1,0:T(8,128)}), f32[8,256,128]{2,1,0:T(8,128)S(1)}, u32[]{:S(2)}, u32[]{:S(2)}) async-start(f32[8,256,128]{2,1,0:T(8,128)} %repeat.1), calls=%async_computation | async-start | bytes 2097152 | tf_op jit(solution)/shard_map/all_to_all | solution.py:34
  40.9 0.1 copy.24
  41.1 0.2 and_select_fusion.3
  41.3 0.1 slice_bitcast_fusion.4
  41.5 2.0 %collective-permute-start.1 = (f32[2,64,128]{2,1,0:T(8,128)S(1)}, f32[2,64,128]{2,1,0:T(8,128)S(1)}, u32[]{:S(2)}, u32[]{:S(2)}) collective-permute-start(f32[2,64,128]{2,1,0:T(8,128)S(1)} %pad_maximum_fusion.1), channel_id=1, source_target_pairs={{0,2},{1,3},{2,0},{3,1},{4,6},{5,7},{6,4},{7,5},{8,10},{9,11},{10,... | collective-permute-start | bytes 196616 | tf_op jit(solution)/shard_map/ppermute | solution.py:58
  43.5 3.6 %collective-permute-start.2 = (f32[2,64,128]{2,1,0:T(8,128)S(1)}, f32[2,64,128]{2,1,0:T(8,128)S(1)}, u32[]{:S(2)}, u32[]{:S(2)}) collective-permute-start(f32[2,64,128]{2,1,0:T(8,128)S(1)} %pad_maximum_fusion.1), channel_id=1, source_target_pairs={{0,4},{1,5},{2,6},{3,7},{4,0},{5,1},{6,2},{7,3},{8,12},{9,13},{10,... | collective-permute-start | bytes 196616 | tf_op jit(solution)/shard_map/ppermute | solution.py:58
  47.1 3.6 %collective-permute-done.2 = f32[2,64,128]{2,1,0:T(8,128)S(1)} collective-permute-done((f32[2,64,128]{2,1,0:T(8,128)S(1)}, f32[2,64,128]{2,1,0:T(8,128)S(1)}, u32[]{:S(2)}, u32[]{:S(2)}) %collective-permute-start.2) | collective-permute-done | bytes 65568 | tf_op jit(solution)/shard_map/ppermute | solution.py:58
  50.7 1.9 collective-permute-done.3
  52.6 0.7 collective-permute-start.4
  53.2 0.3 minimum_reduce_fusion
  53.6 0.1 copy.25.columns_ref
  53.9 0.1 stack.61.weights_ref
  54.0 4.6 %all-to-all-done.nodes_ref = f32[8,256,128]{2,1,0:T(8,128)S(1)} async-done(((f32[8,256,128]{2,1,0:T(8,128)}), f32[8,256,128]{2,1,0:T(8,128)S(1)}, u32[]{:S(2)}, u32[]{:S(2)}) %all-to-all-start) | async-done | bytes 1048608 | tf_op jit(solution)/shard_map/all_to_all | solution.py:34
  58.7 3.2 %transport.1 = f32[16,56,128]{2,1,0:T(8,128)} custom-call(f32[8,256,128]{2,1,0:T(8,128)S(1)} %all-to-all-done.nodes_ref, f32[256,8]{1,0:T(8,128)S(1)} %copy.25.columns_ref, f32[8,128]{1,0:T(8,128)S(1)} %broadcast_in_dim.14.speeds_ref.first_ref, f32[8,8,256]{2,1,0:T(8,128)S(1)} %stack.61.weights_ref), custom_call_target="tpu_custom_call" | custom-call | tf_op jit(solution)/shard_map/transport/pallas_call | solution.py:466
  61.8 6.1 %all-to-all-start.1 = ((f32[16,56,128]{2,1,0:T(8,128)}), f32[16,56,128]{2,1,0:T(8,128)S(1)}, u32[]{:S(2)}, u32[]{:S(2)}) async-start(f32[16,56,128]{2,1,0:T(8,128)} %transport.1), calls=%async_computation.1 | async-start | bytes 917504 | tf_op jit(solution)/shard_map/all_to_all | solution.py:34
  68.0 1.4 collective-permute-start.6
  69.4 2.2 %collective-permute-start.5 = (f32[1,2,16,128]{3,2,1,0:T(8,128)S(1)}, f32[1,2,16,128]{3,2,1,0:T(8,128)S(1)}, u32[]{:S(2)}, u32[]{:S(2)}) collective-permute-start(f32[1,2,16,128]{3,2,1,0:T(8,128)S(1)} %get-tuple-element.79), channel_id=1, source_target_pairs={{0,16},{16,32},{32,48},{48,64},{64,80},{80,96},{96,112},{112,0},{1... | collective-permute-start | bytes 49160 | tf_op jit(solution)/shard_map/ppermute | solution.py:457
  71.6 6.8 %all-to-all-done.1.integrals_ref = f32[16,56,128]{2,1,0:T(8,128)S(1)} async-done(((f32[16,56,128]{2,1,0:T(8,128)}), f32[16,56,128]{2,1,0:T(8,128)S(1)}, u32[]{:S(2)}, u32[]{:S(2)}) %all-to-all-start.1) | async-done | bytes 458784 | tf_op jit(solution)/shard_map/all_to_all | solution.py:34
  78.5 3.7 %maxwell.1 = (f32[16,112,128]{2,1,0:T(8,128)}, f32[1024,8]{1,0:T(8,128)S(1)}, f32[8,1024]{1,0:T(8,128)S(1)}) custom-call(s32[1]{0:T(128)} %bitcast.brick_ref, f32[16,64,128]{2,1,0:T(8,128)S(1)} %constant_dynamic-update-slice_fusion.5.cells_ref, f32[16,56,128]{2,1,0:T(8,128)S(1)} %all-to-all-done.1.integrals_ref, f32[8,256,128]{2,1,0:T(8,128)S(1)} %all-to-all-done.nodes_ref, ...), custom_call_target="tpu_custom_call" | custom-call | tf_op jit(solution)/shard_map/maxwell/pallas_call | solution.py:474
  82.2 3.6 %all-to-all-start.2 = ((f32[16,112,128]{2,1,0:T(8,128)}), f32[16,112,128]{2,1,0:T(8,128)S(1)}, u32[]{:S(2)}, u32[]{:S(2)}) async-start(f32[16,112,128]{2,1,0:T(8,128)} %get-tuple-element.24), calls=%async_computation.2 | async-start | bytes 1835008 | tf_op jit(solution)/shard_map/all_to_all | solution.py:34
  86.0 15.0 %all-to-all-done.2.parts_ref.transport_ref = f32[16,112,128]{2,1,0:T(8,128)S(1)} async-done(((f32[16,112,128]{2,1,0:T(8,128)}), f32[16,112,128]{2,1,0:T(8,128)S(1)}, u32[]{:S(2)}, u32[]{:S(2)}) %all-to-all-start.2) | async-done | bytes 917536 | tf_op jit(solution)/shard_map/all_to_all | solution.py:34
  101.0 1.6 advance.1
  102.6 3.6 %all-to-all-start.3 = ((f32[16,72,128]{2,1,0:T(8,128)}), f32[16,72,128]{2,1,0:T(8,128)S(1)}, u32[]{:S(2)}, u32[]{:S(2)}) async-start(f32[16,72,128]{2,1,0:T(8,128)} %get-tuple-element.26), calls=%async_computation.3 | async-start | bytes 1179648 | tf_op jit(solution)/shard_map/all_to_all | solution.py:34
  106.2 11.5 %all-to-all-done.3.parts_ref = f32[16,72,128]{2,1,0:T(8,128)S(1)} async-done(((f32[16,72,128]{2,1,0:T(8,128)}), f32[16,72,128]{2,1,0:T(8,128)S(1)}, u32[]{:S(2)}, u32[]{:S(2)}) %all-to-all-start.3) | async-done | bytes 589856 | tf_op jit(solution)/shard_map/all_to_all | solution.py:34
  117.8 1.2 products.1
  119.0 1.0 collective-permute-start.7
  120.0 3.7 %back.1 = f32[8,256,128]{2,1,0:T(8,128)} custom-call(f32[16,72,128]{2,1,0:T(8,128)S(1)} %all-to-all-done.3.parts_ref, f32[1024,8]{1,0:T(8,128)S(1)} %get-tuple-element.31.line_ref, f32[8,1024]{1,0:T(8,128)S(1)} %get-tuple-element.32.state_ref, f32[256,2]{1,0:T(8,128)S(1)} %get-tuple-element.56.across_ref), custom_call_target="tpu_custom_call" | custom-call | tf_op jit(solution)/shard_map/back/pallas_call | solution.py:524
  123.7 2.9 %collective-permute-done.7 = f32[8,512]{1,0:T(8,128)S(1)} collective-permute-done((f32[8,512]{1,0:T(8,128)S(1)}, f32[8,512]{1,0:T(8,128)S(1)}, u32[]{:S(2)}, u32[]{:S(2)}) %collective-permute-start.7) | collective-permute-done | bytes 16416 | tf_op jit(solution)/shard_map/ppermute | solution.py:521
  126.6 0.2 fusion.32
  126.9 0.1 copy.27
  127.1 0.6 collective-permute-start.9
  127.6 3.6 %collective-permute-start.10 = (f32[40,128]{1,0:T(8,128)S(1)}, f32[40,128]{1,0:T(8,128)S(1)}, u32[]{:S(2)}, u32[]{:S(2)}) collective-permute-start(f32[40,128]{1,0:T(8,128)S(1)} %pad_add_fusion), channel_id=1, source_target_pairs={{0,24},{1,25},{2,26},{3,27},{4,28},{5,29},{6,30},{7,31},{8,16},{9,... | collective-permute-start | bytes 61448 | tf_op jit(solution)/shard_map/ppermute | solution.py:58
  131.2 3.6 %all-to-all-start.4 = ((f32[8,256,128]{2,1,0:T(8,128)}), f32[8,256,128]{2,1,0:T(8,128)S(1)}, u32[]{:S(2)}, u32[]{:S(2)}) async-start(f32[8,256,128]{2,1,0:T(8,128)} %back.1), calls=%async_computation.4 | async-start | bytes 2097152 | tf_op jit(solution)/shard_map/all_to_all | solution.py:34
  134.9 3.5 %collective-permute-start.12 = (f32[2,40,128]{2,1,0:T(8,128)S(1)}, f32[2,40,128]{2,1,0:T(8,128)S(1)}, u32[]{:S(2)}, u32[]{:S(2)}) collective-permute-start(f32[2,40,128]{2,1,0:T(8,128)S(1)} %pad_maximum_fusion.2), channel_id=1, source_target_pairs={{0,64},{1,65},{2,66},{3,67},{4,68},{5,69},{6,70},{7,71},{8,72},{9,... | collective-permute-start | bytes 122888 | tf_op jit(solution)/shard_map/ppermute | solution.py:58
  138.4 1.2 collective-permute-start.13
  139.5 8.5 %collective-permute-done.12 = f32[2,40,128]{2,1,0:T(8,128)S(1)} collective-permute-done((f32[2,40,128]{2,1,0:T(8,128)S(1)}, f32[2,40,128]{2,1,0:T(8,128)S(1)}, u32[]{:S(2)}, u32[]{:S(2)}) %collective-permute-start.12) | collective-permute-done | bytes 40992 | tf_op jit(solution)/shard_map/ppermute | solution.py:58
  148.0 0.3 collective-permute-done.13
  148.5 0.3 slice_reduce_fusion
  148.8 0.1 copy.28.speeds_ref
  148.9 0.8 collective-permute-done.14
  149.7 1.9 collective-permute-start.17
  151.6 2.2 %collective-permute-start.16 = (f32[4,40,128]{2,1,0:T(8,128)S(1)}, f32[4,40,128]{2,1,0:T(8,128)S(1)}, u32[]{:S(2)}, u32[]{:S(2)}) collective-permute-start(f32[4,40,128]{2,1,0:T(8,128)S(1)} %pad_maximum_fusion), channel_id=1, source_target_pairs={{0,4},{1,5},{2,6},{3,7},{4,0},{5,1},{6,2},{7,3},{8,12},{9,13},{10,... | collective-permute-start | bytes 245768 | tf_op jit(solution)/shard_map/ppermute | solution.py:58
  153.8 0.3 collective-permute-done.15
  154.2 3.5 %collective-permute-done.16 = f32[4,40,128]{2,1,0:T(8,128)S(1)} collective-permute-done((f32[4,40,128]{2,1,0:T(8,128)S(1)}, f32[4,40,128]{2,1,0:T(8,128)S(1)}, u32[]{:S(2)}, u32[]{:S(2)}) %collective-permute-start.16) | collective-permute-done | bytes 81952 | tf_op jit(solution)/shard_map/ppermute | solution.py:58
  157.7 6.7 %middle.1 = (f32[64,128]{1,0:T(8,128)}, f32[256,128]{1,0:T(8,128)S(1)}, f32[128,128]{1,0:T(8,128)S(1)}) custom-call(s32[1]{0:T(128)} %bitcast.brick_ref, f32[16,40,128]{2,1,0:T(8,128)S(1)} %constant_dynamic-update-slice_fusion.17.pieces_ref, f32[16,112,128]{2,1,0:T(8,128)S(1)} %all-to-all-done.2.parts_ref.transport_ref, f32[256,128]{1,0:T(8,128)S(1)} %copy-done.1, ...), custom_call_target="tpu_custom_call" | custom-call | tf_op jit(solution)/shard_map/middle/pallas_call | solution.py:543
  164.4 1.3 collective-permute-done.18
  165.7 2.2 %collective-permute-start.20 = (f32[128,128]{1,0:T(8,128)S(1)}, f32[128,128]{1,0:T(8,128)S(1)}, u32[]{:S(2)}, u32[]{:S(2)}) collective-permute-start(f32[128,128]{1,0:T(8,128)S(1)} %add.402), channel_id=1, source_target_pairs={{0,4},{1,5},{2,6},{3,7},{4,0},{5,1},{6,2},{7,3},{8,12},{9,13},{10,... | collective-permute-start | bytes 196616 | tf_op jit(solution)/shard_map/ppermute | solution.py:58
  167.9 1.9 collective-permute-start.21
  169.8 1.8 collective-permute-done.20
  171.5 1.8 collective-permute-done.21
  173.4 0.7 collective-permute-done.19
  174.0 4.2 %collective-permute-start.23 = (f32[128,128]{1,0:T(8,128)S(1)}, f32[128,128]{1,0:T(8,128)S(1)}, u32[]{:S(2)}, u32[]{:S(2)}) collective-permute-start(f32[128,128]{1,0:T(8,128)S(1)} %add_add_fusion.2), channel_id=1, source_target_pairs={{0,16},{1,17},{2,18},{3,19},{4,20},{5,21},{6,22},{7,23},{8,24},{9,... | collective-permute-start | bytes 196616 | tf_op jit(solution)/shard_map/ppermute | solution.py:58
  178.2 0.6 collective-permute-start.22
  178.8 1.7 collective-permute-done.23
  180.5 3.2 %collective-permute-done.24 = f32[128,128]{1,0:T(8,128)S(1)} collective-permute-done((f32[128,128]{1,0:T(8,128)S(1)}, f32[128,128]{1,0:T(8,128)S(1)}, u32[]{:S(2)}, u32[]{:S(2)}) %collective-permute-start.24) | collective-permute-done | bytes 65568 | tf_op jit(solution)/shard_map/ppermute | solution.py:58
  183.7 1.8 collective-permute-start.26
  185.4 1.6 collective-permute-start.27
  187.1 0.4 collective-permute-start.25
  187.5 2.3 %collective-permute-done.26 = f32[128,128]{1,0:T(8,128)S(1)} collective-permute-done((f32[128,128]{1,0:T(8,128)S(1)}, f32[128,128]{1,0:T(8,128)S(1)}, u32[]{:S(2)}, u32[]{:S(2)}) %collective-permute-start.26) | collective-permute-done | bytes 65568 | tf_op jit(solution)/shard_map/ppermute | solution.py:58
  189.8 1.2 collective-permute-done.27
  190.9 0.4 collective-permute-done.25
  191.4 4.5 %last.1 = (f32[128,128]{1,0:T(8,128)}, f32[256,128]{1,0:T(8,128)}) custom-call(f32[128,128]{1,0:T(8,128)S(1)} %add_add_fusion.gram_ref, f32[256,128]{1,0:T(8,128)S(1)} %get-tuple-element.40.velocity_ref), custom_call_target="tpu_custom_call" | custom-call | tf_op jit(solution)/shard_map/last/pallas_call | solution.py:553
  (86 shorter events, 1.0 us)
Async XLA Ops:
  0.6 40.8 %collective-permute-start = (f32[1,64,128]{2,1,0:T(8,128)}, f32[1,64,128]{2,1,0:T(8,128)S(1)}, u32[]{:S(2)}, u32[]{:S(2)}) collective-permute-start(f32[1,64,128]{2,1,0:T(8,128)} %bitcast.39), channel_id=1, source_target_pairs={{0,1},{1,0},{2,3},{3,2},{4,5},{5,4},{6,7},{7,6},{8,9},{9,8},{10,11... | collective-permute-start | bytes 98312 | tf_op jit(solution)/shard_map/ppermute | solution.py:58
  33.7 7.1 %copy-start = (f32[2,2,16,128]{3,2,1,0:T(8,128)S(1)}, f32[2,2,16,128]{3,2,1,0:T(8,128)}, u32[]{:S(2)}) copy-start(f32[2,2,16,128]{3,2,1,0:T(8,128)} %param.2) | copy-start | bytes 98308
  33.7 24.9 %all-to-all-start = ((f32[8,256,128]{2,1,0:T(8,128)}), f32[8,256,128]{2,1,0:T(8,128)S(1)}, u32[]{:S(2)}, u32[]{:S(2)}) async-start(f32[8,256,128]{2,1,0:T(8,128)} %repeat.1), calls=%async_computation | async-start | bytes 2097152 | tf_op jit(solution)/shard_map/all_to_all | solution.py:34
  41.5 5.6 %collective-permute-start.1 = (f32[2,64,128]{2,1,0:T(8,128)S(1)}, f32[2,64,128]{2,1,0:T(8,128)S(1)}, u32[]{:S(2)}, u32[]{:S(2)}) collective-permute-start(f32[2,64,128]{2,1,0:T(8,128)S(1)} %pad_maximum_fusion.1), channel_id=1, source_target_pairs={{0,2},{1,3},{2,0},{3,1},{4,6},{5,7},{6,4},{7,5},{8,10},{9,11},{10,... | collective-permute-start | bytes 196616 | tf_op jit(solution)/shard_map/ppermute | solution.py:58
  43.5 7.2 %collective-permute-start.2 = (f32[2,64,128]{2,1,0:T(8,128)S(1)}, f32[2,64,128]{2,1,0:T(8,128)S(1)}, u32[]{:S(2)}, u32[]{:S(2)}) collective-permute-start(f32[2,64,128]{2,1,0:T(8,128)S(1)} %pad_maximum_fusion.1), channel_id=1, source_target_pairs={{0,4},{1,5},{2,6},{3,7},{4,0},{5,1},{6,2},{7,3},{8,12},{9,13},{10,... | collective-permute-start | bytes 196616 | tf_op jit(solution)/shard_map/ppermute | solution.py:58
  47.1 5.5 %collective-permute-start.3 = (f32[2,64,128]{2,1,0:T(8,128)S(1)}, f32[2,64,128]{2,1,0:T(8,128)S(1)}, u32[]{:S(2)}, u32[]{:S(2)}) collective-permute-start(f32[2,64,128]{2,1,0:T(8,128)S(1)} %pad_maximum_fusion.1), channel_id=1, source_target_pairs={{0,6},{1,7},{2,4},{3,5},{4,2},{5,3},{6,0},{7,1},{8,14},{9,15},{10,... | collective-permute-start | bytes 196616 | tf_op jit(solution)/shard_map/ppermute | solution.py:58
  52.6 15.4 %collective-permute-start.4 = (f32[8,64,128]{2,1,0:T(8,128)S(1)}, f32[8,64,128]{2,1,0:T(8,128)S(1)}, u32[]{:S(2)}, u32[]{:S(2)}) collective-permute-start(f32[8,64,128]{2,1,0:T(8,128)S(1)} %get-tuple-element.58), channel_id=1, source_target_pairs={{0,8},{1,9},{2,10},{3,11},{4,12},{5,13},{6,14},{7,15},{8,0},{9,1},... | collective-permute-start | bytes 786440 | tf_op jit(solution)/shard_map/ppermute | solution.py:58
  61.8 16.6 %all-to-all-start.1 = ((f32[16,56,128]{2,1,0:T(8,128)}), f32[16,56,128]{2,1,0:T(8,128)S(1)}, u32[]{:S(2)}, u32[]{:S(2)}) async-start(f32[16,56,128]{2,1,0:T(8,128)} %transport.1), calls=%async_computation.1 | async-start | bytes 917504 | tf_op jit(solution)/shard_map/all_to_all | solution.py:34
  68.0 17.8 %collective-permute-start.6 = (f32[1,2,16,128]{3,2,1,0:T(8,128)S(1)}, f32[1,2,16,128]{3,2,1,0:T(8,128)S(1)}, u32[]{:S(2)}, u32[]{:S(2)}) collective-permute-start(f32[1,2,16,128]{3,2,1,0:T(8,128)S(1)} %get-tuple-element.78), channel_id=1, source_target_pairs={{0,112},{16,0},{32,16},{48,32},{64,48},{80,64},{96,80},{112,96},{1... | collective-permute-start | bytes 49160 | tf_op jit(solution)/shard_map/ppermute | solution.py:458
  69.4 16.4 %collective-permute-start.5 = (f32[1,2,16,128]{3,2,1,0:T(8,128)S(1)}, f32[1,2,16,128]{3,2,1,0:T(8,128)S(1)}, u32[]{:S(2)}, u32[]{:S(2)}) collective-permute-start(f32[1,2,16,128]{3,2,1,0:T(8,128)S(1)} %get-tuple-element.79), channel_id=1, source_target_pairs={{0,16},{16,32},{32,48},{48,64},{64,80},{80,96},{96,112},{112,0},{1... | collective-permute-start | bytes 49160 | tf_op jit(solution)/shard_map/ppermute | solution.py:457
  82.2 18.8 %all-to-all-start.2 = ((f32[16,112,128]{2,1,0:T(8,128)}), f32[16,112,128]{2,1,0:T(8,128)S(1)}, u32[]{:S(2)}, u32[]{:S(2)}) async-start(f32[16,112,128]{2,1,0:T(8,128)} %get-tuple-element.24), calls=%async_computation.2 | async-start | bytes 1835008 | tf_op jit(solution)/shard_map/all_to_all | solution.py:34
  102.6 15.2 %all-to-all-start.3 = ((f32[16,72,128]{2,1,0:T(8,128)}), f32[16,72,128]{2,1,0:T(8,128)S(1)}, u32[]{:S(2)}, u32[]{:S(2)}) async-start(f32[16,72,128]{2,1,0:T(8,128)} %get-tuple-element.26), calls=%async_computation.3 | async-start | bytes 1179648 | tf_op jit(solution)/shard_map/all_to_all | solution.py:34
  119.0 7.6 %collective-permute-start.7 = (f32[8,512]{1,0:T(8,128)S(1)}, f32[8,512]{1,0:T(8,128)S(1)}, u32[]{:S(2)}, u32[]{:S(2)}) collective-permute-start(f32[8,512]{1,0:T(8,128)S(1)} %get-tuple-element.29), channel_id=1, source_target_pairs={{0,16},{16,32},{32,48},{48,64},{64,80},{80,96},{96,112},{112,0},{1... | collective-permute-start | bytes 49160 | tf_op jit(solution)/shard_map/ppermute | solution.py:521
  126.8 8.0 %collective-permute-start.8 = (f32[40,128]{1,0:T(8,128)S(1)}, f32[40,128]{1,0:T(8,128)S(1)}, u32[]{:S(2)}, u32[]{:S(2)}) collective-permute-start(f32[40,128]{1,0:T(8,128)S(1)} %pad_add_fusion), channel_id=1, source_target_pairs={{0,16},{1,17},{2,18},{3,19},{4,20},{5,21},{6,22},{7,23},{8,24},{9,... | collective-permute-start | bytes 61448 | tf_op jit(solution)/shard_map/ppermute | solution.py:58
  127.1 7.7 %collective-permute-start.9 = (f32[40,128]{1,0:T(8,128)S(1)}, f32[40,128]{1,0:T(8,128)S(1)}, u32[]{:S(2)}, u32[]{:S(2)}) collective-permute-start(f32[40,128]{1,0:T(8,128)S(1)} %pad_add_fusion), channel_id=1, source_target_pairs={{0,8},{1,9},{2,10},{3,11},{4,12},{5,13},{6,14},{7,15},{8,0},{9,1},... | collective-permute-start | bytes 61448 | tf_op jit(solution)/shard_map/ppermute | solution.py:58
  127.6 7.2 %collective-permute-start.10 = (f32[40,128]{1,0:T(8,128)S(1)}, f32[40,128]{1,0:T(8,128)S(1)}, u32[]{:S(2)}, u32[]{:S(2)}) collective-permute-start(f32[40,128]{1,0:T(8,128)S(1)} %pad_add_fusion), channel_id=1, source_target_pairs={{0,24},{1,25},{2,26},{3,27},{4,28},{5,29},{6,30},{7,31},{8,16},{9,... | collective-permute-start | bytes 61448 | tf_op jit(solution)/shard_map/ppermute | solution.py:58
  131.2 20.4 %all-to-all-start.4 = ((f32[8,256,128]{2,1,0:T(8,128)}), f32[8,256,128]{2,1,0:T(8,128)S(1)}, u32[]{:S(2)}, u32[]{:S(2)}) async-start(f32[8,256,128]{2,1,0:T(8,128)} %back.1), calls=%async_computation.4 | async-start | bytes 2097152 | tf_op jit(solution)/shard_map/all_to_all | solution.py:34
  134.9 13.2 %collective-permute-start.12 = (f32[2,40,128]{2,1,0:T(8,128)S(1)}, f32[2,40,128]{2,1,0:T(8,128)S(1)}, u32[]{:S(2)}, u32[]{:S(2)}) collective-permute-start(f32[2,40,128]{2,1,0:T(8,128)S(1)} %pad_maximum_fusion.2), channel_id=1, source_target_pairs={{0,64},{1,65},{2,66},{3,67},{4,68},{5,69},{6,70},{7,71},{8,72},{9,... | collective-permute-start | bytes 122888 | tf_op jit(solution)/shard_map/ppermute | solution.py:58
  138.4 10.0 %collective-permute-start.13 = (f32[2,40,128]{2,1,0:T(8,128)S(1)}, f32[2,40,128]{2,1,0:T(8,128)S(1)}, u32[]{:S(2)}, u32[]{:S(2)}) collective-permute-start(f32[2,40,128]{2,1,0:T(8,128)S(1)} %pad_maximum_fusion.2), channel_id=1, source_target_pairs={{0,96},{1,97},{2,98},{3,99},{4,100},{5,101},{6,102},{7,103},{8,104... | collective-permute-start | bytes 122888 | tf_op jit(solution)/shard_map/ppermute | solution.py:58
  139.5 8.8 %collective-permute-start.11 = (f32[2,40,128]{2,1,0:T(8,128)S(1)}, f32[2,40,128]{2,1,0:T(8,128)S(1)}, u32[]{:S(2)}, u32[]{:S(2)}) collective-permute-start(f32[2,40,128]{2,1,0:T(8,128)S(1)} %pad_maximum_fusion.2), channel_id=1, source_target_pairs={{0,32},{1,33},{2,34},{3,35},{4,36},{5,37},{6,38},{7,39},{8,40},{9,... | collective-permute-start | bytes 122888 | tf_op jit(solution)/shard_map/ppermute | solution.py:58
  148.4 1.3 collective-permute-start.14
  149.7 4.5 %collective-permute-start.15 = (f32[4,40,128]{2,1,0:T(8,128)S(1)}, f32[4,40,128]{2,1,0:T(8,128)S(1)}, u32[]{:S(2)}, u32[]{:S(2)}) collective-permute-start(f32[4,40,128]{2,1,0:T(8,128)S(1)} %pad_maximum_fusion), channel_id=1, source_target_pairs={{0,2},{1,3},{2,0},{3,1},{4,6},{5,7},{6,4},{7,5},{8,10},{9,11},{10,... | collective-permute-start | bytes 245768 | tf_op jit(solution)/shard_map/ppermute | solution.py:58
  149.7 8.0 %collective-permute-start.17 = (f32[4,40,128]{2,1,0:T(8,128)S(1)}, f32[4,40,128]{2,1,0:T(8,128)S(1)}, u32[]{:S(2)}, u32[]{:S(2)}) collective-permute-start(f32[4,40,128]{2,1,0:T(8,128)S(1)} %pad_maximum_fusion), channel_id=1, source_target_pairs={{0,6},{1,7},{2,4},{3,5},{4,2},{5,3},{6,0},{7,1},{8,14},{9,15},{10,... | collective-permute-start | bytes 245768 | tf_op jit(solution)/shard_map/ppermute | solution.py:58
  151.6 6.0 %collective-permute-start.16 = (f32[4,40,128]{2,1,0:T(8,128)S(1)}, f32[4,40,128]{2,1,0:T(8,128)S(1)}, u32[]{:S(2)}, u32[]{:S(2)}) collective-permute-start(f32[4,40,128]{2,1,0:T(8,128)S(1)} %pad_maximum_fusion), channel_id=1, source_target_pairs={{0,4},{1,5},{2,6},{3,7},{4,0},{5,1},{6,2},{7,3},{8,12},{9,13},{10,... | collective-permute-start | bytes 245768 | tf_op jit(solution)/shard_map/ppermute | solution.py:58
  154.2 3.5 %copy-start.1 = (f32[256,128]{1,0:T(8,128)S(1)}, f32[256,128]{1,0:T(8,128)}, u32[]{:S(2)}) copy-start(f32[256,128]{1,0:T(8,128)} %basis_ref.1) | copy-start | bytes 393220
  164.4 1.3 collective-permute-start.18
  165.7 5.8 %collective-permute-start.20 = (f32[128,128]{1,0:T(8,128)S(1)}, f32[128,128]{1,0:T(8,128)S(1)}, u32[]{:S(2)}, u32[]{:S(2)}) collective-permute-start(f32[128,128]{1,0:T(8,128)S(1)} %add.402), channel_id=1, source_target_pairs={{0,4},{1,5},{2,6},{3,7},{4,0},{5,1},{6,2},{7,3},{8,12},{9,13},{10,... | collective-permute-start | bytes 196616 | tf_op jit(solution)/shard_map/ppermute | solution.py:58
  167.9 5.5 %collective-permute-start.21 = (f32[128,128]{1,0:T(8,128)S(1)}, f32[128,128]{1,0:T(8,128)S(1)}, u32[]{:S(2)}, u32[]{:S(2)}) collective-permute-start(f32[128,128]{1,0:T(8,128)S(1)} %add.402), channel_id=1, source_target_pairs={{0,6},{1,7},{2,4},{3,5},{4,2},{5,3},{6,0},{7,1},{8,14},{9,15},{10,... | collective-permute-start | bytes 196616 | tf_op jit(solution)/shard_map/ppermute | solution.py:58
  169.7 4.3 %collective-permute-start.19 = (f32[128,128]{1,0:T(8,128)S(1)}, f32[128,128]{1,0:T(8,128)S(1)}, u32[]{:S(2)}, u32[]{:S(2)}) collective-permute-start(f32[128,128]{1,0:T(8,128)S(1)} %add.402), channel_id=1, source_target_pairs={{0,2},{1,3},{2,0},{3,1},{4,6},{5,7},{6,4},{7,5},{8,10},{9,11},{10,... | collective-permute-start | bytes 196616 | tf_op jit(solution)/shard_map/ppermute | solution.py:58
  174.0 6.4 %collective-permute-start.23 = (f32[128,128]{1,0:T(8,128)S(1)}, f32[128,128]{1,0:T(8,128)S(1)}, u32[]{:S(2)}, u32[]{:S(2)}) collective-permute-start(f32[128,128]{1,0:T(8,128)S(1)} %add_add_fusion.2), channel_id=1, source_target_pairs={{0,16},{1,17},{2,18},{3,19},{4,20},{5,21},{6,22},{7,23},{8,24},{9,... | collective-permute-start | bytes 196616 | tf_op jit(solution)/shard_map/ppermute | solution.py:58
  178.2 5.5 %collective-permute-start.24 = (f32[128,128]{1,0:T(8,128)S(1)}, f32[128,128]{1,0:T(8,128)S(1)}, u32[]{:S(2)}, u32[]{:S(2)}) collective-permute-start(f32[128,128]{1,0:T(8,128)S(1)} %add_add_fusion.2), channel_id=1, source_target_pairs={{0,24},{1,25},{2,26},{3,27},{4,28},{5,29},{6,30},{7,31},{8,16},{9,... | collective-permute-start | bytes 196616 | tf_op jit(solution)/shard_map/ppermute | solution.py:58
  178.2 5.5 %collective-permute-start.22 = (f32[128,128]{1,0:T(8,128)S(1)}, f32[128,128]{1,0:T(8,128)S(1)}, u32[]{:S(2)}, u32[]{:S(2)}) collective-permute-start(f32[128,128]{1,0:T(8,128)S(1)} %add_add_fusion.2), channel_id=1, source_target_pairs={{0,8},{1,9},{2,10},{3,11},{4,12},{5,13},{6,14},{7,15},{8,0},{9,1},... | collective-permute-start | bytes 196616 | tf_op jit(solution)/shard_map/ppermute | solution.py:58
  183.7 6.1 %collective-permute-start.26 = (f32[128,128]{1,0:T(8,128)S(1)}, f32[128,128]{1,0:T(8,128)S(1)}, u32[]{:S(2)}, u32[]{:S(2)}) collective-permute-start(f32[128,128]{1,0:T(8,128)S(1)} %add_add_fusion.1), channel_id=1, source_target_pairs={{0,64},{1,65},{2,66},{3,67},{4,68},{5,69},{6,70},{7,71},{8,72},{9,... | collective-permute-start | bytes 196616 | tf_op jit(solution)/shard_map/ppermute | solution.py:58
  185.4 5.5 %collective-permute-start.27 = (f32[128,128]{1,0:T(8,128)S(1)}, f32[128,128]{1,0:T(8,128)S(1)}, u32[]{:S(2)}, u32[]{:S(2)}) collective-permute-start(f32[128,128]{1,0:T(8,128)S(1)} %add_add_fusion.1), channel_id=1, source_target_pairs={{0,96},{1,97},{2,98},{3,99},{4,100},{5,101},{6,102},{7,103},{8,104... | collective-permute-start | bytes 196616 | tf_op jit(solution)/shard_map/ppermute | solution.py:58
  187.1 4.3 %collective-permute-start.25 = (f32[128,128]{1,0:T(8,128)S(1)}, f32[128,128]{1,0:T(8,128)S(1)}, u32[]{:S(2)}, u32[]{:S(2)}) collective-permute-start(f32[128,128]{1,0:T(8,128)S(1)} %add_add_fusion.1), channel_id=1, source_target_pairs={{0,32},{1,33},{2,34},{3,35},{4,36},{5,37},{6,38},{7,39},{8,40},{9,... | collective-permute-start | bytes 196616 | tf_op jit(solution)/shard_map/ppermute | solution.py:58

commit v7 on v5

--- a/solution.py
+++ b/solution.py
@@ -146,6 +146,17 @@
             work_ref[stop:, :] = work_ref[stop:, :] - update[stop:, :]
 
 
+def repeat_kernel(source_ref, out_ref, sems):
+    copies = [
+        pltpu.make_async_copy(source_ref, out_ref.at[i], sems.at[i])
+        for i in range(out_ref.shape[0])
+    ]
+    for copy in copies:
+        copy.start()
+    for copy in copies:
+        copy.wait()
+
+
 def contract_three(left, right, left_dim, right_dim):
     left_high, left_low = two_parts(left)
     right_high, right_low = two_parts(right)
@@ -324,15 +335,13 @@
     pieces_ref,
     transport_ref,
     basis_ref,
-    back_ref,
     advanced_ref,
     speeds_ref,
     basis_x_ref,
     velocity_ref,
-    gram_ref,
+    inverse_ref,
     work_ref,
     upper_ref,
-    inverse_ref,
     *,
     lengths,
     time_step,
@@ -378,12 +387,16 @@
         plus = contract_three(now, turned[i], 1, 0)
         drift_sum = drift_sum + jnp.maximum(speed, 0.0) * (now - minus)
         drift_sum = drift_sum + jnp.minimum(speed, 0.0) * (plus - now)
+    velocity_ref[...] = now - time_step * drift_sum - COLLIDE * now
+
+
+def update_kernel(back_ref, velocity_ref, inverse_ref, updated_ref, gram_ref, *, weight_x):
     back = back_ref[0]
     for i in range(1, back_ref.shape[0]):
         back = back + back_ref[i]
-    back_proj = contract(back * weight_x, inverse, 1, 1)
-    updated = now - time_step * drift_sum + COLLIDE * (back_proj - now)
-    velocity_ref[...] = updated
+    back_proj = contract(back * weight_x, inverse_ref[...], 1, 1)
+    updated = velocity_ref[...] + COLLIDE * back_proj
+    updated_ref[...] = updated
     gram_ref[...] = contract(updated, updated, 0, 0) * WEIGHT_V
 
 
@@ -430,7 +443,17 @@
         + [jnp.zeros_like(slab_velocity[0])] * 3,
         axis=1,
     )
-    nodes = to_all(v_basis, "slab")
+    nodes = exchange(
+        pl.pallas_call(
+            repeat_kernel,
+            out_shape=f32(slabs, rows, rank),
+            out_specs=pl.BlockSpec(memory_space=pl.ANY),
+            scratch_shapes=[pltpu.SemaphoreType.DMA((slabs,))],
+            name="repeat",
+            compiler_params=pltpu.CompilerParams(vmem_limit_bytes=VMEM_BYTES),
+        )(v_basis),
+        "slab",
+    )
     k_slab = gather_relative(own_cells, "brick", BRICK_GROUPS)
     k_edges, k_slab = lax.optimization_barrier((k_coeffs, k_slab))
     k_below = lax.ppermute(k_edges[-1:], "slab", up)
@@ -516,15 +539,22 @@
     reduced = gather_more(reduced, both, ((1,), (2, 4, 6)))
 
     speeds = jnp.stack(list(own_velocity) + [jnp.zeros_like(ones)] * 5, axis=1)
-    basis_new, velocity_new, gram_part = pl.pallas_call(
+    basis_new, velocity_part, inverse = pl.pallas_call(
         functools.partial(
             middle_kernel, lengths=lengths, time_step=time_step, weight_x=weight_x
         ),
         out_shape=(f32(cells, rank), f32(rows, rank), f32(rank, rank)),
-        in_specs=vector_specs + [whole] * 6,
-        scratch_shapes=factor_scratch(rank),
-        name="middle", compiler_params=pltpu.CompilerParams(vmem_limit_bytes=VMEM_BYTES),
-    )(brick_id, reduced, second, v_basis, fourth, advanced, speeds)
+        in_specs=vector_specs + [whole] * 5,
+        scratch_shapes=factor_scratch(rank)[:2],
+        name="middle",
+        compiler_params=pltpu.CompilerParams(vmem_limit_bytes=VMEM_BYTES),
+    )(brick_id, reduced, second, v_basis, advanced, speeds)
+    velocity_new, gram_part = pl.pallas_call(
+        functools.partial(update_kernel, weight_x=weight_x),
+        out_shape=(f32(rows, rank), f32(rank, rank)),
+        name="update",
+        compiler_params=pltpu.CompilerParams(vmem_limit_bytes=VMEM_BYTES),
+    )(fourth, velocity_part, inverse)
     gram_v = sum_over(gram_part, ("slab", "brick"), ALL_GROUPS)
     coupling, vbasis_new = pl.pallas_call(
         last_kernel,

time: 160 us -> 158 us (0.988)
  waiting for transfers between devices: 69.8 us -> 65.8 us
  starting transfers between devices: 59.5 us -> 61.3 us
    all_to_all x5, waiting for transfers between devices: 42.5 us -> 38 us  [exchange(): return lax.all_to_all(array, axis, 0, 0, tiled=True)]
    broadcast_in_dim x1 -> x0, local copies, waits for them, and re-layouts: 1.96 us -> none  [to_all(): jnp.broadcast_to(array[None], (copies,) + array.shape)]
    ppermute x25, starting transfers between devices: 29.9 us -> 31.8 us  [from_peer(): return lax.ppermute(values, axis, [(i, i ^ mask) for i in range(peers)])]
    pallas_call x0 -> x2, Pallas kernels: none -> 1.81 us  [the longest x1 1.07 us: local(): pl.pallas_call(repeat_kernel, out_shape=f32(slabs, rows, rank), out_specs...]
  transfers between devices with their start and end apart: 33 -> 33, of which waited for: 23 -> 21; matrix products, arithmetic and copies ran while one was open for 3% -> 1% of each run, Pallas kernels for 7% -> 11%
where the time goes in v7:
time: 158 us
  waiting for transfers between devices  65.8 us (42%)
  starting transfers between devices  61.3 us (39%)
  Pallas kernels  25.9 us (16%)
  local copies, waits for them, and re-layouts  2.34 us (1%)
    all_to_all x5, waiting for transfers between devices, exchange(): return lax.all_to_all(array, axis, 0, 0, tiled=True)  38 us
    ppermute x25, starting transfers between devices, from_peer(): return lax.ppermute(values, axis, [(i, i ^ mask) for i in range(peers)])  31.8 us
    all_to_all x5, starting transfers between devices, exchange(): return lax.all_to_all(array, axis, 0, 0, tiled=True)  25 us
    ppermute x25, waiting for transfers between devices, from_peer(): return lax.ppermute(values, axis, [(i, i ^ mask) for i in range(peers)])  24.9 us
    pallas_call x1, Pallas kernels, local(): pl.pallas_call(functools.partial(middle_kernel, lengths=lengths, time_ste...  6.2 us
    pallas_call x1, Pallas kernels, local(): pl.pallas_call(last_kernel, out_shape=(f32(rank, rank), f32(rows, rank)),...  4.49 us
    pallas_call x1, Pallas kernels, local(): pl.pallas_call(maxwell_kernel, out_shape=(f32(bricks, cells + 6 * height,...  3.73 us
    pallas_call x1, Pallas kernels, local(): pl.pallas_call(back_kernel, out_shape=f32(slabs, rows, rank), name='back'...  3.69 us
  transfers between devices with their start and end apart: 33, of which 21 were waited for; matrix products, arithmetic and copies ran while one was open for 1% of the time, Pallas kernels for 11%

profile of v7, /device:TPU:0, one launch (start us, length us, event | category | flops | bytes accessed | tf_op | source)
XLA Modules:
  0.0 157.7 jit_solution(9839307378822403662)
XLA Ops:
  0.7 0.9 copy-done.1
  1.6 1.1 repeat.1
  2.7 7.0 %all-to-all-start = ((f32[8,256,128]{2,1,0:T(8,128)}), f32[8,256,128]{2,1,0:T(8,128)S(1)}, u32[]{:S(2)}, u32[]{:S(2)}) async-start(f32[8,256,128]{2,1,0:T(8,128)} %repeat.1), calls=%async_computation | async-start | bytes 2097152 | tf_op jit(solution)/shard_map/all_to_all | solution.py:34
  9.9 0.1 copy.24
  10.1 0.2 and_select_fusion.3
  10.5 2.0 %collective-permute-start.1 = (f32[2,64,128]{2,1,0:T(8,128)S(1)}, f32[2,64,128]{2,1,0:T(8,128)S(1)}, u32[]{:S(2)}, u32[]{:S(2)}) collective-permute-start(f32[2,64,128]{2,1,0:T(8,128)S(1)} %pad_maximum_fusion.1), channel_id=1, source_target_pairs={{0,2},{1,3},{2,0},{3,1},{4,6},{5,7},{6,4},{7,5},{8,10},{9,11},{10,... | collective-permute-start | bytes 196616 | tf_op jit(solution)/shard_map/ppermute | solution.py:58
  12.5 3.6 %collective-permute-start.2 = (f32[2,64,128]{2,1,0:T(8,128)S(1)}, f32[2,64,128]{2,1,0:T(8,128)S(1)}, u32[]{:S(2)}, u32[]{:S(2)}) collective-permute-start(f32[2,64,128]{2,1,0:T(8,128)S(1)} %pad_maximum_fusion.1), channel_id=1, source_target_pairs={{0,4},{1,5},{2,6},{3,7},{4,0},{5,1},{6,2},{7,3},{8,12},{9,13},{10,... | collective-permute-start | bytes 196616 | tf_op jit(solution)/shard_map/ppermute | solution.py:58
  16.1 3.6 %collective-permute-done.2 = f32[2,64,128]{2,1,0:T(8,128)S(1)} collective-permute-done((f32[2,64,128]{2,1,0:T(8,128)S(1)}, f32[2,64,128]{2,1,0:T(8,128)S(1)}, u32[]{:S(2)}, u32[]{:S(2)}) %collective-permute-start.2) | collective-permute-done | bytes 65568 | tf_op jit(solution)/shard_map/ppermute | solution.py:58
  19.7 1.9 %collective-permute-done.3 = f32[2,64,128]{2,1,0:T(8,128)S(1)} collective-permute-done((f32[2,64,128]{2,1,0:T(8,128)S(1)}, f32[2,64,128]{2,1,0:T(8,128)S(1)}, u32[]{:S(2)}, u32[]{:S(2)}) %collective-permute-start.3) | collective-permute-done | bytes 65568 | tf_op jit(solution)/shard_map/ppermute | solution.py:58
  21.6 0.7 collective-permute-start.4
  22.3 0.3 minimum_reduce_fusion
  23.0 4.6 %all-to-all-done.nodes_ref = f32[8,256,128]{2,1,0:T(8,128)S(1)} async-done(((f32[8,256,128]{2,1,0:T(8,128)}), f32[8,256,128]{2,1,0:T(8,128)S(1)}, u32[]{:S(2)}, u32[]{:S(2)}) %all-to-all-start) | async-done | bytes 1048608 | tf_op jit(solution)/shard_map/all_to_all | solution.py:34
  27.7 3.1 %transport.1 = f32[16,56,128]{2,1,0:T(8,128)} custom-call(f32[8,256,128]{2,1,0:T(8,128)S(1)} %all-to-all-done.nodes_ref, f32[256,8]{1,0:T(8,128)S(1)} %copy.25.columns_ref, f32[8,128]{1,0:T(8,128)S(1)} %broadcast_in_dim.14.speeds_ref.first_ref, f32[8,8,256]{2,1,0:T(8,128)S(1)} %stack.61.weights_ref), custom_call_target="tpu_custom_call" | custom-call | tf_op jit(solution)/shard_map/transport/pallas_call | solution.py:468
  30.9 6.1 %all-to-all-start.1 = ((f32[16,56,128]{2,1,0:T(8,128)}), f32[16,56,128]{2,1,0:T(8,128)S(1)}, u32[]{:S(2)}, u32[]{:S(2)}) async-start(f32[16,56,128]{2,1,0:T(8,128)} %transport.1), calls=%async_computation.1 | async-start | bytes 917504 | tf_op jit(solution)/shard_map/all_to_all | solution.py:34
  37.0 1.4 collective-permute-start.6
  38.5 2.2 %collective-permute-start.5 = (f32[1,2,16,128]{3,2,1,0:T(8,128)S(1)}, f32[1,2,16,128]{3,2,1,0:T(8,128)S(1)}, u32[]{:S(2)}, u32[]{:S(2)}) collective-permute-start(f32[1,2,16,128]{3,2,1,0:T(8,128)S(1)} %get-tuple-element.79), channel_id=1, source_target_pairs={{0,16},{16,32},{32,48},{48,64},{64,80},{80,96},{96,112},{112,0},{1... | collective-permute-start | bytes 49160 | tf_op jit(solution)/shard_map/ppermute | solution.py:459
  40.7 6.8 %all-to-all-done.1.integrals_ref = f32[16,56,128]{2,1,0:T(8,128)S(1)} async-done(((f32[16,56,128]{2,1,0:T(8,128)}), f32[16,56,128]{2,1,0:T(8,128)S(1)}, u32[]{:S(2)}, u32[]{:S(2)}) %all-to-all-start.1) | async-done | bytes 458784 | tf_op jit(solution)/shard_map/all_to_all | solution.py:34
  47.5 3.7 %maxwell.1 = (f32[16,112,128]{2,1,0:T(8,128)}, f32[1024,8]{1,0:T(8,128)S(1)}, f32[8,1024]{1,0:T(8,128)S(1)}) custom-call(s32[1]{0:T(128)} %bitcast.brick_ref, f32[16,64,128]{2,1,0:T(8,128)S(1)} %constant_dynamic-update-slice_fusion.5.cells_ref, f32[16,56,128]{2,1,0:T(8,128)S(1)} %all-to-all-done.1.integrals_ref, f32[8,256,128]{2,1,0:T(8,128)S(1)} %all-to-all-done.nodes_ref, ...), custom_call_target="tpu_custom_call" | custom-call | tf_op jit(solution)/shard_map/maxwell/pallas_call | solution.py:476
  51.2 3.6 %all-to-all-start.2 = ((f32[16,112,128]{2,1,0:T(8,128)}), f32[16,112,128]{2,1,0:T(8,128)S(1)}, u32[]{:S(2)}, u32[]{:S(2)}) async-start(f32[16,112,128]{2,1,0:T(8,128)} %get-tuple-element.24), calls=%async_computation.2 | async-start | bytes 1835008 | tf_op jit(solution)/shard_map/all_to_all | solution.py:34
  55.0 15.0 %all-to-all-done.2.parts_ref.transport_ref = f32[16,112,128]{2,1,0:T(8,128)S(1)} async-done(((f32[16,112,128]{2,1,0:T(8,128)}), f32[16,112,128]{2,1,0:T(8,128)S(1)}, u32[]{:S(2)}, u32[]{:S(2)}) %all-to-all-start.2) | async-done | bytes 917536 | tf_op jit(solution)/shard_map/all_to_all | solution.py:34
  70.0 1.6 %advance.1 = (f32[16,72,128]{2,1,0:T(8,128)}, f32[64,128]{1,0:T(8,128)S(1)}) custom-call(f32[16,112,128]{2,1,0:T(8,128)S(1)} %all-to-all-done.2.parts_ref.transport_ref, f32[6,64,128]{2,1,0:T(8,128)S(1)} %constant_dynamic-update-slice_fusion.11.steps_ref, f32[64,128]{1,0:T(8,128)S(1)} %bitcast.42), custom_call_target="tpu_custom_call" | custom-call | tf_op jit(solution)/shard_map/advance/pallas_call | solution.py:507
  71.6 3.6 %all-to-all-start.3 = ((f32[16,72,128]{2,1,0:T(8,128)}), f32[16,72,128]{2,1,0:T(8,128)S(1)}, u32[]{:S(2)}, u32[]{:S(2)}) async-start(f32[16,72,128]{2,1,0:T(8,128)} %get-tuple-element.26), calls=%async_computation.3 | async-start | bytes 1179648 | tf_op jit(solution)/shard_map/all_to_all | solution.py:34
  75.2 11.5 %all-to-all-done.3.parts_ref = f32[16,72,128]{2,1,0:T(8,128)S(1)} async-done(((f32[16,72,128]{2,1,0:T(8,128)}), f32[16,72,128]{2,1,0:T(8,128)S(1)}, u32[]{:S(2)}, u32[]{:S(2)}) %all-to-all-start.3) | async-done | bytes 589856 | tf_op jit(solution)/shard_map/all_to_all | solution.py:34
  86.8 1.2 products.1
  88.0 1.0 collective-permute-start.7
  89.0 3.7 %back.1 = f32[8,256,128]{2,1,0:T(8,128)} custom-call(f32[16,72,128]{2,1,0:T(8,128)S(1)} %all-to-all-done.3.parts_ref, f32[1024,8]{1,0:T(8,128)S(1)} %get-tuple-element.31.line_ref, f32[8,1024]{1,0:T(8,128)S(1)} %get-tuple-element.32.state_ref, f32[256,2]{1,0:T(8,128)S(1)} %get-tuple-element.56.across_ref), custom_call_target="tpu_custom_call" | custom-call | tf_op jit(solution)/shard_map/back/pallas_call | solution.py:526
  92.7 2.9 %collective-permute-done.7 = f32[8,512]{1,0:T(8,128)S(1)} collective-permute-done((f32[8,512]{1,0:T(8,128)S(1)}, f32[8,512]{1,0:T(8,128)S(1)}, u32[]{:S(2)}, u32[]{:S(2)}) %collective-permute-start.7) | collective-permute-done | bytes 16416 | tf_op jit(solution)/shard_map/ppermute | solution.py:523
  95.6 0.2 fusion.32
  95.9 0.1 copy.27
  96.1 0.6 collective-permute-start.9
  96.7 3.6 %collective-permute-start.10 = (f32[40,128]{1,0:T(8,128)S(1)}, f32[40,128]{1,0:T(8,128)S(1)}, u32[]{:S(2)}, u32[]{:S(2)}) collective-permute-start(f32[40,128]{1,0:T(8,128)S(1)} %pad_add_fusion), channel_id=1, source_target_pairs={{0,24},{1,25},{2,26},{3,27},{4,28},{5,29},{6,30},{7,31},{8,16},{9,... | collective-permute-start | bytes 61448 | tf_op jit(solution)/shard_map/ppermute | solution.py:58
  100.2 1.0 collective-permute-done.8
  101.2 0.8 collective-permute-done.10
  102.0 1.9 %collective-permute-start.12 = (f32[2,40,128]{2,1,0:T(8,128)S(1)}, f32[2,40,128]{2,1,0:T(8,128)S(1)}, u32[]{:S(2)}, u32[]{:S(2)}) collective-permute-start(f32[2,40,128]{2,1,0:T(8,128)S(1)} %pad_maximum_fusion.2), channel_id=1, source_target_pairs={{0,64},{1,65},{2,66},{3,67},{4,68},{5,69},{6,70},{7,71},{8,72},{9,... | collective-permute-start | bytes 122888 | tf_op jit(solution)/shard_map/ppermute | solution.py:58
  103.9 0.7 collective-permute-start.13
  104.6 1.0 collective-permute-start.11
  105.6 4.6 %all-to-all-start.4 = ((f32[8,256,128]{2,1,0:T(8,128)}), f32[8,256,128]{2,1,0:T(8,128)S(1)}, u32[]{:S(2)}, u32[]{:S(2)}) async-start(f32[8,256,128]{2,1,0:T(8,128)} %back.1), calls=%async_computation.4 | async-start | bytes 2097152 | tf_op jit(solution)/shard_map/all_to_all | solution.py:34
  110.3 0.3 slice_reduce_fusion
  110.6 0.1 copy.28.speeds_ref
  110.8 0.8 collective-permute-done.14
  111.5 2.4 %collective-permute-start.16 = (f32[4,40,128]{2,1,0:T(8,128)S(1)}, f32[4,40,128]{2,1,0:T(8,128)S(1)}, u32[]{:S(2)}, u32[]{:S(2)}) collective-permute-start(f32[4,40,128]{2,1,0:T(8,128)S(1)} %pad_maximum_fusion), channel_id=1, source_target_pairs={{0,4},{1,5},{2,6},{3,7},{4,0},{5,1},{6,2},{7,3},{8,12},{9,13},{10,... | collective-permute-start | bytes 245768 | tf_op jit(solution)/shard_map/ppermute | solution.py:58
  113.9 2.3 %collective-permute-start.17 = (f32[4,40,128]{2,1,0:T(8,128)S(1)}, f32[4,40,128]{2,1,0:T(8,128)S(1)}, u32[]{:S(2)}, u32[]{:S(2)}) collective-permute-start(f32[4,40,128]{2,1,0:T(8,128)S(1)} %pad_maximum_fusion), channel_id=1, source_target_pairs={{0,6},{1,7},{2,4},{3,5},{4,2},{5,3},{6,0},{7,1},{8,14},{9,15},{10,... | collective-permute-start | bytes 245768 | tf_op jit(solution)/shard_map/ppermute | solution.py:58
  116.2 0.6 collective-permute-done.15
  116.8 1.4 collective-permute-done.16
  118.3 1.7 %collective-permute-done.17 = f32[4,40,128]{2,1,0:T(8,128)S(1)} collective-permute-done((f32[4,40,128]{2,1,0:T(8,128)S(1)}, f32[4,40,128]{2,1,0:T(8,128)S(1)}, u32[]{:S(2)}, u32[]{:S(2)}) %collective-permute-start.17) | collective-permute-done | bytes 81952 | tf_op jit(solution)/shard_map/ppermute | solution.py:58
  119.9 6.2 %middle.1 = (f32[64,128]{1,0:T(8,128)}, f32[256,128]{1,0:T(8,128)S(1)}, f32[128,128]{1,0:T(8,128)S(1)}) custom-call(s32[1]{0:T(128)} %bitcast.brick_ref, f32[16,40,128]{2,1,0:T(8,128)S(1)} %constant_dynamic-update-slice_fusion.17.pieces_ref, f32[16,112,128]{2,1,0:T(8,128)S(1)} %all-to-all-done.2.parts_ref.transport_ref, f32[256,128]{1,0:T(8,128)S(1)} %copy-done.2, ...), custom_call_target="tpu_custom_call" | custom-call | tf_op jit(solution)/shard_map/middle/pallas_call | solution.py:542
  126.1 0.7 update.1
  127.0 1.2 collective-permute-done.18
  128.2 1.3 collective-permute-start.20
  129.5 1.7 %collective-permute-start.21 = (f32[128,128]{1,0:T(8,128)S(1)}, f32[128,128]{1,0:T(8,128)S(1)}, u32[]{:S(2)}, u32[]{:S(2)}) collective-permute-start(f32[128,128]{1,0:T(8,128)S(1)} %add.402), channel_id=1, source_target_pairs={{0,6},{1,7},{2,4},{3,5},{4,2},{5,3},{6,0},{7,1},{8,14},{9,15},{10,... | collective-permute-start | bytes 196616 | tf_op jit(solution)/shard_map/ppermute | solution.py:58
  131.2 0.6 collective-permute-start.19
  131.8 2.3 %collective-permute-done.20 = f32[128,128]{1,0:T(8,128)S(1)} collective-permute-done((f32[128,128]{1,0:T(8,128)S(1)}, f32[128,128]{1,0:T(8,128)S(1)}, u32[]{:S(2)}, u32[]{:S(2)}) %collective-permute-start.20) | collective-permute-done | bytes 65568 | tf_op jit(solution)/shard_map/ppermute | solution.py:58
  134.1 1.2 collective-permute-done.21
  135.4 0.1 collective-permute-done.19
  135.5 3.6 %collective-permute-start.23 = (f32[128,128]{1,0:T(8,128)S(1)}, f32[128,128]{1,0:T(8,128)S(1)}, u32[]{:S(2)}, u32[]{:S(2)}) collective-permute-start(f32[128,128]{1,0:T(8,128)S(1)} %add_add_fusion.2), channel_id=1, source_target_pairs={{0,16},{1,17},{2,18},{3,19},{4,20},{5,21},{6,22},{7,23},{8,24},{9,... | collective-permute-start | bytes 196616 | tf_op jit(solution)/shard_map/ppermute | solution.py:58
  139.1 0.6 collective-permute-start.24
  139.7 0.8 collective-permute-start.22
  140.5 1.0 collective-permute-done.23
  141.5 3.1 %collective-permute-done.24 = f32[128,128]{1,0:T(8,128)S(1)} collective-permute-done((f32[128,128]{1,0:T(8,128)S(1)}, f32[128,128]{1,0:T(8,128)S(1)}, u32[]{:S(2)}, u32[]{:S(2)}) %collective-permute-start.24) | collective-permute-done | bytes 65568 | tf_op jit(solution)/shard_map/ppermute | solution.py:58
  144.6 3.0 %collective-permute-start.26 = (f32[128,128]{1,0:T(8,128)S(1)}, f32[128,128]{1,0:T(8,128)S(1)}, u32[]{:S(2)}, u32[]{:S(2)}) collective-permute-start(f32[128,128]{1,0:T(8,128)S(1)} %add_add_fusion.1), channel_id=1, source_target_pairs={{0,64},{1,65},{2,66},{3,67},{4,68},{5,69},{6,70},{7,71},{8,72},{9,... | collective-permute-start | bytes 196616 | tf_op jit(solution)/shard_map/ppermute | solution.py:58
  147.7 1.2 collective-permute-start.27
  148.8 1.7 %collective-permute-done.26 = f32[128,128]{1,0:T(8,128)S(1)} collective-permute-done((f32[128,128]{1,0:T(8,128)S(1)}, f32[128,128]{1,0:T(8,128)S(1)}, u32[]{:S(2)}, u32[]{:S(2)}) %collective-permute-start.26) | collective-permute-done | bytes 65568 | tf_op jit(solution)/shard_map/ppermute | solution.py:58
  150.6 2.6 %collective-permute-done.27 = f32[128,128]{1,0:T(8,128)S(1)} collective-permute-done((f32[128,128]{1,0:T(8,128)S(1)}, f32[128,128]{1,0:T(8,128)S(1)}, u32[]{:S(2)}, u32[]{:S(2)}) %collective-permute-start.27) | collective-permute-done | bytes 65568 | tf_op jit(solution)/shard_map/ppermute | solution.py:58
  153.2 4.5 %last.1 = (f32[128,128]{1,0:T(8,128)}, f32[256,128]{1,0:T(8,128)}) custom-call(f32[128,128]{1,0:T(8,128)S(1)} %add_add_fusion.gram_ref, f32[256,128]{1,0:T(8,128)S(1)} %get-tuple-element.40.velocity_ref), custom_call_target="tpu_custom_call" | custom-call | tf_op jit(solution)/shard_map/last/pallas_call | solution.py:559
  (89 shorter events, 1.5 us)
Async XLA Ops:
  0.6 9.9 %collective-permute-start = (f32[1,64,128]{2,1,0:T(8,128)}, f32[1,64,128]{2,1,0:T(8,128)S(1)}, u32[]{:S(2)}, u32[]{:S(2)}) collective-permute-start(f32[1,64,128]{2,1,0:T(8,128)} %bitcast.39), channel_id=1, source_target_pairs={{0,1},{1,0},{2,3},{3,2},{4,5},{5,4},{6,7},{7,6},{8,9},{9,8},{10,11... | collective-permute-start | bytes 98312 | tf_op jit(solution)/shard_map/ppermute | solution.py:58
  0.7 0.9 copy-start.1
  2.7 7.1 %copy-start = (f32[2,2,16,128]{3,2,1,0:T(8,128)S(1)}, f32[2,2,16,128]{3,2,1,0:T(8,128)}, u32[]{:S(2)}) copy-start(f32[2,2,16,128]{3,2,1,0:T(8,128)} %param.2) | copy-start | bytes 98308
  2.7 24.9 %all-to-all-start = ((f32[8,256,128]{2,1,0:T(8,128)}), f32[8,256,128]{2,1,0:T(8,128)S(1)}, u32[]{:S(2)}, u32[]{:S(2)}) async-start(f32[8,256,128]{2,1,0:T(8,128)} %repeat.1), calls=%async_computation | async-start | bytes 2097152 | tf_op jit(solution)/shard_map/all_to_all | solution.py:34
  10.5 5.6 %collective-permute-start.1 = (f32[2,64,128]{2,1,0:T(8,128)S(1)}, f32[2,64,128]{2,1,0:T(8,128)S(1)}, u32[]{:S(2)}, u32[]{:S(2)}) collective-permute-start(f32[2,64,128]{2,1,0:T(8,128)S(1)} %pad_maximum_fusion.1), channel_id=1, source_target_pairs={{0,2},{1,3},{2,0},{3,1},{4,6},{5,7},{6,4},{7,5},{8,10},{9,11},{10,... | collective-permute-start | bytes 196616 | tf_op jit(solution)/shard_map/ppermute | solution.py:58
  12.5 7.2 %collective-permute-start.2 = (f32[2,64,128]{2,1,0:T(8,128)S(1)}, f32[2,64,128]{2,1,0:T(8,128)S(1)}, u32[]{:S(2)}, u32[]{:S(2)}) collective-permute-start(f32[2,64,128]{2,1,0:T(8,128)S(1)} %pad_maximum_fusion.1), channel_id=1, source_target_pairs={{0,4},{1,5},{2,6},{3,7},{4,0},{5,1},{6,2},{7,3},{8,12},{9,13},{10,... | collective-permute-start | bytes 196616 | tf_op jit(solution)/shard_map/ppermute | solution.py:58
  16.1 5.5 %collective-permute-start.3 = (f32[2,64,128]{2,1,0:T(8,128)S(1)}, f32[2,64,128]{2,1,0:T(8,128)S(1)}, u32[]{:S(2)}, u32[]{:S(2)}) collective-permute-start(f32[2,64,128]{2,1,0:T(8,128)S(1)} %pad_maximum_fusion.1), channel_id=1, source_target_pairs={{0,6},{1,7},{2,4},{3,5},{4,2},{5,3},{6,0},{7,1},{8,14},{9,15},{10,... | collective-permute-start | bytes 196616 | tf_op jit(solution)/shard_map/ppermute | solution.py:58
  21.6 15.4 %collective-permute-start.4 = (f32[8,64,128]{2,1,0:T(8,128)S(1)}, f32[8,64,128]{2,1,0:T(8,128)S(1)}, u32[]{:S(2)}, u32[]{:S(2)}) collective-permute-start(f32[8,64,128]{2,1,0:T(8,128)S(1)} %get-tuple-element.58), channel_id=1, source_target_pairs={{0,8},{1,9},{2,10},{3,11},{4,12},{5,13},{6,14},{7,15},{8,0},{9,1},... | collective-permute-start | bytes 786440 | tf_op jit(solution)/shard_map/ppermute | solution.py:58
  30.9 16.6 %all-to-all-start.1 = ((f32[16,56,128]{2,1,0:T(8,128)}), f32[16,56,128]{2,1,0:T(8,128)S(1)}, u32[]{:S(2)}, u32[]{:S(2)}) async-start(f32[16,56,128]{2,1,0:T(8,128)} %transport.1), calls=%async_computation.1 | async-start | bytes 917504 | tf_op jit(solution)/shard_map/all_to_all | solution.py:34
  37.0 17.8 %collective-permute-start.6 = (f32[1,2,16,128]{3,2,1,0:T(8,128)S(1)}, f32[1,2,16,128]{3,2,1,0:T(8,128)S(1)}, u32[]{:S(2)}, u32[]{:S(2)}) collective-permute-start(f32[1,2,16,128]{3,2,1,0:T(8,128)S(1)} %get-tuple-element.78), channel_id=1, source_target_pairs={{0,112},{16,0},{32,16},{48,32},{64,48},{80,64},{96,80},{112,96},{1... | collective-permute-start | bytes 49160 | tf_op jit(solution)/shard_map/ppermute | solution.py:460
  38.5 16.4 %collective-permute-start.5 = (f32[1,2,16,128]{3,2,1,0:T(8,128)S(1)}, f32[1,2,16,128]{3,2,1,0:T(8,128)S(1)}, u32[]{:S(2)}, u32[]{:S(2)}) collective-permute-start(f32[1,2,16,128]{3,2,1,0:T(8,128)S(1)} %get-tuple-element.79), channel_id=1, source_target_pairs={{0,16},{16,32},{32,48},{48,64},{64,80},{80,96},{96,112},{112,0},{1... | collective-permute-start | bytes 49160 | tf_op jit(solution)/shard_map/ppermute | solution.py:459
  51.2 18.8 %all-to-all-start.2 = ((f32[16,112,128]{2,1,0:T(8,128)}), f32[16,112,128]{2,1,0:T(8,128)S(1)}, u32[]{:S(2)}, u32[]{:S(2)}) async-start(f32[16,112,128]{2,1,0:T(8,128)} %get-tuple-element.24), calls=%async_computation.2 | async-start | bytes 1835008 | tf_op jit(solution)/shard_map/all_to_all | solution.py:34
  71.6 15.2 %all-to-all-start.3 = ((f32[16,72,128]{2,1,0:T(8,128)}), f32[16,72,128]{2,1,0:T(8,128)S(1)}, u32[]{:S(2)}, u32[]{:S(2)}) async-start(f32[16,72,128]{2,1,0:T(8,128)} %get-tuple-element.26), calls=%async_computation.3 | async-start | bytes 1179648 | tf_op jit(solution)/shard_map/all_to_all | solution.py:34
  88.0 7.6 %collective-permute-start.7 = (f32[8,512]{1,0:T(8,128)S(1)}, f32[8,512]{1,0:T(8,128)S(1)}, u32[]{:S(2)}, u32[]{:S(2)}) collective-permute-start(f32[8,512]{1,0:T(8,128)S(1)} %get-tuple-element.29), channel_id=1, source_target_pairs={{0,16},{16,32},{32,48},{48,64},{64,80},{80,96},{96,112},{112,0},{1... | collective-permute-start | bytes 49160 | tf_op jit(solution)/shard_map/ppermute | solution.py:523
  95.8 5.4 %collective-permute-start.8 = (f32[40,128]{1,0:T(8,128)S(1)}, f32[40,128]{1,0:T(8,128)S(1)}, u32[]{:S(2)}, u32[]{:S(2)}) collective-permute-start(f32[40,128]{1,0:T(8,128)S(1)} %pad_add_fusion), channel_id=1, source_target_pairs={{0,16},{1,17},{2,18},{3,19},{4,20},{5,21},{6,22},{7,23},{8,24},{9,... | collective-permute-start | bytes 61448 | tf_op jit(solution)/shard_map/ppermute | solution.py:58
  96.1 5.1 %collective-permute-start.9 = (f32[40,128]{1,0:T(8,128)S(1)}, f32[40,128]{1,0:T(8,128)S(1)}, u32[]{:S(2)}, u32[]{:S(2)}) collective-permute-start(f32[40,128]{1,0:T(8,128)S(1)} %pad_add_fusion), channel_id=1, source_target_pairs={{0,8},{1,9},{2,10},{3,11},{4,12},{5,13},{6,14},{7,15},{8,0},{9,1},... | collective-permute-start | bytes 61448 | tf_op jit(solution)/shard_map/ppermute | solution.py:58
  96.7 5.3 %collective-permute-start.10 = (f32[40,128]{1,0:T(8,128)S(1)}, f32[40,128]{1,0:T(8,128)S(1)}, u32[]{:S(2)}, u32[]{:S(2)}) collective-permute-start(f32[40,128]{1,0:T(8,128)S(1)} %pad_add_fusion), channel_id=1, source_target_pairs={{0,24},{1,25},{2,26},{3,27},{4,28},{5,29},{6,30},{7,31},{8,16},{9,... | collective-permute-start | bytes 61448 | tf_op jit(solution)/shard_map/ppermute | solution.py:58
  102.0 8.2 %collective-permute-start.12 = (f32[2,40,128]{2,1,0:T(8,128)S(1)}, f32[2,40,128]{2,1,0:T(8,128)S(1)}, u32[]{:S(2)}, u32[]{:S(2)}) collective-permute-start(f32[2,40,128]{2,1,0:T(8,128)S(1)} %pad_maximum_fusion.2), channel_id=1, source_target_pairs={{0,64},{1,65},{2,66},{3,67},{4,68},{5,69},{6,70},{7,71},{8,72},{9,... | collective-permute-start | bytes 122888 | tf_op jit(solution)/shard_map/ppermute | solution.py:58
  103.9 6.3 %collective-permute-start.13 = (f32[2,40,128]{2,1,0:T(8,128)S(1)}, f32[2,40,128]{2,1,0:T(8,128)S(1)}, u32[]{:S(2)}, u32[]{:S(2)}) collective-permute-start(f32[2,40,128]{2,1,0:T(8,128)S(1)} %pad_maximum_fusion.2), channel_id=1, source_target_pairs={{0,96},{1,97},{2,98},{3,99},{4,100},{5,101},{6,102},{7,103},{8,104... | collective-permute-start | bytes 122888 | tf_op jit(solution)/shard_map/ppermute | solution.py:58
  104.6 5.6 %collective-permute-start.11 = (f32[2,40,128]{2,1,0:T(8,128)S(1)}, f32[2,40,128]{2,1,0:T(8,128)S(1)}, u32[]{:S(2)}, u32[]{:S(2)}) collective-permute-start(f32[2,40,128]{2,1,0:T(8,128)S(1)} %pad_maximum_fusion.2), channel_id=1, source_target_pairs={{0,32},{1,33},{2,34},{3,35},{4,36},{5,37},{6,38},{7,39},{8,40},{9,... | collective-permute-start | bytes 122888 | tf_op jit(solution)/shard_map/ppermute | solution.py:58
  105.6 20.5 %all-to-all-start.4 = ((f32[8,256,128]{2,1,0:T(8,128)}), f32[8,256,128]{2,1,0:T(8,128)S(1)}, u32[]{:S(2)}, u32[]{:S(2)}) async-start(f32[8,256,128]{2,1,0:T(8,128)} %back.1), calls=%async_computation.4 | async-start | bytes 2097152 | tf_op jit(solution)/shard_map/all_to_all | solution.py:34
  110.2 1.3 collective-permute-start.14
  111.5 5.3 %collective-permute-start.15 = (f32[4,40,128]{2,1,0:T(8,128)S(1)}, f32[4,40,128]{2,1,0:T(8,128)S(1)}, u32[]{:S(2)}, u32[]{:S(2)}) collective-permute-start(f32[4,40,128]{2,1,0:T(8,128)S(1)} %pad_maximum_fusion), channel_id=1, source_target_pairs={{0,2},{1,3},{2,0},{3,1},{4,6},{5,7},{6,4},{7,5},{8,10},{9,11},{10,... | collective-permute-start | bytes 245768 | tf_op jit(solution)/shard_map/ppermute | solution.py:58
  111.5 6.7 %collective-permute-start.16 = (f32[4,40,128]{2,1,0:T(8,128)S(1)}, f32[4,40,128]{2,1,0:T(8,128)S(1)}, u32[]{:S(2)}, u32[]{:S(2)}) collective-permute-start(f32[4,40,128]{2,1,0:T(8,128)S(1)} %pad_maximum_fusion), channel_id=1, source_target_pairs={{0,4},{1,5},{2,6},{3,7},{4,0},{5,1},{6,2},{7,3},{8,12},{9,13},{10,... | collective-permute-start | bytes 245768 | tf_op jit(solution)/shard_map/ppermute | solution.py:58
  113.9 6.0 %collective-permute-start.17 = (f32[4,40,128]{2,1,0:T(8,128)S(1)}, f32[4,40,128]{2,1,0:T(8,128)S(1)}, u32[]{:S(2)}, u32[]{:S(2)}) collective-permute-start(f32[4,40,128]{2,1,0:T(8,128)S(1)} %pad_maximum_fusion), channel_id=1, source_target_pairs={{0,6},{1,7},{2,4},{3,5},{4,2},{5,3},{6,0},{7,1},{8,14},{9,15},{10,... | collective-permute-start | bytes 245768 | tf_op jit(solution)/shard_map/ppermute | solution.py:58
  116.8 3.1 %copy-start.2 = (f32[256,128]{1,0:T(8,128)S(1)}, f32[256,128]{1,0:T(8,128)}, u32[]{:S(2)}) copy-start(f32[256,128]{1,0:T(8,128)} %basis_ref.1) | copy-start | bytes 393220
  126.9 1.3 collective-permute-start.18
  128.2 5.9 %collective-permute-start.20 = (f32[128,128]{1,0:T(8,128)S(1)}, f32[128,128]{1,0:T(8,128)S(1)}, u32[]{:S(2)}, u32[]{:S(2)}) collective-permute-start(f32[128,128]{1,0:T(8,128)S(1)} %add.402), channel_id=1, source_target_pairs={{0,4},{1,5},{2,6},{3,7},{4,0},{5,1},{6,2},{7,3},{8,12},{9,13},{10,... | collective-permute-start | bytes 196616 | tf_op jit(solution)/shard_map/ppermute | solution.py:58
  129.5 5.8 %collective-permute-start.21 = (f32[128,128]{1,0:T(8,128)S(1)}, f32[128,128]{1,0:T(8,128)S(1)}, u32[]{:S(2)}, u32[]{:S(2)}) collective-permute-start(f32[128,128]{1,0:T(8,128)S(1)} %add.402), channel_id=1, source_target_pairs={{0,6},{1,7},{2,4},{3,5},{4,2},{5,3},{6,0},{7,1},{8,14},{9,15},{10,... | collective-permute-start | bytes 196616 | tf_op jit(solution)/shard_map/ppermute | solution.py:58
  131.2 4.3 %collective-permute-start.19 = (f32[128,128]{1,0:T(8,128)S(1)}, f32[128,128]{1,0:T(8,128)S(1)}, u32[]{:S(2)}, u32[]{:S(2)}) collective-permute-start(f32[128,128]{1,0:T(8,128)S(1)} %add.402), channel_id=1, source_target_pairs={{0,2},{1,3},{2,0},{3,1},{4,6},{5,7},{6,4},{7,5},{8,10},{9,11},{10,... | collective-permute-start | bytes 196616 | tf_op jit(solution)/shard_map/ppermute | solution.py:58
  135.5 6.0 %collective-permute-start.23 = (f32[128,128]{1,0:T(8,128)S(1)}, f32[128,128]{1,0:T(8,128)S(1)}, u32[]{:S(2)}, u32[]{:S(2)}) collective-permute-start(f32[128,128]{1,0:T(8,128)S(1)} %add_add_fusion.2), channel_id=1, source_target_pairs={{0,16},{1,17},{2,18},{3,19},{4,20},{5,21},{6,22},{7,23},{8,24},{9,... | collective-permute-start | bytes 196616 | tf_op jit(solution)/shard_map/ppermute | solution.py:58
  139.1 5.5 %collective-permute-start.24 = (f32[128,128]{1,0:T(8,128)S(1)}, f32[128,128]{1,0:T(8,128)S(1)}, u32[]{:S(2)}, u32[]{:S(2)}) collective-permute-start(f32[128,128]{1,0:T(8,128)S(1)} %add_add_fusion.2), channel_id=1, source_target_pairs={{0,24},{1,25},{2,26},{3,27},{4,28},{5,29},{6,30},{7,31},{8,16},{9,... | collective-permute-start | bytes 196616 | tf_op jit(solution)/shard_map/ppermute | solution.py:58
  139.7 4.9 %collective-permute-start.22 = (f32[128,128]{1,0:T(8,128)S(1)}, f32[128,128]{1,0:T(8,128)S(1)}, u32[]{:S(2)}, u32[]{:S(2)}) collective-permute-start(f32[128,128]{1,0:T(8,128)S(1)} %add_add_fusion.2), channel_id=1, source_target_pairs={{0,8},{1,9},{2,10},{3,11},{4,12},{5,13},{6,14},{7,15},{8,0},{9,1},... | collective-permute-start | bytes 196616 | tf_op jit(solution)/shard_map/ppermute | solution.py:58
  144.6 6.0 %collective-permute-start.26 = (f32[128,128]{1,0:T(8,128)S(1)}, f32[128,128]{1,0:T(8,128)S(1)}, u32[]{:S(2)}, u32[]{:S(2)}) collective-permute-start(f32[128,128]{1,0:T(8,128)S(1)} %add_add_fusion.1), channel_id=1, source_target_pairs={{0,64},{1,65},{2,66},{3,67},{4,68},{5,69},{6,70},{7,71},{8,72},{9,... | collective-permute-start | bytes 196616 | tf_op jit(solution)/shard_map/ppermute | solution.py:58
  147.7 5.5 %collective-permute-start.27 = (f32[128,128]{1,0:T(8,128)S(1)}, f32[128,128]{1,0:T(8,128)S(1)}, u32[]{:S(2)}, u32[]{:S(2)}) collective-permute-start(f32[128,128]{1,0:T(8,128)S(1)} %add_add_fusion.1), channel_id=1, source_target_pairs={{0,96},{1,97},{2,98},{3,99},{4,100},{5,101},{6,102},{7,103},{8,104... | collective-permute-start | bytes 196616 | tf_op jit(solution)/shard_map/ppermute | solution.py:58
  148.8 4.3 %collective-permute-start.25 = (f32[128,128]{1,0:T(8,128)S(1)}, f32[128,128]{1,0:T(8,128)S(1)}, u32[]{:S(2)}, u32[]{:S(2)}) collective-permute-start(f32[128,128]{1,0:T(8,128)S(1)} %add_add_fusion.1), channel_id=1, source_target_pairs={{0,32},{1,33},{2,34},{3,35},{4,36},{5,37},{6,38},{7,39},{8,40},{9,... | collective-permute-start | bytes 196616 | tf_op jit(solution)/shard_map/ppermute | solution.py:58

commit v8 on v7

--- a/solution.py
+++ b/solution.py
@@ -193,17 +193,31 @@
         sums[1] = sums[1] + jnp.minimum(speed, 0.0) * plain
         for i in range(4):
             sums[2 + i] = sums[2 + i] + product[:, (i + 1) * rank : (i + 2) * rank]
+    row = lax.broadcasted_iota(jnp.int32, (rank, rank), 0)
+    col = lax.broadcasted_iota(jnp.int32, (rank, rank), 1)
+    block_row = lax.broadcasted_iota(jnp.int32, (8, rank), 0)
+    height = rank // bricks
+    for i in range(3):
+        plus, minus = sums[2 * i], sums[2 * i + 1]
+        diagonal = jnp.sum(jnp.where(row == col, minus, 0.0), axis=0, keepdims=True)
+        vectors = vectors + jnp.where(block_row == 5 + i, diagonal, 0.0)
+        packed = jnp.where(col >= row, plus, minus) * WEIGHT_V
+        start = 8 + i * height
+        out_ref[:, start : start + height, :] = packed.reshape(bricks, height, rank)
     out_ref[:, :8, :] = jnp.broadcast_to((vectors * WEIGHT_V)[None], (bricks, 8, rank))
-    height = rank // bricks
-    for i in range(6):
-        start = 8 + i * height
-        out_ref[:, start : start + height, :] = (sums[i] * WEIGHT_V).reshape(
-            bricks, height, rank
-        )
 
 
 def maxwell_kernel(
-    brick_ref, cells_ref, integrals_ref, nodes_ref, first_ref, across_ref, part_ref, line_ref, state_ref
+    brick_ref,
+    cells_ref,
+    integrals_ref,
+    nodes_ref,
+    first_ref,
+    across_ref,
+    part_ref,
+    line_ref,
+    state_ref,
+    vectors_ref,
 ):
     bricks, cells, rank = cells_ref.shape
     groups, rows, _ = nodes_ref.shape
@@ -215,6 +229,7 @@
         integrals = integrals + integrals_ref[i]
     height = integrals.shape[0] - 8
     part_ref[:, cells:, :] = jnp.broadcast_to(integrals[8:][None], (bricks, height, rank))
+    vectors_ref[...] = integrals[:8]
     moments = contract(integrals[:8], k_flat, 1, 1)
     density, drift, temper = cell_state([moments[i : i + 1] for i in range(5)])
     slope = -0.5 / temper
@@ -310,7 +325,17 @@
         out_ref[group + 1] = product[:, rank:]
 
 
-def advance_kernel(parts_ref, steps_ref, cells_ref, payload_ref, advanced_ref, *, time_step):
+def advance_kernel(
+    parts_ref,
+    steps_ref,
+    cells_ref,
+    vectors_ref,
+    payload_ref,
+    advanced_ref,
+    transport_ref,
+    *,
+    time_step,
+):
     cells, rank = cells_ref.shape
     bricks = parts_ref.shape[0]
     height = rank // bricks
@@ -319,9 +344,19 @@
         maxwell_proj = maxwell_proj + parts_ref[i, :cells, :]
     maxwell_proj = maxwell_proj * WEIGHT_V
     flux = jnp.zeros((cells, rank), jnp.float32)
-    for i in range(6):
-        block = parts_ref[:, cells + i * height : cells + (i + 1) * height, :].reshape(rank, rank)
-        flux = flux + contract(steps_ref[i], block, 1, 0)
+    row = lax.broadcasted_iota(jnp.int32, (rank, rank), 0)
+    col = lax.broadcasted_iota(jnp.int32, (rank, rank), 1)
+    for i in range(3):
+        start = cells + i * height
+        packed = parts_ref[:, start : start + height, :].reshape(rank, rank)
+        turned = packed.T
+        plus = jnp.where(col >= row, packed, turned)
+        minus = jnp.where(col < row, packed, turned)
+        minus = jnp.where(col == row, vectors_ref[5 + i : 6 + i, :], minus)
+        transport_ref[2 * i] = plus
+        transport_ref[2 * i + 1] = minus
+        flux = flux + contract(steps_ref[2 * i], plus, 1, 0)
+        flux = flux + contract(steps_ref[2 * i + 1], minus, 1, 0)
     own = cells_ref[...]
     advanced = own - time_step * flux + COLLIDE * (maxwell_proj - own)
     advanced_ref[...] = advanced
@@ -350,14 +385,12 @@
     bricks, _, rank = pieces_ref.shape
     rows = basis_ref.shape[0]
     height = rank // bricks
-    cells = advanced_ref.shape[0]
     masks = [j ^ brick_ref[0] for j in range(bricks)]
     slots = [((m >> 1) & 3) * 4 + (m & 1) * 2 + (m >> 3) for m in masks]
 
     def piece(ref, i):
         if ref is transport_ref:
-            start = cells + i * height
-            return ref[:, start : start + height, :].reshape(rank, rank)
+            return ref[i]
         rows_of = [ref[slot, i * height : (i + 1) * height, :] for slot in slots]
         return jnp.concatenate(rows_of, axis=0)
 
@@ -466,19 +499,20 @@
     first_velocity = velocities(owner * rows)[0]
     first_speeds = jnp.broadcast_to(first_velocity[:, None], (slabs, rank))
     transport_part = pl.pallas_call(
-        transport_kernel, out_shape=f32(bricks, 8 + 6 * height, rank), name="transport", compiler_params=pltpu.CompilerParams(vmem_limit_bytes=VMEM_BYTES)
+        transport_kernel, out_shape=f32(bricks, 8 + 3 * height, rank), name="transport", compiler_params=pltpu.CompilerParams(vmem_limit_bytes=VMEM_BYTES)
     )(nodes, columns, first_speeds, weights)
     integrals = exchange(transport_part, "brick")
 
     brick_id = brick.astype(jnp.int32)[None]
     vector_specs = [pl.BlockSpec(memory_space=pltpu.SMEM)]
     whole = pl.BlockSpec(memory_space=pltpu.VMEM)
-    payload, line, state = pl.pallas_call(
+    payload, line, state, vectors = pl.pallas_call(
         maxwell_kernel,
         out_shape=(
-            f32(bricks, cells + 6 * height, rank),
+            f32(bricks, cells + 3 * height, rank),
             f32(slab_cells, slabs),
             f32(8, slab_cells),
+            f32(8, rank),
         ),
         in_specs=vector_specs + [whole] * 5,
         name="maxwell", compiler_params=pltpu.CompilerParams(vmem_limit_bytes=VMEM_BYTES),
@@ -504,11 +538,15 @@
     for axis_id in range(3):
         steps.append(((k_coeffs - lower[axis_id]) * lengths[axis_id]).reshape(cells, rank))
         steps.append(((upper[axis_id] - k_coeffs) * lengths[axis_id]).reshape(cells, rank))
-    payload, advanced = pl.pallas_call(
+    payload, advanced, transport = pl.pallas_call(
         functools.partial(advance_kernel, time_step=time_step),
-        out_shape=(f32(bricks, cells + height, rank), f32(cells, rank)),
+        out_shape=(
+            f32(bricks, cells + height, rank),
+            f32(cells, rank),
+            f32(6, rank, rank),
+        ),
         name="advance", compiler_params=pltpu.CompilerParams(vmem_limit_bytes=VMEM_BYTES),
-    )(second, jnp.stack(steps), own_cells)
+    )(second, jnp.stack(steps), own_cells, vectors)
     third = exchange(payload, "brick")
 
     pieces, chosen = pl.pallas_call(
@@ -548,7 +586,7 @@
         scratch_shapes=factor_scratch(rank)[:2],
         name="middle",
         compiler_params=pltpu.CompilerParams(vmem_limit_bytes=VMEM_BYTES),
-    )(brick_id, reduced, second, v_basis, advanced, speeds)
+    )(brick_id, reduced, transport, v_basis, advanced, speeds)
     velocity_new, gram_part = pl.pallas_call(
         functools.partial(update_kernel, weight_x=weight_x),
         out_shape=(f32(rows, rank), f32(rank, rank)),

time: 158 us -> 162 us (1.025)
  starting transfers between devices: 61.3 us -> 67.1 us
  waiting for transfers between devices: 65.8 us -> 63.5 us
    all_to_all x5, waiting for transfers between devices: 38 us -> 32.4 us  [exchange(): return lax.all_to_all(array, axis, 0, 0, tiled=True)]
    ppermute x25, waiting for transfers between devices: 24.9 us -> 30.1 us  [from_peer(): return lax.ppermute(values, axis, [(i, i ^ mask) for i in range(peers)])]
    ppermute x1, starting transfers between devices: 1.42 us -> 5.68 us  [local(): k_above = lax.ppermute(k_edges[:1], 'slab', down)]
    ppermute x1, starting transfers between devices: 1 us -> 3.19 us  [local(): chosen_below = lax.ppermute(chosen, 'slab', up)]
    ppermute x1, starting transfers between devices: 2.18 us -> 0.01 us  [local(): k_below = lax.ppermute(k_edges[-1:], 'slab', up)]
    ppermute x1, waiting for transfers between devices: 2.87 us -> 0.95 us  [local(): chosen_below = lax.ppermute(chosen, 'slab', up)]
    ppermute x25, starting transfers between devices: 31.8 us -> 33.6 us  [from_peer(): return lax.ppermute(values, axis, [(i, i ^ mask) for i in range(peers)])]
  transfers between devices with their start and end apart: 33 -> 33, of which waited for: 21 -> 21; matrix products, arithmetic and copies ran while one was open for 1% -> 1% of each run, Pallas kernels for 11% -> 9%
where the time goes in v8:
time: 162 us; the launch traced here: 161 us
  starting transfers between devices  67.1 us (41%)
  waiting for transfers between devices  63.5 us (39%)
  Pallas kernels  25.9 us (16%)
  local copies, waits for them, and re-layouts  2.35 us (1%)
    ppermute x25, starting transfers between devices, from_peer(): return lax.ppermute(values, axis, [(i, i ^ mask) for i in range(peers)])  33.6 us
    all_to_all x5, waiting for transfers between devices, exchange(): return lax.all_to_all(array, axis, 0, 0, tiled=True)  32.4 us
    ppermute x25, waiting for transfers between devices, from_peer(): return lax.ppermute(values, axis, [(i, i ^ mask) for i in range(peers)])  30.1 us
    all_to_all x5, starting transfers between devices, exchange(): return lax.all_to_all(array, axis, 0, 0, tiled=True)  24.7 us
    pallas_call x1, Pallas kernels, local(): pl.pallas_call(functools.partial(middle_kernel, lengths=lengths, time_ste...  6.2 us
    ppermute x1, starting transfers between devices, local(): k_above = lax.ppermute(k_edges[:1], 'slab', down)  5.68 us
    pallas_call x1, Pallas kernels, local(): pl.pallas_call(last_kernel, out_shape=(f32(rank, rank), f32(rows, rank)),...  4.5 us
    pallas_call x1, Pallas kernels, local(): pl.pallas_call(back_kernel, out_shape=f32(slabs, rows, rank), name='back'...  3.68 us
  transfers between devices with their start and end apart: 33, of which 21 were waited for; matrix products, arithmetic and copies ran while one was open for 1% of the time, Pallas kernels for 9%

profile of v8, /device:TPU:0, one launch (start us, length us, event | category | flops | bytes accessed | tf_op | source)
XLA Modules:
  0.0 161.2 jit_solution(311354327362526026)
XLA Ops:
  0.7 0.9 copy-done.1
  1.6 1.1 repeat.1
  2.7 7.0 %all-to-all-start = ((f32[8,256,128]{2,1,0:T(8,128)}), f32[8,256,128]{2,1,0:T(8,128)S(1)}, u32[]{:S(2)}, u32[]{:S(2)}) async-start(f32[8,256,128]{2,1,0:T(8,128)} %repeat.1), calls=%async_computation | async-start | bytes 2097152 | tf_op jit(solution)/shard_map/all_to_all | solution.py:34
  9.9 0.1 copy.24
  10.1 0.2 and_select_fusion.3
  10.5 2.0 %collective-permute-start.1 = (f32[2,64,128]{2,1,0:T(8,128)S(1)}, f32[2,64,128]{2,1,0:T(8,128)S(1)}, u32[]{:S(2)}, u32[]{:S(2)}) collective-permute-start(f32[2,64,128]{2,1,0:T(8,128)S(1)} %pad_maximum_fusion.1), channel_id=1, source_target_pairs={{0,2},{1,3},{2,0},{3,1},{4,6},{5,7},{6,4},{7,5},{8,10},{9,11},{10,... | collective-permute-start | bytes 196616 | tf_op jit(solution)/shard_map/ppermute | solution.py:58
  12.5 3.6 %collective-permute-start.2 = (f32[2,64,128]{2,1,0:T(8,128)S(1)}, f32[2,64,128]{2,1,0:T(8,128)S(1)}, u32[]{:S(2)}, u32[]{:S(2)}) collective-permute-start(f32[2,64,128]{2,1,0:T(8,128)S(1)} %pad_maximum_fusion.1), channel_id=1, source_target_pairs={{0,4},{1,5},{2,6},{3,7},{4,0},{5,1},{6,2},{7,3},{8,12},{9,13},{10,... | collective-permute-start | bytes 196616 | tf_op jit(solution)/shard_map/ppermute | solution.py:58
  16.1 3.6 %collective-permute-done.2 = f32[2,64,128]{2,1,0:T(8,128)S(1)} collective-permute-done((f32[2,64,128]{2,1,0:T(8,128)S(1)}, f32[2,64,128]{2,1,0:T(8,128)S(1)}, u32[]{:S(2)}, u32[]{:S(2)}) %collective-permute-start.2) | collective-permute-done | bytes 65568 | tf_op jit(solution)/shard_map/ppermute | solution.py:58
  19.7 1.9 %collective-permute-done.3 = f32[2,64,128]{2,1,0:T(8,128)S(1)} collective-permute-done((f32[2,64,128]{2,1,0:T(8,128)S(1)}, f32[2,64,128]{2,1,0:T(8,128)S(1)}, u32[]{:S(2)}, u32[]{:S(2)}) %collective-permute-start.3) | collective-permute-done | bytes 65568 | tf_op jit(solution)/shard_map/ppermute | solution.py:58
  21.6 0.7 collective-permute-start.4
  22.3 0.3 minimum_reduce_fusion
  22.7 0.1 copy.25.columns_ref
  23.0 5.8 %collective-permute-done.4 = f32[8,64,128]{2,1,0:T(8,128)S(1)} collective-permute-done((f32[8,64,128]{2,1,0:T(8,128)S(1)}, f32[8,64,128]{2,1,0:T(8,128)S(1)}, u32[]{:S(2)}, u32[]{:S(2)}) %collective-permute-start.4) | collective-permute-done | bytes 262176 | tf_op jit(solution)/shard_map/ppermute | solution.py:58
  28.8 5.7 %collective-permute-start.6 = (f32[1,2,16,128]{3,2,1,0:T(8,128)S(1)}, f32[1,2,16,128]{3,2,1,0:T(8,128)S(1)}, u32[]{:S(2)}, u32[]{:S(2)}) collective-permute-start(f32[1,2,16,128]{3,2,1,0:T(8,128)S(1)} %get-tuple-element.82), channel_id=1, source_target_pairs={{0,112},{16,0},{32,16},{48,32},{64,48},{80,64},{96,80},{112,96},{1... | collective-permute-start | bytes 49160 | tf_op jit(solution)/shard_map/ppermute | solution.py:493
  34.6 3.1 %transport.1 = f32[16,32,128]{2,1,0:T(8,128)} custom-call(f32[8,256,128]{2,1,0:T(8,128)S(1)} %all-to-all-done.nodes_ref, f32[256,8]{1,0:T(8,128)S(1)} %copy.25.columns_ref, f32[8,128]{1,0:T(8,128)S(1)} %broadcast_in_dim.14.speeds_ref.first_ref, f32[8,8,256]{2,1,0:T(8,128)S(1)} %stack.61.weights_ref), custom_call_target="tpu_custom_call" | custom-call | tf_op jit(solution)/shard_map/transport/pallas_call | solution.py:501
  37.7 5.4 %all-to-all-start.1 = ((f32[16,32,128]{2,1,0:T(8,128)}), f32[16,32,128]{2,1,0:T(8,128)S(1)}, u32[]{:S(2)}, u32[]{:S(2)}) async-start(f32[16,32,128]{2,1,0:T(8,128)} %transport.1), calls=%async_computation.1 | async-start | bytes 524288 | tf_op jit(solution)/shard_map/all_to_all | solution.py:34
  43.2 7.9 %all-to-all-done.1.integrals_ref = f32[16,32,128]{2,1,0:T(8,128)S(1)} async-done(((f32[16,32,128]{2,1,0:T(8,128)}), f32[16,32,128]{2,1,0:T(8,128)S(1)}, u32[]{:S(2)}, u32[]{:S(2)}) %all-to-all-start.1) | async-done | bytes 262176 | tf_op jit(solution)/shard_map/all_to_all | solution.py:34
  51.2 3.7 %maxwell.1 = (f32[16,88,128]{2,1,0:T(8,128)}, f32[1024,8]{1,0:T(8,128)S(1)}, f32[8,1024]{1,0:T(8,128)S(1)}, f32[8,128]{1,0:T(8,128)S(1)}) custom-call(s32[1]{0:T(128)} %bitcast.brick_ref, f32[16,64,128]{2,1,0:T(8,128)S(1)} %constant_dynamic-update-slice_fusion.5.cells_ref, f32[16,32,128]{2,1,0:T(8,128)S(1)} %all-to-all-done.1.integrals_ref, ...), custom_call_target="tpu_custom_call" | custom-call | tf_op jit(solution)/shard_map/maxwell/pallas_call | solution.py:509
  54.8 3.6 %all-to-all-start.2 = ((f32[16,88,128]{2,1,0:T(8,128)}), f32[16,88,128]{2,1,0:T(8,128)S(1)}, u32[]{:S(2)}, u32[]{:S(2)}) async-start(f32[16,88,128]{2,1,0:T(8,128)} %get-tuple-element.26), calls=%async_computation.2 | async-start | bytes 1441792 | tf_op jit(solution)/shard_map/all_to_all | solution.py:34
  58.5 12.9 %all-to-all-done.2.parts_ref = f32[16,88,128]{2,1,0:T(8,128)S(1)} async-done(((f32[16,88,128]{2,1,0:T(8,128)}), f32[16,88,128]{2,1,0:T(8,128)S(1)}, u32[]{:S(2)}, u32[]{:S(2)}) %all-to-all-start.2) | async-done | bytes 720928 | tf_op jit(solution)/shard_map/all_to_all | solution.py:34
  71.5 1.7 %advance.1 = (f32[16,72,128]{2,1,0:T(8,128)}, f32[64,128]{1,0:T(8,128)S(1)}, f32[6,128,128]{2,1,0:T(8,128)S(1)}) custom-call(f32[16,88,128]{2,1,0:T(8,128)S(1)} %all-to-all-done.2.parts_ref, f32[6,64,128]{2,1,0:T(8,128)S(1)} %constant_dynamic-update-slice_fusion.11.steps_ref, f32[64,128]{1,0:T(8,128)S(1)} %bitcast.42, f32[8,128]{1,0:T(8,128)S(1)} %get-tuple-element.28.vectors_ref), custom_call_target="tpu_custom_call" | custom-call | tf_op jit(solution)/shard_map/advance/pallas_call | solution.py:541
  73.2 3.6 %all-to-all-start.3 = ((f32[16,72,128]{2,1,0:T(8,128)}), f32[16,72,128]{2,1,0:T(8,128)S(1)}, u32[]{:S(2)}, u32[]{:S(2)}) async-start(f32[16,72,128]{2,1,0:T(8,128)} %get-tuple-element.29), calls=%async_computation.3 | async-start | bytes 1179648 | tf_op jit(solution)/shard_map/all_to_all | solution.py:34
  76.8 11.5 %all-to-all-done.3.parts_ref = f32[16,72,128]{2,1,0:T(8,128)S(1)} async-done(((f32[16,72,128]{2,1,0:T(8,128)}), f32[16,72,128]{2,1,0:T(8,128)S(1)}, u32[]{:S(2)}, u32[]{:S(2)}) %all-to-all-start.3) | async-done | bytes 589856 | tf_op jit(solution)/shard_map/all_to_all | solution.py:34
  88.3 1.2 products.1
  89.6 3.2 %collective-permute-start.7 = (f32[8,512]{1,0:T(8,128)S(1)}, f32[8,512]{1,0:T(8,128)S(1)}, u32[]{:S(2)}, u32[]{:S(2)}) collective-permute-start(f32[8,512]{1,0:T(8,128)S(1)} %get-tuple-element.32), channel_id=1, source_target_pairs={{0,16},{16,32},{32,48},{48,64},{64,80},{80,96},{96,112},{112,0},{1... | collective-permute-start | bytes 49160 | tf_op jit(solution)/shard_map/ppermute | solution.py:561
  92.8 3.7 %back.1 = f32[8,256,128]{2,1,0:T(8,128)} custom-call(f32[16,72,128]{2,1,0:T(8,128)S(1)} %all-to-all-done.3.parts_ref, f32[1024,8]{1,0:T(8,128)S(1)} %get-tuple-element.34.line_ref, f32[8,1024]{1,0:T(8,128)S(1)} %get-tuple-element.35.state_ref, f32[256,2]{1,0:T(8,128)S(1)} %get-tuple-element.60.across_ref), custom_call_target="tpu_custom_call" | custom-call | tf_op jit(solution)/shard_map/back/pallas_call | solution.py:564
  96.5 1.0 collective-permute-done.7
  97.4 0.2 fusion.32
  97.7 0.6 collective-permute-start.8
  98.3 0.1 copy.27
  98.6 3.5 %collective-permute-start.10 = (f32[40,128]{1,0:T(8,128)S(1)}, f32[40,128]{1,0:T(8,128)S(1)}, u32[]{:S(2)}, u32[]{:S(2)}) collective-permute-start(f32[40,128]{1,0:T(8,128)S(1)} %pad_add_fusion), channel_id=1, source_target_pairs={{0,24},{1,25},{2,26},{3,27},{4,28},{5,29},{6,30},{7,31},{8,16},{9,... | collective-permute-start | bytes 61448 | tf_op jit(solution)/shard_map/ppermute | solution.py:58
  102.1 1.0 collective-permute-done.8
  103.0 0.8 collective-permute-done.10
  103.9 2.7 %collective-permute-start.12 = (f32[2,40,128]{2,1,0:T(8,128)S(1)}, f32[2,40,128]{2,1,0:T(8,128)S(1)}, u32[]{:S(2)}, u32[]{:S(2)}) collective-permute-start(f32[2,40,128]{2,1,0:T(8,128)S(1)} %pad_maximum_fusion.2), channel_id=1, source_target_pairs={{0,64},{1,65},{2,66},{3,67},{4,68},{5,69},{6,70},{7,71},{8,72},{9,... | collective-permute-start | bytes 122888 | tf_op jit(solution)/shard_map/ppermute | solution.py:58
  106.5 1.0 collective-permute-start.13
  107.5 0.6 collective-permute-start.11
  108.1 5.1 %all-to-all-start.4 = ((f32[8,256,128]{2,1,0:T(8,128)}), f32[8,256,128]{2,1,0:T(8,128)S(1)}, u32[]{:S(2)}, u32[]{:S(2)}) async-start(f32[8,256,128]{2,1,0:T(8,128)} %back.1), calls=%async_computation.4 | async-start | bytes 2097152 | tf_op jit(solution)/shard_map/all_to_all | solution.py:34
  113.4 0.3 slice_reduce_fusion
  113.7 0.1 copy.28.speeds_ref
  113.8 0.8 collective-permute-done.14
  114.6 2.4 %collective-permute-start.16 = (f32[4,40,128]{2,1,0:T(8,128)S(1)}, f32[4,40,128]{2,1,0:T(8,128)S(1)}, u32[]{:S(2)}, u32[]{:S(2)}) collective-permute-start(f32[4,40,128]{2,1,0:T(8,128)S(1)} %pad_maximum_fusion), channel_id=1, source_target_pairs={{0,4},{1,5},{2,6},{3,7},{4,0},{5,1},{6,2},{7,3},{8,12},{9,13},{10,... | collective-permute-start | bytes 245768 | tf_op jit(solution)/shard_map/ppermute | solution.py:58
  116.9 2.3 %collective-permute-start.17 = (f32[4,40,128]{2,1,0:T(8,128)S(1)}, f32[4,40,128]{2,1,0:T(8,128)S(1)}, u32[]{:S(2)}, u32[]{:S(2)}) collective-permute-start(f32[4,40,128]{2,1,0:T(8,128)S(1)} %pad_maximum_fusion), channel_id=1, source_target_pairs={{0,6},{1,7},{2,4},{3,5},{4,2},{5,3},{6,0},{7,1},{8,14},{9,15},{10,... | collective-permute-start | bytes 245768 | tf_op jit(solution)/shard_map/ppermute | solution.py:58
  119.3 0.6 collective-permute-done.15
  119.9 1.4 collective-permute-done.16
  121.3 1.7 %collective-permute-done.17 = f32[4,40,128]{2,1,0:T(8,128)S(1)} collective-permute-done((f32[4,40,128]{2,1,0:T(8,128)S(1)}, f32[4,40,128]{2,1,0:T(8,128)S(1)}, u32[]{:S(2)}, u32[]{:S(2)}) %collective-permute-start.17) | collective-permute-done | bytes 81952 | tf_op jit(solution)/shard_map/ppermute | solution.py:58
  123.0 6.2 %middle.1 = (f32[64,128]{1,0:T(8,128)}, f32[256,128]{1,0:T(8,128)S(1)}, f32[128,128]{1,0:T(8,128)S(1)}) custom-call(s32[1]{0:T(128)} %bitcast.brick_ref, f32[16,40,128]{2,1,0:T(8,128)S(1)} %constant_dynamic-update-slice_fusion.17.pieces_ref, f32[6,128,128]{2,1,0:T(8,128)S(1)} %get-tuple-element.37.transport_ref, f32[256,128]{1,0:T(8,128)S(1)} %copy-done.2, ...), custom_call_target="tpu_custom_call" | custom-call | tf_op jit(solution)/shard_map/middle/pallas_call | solution.py:580
  129.2 0.7 update.1
  130.0 1.2 collective-permute-done.18
  131.2 1.3 collective-permute-start.20
  132.6 1.7 %collective-permute-start.21 = (f32[128,128]{1,0:T(8,128)S(1)}, f32[128,128]{1,0:T(8,128)S(1)}, u32[]{:S(2)}, u32[]{:S(2)}) collective-permute-start(f32[128,128]{1,0:T(8,128)S(1)} %add.402), channel_id=1, source_target_pairs={{0,6},{1,7},{2,4},{3,5},{4,2},{5,3},{6,0},{7,1},{8,14},{9,15},{10,... | collective-permute-start | bytes 196616 | tf_op jit(solution)/shard_map/ppermute | solution.py:58
  134.3 0.6 collective-permute-start.19
  134.8 2.3 %collective-permute-done.20 = f32[128,128]{1,0:T(8,128)S(1)} collective-permute-done((f32[128,128]{1,0:T(8,128)S(1)}, f32[128,128]{1,0:T(8,128)S(1)}, u32[]{:S(2)}, u32[]{:S(2)}) %collective-permute-start.20) | collective-permute-done | bytes 65568 | tf_op jit(solution)/shard_map/ppermute | solution.py:58
  137.2 1.2 collective-permute-done.21
  138.4 0.1 collective-permute-done.19
  138.5 3.6 %collective-permute-start.23 = (f32[128,128]{1,0:T(8,128)S(1)}, f32[128,128]{1,0:T(8,128)S(1)}, u32[]{:S(2)}, u32[]{:S(2)}) collective-permute-start(f32[128,128]{1,0:T(8,128)S(1)} %add_add_fusion.2), channel_id=1, source_target_pairs={{0,16},{1,17},{2,18},{3,19},{4,20},{5,21},{6,22},{7,23},{8,24},{9,... | collective-permute-start | bytes 196616 | tf_op jit(solution)/shard_map/ppermute | solution.py:58
  142.1 1.2 collective-permute-start.24
  143.4 0.8 collective-permute-start.22
  144.1 0.3 collective-permute-done.23
  144.4 3.2 %collective-permute-done.24 = f32[128,128]{1,0:T(8,128)S(1)} collective-permute-done((f32[128,128]{1,0:T(8,128)S(1)}, f32[128,128]{1,0:T(8,128)S(1)}, u32[]{:S(2)}, u32[]{:S(2)}) %collective-permute-start.24) | collective-permute-done | bytes 65568 | tf_op jit(solution)/shard_map/ppermute | solution.py:58
  147.7 3.5 %collective-permute-start.26 = (f32[128,128]{1,0:T(8,128)S(1)}, f32[128,128]{1,0:T(8,128)S(1)}, u32[]{:S(2)}, u32[]{:S(2)}) collective-permute-start(f32[128,128]{1,0:T(8,128)S(1)} %add_add_fusion.1), channel_id=1, source_target_pairs={{0,64},{1,65},{2,66},{3,67},{4,68},{5,69},{6,70},{7,71},{8,72},{9,... | collective-permute-start | bytes 196616 | tf_op jit(solution)/shard_map/ppermute | solution.py:58
  151.2 1.2 collective-permute-start.27
  152.3 1.2 collective-permute-done.26
  153.5 3.1 %collective-permute-done.27 = f32[128,128]{1,0:T(8,128)S(1)} collective-permute-done((f32[128,128]{1,0:T(8,128)S(1)}, f32[128,128]{1,0:T(8,128)S(1)}, u32[]{:S(2)}, u32[]{:S(2)}) %collective-permute-start.27) | collective-permute-done | bytes 65568 | tf_op jit(solution)/shard_map/ppermute | solution.py:58
  156.7 4.5 %last.1 = (f32[128,128]{1,0:T(8,128)}, f32[256,128]{1,0:T(8,128)}) custom-call(f32[128,128]{1,0:T(8,128)S(1)} %add_add_fusion.gram_ref, f32[256,128]{1,0:T(8,128)S(1)} %get-tuple-element.44.velocity_ref), custom_call_target="tpu_custom_call" | custom-call | tf_op jit(solution)/shard_map/last/pallas_call | solution.py:597
  (89 shorter events, 1.4 us)
Async XLA Ops:
  0.6 9.9 %collective-permute-start = (f32[1,64,128]{2,1,0:T(8,128)}, f32[1,64,128]{2,1,0:T(8,128)S(1)}, u32[]{:S(2)}, u32[]{:S(2)}) collective-permute-start(f32[1,64,128]{2,1,0:T(8,128)} %bitcast.39), channel_id=1, source_target_pairs={{0,1},{1,0},{2,3},{3,2},{4,5},{5,4},{6,7},{7,6},{8,9},{9,8},{10,11... | collective-permute-start | bytes 98312 | tf_op jit(solution)/shard_map/ppermute | solution.py:58
  0.7 0.9 copy-start.1
  2.7 7.1 %copy-start = (f32[2,2,16,128]{3,2,1,0:T(8,128)S(1)}, f32[2,2,16,128]{3,2,1,0:T(8,128)}, u32[]{:S(2)}) copy-start(f32[2,2,16,128]{3,2,1,0:T(8,128)} %param.2) | copy-start | bytes 98308
  2.7 31.8 %all-to-all-start = ((f32[8,256,128]{2,1,0:T(8,128)}), f32[8,256,128]{2,1,0:T(8,128)S(1)}, u32[]{:S(2)}, u32[]{:S(2)}) async-start(f32[8,256,128]{2,1,0:T(8,128)} %repeat.1), calls=%async_computation | async-start | bytes 2097152 | tf_op jit(solution)/shard_map/all_to_all | solution.py:34
  10.5 5.6 %collective-permute-start.1 = (f32[2,64,128]{2,1,0:T(8,128)S(1)}, f32[2,64,128]{2,1,0:T(8,128)S(1)}, u32[]{:S(2)}, u32[]{:S(2)}) collective-permute-start(f32[2,64,128]{2,1,0:T(8,128)S(1)} %pad_maximum_fusion.1), channel_id=1, source_target_pairs={{0,2},{1,3},{2,0},{3,1},{4,6},{5,7},{6,4},{7,5},{8,10},{9,11},{10,... | collective-permute-start | bytes 196616 | tf_op jit(solution)/shard_map/ppermute | solution.py:58
  12.5 7.2 %collective-permute-start.2 = (f32[2,64,128]{2,1,0:T(8,128)S(1)}, f32[2,64,128]{2,1,0:T(8,128)S(1)}, u32[]{:S(2)}, u32[]{:S(2)}) collective-permute-start(f32[2,64,128]{2,1,0:T(8,128)S(1)} %pad_maximum_fusion.1), channel_id=1, source_target_pairs={{0,4},{1,5},{2,6},{3,7},{4,0},{5,1},{6,2},{7,3},{8,12},{9,13},{10,... | collective-permute-start | bytes 196616 | tf_op jit(solution)/shard_map/ppermute | solution.py:58
  16.1 5.5 %collective-permute-start.3 = (f32[2,64,128]{2,1,0:T(8,128)S(1)}, f32[2,64,128]{2,1,0:T(8,128)S(1)}, u32[]{:S(2)}, u32[]{:S(2)}) collective-permute-start(f32[2,64,128]{2,1,0:T(8,128)S(1)} %pad_maximum_fusion.1), channel_id=1, source_target_pairs={{0,6},{1,7},{2,4},{3,5},{4,2},{5,3},{6,0},{7,1},{8,14},{9,15},{10,... | collective-permute-start | bytes 196616 | tf_op jit(solution)/shard_map/ppermute | solution.py:58
  21.6 7.2 %collective-permute-start.4 = (f32[8,64,128]{2,1,0:T(8,128)S(1)}, f32[8,64,128]{2,1,0:T(8,128)S(1)}, u32[]{:S(2)}, u32[]{:S(2)}) collective-permute-start(f32[8,64,128]{2,1,0:T(8,128)S(1)} %get-tuple-element.62), channel_id=1, source_target_pairs={{0,8},{1,9},{2,10},{3,11},{4,12},{5,13},{6,14},{7,15},{8,0},{9,1},... | collective-permute-start | bytes 786440 | tf_op jit(solution)/shard_map/ppermute | solution.py:58
  28.8 14.3 %collective-permute-start.6 = (f32[1,2,16,128]{3,2,1,0:T(8,128)S(1)}, f32[1,2,16,128]{3,2,1,0:T(8,128)S(1)}, u32[]{:S(2)}, u32[]{:S(2)}) collective-permute-start(f32[1,2,16,128]{3,2,1,0:T(8,128)S(1)} %get-tuple-element.82), channel_id=1, source_target_pairs={{0,112},{16,0},{32,16},{48,32},{64,48},{80,64},{96,80},{112,96},{1... | collective-permute-start | bytes 49160 | tf_op jit(solution)/shard_map/ppermute | solution.py:493
  34.5 8.7 %collective-permute-start.5 = (f32[1,2,16,128]{3,2,1,0:T(8,128)S(1)}, f32[1,2,16,128]{3,2,1,0:T(8,128)S(1)}, u32[]{:S(2)}, u32[]{:S(2)}) collective-permute-start(f32[1,2,16,128]{3,2,1,0:T(8,128)S(1)} %get-tuple-element.83), channel_id=1, source_target_pairs={{0,16},{16,32},{32,48},{48,64},{64,80},{80,96},{96,112},{112,0},{1... | collective-permute-start | bytes 49160 | tf_op jit(solution)/shard_map/ppermute | solution.py:492
  37.7 13.5 %all-to-all-start.1 = ((f32[16,32,128]{2,1,0:T(8,128)}), f32[16,32,128]{2,1,0:T(8,128)S(1)}, u32[]{:S(2)}, u32[]{:S(2)}) async-start(f32[16,32,128]{2,1,0:T(8,128)} %transport.1), calls=%async_computation.1 | async-start | bytes 524288 | tf_op jit(solution)/shard_map/all_to_all | solution.py:34
  54.8 16.6 %all-to-all-start.2 = ((f32[16,88,128]{2,1,0:T(8,128)}), f32[16,88,128]{2,1,0:T(8,128)S(1)}, u32[]{:S(2)}, u32[]{:S(2)}) async-start(f32[16,88,128]{2,1,0:T(8,128)} %get-tuple-element.26), calls=%async_computation.2 | async-start | bytes 1441792 | tf_op jit(solution)/shard_map/all_to_all | solution.py:34
  73.2 15.2 %all-to-all-start.3 = ((f32[16,72,128]{2,1,0:T(8,128)}), f32[16,72,128]{2,1,0:T(8,128)S(1)}, u32[]{:S(2)}, u32[]{:S(2)}) async-start(f32[16,72,128]{2,1,0:T(8,128)} %get-tuple-element.29), calls=%async_computation.3 | async-start | bytes 1179648 | tf_op jit(solution)/shard_map/all_to_all | solution.py:34
  89.6 7.9 %collective-permute-start.7 = (f32[8,512]{1,0:T(8,128)S(1)}, f32[8,512]{1,0:T(8,128)S(1)}, u32[]{:S(2)}, u32[]{:S(2)}) collective-permute-start(f32[8,512]{1,0:T(8,128)S(1)} %get-tuple-element.32), channel_id=1, source_target_pairs={{0,16},{16,32},{32,48},{48,64},{64,80},{80,96},{96,112},{112,0},{1... | collective-permute-start | bytes 49160 | tf_op jit(solution)/shard_map/ppermute | solution.py:561
  97.7 5.4 %collective-permute-start.8 = (f32[40,128]{1,0:T(8,128)S(1)}, f32[40,128]{1,0:T(8,128)S(1)}, u32[]{:S(2)}, u32[]{:S(2)}) collective-permute-start(f32[40,128]{1,0:T(8,128)S(1)} %pad_add_fusion), channel_id=1, source_target_pairs={{0,16},{1,17},{2,18},{3,19},{4,20},{5,21},{6,22},{7,23},{8,24},{9,... | collective-permute-start | bytes 61448 | tf_op jit(solution)/shard_map/ppermute | solution.py:58
  98.5 4.6 %collective-permute-start.9 = (f32[40,128]{1,0:T(8,128)S(1)}, f32[40,128]{1,0:T(8,128)S(1)}, u32[]{:S(2)}, u32[]{:S(2)}) collective-permute-start(f32[40,128]{1,0:T(8,128)S(1)} %pad_add_fusion), channel_id=1, source_target_pairs={{0,8},{1,9},{2,10},{3,11},{4,12},{5,13},{6,14},{7,15},{8,0},{9,1},... | collective-permute-start | bytes 61448 | tf_op jit(solution)/shard_map/ppermute | solution.py:58
  98.6 5.3 %collective-permute-start.10 = (f32[40,128]{1,0:T(8,128)S(1)}, f32[40,128]{1,0:T(8,128)S(1)}, u32[]{:S(2)}, u32[]{:S(2)}) collective-permute-start(f32[40,128]{1,0:T(8,128)S(1)} %pad_add_fusion), channel_id=1, source_target_pairs={{0,24},{1,25},{2,26},{3,27},{4,28},{5,29},{6,30},{7,31},{8,16},{9,... | collective-permute-start | bytes 61448 | tf_op jit(solution)/shard_map/ppermute | solution.py:58
  103.9 9.4 %collective-permute-start.12 = (f32[2,40,128]{2,1,0:T(8,128)S(1)}, f32[2,40,128]{2,1,0:T(8,128)S(1)}, u32[]{:S(2)}, u32[]{:S(2)}) collective-permute-start(f32[2,40,128]{2,1,0:T(8,128)S(1)} %pad_maximum_fusion.2), channel_id=1, source_target_pairs={{0,64},{1,65},{2,66},{3,67},{4,68},{5,69},{6,70},{7,71},{8,72},{9,... | collective-permute-start | bytes 122888 | tf_op jit(solution)/shard_map/ppermute | solution.py:58
  106.5 6.7 %collective-permute-start.13 = (f32[2,40,128]{2,1,0:T(8,128)S(1)}, f32[2,40,128]{2,1,0:T(8,128)S(1)}, u32[]{:S(2)}, u32[]{:S(2)}) collective-permute-start(f32[2,40,128]{2,1,0:T(8,128)S(1)} %pad_maximum_fusion.2), channel_id=1, source_target_pairs={{0,96},{1,97},{2,98},{3,99},{4,100},{5,101},{6,102},{7,103},{8,104... | collective-permute-start | bytes 122888 | tf_op jit(solution)/shard_map/ppermute | solution.py:58
  107.5 5.7 %collective-permute-start.11 = (f32[2,40,128]{2,1,0:T(8,128)S(1)}, f32[2,40,128]{2,1,0:T(8,128)S(1)}, u32[]{:S(2)}, u32[]{:S(2)}) collective-permute-start(f32[2,40,128]{2,1,0:T(8,128)S(1)} %pad_maximum_fusion.2), channel_id=1, source_target_pairs={{0,32},{1,33},{2,34},{3,35},{4,36},{5,37},{6,38},{7,39},{8,40},{9,... | collective-permute-start | bytes 122888 | tf_op jit(solution)/shard_map/ppermute | solution.py:58
  108.1 21.0 %all-to-all-start.4 = ((f32[8,256,128]{2,1,0:T(8,128)}), f32[8,256,128]{2,1,0:T(8,128)S(1)}, u32[]{:S(2)}, u32[]{:S(2)}) async-start(f32[8,256,128]{2,1,0:T(8,128)} %back.1), calls=%async_computation.4 | async-start | bytes 2097152 | tf_op jit(solution)/shard_map/all_to_all | solution.py:34
  113.3 1.3 collective-permute-start.14
  114.6 5.3 %collective-permute-start.15 = (f32[4,40,128]{2,1,0:T(8,128)S(1)}, f32[4,40,128]{2,1,0:T(8,128)S(1)}, u32[]{:S(2)}, u32[]{:S(2)}) collective-permute-start(f32[4,40,128]{2,1,0:T(8,128)S(1)} %pad_maximum_fusion), channel_id=1, source_target_pairs={{0,2},{1,3},{2,0},{3,1},{4,6},{5,7},{6,4},{7,5},{8,10},{9,11},{10,... | collective-permute-start | bytes 245768 | tf_op jit(solution)/shard_map/ppermute | solution.py:58
  114.6 6.7 %collective-permute-start.16 = (f32[4,40,128]{2,1,0:T(8,128)S(1)}, f32[4,40,128]{2,1,0:T(8,128)S(1)}, u32[]{:S(2)}, u32[]{:S(2)}) collective-permute-start(f32[4,40,128]{2,1,0:T(8,128)S(1)} %pad_maximum_fusion), channel_id=1, source_target_pairs={{0,4},{1,5},{2,6},{3,7},{4,0},{5,1},{6,2},{7,3},{8,12},{9,13},{10,... | collective-permute-start | bytes 245768 | tf_op jit(solution)/shard_map/ppermute | solution.py:58
  116.9 6.0 %collective-permute-start.17 = (f32[4,40,128]{2,1,0:T(8,128)S(1)}, f32[4,40,128]{2,1,0:T(8,128)S(1)}, u32[]{:S(2)}, u32[]{:S(2)}) collective-permute-start(f32[4,40,128]{2,1,0:T(8,128)S(1)} %pad_maximum_fusion), channel_id=1, source_target_pairs={{0,6},{1,7},{2,4},{3,5},{4,2},{5,3},{6,0},{7,1},{8,14},{9,15},{10,... | collective-permute-start | bytes 245768 | tf_op jit(solution)/shard_map/ppermute | solution.py:58
  119.9 3.1 %copy-start.2 = (f32[256,128]{1,0:T(8,128)S(1)}, f32[256,128]{1,0:T(8,128)}, u32[]{:S(2)}) copy-start(f32[256,128]{1,0:T(8,128)} %basis_ref.1) | copy-start | bytes 393220
  129.9 1.3 collective-permute-start.18
  131.2 5.9 %collective-permute-start.20 = (f32[128,128]{1,0:T(8,128)S(1)}, f32[128,128]{1,0:T(8,128)S(1)}, u32[]{:S(2)}, u32[]{:S(2)}) collective-permute-start(f32[128,128]{1,0:T(8,128)S(1)} %add.402), channel_id=1, source_target_pairs={{0,4},{1,5},{2,6},{3,7},{4,0},{5,1},{6,2},{7,3},{8,12},{9,13},{10,... | collective-permute-start | bytes 196616 | tf_op jit(solution)/shard_map/ppermute | solution.py:58
  132.6 5.8 %collective-permute-start.21 = (f32[128,128]{1,0:T(8,128)S(1)}, f32[128,128]{1,0:T(8,128)S(1)}, u32[]{:S(2)}, u32[]{:S(2)}) collective-permute-start(f32[128,128]{1,0:T(8,128)S(1)} %add.402), channel_id=1, source_target_pairs={{0,6},{1,7},{2,4},{3,5},{4,2},{5,3},{6,0},{7,1},{8,14},{9,15},{10,... | collective-permute-start | bytes 196616 | tf_op jit(solution)/shard_map/ppermute | solution.py:58
  134.3 4.3 %collective-permute-start.19 = (f32[128,128]{1,0:T(8,128)S(1)}, f32[128,128]{1,0:T(8,128)S(1)}, u32[]{:S(2)}, u32[]{:S(2)}) collective-permute-start(f32[128,128]{1,0:T(8,128)S(1)} %add.402), channel_id=1, source_target_pairs={{0,2},{1,3},{2,0},{3,1},{4,6},{5,7},{6,4},{7,5},{8,10},{9,11},{10,... | collective-permute-start | bytes 196616 | tf_op jit(solution)/shard_map/ppermute | solution.py:58
  138.5 5.8 %collective-permute-start.23 = (f32[128,128]{1,0:T(8,128)S(1)}, f32[128,128]{1,0:T(8,128)S(1)}, u32[]{:S(2)}, u32[]{:S(2)}) collective-permute-start(f32[128,128]{1,0:T(8,128)S(1)} %add_add_fusion.2), channel_id=1, source_target_pairs={{0,16},{1,17},{2,18},{3,19},{4,20},{5,21},{6,22},{7,23},{8,24},{9,... | collective-permute-start | bytes 196616 | tf_op jit(solution)/shard_map/ppermute | solution.py:58
  142.1 5.5 %collective-permute-start.24 = (f32[128,128]{1,0:T(8,128)S(1)}, f32[128,128]{1,0:T(8,128)S(1)}, u32[]{:S(2)}, u32[]{:S(2)}) collective-permute-start(f32[128,128]{1,0:T(8,128)S(1)} %add_add_fusion.2), channel_id=1, source_target_pairs={{0,24},{1,25},{2,26},{3,27},{4,28},{5,29},{6,30},{7,31},{8,16},{9,... | collective-permute-start | bytes 196616 | tf_op jit(solution)/shard_map/ppermute | solution.py:58
  143.4 4.3 %collective-permute-start.22 = (f32[128,128]{1,0:T(8,128)S(1)}, f32[128,128]{1,0:T(8,128)S(1)}, u32[]{:S(2)}, u32[]{:S(2)}) collective-permute-start(f32[128,128]{1,0:T(8,128)S(1)} %add_add_fusion.2), channel_id=1, source_target_pairs={{0,8},{1,9},{2,10},{3,11},{4,12},{5,13},{6,14},{7,15},{8,0},{9,1},... | collective-permute-start | bytes 196616 | tf_op jit(solution)/shard_map/ppermute | solution.py:58
  147.7 5.8 %collective-permute-start.26 = (f32[128,128]{1,0:T(8,128)S(1)}, f32[128,128]{1,0:T(8,128)S(1)}, u32[]{:S(2)}, u32[]{:S(2)}) collective-permute-start(f32[128,128]{1,0:T(8,128)S(1)} %add_add_fusion.1), channel_id=1, source_target_pairs={{0,64},{1,65},{2,66},{3,67},{4,68},{5,69},{6,70},{7,71},{8,72},{9,... | collective-permute-start | bytes 196616 | tf_op jit(solution)/shard_map/ppermute | solution.py:58
  151.2 5.5 %collective-permute-start.27 = (f32[128,128]{1,0:T(8,128)S(1)}, f32[128,128]{1,0:T(8,128)S(1)}, u32[]{:S(2)}, u32[]{:S(2)}) collective-permute-start(f32[128,128]{1,0:T(8,128)S(1)} %add_add_fusion.1), channel_id=1, source_target_pairs={{0,96},{1,97},{2,98},{3,99},{4,100},{5,101},{6,102},{7,103},{8,104... | collective-permute-start | bytes 196616 | tf_op jit(solution)/shard_map/ppermute | solution.py:58
  152.3 4.3 %collective-permute-start.25 = (f32[128,128]{1,0:T(8,128)S(1)}, f32[128,128]{1,0:T(8,128)S(1)}, u32[]{:S(2)}, u32[]{:S(2)}) collective-permute-start(f32[128,128]{1,0:T(8,128)S(1)} %add_add_fusion.1), channel_id=1, source_target_pairs={{0,32},{1,33},{2,34},{3,35},{4,36},{5,37},{6,38},{7,39},{8,40},{9,... | collective-permute-start | bytes 196616 | tf_op jit(solution)/shard_map/ppermute | solution.py:58

commit v9 on v8

--- a/solution.py
+++ b/solution.py
@@ -146,11 +146,19 @@
             work_ref[stop:, :] = work_ref[stop:, :] - update[stop:, :]
 
 
-def repeat_kernel(source_ref, out_ref, sems):
-    copies = [
-        pltpu.make_async_copy(source_ref, out_ref.at[i], sems.at[i])
-        for i in range(out_ref.shape[0])
-    ]
+def repeat_kernel(below_ref, source_ref, cells_ref, out_ref, sems):
+    rows = source_ref.shape[0]
+    plane = out_ref.shape[1] - rows
+    last = cells_ref.shape[0] - plane
+    copies = []
+    for i in range(out_ref.shape[0]):
+        start = pl.multiple_of(jnp.where(below_ref[0] == i, 0, last), 8)
+        copies.append(pltpu.make_async_copy(source_ref, out_ref.at[i, :rows], sems.at[0, i]))
+        copies.append(
+            pltpu.make_async_copy(
+                cells_ref.at[pl.ds(start, plane)], out_ref.at[i, rows:], sems.at[1, i]
+            )
+        )
     for copy in copies:
         copy.start()
     for copy in copies:
@@ -170,13 +178,14 @@
 
 
 def transport_kernel(nodes_ref, columns_ref, speeds_ref, weights_ref, out_ref):
-    groups, rows, rank = nodes_ref.shape
+    groups, _, rank = nodes_ref.shape
+    rows = columns_ref.shape[0]
     bricks = out_ref.shape[0]
     factors = [jnp.broadcast_to(columns_ref[:, i : i + 1], (rows, rank)) for i in range(4)]
     sums = [jnp.zeros((rank, rank), jnp.float32) for _ in range(6)]
     vectors = jnp.zeros((8, rank), jnp.float32)
     for group in range(groups):
-        nodes = nodes_ref[group]
+        nodes = nodes_ref[group, :rows]
         weighted = jnp.concatenate([nodes] + [nodes * factor for factor in factors], axis=1)
         high, low = two_parts(weighted)
         node_high, node_low = high[:, :rank], low[:, :rank]
@@ -220,7 +229,7 @@
     vectors_ref,
 ):
     bricks, cells, rank = cells_ref.shape
-    groups, rows, _ = nodes_ref.shape
+    groups, rows = nodes_ref.shape[0], across_ref.shape[1]
     total = bricks * cells
     brick = brick_ref[0]
     k_flat = jnp.concatenate([cells_ref[i ^ brick] for i in range(bricks)], axis=0)
@@ -248,7 +257,7 @@
     result = jnp.zeros((total, rank), jnp.float32)
     for group in range(0, groups, 2):
         node_high, node_low = two_parts(
-            jnp.concatenate([nodes_ref[group], nodes_ref[group + 1]], axis=1)
+            jnp.concatenate([nodes_ref[i, :rows] for i in (group, group + 1)], axis=1)
         )
         product = lax.dot_general(
             lhs,
@@ -462,7 +471,6 @@
     half = slab_cells // cells_x
     height = rank // bricks
     up = [(i, (i + 1) % slabs) for i in range(slabs)]
-    down = [(i, (i - 1) % slabs) for i in range(slabs)]
     own_cells = k_coeffs.reshape(cells, rank)
 
     own_ids = (slab * bricks + brick) * rows + jnp.arange(rows, dtype=jnp.int32)
@@ -476,21 +484,27 @@
         + [jnp.zeros_like(slab_velocity[0])] * 3,
         axis=1,
     )
+    plane = cells // cells_x
+    vector_specs = [pl.BlockSpec(memory_space=pltpu.SMEM)]
+    whole = pl.BlockSpec(memory_space=pltpu.VMEM)
     nodes = exchange(
         pl.pallas_call(
             repeat_kernel,
-            out_shape=f32(slabs, rows, rank),
+            out_shape=f32(slabs, rows + plane, rank),
+            in_specs=vector_specs + [whole] * 2,
             out_specs=pl.BlockSpec(memory_space=pl.ANY),
-            scratch_shapes=[pltpu.SemaphoreType.DMA((slabs,))],
+            scratch_shapes=[pltpu.SemaphoreType.DMA((2, slabs))],
             name="repeat",
             compiler_params=pltpu.CompilerParams(vmem_limit_bytes=VMEM_BYTES),
-        )(v_basis),
+        )(((slab + slabs - 1) % slabs).astype(jnp.int32)[None], v_basis, own_cells),
         "slab",
     )
     k_slab = gather_relative(own_cells, "brick", BRICK_GROUPS)
-    k_edges, k_slab = lax.optimization_barrier((k_coeffs, k_slab))
-    k_below = lax.ppermute(k_edges[-1:], "slab", up)
-    k_above = lax.ppermute(k_edges[:1], "slab", down)
+    below, above = ((slab + shift) % slabs for shift in (slabs - 1, 1))
+    k_below, k_above = (
+        lax.dynamic_slice(nodes, (peer, rows, 0), (1, plane, rank)).reshape(k_coeffs[:1].shape)
+        for peer in (below, above)
+    )
 
     across = velocities(brick * rows + jnp.arange(rows, dtype=jnp.int32))
     columns = [f(across[i]) for i in (1, 2) for f in (lambda v: jnp.maximum(v, 0.0), lambda v: jnp.minimum(v, 0.0))]
@@ -504,8 +518,6 @@
     integrals = exchange(transport_part, "brick")
 
     brick_id = brick.astype(jnp.int32)[None]
-    vector_specs = [pl.BlockSpec(memory_space=pltpu.SMEM)]
-    whole = pl.BlockSpec(memory_space=pltpu.VMEM)
     payload, line, state, vectors = pl.pallas_call(
         maxwell_kernel,
         out_shape=(

time: 162 us -> 163 us (level)
  blocking collectives: 0 us -> 14.2 us
  waiting for transfers between devices: 63.5 us -> 56.2 us
  starting transfers between devices: 67.1 us -> 61.8 us
    all_to_all x0 -> x1, blocking collectives: none -> 14.2 us  [exchange(): return lax.all_to_all(array, axis, 0, 0, tiled=True)]
    all_to_all x5 -> x4, waiting for transfers between devices: 32.4 us -> 20.9 us  [exchange(): return lax.all_to_all(array, axis, 0, 0, tiled=True)]
    ppermute x2 -> x0, starting transfers between devices: 5.68 us -> none  [the longest x1 5.68 us: local(): k_above = lax.ppermute(k_edges[:1], 'slab', down)]
    ppermute x25, waiting for transfers between devices: 30.1 us -> 35.2 us  [from_peer(): return lax.ppermute(values, axis, [(i, i ^ mask) for i in range(peers)])]
    all_to_all x5 -> x4, starting transfers between devices: 24.7 us -> 22.5 us  [exchange(): return lax.all_to_all(array, axis, 0, 0, tiled=True)]
    ppermute x25, starting transfers between devices: 33.6 us -> 35.4 us  [from_peer(): return lax.ppermute(values, axis, [(i, i ^ mask) for i in range(peers)])]
  transfers between devices with their start and end apart: 33 -> 30, of which waited for: 21 -> 20; matrix products, arithmetic and copies ran while one was open for 1% -> 1% of each run, Pallas kernels for 9% -> 7%
where the time goes in v9:
time: 163 us
  starting transfers between devices  61.8 us (38%)
  waiting for transfers between devices  56.2 us (34%)
  Pallas kernels  25.1 us (15%)
  blocking collectives  14.2 us (9%)
  local copies, waits for them, and re-layouts  3.16 us (2%)
    ppermute x25, starting transfers between devices, from_peer(): return lax.ppermute(values, axis, [(i, i ^ mask) for i in range(peers)])  35.4 us
    ppermute x25, waiting for transfers between devices, from_peer(): return lax.ppermute(values, axis, [(i, i ^ mask) for i in range(peers)])  35.2 us
    all_to_all x4, starting transfers between devices, exchange(): return lax.all_to_all(array, axis, 0, 0, tiled=True)  22.5 us
    all_to_all x4, waiting for transfers between devices, exchange(): return lax.all_to_all(array, axis, 0, 0, tiled=True)  20.9 us
    all_to_all x1, blocking collectives, exchange(): return lax.all_to_all(array, axis, 0, 0, tiled=True)  14.2 us
    pallas_call x1, Pallas kernels, local(): pl.pallas_call(functools.partial(middle_kernel, lengths=lengths, time_ste...  6.2 us
    pallas_call x1, Pallas kernels, local(): pl.pallas_call(last_kernel, out_shape=(f32(rank, rank), f32(rows, rank)),...  4.49 us
    ppermute x1, starting transfers between devices, local(): chosen_below = lax.ppermute(chosen, 'slab', up)  3.87 us
  transfers between devices with their start and end apart: 30, of which 20 were waited for; matrix products, arithmetic and copies ran while one was open for 1% of the time, Pallas kernels for 7%

profile of v9, /device:TPU:0, one launch (start us, length us, event | category | flops | bytes accessed | tf_op | source)
XLA Modules:
  0.0 162.8 jit_solution(1164973876988168146)
XLA Ops:
  0.7 0.7 copy-done
  1.5 0.9 copy-done.2
  2.4 1.2 repeat.1
  3.6 7.0 %all-to-all-start = ((f32[8,288,128]{2,1,0:T(8,128)}), f32[8,288,128]{2,1,0:T(8,128)S(1)}, u32[]{:S(2)}, u32[]{:S(2)}) async-start(f32[8,288,128]{2,1,0:T(8,128)} %repeat.1), calls=%async_computation | async-start | bytes 2359296 | tf_op jit(solution)/shard_map/all_to_all | solution.py:34
  10.8 0.1 copy.24
  11.0 0.3 minimum_reduce_fusion
  11.3 0.1 slice_bitcast_fusion.4
  11.4 0.2 and_select_fusion.3
  11.8 0.1 copy.25.columns_ref
  12.1 0.1 stack.61.weights_ref
  12.2 2.0 %collective-permute-start.1 = (f32[2,64,128]{2,1,0:T(8,128)S(1)}, f32[2,64,128]{2,1,0:T(8,128)S(1)}, u32[]{:S(2)}, u32[]{:S(2)}) collective-permute-start(f32[2,64,128]{2,1,0:T(8,128)S(1)} %pad_maximum_fusion.1), channel_id=1, source_target_pairs={{0,2},{1,3},{2,0},{3,1},{4,6},{5,7},{6,4},{7,5},{8,10},{9,11},{10,... | collective-permute-start | bytes 196616 | tf_op jit(solution)/shard_map/ppermute | solution.py:58
  14.2 3.6 %collective-permute-start.2 = (f32[2,64,128]{2,1,0:T(8,128)S(1)}, f32[2,64,128]{2,1,0:T(8,128)S(1)}, u32[]{:S(2)}, u32[]{:S(2)}) collective-permute-start(f32[2,64,128]{2,1,0:T(8,128)S(1)} %pad_maximum_fusion.1), channel_id=1, source_target_pairs={{0,4},{1,5},{2,6},{3,7},{4,0},{5,1},{6,2},{7,3},{8,12},{9,13},{10,... | collective-permute-start | bytes 196616 | tf_op jit(solution)/shard_map/ppermute | solution.py:58
  17.9 3.5 %collective-permute-done.2 = f32[2,64,128]{2,1,0:T(8,128)S(1)} collective-permute-done((f32[2,64,128]{2,1,0:T(8,128)S(1)}, f32[2,64,128]{2,1,0:T(8,128)S(1)}, u32[]{:S(2)}, u32[]{:S(2)}) %collective-permute-start.2) | collective-permute-done | bytes 65568 | tf_op jit(solution)/shard_map/ppermute | solution.py:58
  21.4 1.9 %collective-permute-done.3 = f32[2,64,128]{2,1,0:T(8,128)S(1)} collective-permute-done((f32[2,64,128]{2,1,0:T(8,128)S(1)}, f32[2,64,128]{2,1,0:T(8,128)S(1)}, u32[]{:S(2)}, u32[]{:S(2)}) %collective-permute-start.3) | collective-permute-done | bytes 65568 | tf_op jit(solution)/shard_map/ppermute | solution.py:58
  23.3 0.7 collective-permute-start.4
  24.0 6.7 %collective-permute-done.4 = f32[8,64,128]{2,1,0:T(8,128)S(1)} collective-permute-done((f32[8,64,128]{2,1,0:T(8,128)S(1)}, f32[8,64,128]{2,1,0:T(8,128)S(1)}, u32[]{:S(2)}, u32[]{:S(2)}) %collective-permute-start.4) | collective-permute-done | bytes 262176 | tf_op jit(solution)/shard_map/ppermute | solution.py:58
  30.9 3.1 %transport.1 = f32[16,32,128]{2,1,0:T(8,128)} custom-call(f32[8,288,128]{2,1,0:T(8,128)S(1)} %all-to-all-done.nodes_ref, f32[256,8]{1,0:T(8,128)S(1)} %copy.25.columns_ref, f32[8,128]{1,0:T(8,128)S(1)} %broadcast_in_dim.18.speeds_ref.first_ref, f32[8,8,256]{2,1,0:T(8,128)S(1)} %stack.61.weights_ref), custom_call_target="tpu_custom_call" | custom-call | tf_op jit(solution)/shard_map/transport/pallas_call | solution.py:515
  34.0 6.5 %all-to-all-start.1 = ((f32[16,32,128]{2,1,0:T(8,128)}), f32[16,32,128]{2,1,0:T(8,128)S(1)}, u32[]{:S(2)}, u32[]{:S(2)}) async-start(f32[16,32,128]{2,1,0:T(8,128)} %transport.1), calls=%async_computation.1 | async-start | bytes 524288 | tf_op jit(solution)/shard_map/all_to_all | solution.py:34
  40.6 8.0 %all-to-all-done.1.integrals_ref = f32[16,32,128]{2,1,0:T(8,128)S(1)} async-done(((f32[16,32,128]{2,1,0:T(8,128)}), f32[16,32,128]{2,1,0:T(8,128)S(1)}, u32[]{:S(2)}, u32[]{:S(2)}) %all-to-all-start.1) | async-done | bytes 262176 | tf_op jit(solution)/shard_map/all_to_all | solution.py:34
  48.6 3.7 %maxwell.1 = (f32[16,88,128]{2,1,0:T(8,128)}, f32[1024,8]{1,0:T(8,128)S(1)}, f32[8,1024]{1,0:T(8,128)S(1)}, f32[8,128]{1,0:T(8,128)S(1)}) custom-call(s32[1]{0:T(128)} %bitcast.brick_ref, f32[16,64,128]{2,1,0:T(8,128)S(1)} %constant_dynamic-update-slice_fusion.5.cells_ref, f32[16,32,128]{2,1,0:T(8,128)S(1)} %all-to-all-done.1.integrals_ref, ...), custom_call_target="tpu_custom_call" | custom-call | tf_op jit(solution)/shard_map/maxwell/pallas_call | solution.py:521
  52.2 3.6 %all-to-all-start.2 = ((f32[16,88,128]{2,1,0:T(8,128)}), f32[16,88,128]{2,1,0:T(8,128)S(1)}, u32[]{:S(2)}, u32[]{:S(2)}) async-start(f32[16,88,128]{2,1,0:T(8,128)} %get-tuple-element.23), calls=%async_computation.2 | async-start | bytes 1441792 | tf_op jit(solution)/shard_map/all_to_all | solution.py:34
  55.9 12.9 %all-to-all-done.2.parts_ref = f32[16,88,128]{2,1,0:T(8,128)S(1)} async-done(((f32[16,88,128]{2,1,0:T(8,128)}), f32[16,88,128]{2,1,0:T(8,128)S(1)}, u32[]{:S(2)}, u32[]{:S(2)}) %all-to-all-start.2) | async-done | bytes 720928 | tf_op jit(solution)/shard_map/all_to_all | solution.py:34
  68.8 0.9 advance.1
  69.7 14.2 %all_to_all.25.parts_ref = f32[16,72,128]{2,1,0:T(8,128)S(1)} all-to-all(f32[16,72,128]{2,1,0:T(8,128)S(1)} %get-tuple-element.25), channel_id=1, replica_groups=mesh['slab'=8,'brick'=16] {'brick'}, dimensions={0} | all-to-all | bytes 1179648 | tf_op jit(solution)/shard_map/all_to_all | solution.py:34
  83.9 1.2 products.1
  85.1 3.9 %collective-permute-start.5 = (f32[8,512]{1,0:T(8,128)S(1)}, f32[8,512]{1,0:T(8,128)S(1)}, u32[]{:S(2)}, u32[]{:S(2)}) collective-permute-start(f32[8,512]{1,0:T(8,128)S(1)} %get-tuple-element.28), channel_id=1, source_target_pairs={{0,16},{16,32},{32,48},{48,64},{64,80},{80,96},{96,112},{112,0},{1... | collective-permute-start | bytes 49160 | tf_op jit(solution)/shard_map/ppermute | solution.py:573
  89.0 3.7 %back.1 = f32[8,256,128]{2,1,0:T(8,128)} custom-call(f32[16,72,128]{2,1,0:T(8,128)S(1)} %all_to_all.25.parts_ref, f32[1024,8]{1,0:T(8,128)S(1)} %get-tuple-element.30.line_ref, f32[8,1024]{1,0:T(8,128)S(1)} %get-tuple-element.31.state_ref, f32[256,2]{1,0:T(8,128)S(1)} %get-tuple-element.58.across_ref), custom_call_target="tpu_custom_call" | custom-call | tf_op jit(solution)/shard_map/back/pallas_call | solution.py:576
  92.7 0.2 fusion.31
  93.0 1.6 collective-permute-start.6
  94.6 0.1 copy.27
  94.8 2.6 %collective-permute-start.8 = (f32[40,128]{1,0:T(8,128)S(1)}, f32[40,128]{1,0:T(8,128)S(1)}, u32[]{:S(2)}, u32[]{:S(2)}) collective-permute-start(f32[40,128]{1,0:T(8,128)S(1)} %pad_add_fusion), channel_id=1, source_target_pairs={{0,24},{1,25},{2,26},{3,27},{4,28},{5,29},{6,30},{7,31},{8,16},{9,... | collective-permute-start | bytes 61448 | tf_op jit(solution)/shard_map/ppermute | solution.py:58
  97.4 1.0 collective-permute-done.6
  98.3 0.2 collective-permute-done.7
  98.6 1.3 collective-permute-done.8
  99.9 2.8 %collective-permute-start.10 = (f32[2,40,128]{2,1,0:T(8,128)S(1)}, f32[2,40,128]{2,1,0:T(8,128)S(1)}, u32[]{:S(2)}, u32[]{:S(2)}) collective-permute-start(f32[2,40,128]{2,1,0:T(8,128)S(1)} %pad_maximum_fusion.2), channel_id=1, source_target_pairs={{0,64},{1,65},{2,66},{3,67},{4,68},{5,69},{6,70},{7,71},{8,72},{9,... | collective-permute-start | bytes 122888 | tf_op jit(solution)/shard_map/ppermute | solution.py:58
  102.7 1.3 collective-permute-start.11
  104.0 5.4 %all-to-all-start.4 = ((f32[8,256,128]{2,1,0:T(8,128)}), f32[8,256,128]{2,1,0:T(8,128)S(1)}, u32[]{:S(2)}, u32[]{:S(2)}) async-start(f32[8,256,128]{2,1,0:T(8,128)} %back.1), calls=%async_computation.4 | async-start | bytes 2097152 | tf_op jit(solution)/shard_map/all_to_all | solution.py:34
  109.6 0.3 slice_reduce_fusion
  109.9 0.1 copy.28.speeds_ref
  110.0 0.8 collective-permute-done.12
  110.8 0.6 collective-permute-start.13
  111.3 2.1 %collective-permute-start.14 = (f32[4,40,128]{2,1,0:T(8,128)S(1)}, f32[4,40,128]{2,1,0:T(8,128)S(1)}, u32[]{:S(2)}, u32[]{:S(2)}) collective-permute-start(f32[4,40,128]{2,1,0:T(8,128)S(1)} %pad_maximum_fusion), channel_id=1, source_target_pairs={{0,4},{1,5},{2,6},{3,7},{4,0},{5,1},{6,2},{7,3},{8,12},{9,13},{10,... | collective-permute-start | bytes 245768 | tf_op jit(solution)/shard_map/ppermute | solution.py:58
  113.4 2.1 %collective-permute-start.15 = (f32[4,40,128]{2,1,0:T(8,128)S(1)}, f32[4,40,128]{2,1,0:T(8,128)S(1)}, u32[]{:S(2)}, u32[]{:S(2)}) collective-permute-start(f32[4,40,128]{2,1,0:T(8,128)S(1)} %pad_maximum_fusion), channel_id=1, source_target_pairs={{0,6},{1,7},{2,4},{3,5},{4,2},{5,3},{6,0},{7,1},{8,14},{9,15},{10,... | collective-permute-start | bytes 245768 | tf_op jit(solution)/shard_map/ppermute | solution.py:58
  115.5 0.6 collective-permute-done.13
  116.1 1.7 %collective-permute-done.14 = f32[4,40,128]{2,1,0:T(8,128)S(1)} collective-permute-done((f32[4,40,128]{2,1,0:T(8,128)S(1)}, f32[4,40,128]{2,1,0:T(8,128)S(1)}, u32[]{:S(2)}, u32[]{:S(2)}) %collective-permute-start.14) | collective-permute-done | bytes 81952 | tf_op jit(solution)/shard_map/ppermute | solution.py:58
  117.8 1.7 %collective-permute-done.15 = f32[4,40,128]{2,1,0:T(8,128)S(1)} collective-permute-done((f32[4,40,128]{2,1,0:T(8,128)S(1)}, f32[4,40,128]{2,1,0:T(8,128)S(1)}, u32[]{:S(2)}, u32[]{:S(2)}) %collective-permute-start.15) | collective-permute-done | bytes 81952 | tf_op jit(solution)/shard_map/ppermute | solution.py:58
  119.4 6.2 %middle.1 = (f32[64,128]{1,0:T(8,128)}, f32[256,128]{1,0:T(8,128)S(1)}, f32[128,128]{1,0:T(8,128)S(1)}) custom-call(s32[1]{0:T(128)} %bitcast.brick_ref, f32[16,40,128]{2,1,0:T(8,128)S(1)} %constant_dynamic-update-slice_fusion.23.pieces_ref, f32[6,128,128]{2,1,0:T(8,128)S(1)} %get-tuple-element.33.transport_ref, f32[256,128]{1,0:T(8,128)S(1)} %copy-done.3, ...), custom_call_target="tpu_custom_call" | custom-call | tf_op jit(solution)/shard_map/middle/pallas_call | solution.py:592
  125.6 0.7 update.1
  126.5 1.2 collective-permute-done.16
  127.8 3.5 %collective-permute-start.18 = (f32[128,128]{1,0:T(8,128)S(1)}, f32[128,128]{1,0:T(8,128)S(1)}, u32[]{:S(2)}, u32[]{:S(2)}) collective-permute-start(f32[128,128]{1,0:T(8,128)S(1)} %add.428), channel_id=1, source_target_pairs={{0,4},{1,5},{2,6},{3,7},{4,0},{5,1},{6,2},{7,3},{8,12},{9,13},{10,... | collective-permute-start | bytes 196616 | tf_op jit(solution)/shard_map/ppermute | solution.py:58
  131.3 1.2 collective-permute-start.19
  132.5 0.1 collective-permute-done.17
  132.6 2.3 %collective-permute-done.18 = f32[128,128]{1,0:T(8,128)S(1)} collective-permute-done((f32[128,128]{1,0:T(8,128)S(1)}, f32[128,128]{1,0:T(8,128)S(1)}, u32[]{:S(2)}, u32[]{:S(2)}) %collective-permute-start.18) | collective-permute-done | bytes 65568 | tf_op jit(solution)/shard_map/ppermute | solution.py:58
  134.9 1.9 %collective-permute-done.19 = f32[128,128]{1,0:T(8,128)S(1)} collective-permute-done((f32[128,128]{1,0:T(8,128)S(1)}, f32[128,128]{1,0:T(8,128)S(1)}, u32[]{:S(2)}, u32[]{:S(2)}) %collective-permute-start.19) | collective-permute-done | bytes 65568 | tf_op jit(solution)/shard_map/ppermute | solution.py:58
  136.8 2.1 %collective-permute-start.20 = (f32[128,128]{1,0:T(8,128)S(1)}, f32[128,128]{1,0:T(8,128)S(1)}, u32[]{:S(2)}, u32[]{:S(2)}) collective-permute-start(f32[128,128]{1,0:T(8,128)S(1)} %add_add_fusion.2), channel_id=1, source_target_pairs={{0,8},{1,9},{2,10},{3,11},{4,12},{5,13},{6,14},{7,15},{8,0},{9,1},... | collective-permute-start | bytes 196616 | tf_op jit(solution)/shard_map/ppermute | solution.py:58
  139.0 4.1 %collective-permute-start.21 = (f32[128,128]{1,0:T(8,128)S(1)}, f32[128,128]{1,0:T(8,128)S(1)}, u32[]{:S(2)}, u32[]{:S(2)}) collective-permute-start(f32[128,128]{1,0:T(8,128)S(1)} %add_add_fusion.2), channel_id=1, source_target_pairs={{0,16},{1,17},{2,18},{3,19},{4,20},{5,21},{6,22},{7,23},{8,24},{9,... | collective-permute-start | bytes 196616 | tf_op jit(solution)/shard_map/ppermute | solution.py:58
  143.1 3.0 %collective-permute-done.21 = f32[128,128]{1,0:T(8,128)S(1)} collective-permute-done((f32[128,128]{1,0:T(8,128)S(1)}, f32[128,128]{1,0:T(8,128)S(1)}, u32[]{:S(2)}, u32[]{:S(2)}) %collective-permute-start.21) | collective-permute-done | bytes 65568 | tf_op jit(solution)/shard_map/ppermute | solution.py:58
  146.1 2.4 %collective-permute-done.22 = f32[128,128]{1,0:T(8,128)S(1)} collective-permute-done((f32[128,128]{1,0:T(8,128)S(1)}, f32[128,128]{1,0:T(8,128)S(1)}, u32[]{:S(2)}, u32[]{:S(2)}) %collective-permute-start.22) | collective-permute-done | bytes 65568 | tf_op jit(solution)/shard_map/ppermute | solution.py:58
  148.6 1.5 collective-permute-start.23
  150.1 2.7 %collective-permute-start.24 = (f32[128,128]{1,0:T(8,128)S(1)}, f32[128,128]{1,0:T(8,128)S(1)}, u32[]{:S(2)}, u32[]{:S(2)}) collective-permute-start(f32[128,128]{1,0:T(8,128)S(1)} %add_add_fusion.1), channel_id=1, source_target_pairs={{0,64},{1,65},{2,66},{3,67},{4,68},{5,69},{6,70},{7,71},{8,72},{9,... | collective-permute-start | bytes 196616 | tf_op jit(solution)/shard_map/ppermute | solution.py:58
  152.8 0.6 collective-permute-start.25
  153.4 2.5 %collective-permute-done.24 = f32[128,128]{1,0:T(8,128)S(1)} collective-permute-done((f32[128,128]{1,0:T(8,128)S(1)}, f32[128,128]{1,0:T(8,128)S(1)}, u32[]{:S(2)}, u32[]{:S(2)}) %collective-permute-start.24) | collective-permute-done | bytes 65568 | tf_op jit(solution)/shard_map/ppermute | solution.py:58
  155.9 2.4 %collective-permute-done.25 = f32[128,128]{1,0:T(8,128)S(1)} collective-permute-done((f32[128,128]{1,0:T(8,128)S(1)}, f32[128,128]{1,0:T(8,128)S(1)}, u32[]{:S(2)}, u32[]{:S(2)}) %collective-permute-start.25) | collective-permute-done | bytes 65568 | tf_op jit(solution)/shard_map/ppermute | solution.py:58
  158.3 4.5 %last.1 = (f32[128,128]{1,0:T(8,128)}, f32[256,128]{1,0:T(8,128)}) custom-call(f32[128,128]{1,0:T(8,128)S(1)} %add_add_fusion.gram_ref, f32[256,128]{1,0:T(8,128)S(1)} %get-tuple-element.40.velocity_ref), custom_call_target="tpu_custom_call" | custom-call | tf_op jit(solution)/shard_map/last/pallas_call | solution.py:609
  (91 shorter events, 1.3 us)
Async XLA Ops:
  0.6 11.6 %collective-permute-start = (f32[1,64,128]{2,1,0:T(8,128)}, f32[1,64,128]{2,1,0:T(8,128)S(1)}, u32[]{:S(2)}, u32[]{:S(2)}) collective-permute-start(f32[1,64,128]{2,1,0:T(8,128)} %bitcast.48), channel_id=1, source_target_pairs={{0,1},{1,0},{2,3},{3,2},{4,5},{5,4},{6,7},{7,6},{8,9},{9,8},{10,11... | collective-permute-start | bytes 98312 | tf_op jit(solution)/shard_map/ppermute | solution.py:58
  0.7 0.8 copy-start
  1.5 0.9 copy-start.2
  3.6 7.0 %copy-start.1 = (f32[2,2,16,128]{3,2,1,0:T(8,128)S(1)}, f32[2,2,16,128]{3,2,1,0:T(8,128)}, u32[]{:S(2)}) copy-start(f32[2,2,16,128]{3,2,1,0:T(8,128)} %param.2) | copy-start | bytes 98308
  3.6 27.2 %all-to-all-start = ((f32[8,288,128]{2,1,0:T(8,128)}), f32[8,288,128]{2,1,0:T(8,128)S(1)}, u32[]{:S(2)}, u32[]{:S(2)}) async-start(f32[8,288,128]{2,1,0:T(8,128)} %repeat.1), calls=%async_computation | async-start | bytes 2359296 | tf_op jit(solution)/shard_map/all_to_all | solution.py:34
  12.2 5.6 %collective-permute-start.1 = (f32[2,64,128]{2,1,0:T(8,128)S(1)}, f32[2,64,128]{2,1,0:T(8,128)S(1)}, u32[]{:S(2)}, u32[]{:S(2)}) collective-permute-start(f32[2,64,128]{2,1,0:T(8,128)S(1)} %pad_maximum_fusion.1), channel_id=1, source_target_pairs={{0,2},{1,3},{2,0},{3,1},{4,6},{5,7},{6,4},{7,5},{8,10},{9,11},{10,... | collective-permute-start | bytes 196616 | tf_op jit(solution)/shard_map/ppermute | solution.py:58
  14.2 7.2 %collective-permute-start.2 = (f32[2,64,128]{2,1,0:T(8,128)S(1)}, f32[2,64,128]{2,1,0:T(8,128)S(1)}, u32[]{:S(2)}, u32[]{:S(2)}) collective-permute-start(f32[2,64,128]{2,1,0:T(8,128)S(1)} %pad_maximum_fusion.1), channel_id=1, source_target_pairs={{0,4},{1,5},{2,6},{3,7},{4,0},{5,1},{6,2},{7,3},{8,12},{9,13},{10,... | collective-permute-start | bytes 196616 | tf_op jit(solution)/shard_map/ppermute | solution.py:58
  17.8 5.5 %collective-permute-start.3 = (f32[2,64,128]{2,1,0:T(8,128)S(1)}, f32[2,64,128]{2,1,0:T(8,128)S(1)}, u32[]{:S(2)}, u32[]{:S(2)}) collective-permute-start(f32[2,64,128]{2,1,0:T(8,128)S(1)} %pad_maximum_fusion.1), channel_id=1, source_target_pairs={{0,6},{1,7},{2,4},{3,5},{4,2},{5,3},{6,0},{7,1},{8,14},{9,15},{10,... | collective-permute-start | bytes 196616 | tf_op jit(solution)/shard_map/ppermute | solution.py:58
  23.3 7.4 %collective-permute-start.4 = (f32[8,64,128]{2,1,0:T(8,128)S(1)}, f32[8,64,128]{2,1,0:T(8,128)S(1)}, u32[]{:S(2)}, u32[]{:S(2)}) collective-permute-start(f32[8,64,128]{2,1,0:T(8,128)S(1)} %get-tuple-element.60), channel_id=1, source_target_pairs={{0,8},{1,9},{2,10},{3,11},{4,12},{5,13},{6,14},{7,15},{8,0},{9,1},... | collective-permute-start | bytes 786440 | tf_op jit(solution)/shard_map/ppermute | solution.py:58
  34.0 14.5 %all-to-all-start.1 = ((f32[16,32,128]{2,1,0:T(8,128)}), f32[16,32,128]{2,1,0:T(8,128)S(1)}, u32[]{:S(2)}, u32[]{:S(2)}) async-start(f32[16,32,128]{2,1,0:T(8,128)} %transport.1), calls=%async_computation.1 | async-start | bytes 524288 | tf_op jit(solution)/shard_map/all_to_all | solution.py:34
  52.2 16.6 %all-to-all-start.2 = ((f32[16,88,128]{2,1,0:T(8,128)}), f32[16,88,128]{2,1,0:T(8,128)S(1)}, u32[]{:S(2)}, u32[]{:S(2)}) async-start(f32[16,88,128]{2,1,0:T(8,128)} %get-tuple-element.23), calls=%async_computation.2 | async-start | bytes 1441792 | tf_op jit(solution)/shard_map/all_to_all | solution.py:34
  85.1 7.6 %collective-permute-start.5 = (f32[8,512]{1,0:T(8,128)S(1)}, f32[8,512]{1,0:T(8,128)S(1)}, u32[]{:S(2)}, u32[]{:S(2)}) collective-permute-start(f32[8,512]{1,0:T(8,128)S(1)} %get-tuple-element.28), channel_id=1, source_target_pairs={{0,16},{16,32},{32,48},{48,64},{64,80},{80,96},{96,112},{112,0},{1... | collective-permute-start | bytes 49160 | tf_op jit(solution)/shard_map/ppermute | solution.py:573
  93.0 5.4 %collective-permute-start.6 = (f32[40,128]{1,0:T(8,128)S(1)}, f32[40,128]{1,0:T(8,128)S(1)}, u32[]{:S(2)}, u32[]{:S(2)}) collective-permute-start(f32[40,128]{1,0:T(8,128)S(1)} %pad_add_fusion), channel_id=1, source_target_pairs={{0,16},{1,17},{2,18},{3,19},{4,20},{5,21},{6,22},{7,23},{8,24},{9,... | collective-permute-start | bytes 61448 | tf_op jit(solution)/shard_map/ppermute | solution.py:58
  94.7 3.9 %collective-permute-start.7 = (f32[40,128]{1,0:T(8,128)S(1)}, f32[40,128]{1,0:T(8,128)S(1)}, u32[]{:S(2)}, u32[]{:S(2)}) collective-permute-start(f32[40,128]{1,0:T(8,128)S(1)} %pad_add_fusion), channel_id=1, source_target_pairs={{0,8},{1,9},{2,10},{3,11},{4,12},{5,13},{6,14},{7,15},{8,0},{9,1},... | collective-permute-start | bytes 61448 | tf_op jit(solution)/shard_map/ppermute | solution.py:58
  94.8 5.1 %collective-permute-start.8 = (f32[40,128]{1,0:T(8,128)S(1)}, f32[40,128]{1,0:T(8,128)S(1)}, u32[]{:S(2)}, u32[]{:S(2)}) collective-permute-start(f32[40,128]{1,0:T(8,128)S(1)} %pad_add_fusion), channel_id=1, source_target_pairs={{0,24},{1,25},{2,26},{3,27},{4,28},{5,29},{6,30},{7,31},{8,16},{9,... | collective-permute-start | bytes 61448 | tf_op jit(solution)/shard_map/ppermute | solution.py:58
  99.9 9.5 %collective-permute-start.10 = (f32[2,40,128]{2,1,0:T(8,128)S(1)}, f32[2,40,128]{2,1,0:T(8,128)S(1)}, u32[]{:S(2)}, u32[]{:S(2)}) collective-permute-start(f32[2,40,128]{2,1,0:T(8,128)S(1)} %pad_maximum_fusion.2), channel_id=1, source_target_pairs={{0,64},{1,65},{2,66},{3,67},{4,68},{5,69},{6,70},{7,71},{8,72},{9,... | collective-permute-start | bytes 122888 | tf_op jit(solution)/shard_map/ppermute | solution.py:58
  102.7 6.8 %collective-permute-start.11 = (f32[2,40,128]{2,1,0:T(8,128)S(1)}, f32[2,40,128]{2,1,0:T(8,128)S(1)}, u32[]{:S(2)}, u32[]{:S(2)}) collective-permute-start(f32[2,40,128]{2,1,0:T(8,128)S(1)} %pad_maximum_fusion.2), channel_id=1, source_target_pairs={{0,96},{1,97},{2,98},{3,99},{4,100},{5,101},{6,102},{7,103},{8,104... | collective-permute-start | bytes 122888 | tf_op jit(solution)/shard_map/ppermute | solution.py:58
  104.0 5.5 %collective-permute-start.9 = (f32[2,40,128]{2,1,0:T(8,128)S(1)}, f32[2,40,128]{2,1,0:T(8,128)S(1)}, u32[]{:S(2)}, u32[]{:S(2)}) collective-permute-start(f32[2,40,128]{2,1,0:T(8,128)S(1)} %pad_maximum_fusion.2), channel_id=1, source_target_pairs={{0,32},{1,33},{2,34},{3,35},{4,36},{5,37},{6,38},{7,39},{8,40},{9,... | collective-permute-start | bytes 122888 | tf_op jit(solution)/shard_map/ppermute | solution.py:58
  104.0 21.6 %all-to-all-start.4 = ((f32[8,256,128]{2,1,0:T(8,128)}), f32[8,256,128]{2,1,0:T(8,128)S(1)}, u32[]{:S(2)}, u32[]{:S(2)}) async-start(f32[8,256,128]{2,1,0:T(8,128)} %back.1), calls=%async_computation.4 | async-start | bytes 2097152 | tf_op jit(solution)/shard_map/all_to_all | solution.py:34
  109.4 10.0 %copy-start.3 = (f32[256,128]{1,0:T(8,128)S(1)}, f32[256,128]{1,0:T(8,128)}, u32[]{:S(2)}) copy-start(f32[256,128]{1,0:T(8,128)} %basis_ref.1) | copy-start | bytes 393220
  109.5 1.3 collective-permute-start.12
  110.8 5.3 %collective-permute-start.13 = (f32[4,40,128]{2,1,0:T(8,128)S(1)}, f32[4,40,128]{2,1,0:T(8,128)S(1)}, u32[]{:S(2)}, u32[]{:S(2)}) collective-permute-start(f32[4,40,128]{2,1,0:T(8,128)S(1)} %pad_maximum_fusion), channel_id=1, source_target_pairs={{0,2},{1,3},{2,0},{3,1},{4,6},{5,7},{6,4},{7,5},{8,10},{9,11},{10,... | collective-permute-start | bytes 245768 | tf_op jit(solution)/shard_map/ppermute | solution.py:58
  111.3 6.4 %collective-permute-start.14 = (f32[4,40,128]{2,1,0:T(8,128)S(1)}, f32[4,40,128]{2,1,0:T(8,128)S(1)}, u32[]{:S(2)}, u32[]{:S(2)}) collective-permute-start(f32[4,40,128]{2,1,0:T(8,128)S(1)} %pad_maximum_fusion), channel_id=1, source_target_pairs={{0,4},{1,5},{2,6},{3,7},{4,0},{5,1},{6,2},{7,3},{8,12},{9,13},{10,... | collective-permute-start | bytes 245768 | tf_op jit(solution)/shard_map/ppermute | solution.py:58
  113.4 6.0 %collective-permute-start.15 = (f32[4,40,128]{2,1,0:T(8,128)S(1)}, f32[4,40,128]{2,1,0:T(8,128)S(1)}, u32[]{:S(2)}, u32[]{:S(2)}) collective-permute-start(f32[4,40,128]{2,1,0:T(8,128)S(1)} %pad_maximum_fusion), channel_id=1, source_target_pairs={{0,6},{1,7},{2,4},{3,5},{4,2},{5,3},{6,0},{7,1},{8,14},{9,15},{10,... | collective-permute-start | bytes 245768 | tf_op jit(solution)/shard_map/ppermute | solution.py:58
  126.4 1.3 collective-permute-start.16
  127.7 4.9 %collective-permute-start.17 = (f32[128,128]{1,0:T(8,128)S(1)}, f32[128,128]{1,0:T(8,128)S(1)}, u32[]{:S(2)}, u32[]{:S(2)}) collective-permute-start(f32[128,128]{1,0:T(8,128)S(1)} %add.428), channel_id=1, source_target_pairs={{0,2},{1,3},{2,0},{3,1},{4,6},{5,7},{6,4},{7,5},{8,10},{9,11},{10,... | collective-permute-start | bytes 196616 | tf_op jit(solution)/shard_map/ppermute | solution.py:58
  127.8 7.1 %collective-permute-start.18 = (f32[128,128]{1,0:T(8,128)S(1)}, f32[128,128]{1,0:T(8,128)S(1)}, u32[]{:S(2)}, u32[]{:S(2)}) collective-permute-start(f32[128,128]{1,0:T(8,128)S(1)} %add.428), channel_id=1, source_target_pairs={{0,4},{1,5},{2,6},{3,7},{4,0},{5,1},{6,2},{7,3},{8,12},{9,13},{10,... | collective-permute-start | bytes 196616 | tf_op jit(solution)/shard_map/ppermute | solution.py:58
  131.3 5.5 %collective-permute-start.19 = (f32[128,128]{1,0:T(8,128)S(1)}, f32[128,128]{1,0:T(8,128)S(1)}, u32[]{:S(2)}, u32[]{:S(2)}) collective-permute-start(f32[128,128]{1,0:T(8,128)S(1)} %add.428), channel_id=1, source_target_pairs={{0,6},{1,7},{2,4},{3,5},{4,2},{5,3},{6,0},{7,1},{8,14},{9,15},{10,... | collective-permute-start | bytes 196616 | tf_op jit(solution)/shard_map/ppermute | solution.py:58
  136.8 6.3 %collective-permute-start.20 = (f32[128,128]{1,0:T(8,128)S(1)}, f32[128,128]{1,0:T(8,128)S(1)}, u32[]{:S(2)}, u32[]{:S(2)}) collective-permute-start(f32[128,128]{1,0:T(8,128)S(1)} %add_add_fusion.2), channel_id=1, source_target_pairs={{0,8},{1,9},{2,10},{3,11},{4,12},{5,13},{6,14},{7,15},{8,0},{9,1},... | collective-permute-start | bytes 196616 | tf_op jit(solution)/shard_map/ppermute | solution.py:58
  139.0 7.2 %collective-permute-start.21 = (f32[128,128]{1,0:T(8,128)S(1)}, f32[128,128]{1,0:T(8,128)S(1)}, u32[]{:S(2)}, u32[]{:S(2)}) collective-permute-start(f32[128,128]{1,0:T(8,128)S(1)} %add_add_fusion.2), channel_id=1, source_target_pairs={{0,16},{1,17},{2,18},{3,19},{4,20},{5,21},{6,22},{7,23},{8,24},{9,... | collective-permute-start | bytes 196616 | tf_op jit(solution)/shard_map/ppermute | solution.py:58
  143.1 5.5 %collective-permute-start.22 = (f32[128,128]{1,0:T(8,128)S(1)}, f32[128,128]{1,0:T(8,128)S(1)}, u32[]{:S(2)}, u32[]{:S(2)}) collective-permute-start(f32[128,128]{1,0:T(8,128)S(1)} %add_add_fusion.2), channel_id=1, source_target_pairs={{0,24},{1,25},{2,26},{3,27},{4,28},{5,29},{6,30},{7,31},{8,16},{9,... | collective-permute-start | bytes 196616 | tf_op jit(solution)/shard_map/ppermute | solution.py:58
  148.6 4.8 %collective-permute-start.23 = (f32[128,128]{1,0:T(8,128)S(1)}, f32[128,128]{1,0:T(8,128)S(1)}, u32[]{:S(2)}, u32[]{:S(2)}) collective-permute-start(f32[128,128]{1,0:T(8,128)S(1)} %add_add_fusion.1), channel_id=1, source_target_pairs={{0,32},{1,33},{2,34},{3,35},{4,36},{5,37},{6,38},{7,39},{8,40},{9,... | collective-permute-start | bytes 196616 | tf_op jit(solution)/shard_map/ppermute | solution.py:58
  150.1 5.8 %collective-permute-start.24 = (f32[128,128]{1,0:T(8,128)S(1)}, f32[128,128]{1,0:T(8,128)S(1)}, u32[]{:S(2)}, u32[]{:S(2)}) collective-permute-start(f32[128,128]{1,0:T(8,128)S(1)} %add_add_fusion.1), channel_id=1, source_target_pairs={{0,64},{1,65},{2,66},{3,67},{4,68},{5,69},{6,70},{7,71},{8,72},{9,... | collective-permute-start | bytes 196616 | tf_op jit(solution)/shard_map/ppermute | solution.py:58
  152.8 5.5 %collective-permute-start.25 = (f32[128,128]{1,0:T(8,128)S(1)}, f32[128,128]{1,0:T(8,128)S(1)}, u32[]{:S(2)}, u32[]{:S(2)}) collective-permute-start(f32[128,128]{1,0:T(8,128)S(1)} %add_add_fusion.1), channel_id=1, source_target_pairs={{0,96},{1,97},{2,98},{3,99},{4,100},{5,101},{6,102},{7,103},{8,104... | collective-permute-start | bytes 196616 | tf_op jit(solution)/shard_map/ppermute | solution.py:58

commit v10 on v9

--- a/solution.py
+++ b/solution.py
@@ -82,7 +82,11 @@
     return array
 
 
-BRICK_GROUPS = ((1,), (2, 4, 6), (8,))
+def slot_of(mask):
+    return (mask & 1) * 8 + ((mask >> 1) & 3) * 2 + (mask >> 3)
+
+
+BRICK_GROUPS = ((8,), (2, 4, 6), (1,))
 ALL_GROUPS = ((1,), (2, 4, 6), (8, 16, 24), (32, 64, 96))
 
 
@@ -232,7 +236,7 @@
     groups, rows = nodes_ref.shape[0], across_ref.shape[1]
     total = bricks * cells
     brick = brick_ref[0]
-    k_flat = jnp.concatenate([cells_ref[i ^ brick] for i in range(bricks)], axis=0)
+    k_flat = jnp.concatenate([cells_ref[slot_of(i ^ brick)] for i in range(bricks)], axis=0)
     integrals = integrals_ref[0]
     for i in range(1, bricks):
         integrals = integrals + integrals_ref[i]
@@ -395,7 +399,7 @@
     rows = basis_ref.shape[0]
     height = rank // bricks
     masks = [j ^ brick_ref[0] for j in range(bricks)]
-    slots = [((m >> 1) & 3) * 4 + (m & 1) * 2 + (m >> 3) for m in masks]
+    slots = [slot_of(mask) for mask in masks]
 
     def piece(ref, i):
         if ref is transport_ref:
@@ -516,6 +520,7 @@
         transport_kernel, out_shape=f32(bricks, 8 + 3 * height, rank), name="transport", compiler_params=pltpu.CompilerParams(vmem_limit_bytes=VMEM_BYTES)
     )(nodes, columns, first_speeds, weights)
     integrals = exchange(transport_part, "brick")
+    k_slab, _ = lax.optimization_barrier((k_slab, transport_part))
 
     brick_id = brick.astype(jnp.int32)[None]
     payload, line, state, vectors = pl.pallas_call(
@@ -532,8 +537,8 @@
     second = exchange(payload, "brick")
 
     slab_grid = k_slab.reshape(bricks, cells_x, cells_y, cells_z, rank)
-    left = ((brick - 1) % bricks) ^ brick
-    right = ((brick + 1) % bricks) ^ brick
+    left = slot_of(((brick - 1) % bricks) ^ brick)
+    right = slot_of(((brick + 1) % bricks) ^ brick)
     left = lax.dynamic_index_in_dim(slab_grid, left, 0, keepdims=False)
     right = lax.dynamic_index_in_dim(slab_grid, right, 0, keepdims=False)
     lower = [
@@ -586,7 +591,7 @@
     lower_x, upper_x, cross_x = (from_peer(pieces, both, mask) for mask in (8, 16, 24))
     reduced = jnp.stack([pieces + upper_x, lower_x + cross_x])
     reduced = sum_over(reduced, both, ((32, 64, 96),))
-    reduced = gather_more(reduced, both, ((1,), (2, 4, 6)))
+    reduced = gather_more(reduced, both, ((2, 4, 6), (1,)))
 
     speeds = jnp.stack(list(own_velocity) + [jnp.zeros_like(ones)] * 5, axis=1)
     basis_new, velocity_part, inverse = pl.pallas_call(

time: 163 us -> 167 us (1.025)
  waiting for transfers between devices: 56.2 us -> 62.5 us
  starting transfers between devices: 61.8 us -> 59.4 us
    ppermute x25, waiting for transfers between devices: 35.2 us -> 41.5 us  [from_peer(): return lax.ppermute(values, axis, [(i, i ^ mask) for i in range(peers)])]
    all_to_all x4, starting transfers between devices: 22.5 us -> 19.7 us  [exchange(): return lax.all_to_all(array, axis, 0, 0, tiled=True)]
  transfers between devices with their start and end apart: 30 -> 30, of which waited for: 20 -> 21; matrix products, arithmetic and copies ran while one was open for 1% -> 1% of each run, Pallas kernels for 7% -> 6%
where the time goes in v10:
time: 167 us
  waiting for transfers between devices  62.5 us (37%)
  starting transfers between devices  59.4 us (36%)
  Pallas kernels  25.1 us (15%)
  blocking collectives  14.2 us (9%)
  local copies, waits for them, and re-layouts  3.12 us (2%)
    ppermute x25, waiting for transfers between devices, from_peer(): return lax.ppermute(values, axis, [(i, i ^ mask) for i in range(peers)])  41.5 us
    ppermute x25, starting transfers between devices, from_peer(): return lax.ppermute(values, axis, [(i, i ^ mask) for i in range(peers)])  35.6 us
    all_to_all x4, waiting for transfers between devices, exchange(): return lax.all_to_all(array, axis, 0, 0, tiled=True)  20.9 us
    all_to_all x4, starting transfers between devices, exchange(): return lax.all_to_all(array, axis, 0, 0, tiled=True)  19.7 us
    all_to_all x1, blocking collectives, exchange(): return lax.all_to_all(array, axis, 0, 0, tiled=True)  14.2 us
    pallas_call x1, Pallas kernels, local(): pl.pallas_call(functools.partial(middle_kernel, lengths=lengths, time_ste...  6.2 us
    pallas_call x1, Pallas kernels, local(): pl.pallas_call(last_kernel, out_shape=(f32(rank, rank), f32(rows, rank)),...  4.49 us
    ppermute x1, starting transfers between devices, local(): chosen_below = lax.ppermute(chosen, 'slab', up)  4.1 us
  transfers between devices with their start and end apart: 30, of which 21 were waited for; matrix products, arithmetic and copies ran while one was open for 1% of the time, Pallas kernels for 6%

profile of v10, /device:TPU:0, one launch (start us, length us, event | category | flops | bytes accessed | tf_op | source)
XLA Modules:
  0.0 166.7 jit_solution(2474377057122906363)
XLA Ops:
  0.7 0.7 copy-done
  1.4 0.9 copy-done.2
  2.3 1.2 repeat.1
  3.5 7.0 %all-to-all-start = ((f32[8,288,128]{2,1,0:T(8,128)}), f32[8,288,128]{2,1,0:T(8,128)S(1)}, u32[]{:S(2)}, u32[]{:S(2)}) async-start(f32[8,288,128]{2,1,0:T(8,128)} %repeat.1), calls=%async_computation | async-start | bytes 2359296 | tf_op jit(solution)/shard_map/all_to_all | solution.py:34
  10.5 0.7 collective-permute-start
  11.4 0.1 copy.24
  11.5 0.2 and_select_fusion.3
  11.8 0.1 slice_bitcast_fusion.4
  12.0 13.1 %collective-permute-done = f32[1,64,128]{2,1,0:T(8,128)S(1)} collective-permute-done((f32[1,64,128]{2,1,0:T(8,128)S(1)}, f32[1,64,128]{2,1,0:T(8,128)S(1)}, u32[]{:S(2)}, u32[]{:S(2)}) %collective-permute-start) | collective-permute-done | bytes 32800 | tf_op jit(solution)/shard_map/ppermute | solution.py:58
  25.1 1.9 %collective-permute-start.1 = (f32[2,64,128]{2,1,0:T(8,128)S(1)}, f32[2,64,128]{2,1,0:T(8,128)S(1)}, u32[]{:S(2)}, u32[]{:S(2)}) collective-permute-start(f32[2,64,128]{2,1,0:T(8,128)S(1)} %pad_maximum_fusion.1), channel_id=1, source_target_pairs={{0,2},{1,3},{2,0},{3,1},{4,6},{5,7},{6,4},{7,5},{8,10},{9,11},{10,... | collective-permute-start | bytes 196616 | tf_op jit(solution)/shard_map/ppermute | solution.py:58
  27.0 3.6 %collective-permute-start.2 = (f32[2,64,128]{2,1,0:T(8,128)S(1)}, f32[2,64,128]{2,1,0:T(8,128)S(1)}, u32[]{:S(2)}, u32[]{:S(2)}) collective-permute-start(f32[2,64,128]{2,1,0:T(8,128)S(1)} %pad_maximum_fusion.1), channel_id=1, source_target_pairs={{0,4},{1,5},{2,6},{3,7},{4,0},{5,1},{6,2},{7,3},{8,12},{9,13},{10,... | collective-permute-start | bytes 196616 | tf_op jit(solution)/shard_map/ppermute | solution.py:58
  30.6 3.0 %collective-permute-done.2 = f32[2,64,128]{2,1,0:T(8,128)S(1)} collective-permute-done((f32[2,64,128]{2,1,0:T(8,128)S(1)}, f32[2,64,128]{2,1,0:T(8,128)S(1)}, u32[]{:S(2)}, u32[]{:S(2)}) %collective-permute-start.2) | collective-permute-done | bytes 65568 | tf_op jit(solution)/shard_map/ppermute | solution.py:58
  33.6 2.4 %collective-permute-done.3 = f32[2,64,128]{2,1,0:T(8,128)S(1)} collective-permute-done((f32[2,64,128]{2,1,0:T(8,128)S(1)}, f32[2,64,128]{2,1,0:T(8,128)S(1)}, u32[]{:S(2)}, u32[]{:S(2)}) %collective-permute-start.3) | collective-permute-done | bytes 65568 | tf_op jit(solution)/shard_map/ppermute | solution.py:58
  36.2 0.3 minimum_reduce_fusion
  36.6 0.1 copy.25.columns_ref
  37.0 0.7 collective-permute-done.4
  37.8 3.1 %transport.1 = f32[16,32,128]{2,1,0:T(8,128)} custom-call(f32[8,288,128]{2,1,0:T(8,128)S(1)} %all-to-all-done.nodes_ref, f32[256,8]{1,0:T(8,128)S(1)} %copy.25.columns_ref, f32[8,128]{1,0:T(8,128)S(1)} %broadcast_in_dim.18.speeds_ref.first_ref, f32[8,8,256]{2,1,0:T(8,128)S(1)} %stack.61.weights_ref), custom_call_target="tpu_custom_call" | custom-call | tf_op jit(solution)/shard_map/transport/pallas_call | solution.py:519
  40.9 3.5 %all-to-all-start.1 = ((f32[16,32,128]{2,1,0:T(8,128)}), f32[16,32,128]{2,1,0:T(8,128)S(1)}, u32[]{:S(2)}, u32[]{:S(2)}) async-start(f32[16,32,128]{2,1,0:T(8,128)} %transport.1), calls=%async_computation.1 | async-start | bytes 524288 | tf_op jit(solution)/shard_map/all_to_all | solution.py:34
  44.5 7.9 %all-to-all-done.1.integrals_ref = f32[16,32,128]{2,1,0:T(8,128)S(1)} async-done(((f32[16,32,128]{2,1,0:T(8,128)}), f32[16,32,128]{2,1,0:T(8,128)S(1)}, u32[]{:S(2)}, u32[]{:S(2)}) %all-to-all-start.1) | async-done | bytes 262176 | tf_op jit(solution)/shard_map/all_to_all | solution.py:34
  52.4 3.7 %maxwell.1 = (f32[16,88,128]{2,1,0:T(8,128)}, f32[1024,8]{1,0:T(8,128)S(1)}, f32[8,1024]{1,0:T(8,128)S(1)}, f32[8,128]{1,0:T(8,128)S(1)}) custom-call(s32[1]{0:T(128)} %bitcast.brick_ref, f32[16,64,128]{2,1,0:T(8,128)S(1)} %constant_dynamic-update-slice_fusion.5.cells_ref, f32[16,32,128]{2,1,0:T(8,128)S(1)} %all-to-all-done.1.integrals_ref, ...), custom_call_target="tpu_custom_call" | custom-call | tf_op jit(solution)/shard_map/maxwell/pallas_call | solution.py:526
  56.1 3.6 %all-to-all-start.2 = ((f32[16,88,128]{2,1,0:T(8,128)}), f32[16,88,128]{2,1,0:T(8,128)S(1)}, u32[]{:S(2)}, u32[]{:S(2)}) async-start(f32[16,88,128]{2,1,0:T(8,128)} %get-tuple-element.25), calls=%async_computation.2 | async-start | bytes 1441792 | tf_op jit(solution)/shard_map/all_to_all | solution.py:34
  59.8 12.9 %all-to-all-done.2.parts_ref = f32[16,88,128]{2,1,0:T(8,128)S(1)} async-done(((f32[16,88,128]{2,1,0:T(8,128)}), f32[16,88,128]{2,1,0:T(8,128)S(1)}, u32[]{:S(2)}, u32[]{:S(2)}) %all-to-all-start.2) | async-done | bytes 720928 | tf_op jit(solution)/shard_map/all_to_all | solution.py:34
  72.7 0.9 advance.1
  73.6 14.2 %all_to_all.25.parts_ref = f32[16,72,128]{2,1,0:T(8,128)S(1)} all-to-all(f32[16,72,128]{2,1,0:T(8,128)S(1)} %get-tuple-element.27), channel_id=1, replica_groups=mesh['slab'=8,'brick'=16] {'brick'}, dimensions={0} | all-to-all | bytes 1179648 | tf_op jit(solution)/shard_map/all_to_all | solution.py:34
  87.8 1.2 products.1
  89.0 4.1 %collective-permute-start.5 = (f32[8,512]{1,0:T(8,128)S(1)}, f32[8,512]{1,0:T(8,128)S(1)}, u32[]{:S(2)}, u32[]{:S(2)}) collective-permute-start(f32[8,512]{1,0:T(8,128)S(1)} %get-tuple-element.30), channel_id=1, source_target_pairs={{0,16},{16,32},{32,48},{48,64},{64,80},{80,96},{96,112},{112,0},{1... | collective-permute-start | bytes 49160 | tf_op jit(solution)/shard_map/ppermute | solution.py:578
  93.1 3.7 %back.1 = f32[8,256,128]{2,1,0:T(8,128)} custom-call(f32[16,72,128]{2,1,0:T(8,128)S(1)} %all_to_all.25.parts_ref, f32[1024,8]{1,0:T(8,128)S(1)} %get-tuple-element.32.line_ref, f32[8,1024]{1,0:T(8,128)S(1)} %get-tuple-element.33.state_ref, f32[256,2]{1,0:T(8,128)S(1)} %get-tuple-element.60.across_ref), custom_call_target="tpu_custom_call" | custom-call | tf_op jit(solution)/shard_map/back/pallas_call | solution.py:581
  96.8 0.1 collective-permute-done.5
  96.9 0.2 fusion.31
  97.2 1.5 collective-permute-start.6
  98.7 0.1 copy.27
  98.9 2.7 %collective-permute-start.8 = (f32[40,128]{1,0:T(8,128)S(1)}, f32[40,128]{1,0:T(8,128)S(1)}, u32[]{:S(2)}, u32[]{:S(2)}) collective-permute-start(f32[40,128]{1,0:T(8,128)S(1)} %pad_add_fusion), channel_id=1, source_target_pairs={{0,24},{1,25},{2,26},{3,27},{4,28},{5,29},{6,30},{7,31},{8,16},{9,... | collective-permute-start | bytes 61448 | tf_op jit(solution)/shard_map/ppermute | solution.py:58
  101.6 1.0 collective-permute-done.6
  102.5 0.1 collective-permute-done.7
  102.7 1.3 collective-permute-done.8
  104.0 3.0 %collective-permute-start.10 = (f32[2,40,128]{2,1,0:T(8,128)S(1)}, f32[2,40,128]{2,1,0:T(8,128)S(1)}, u32[]{:S(2)}, u32[]{:S(2)}) collective-permute-start(f32[2,40,128]{2,1,0:T(8,128)S(1)} %pad_maximum_fusion.2), channel_id=1, source_target_pairs={{0,64},{1,65},{2,66},{3,67},{4,68},{5,69},{6,70},{7,71},{8,72},{9,... | collective-permute-start | bytes 122888 | tf_op jit(solution)/shard_map/ppermute | solution.py:58
  107.0 1.2 collective-permute-start.11
  108.2 5.5 %all-to-all-start.4 = ((f32[8,256,128]{2,1,0:T(8,128)}), f32[8,256,128]{2,1,0:T(8,128)S(1)}, u32[]{:S(2)}, u32[]{:S(2)}) async-start(f32[8,256,128]{2,1,0:T(8,128)} %back.1), calls=%async_computation.4 | async-start | bytes 2097152 | tf_op jit(solution)/shard_map/all_to_all | solution.py:34
  113.8 0.6 collective-permute-start.12
  114.5 2.1 %collective-permute-start.13 = (f32[2,40,128]{2,1,0:T(8,128)S(1)}, f32[2,40,128]{2,1,0:T(8,128)S(1)}, u32[]{:S(2)}, u32[]{:S(2)}) collective-permute-start(f32[2,40,128]{2,1,0:T(8,128)S(1)} %get-tuple-element.53), channel_id=1, source_target_pairs={{0,4},{1,5},{2,6},{3,7},{4,0},{5,1},{6,2},{7,3},{8,12},{9,13},{10,... | collective-permute-start | bytes 122888 | tf_op jit(solution)/shard_map/ppermute | solution.py:58
  116.6 2.1 %collective-permute-start.14 = (f32[2,40,128]{2,1,0:T(8,128)S(1)}, f32[2,40,128]{2,1,0:T(8,128)S(1)}, u32[]{:S(2)}, u32[]{:S(2)}) collective-permute-start(f32[2,40,128]{2,1,0:T(8,128)S(1)} %get-tuple-element.53), channel_id=1, source_target_pairs={{0,6},{1,7},{2,4},{3,5},{4,2},{5,3},{6,0},{7,1},{8,14},{9,15},{10,... | collective-permute-start | bytes 122888 | tf_op jit(solution)/shard_map/ppermute | solution.py:58
  118.6 0.3 slice_reduce_fusion
  118.9 0.1 copy.28.speeds_ref
  119.1 0.9 collective-permute-done.13
  120.0 1.8 %collective-permute-done.14 = f32[2,40,128]{2,1,0:T(8,128)S(1)} collective-permute-done((f32[2,40,128]{2,1,0:T(8,128)S(1)}, f32[2,40,128]{2,1,0:T(8,128)S(1)}, u32[]{:S(2)}, u32[]{:S(2)}) %collective-permute-start.14) | collective-permute-done | bytes 40992 | tf_op jit(solution)/shard_map/ppermute | solution.py:58
  121.9 1.3 collective-permute-done.15
  123.3 6.2 %middle.1 = (f32[64,128]{1,0:T(8,128)}, f32[256,128]{1,0:T(8,128)S(1)}, f32[128,128]{1,0:T(8,128)S(1)}) custom-call(s32[1]{0:T(128)} %bitcast.brick_ref, f32[16,40,128]{2,1,0:T(8,128)S(1)} %constant_dynamic-update-slice_fusion.17.pieces_ref, f32[6,128,128]{2,1,0:T(8,128)S(1)} %get-tuple-element.35.transport_ref, f32[256,128]{1,0:T(8,128)S(1)} %copy-done.3, ...), custom_call_target="tpu_custom_call" | custom-call | tf_op jit(solution)/shard_map/middle/pallas_call | solution.py:597
  129.5 0.7 update.1
  130.2 0.2 collective-permute-start.16
  130.5 1.1 collective-permute-done.16
  131.7 3.5 %collective-permute-start.18 = (f32[128,128]{1,0:T(8,128)S(1)}, f32[128,128]{1,0:T(8,128)S(1)}, u32[]{:S(2)}, u32[]{:S(2)}) collective-permute-start(f32[128,128]{1,0:T(8,128)S(1)} %add.444), channel_id=1, source_target_pairs={{0,4},{1,5},{2,6},{3,7},{4,0},{5,1},{6,2},{7,3},{8,12},{9,13},{10,... | collective-permute-start | bytes 196616 | tf_op jit(solution)/shard_map/ppermute | solution.py:58
  135.2 1.2 collective-permute-start.19
  136.4 2.3 %collective-permute-done.18 = f32[128,128]{1,0:T(8,128)S(1)} collective-permute-done((f32[128,128]{1,0:T(8,128)S(1)}, f32[128,128]{1,0:T(8,128)S(1)}, u32[]{:S(2)}, u32[]{:S(2)}) %collective-permute-start.18) | collective-permute-done | bytes 65568 | tf_op jit(solution)/shard_map/ppermute | solution.py:58
  138.7 1.9 %collective-permute-done.19 = f32[128,128]{1,0:T(8,128)S(1)} collective-permute-done((f32[128,128]{1,0:T(8,128)S(1)}, f32[128,128]{1,0:T(8,128)S(1)}, u32[]{:S(2)}, u32[]{:S(2)}) %collective-permute-start.19) | collective-permute-done | bytes 65568 | tf_op jit(solution)/shard_map/ppermute | solution.py:58
  140.7 2.1 %collective-permute-start.20 = (f32[128,128]{1,0:T(8,128)S(1)}, f32[128,128]{1,0:T(8,128)S(1)}, u32[]{:S(2)}, u32[]{:S(2)}) collective-permute-start(f32[128,128]{1,0:T(8,128)S(1)} %add_add_fusion.2), channel_id=1, source_target_pairs={{0,8},{1,9},{2,10},{3,11},{4,12},{5,13},{6,14},{7,15},{8,0},{9,1},... | collective-permute-start | bytes 196616 | tf_op jit(solution)/shard_map/ppermute | solution.py:58
  142.8 4.1 %collective-permute-start.21 = (f32[128,128]{1,0:T(8,128)S(1)}, f32[128,128]{1,0:T(8,128)S(1)}, u32[]{:S(2)}, u32[]{:S(2)}) collective-permute-start(f32[128,128]{1,0:T(8,128)S(1)} %add_add_fusion.2), channel_id=1, source_target_pairs={{0,16},{1,17},{2,18},{3,19},{4,20},{5,21},{6,22},{7,23},{8,24},{9,... | collective-permute-start | bytes 196616 | tf_op jit(solution)/shard_map/ppermute | solution.py:58
  146.9 3.0 %collective-permute-done.21 = f32[128,128]{1,0:T(8,128)S(1)} collective-permute-done((f32[128,128]{1,0:T(8,128)S(1)}, f32[128,128]{1,0:T(8,128)S(1)}, u32[]{:S(2)}, u32[]{:S(2)}) %collective-permute-start.21) | collective-permute-done | bytes 65568 | tf_op jit(solution)/shard_map/ppermute | solution.py:58
  150.0 2.4 %collective-permute-done.22 = f32[128,128]{1,0:T(8,128)S(1)} collective-permute-done((f32[128,128]{1,0:T(8,128)S(1)}, f32[128,128]{1,0:T(8,128)S(1)}, u32[]{:S(2)}, u32[]{:S(2)}) %collective-permute-start.22) | collective-permute-done | bytes 65568 | tf_op jit(solution)/shard_map/ppermute | solution.py:58
  152.4 1.5 collective-permute-start.23
  154.0 2.7 %collective-permute-start.24 = (f32[128,128]{1,0:T(8,128)S(1)}, f32[128,128]{1,0:T(8,128)S(1)}, u32[]{:S(2)}, u32[]{:S(2)}) collective-permute-start(f32[128,128]{1,0:T(8,128)S(1)} %add_add_fusion.1), channel_id=1, source_target_pairs={{0,64},{1,65},{2,66},{3,67},{4,68},{5,69},{6,70},{7,71},{8,72},{9,... | collective-permute-start | bytes 196616 | tf_op jit(solution)/shard_map/ppermute | solution.py:58
  156.7 0.6 collective-permute-start.25
  157.2 2.5 %collective-permute-done.24 = f32[128,128]{1,0:T(8,128)S(1)} collective-permute-done((f32[128,128]{1,0:T(8,128)S(1)}, f32[128,128]{1,0:T(8,128)S(1)}, u32[]{:S(2)}, u32[]{:S(2)}) %collective-permute-start.24) | collective-permute-done | bytes 65568 | tf_op jit(solution)/shard_map/ppermute | solution.py:58
  159.7 2.4 %collective-permute-done.25 = f32[128,128]{1,0:T(8,128)S(1)} collective-permute-done((f32[128,128]{1,0:T(8,128)S(1)}, f32[128,128]{1,0:T(8,128)S(1)}, u32[]{:S(2)}, u32[]{:S(2)}) %collective-permute-start.25) | collective-permute-done | bytes 65568 | tf_op jit(solution)/shard_map/ppermute | solution.py:58
  162.2 4.5 %last.1 = (f32[128,128]{1,0:T(8,128)}, f32[256,128]{1,0:T(8,128)}) custom-call(f32[128,128]{1,0:T(8,128)S(1)} %add_add_fusion.gram_ref, f32[256,128]{1,0:T(8,128)S(1)} %get-tuple-element.42.velocity_ref), custom_call_target="tpu_custom_call" | custom-call | tf_op jit(solution)/shard_map/last/pallas_call | solution.py:614
  (85 shorter events, 1.4 us)
Async XLA Ops:
  0.6 0.8 copy-start
  1.4 0.9 copy-start.2
  3.5 7.0 %copy-start.1 = (f32[2,2,16,128]{3,2,1,0:T(8,128)S(1)}, f32[2,2,16,128]{3,2,1,0:T(8,128)}, u32[]{:S(2)}) copy-start(f32[2,2,16,128]{3,2,1,0:T(8,128)} %param.2) | copy-start | bytes 98308
  3.5 34.2 %all-to-all-start = ((f32[8,288,128]{2,1,0:T(8,128)}), f32[8,288,128]{2,1,0:T(8,128)S(1)}, u32[]{:S(2)}, u32[]{:S(2)}) async-start(f32[8,288,128]{2,1,0:T(8,128)} %repeat.1), calls=%async_computation | async-start | bytes 2359296 | tf_op jit(solution)/shard_map/all_to_all | solution.py:34
  10.5 14.5 %collective-permute-start = (f32[1,64,128]{2,1,0:T(8,128)S(1)}, f32[1,64,128]{2,1,0:T(8,128)S(1)}, u32[]{:S(2)}, u32[]{:S(2)}) collective-permute-start(f32[1,64,128]{2,1,0:T(8,128)S(1)} %bitcast.43), channel_id=1, source_target_pairs={{0,8},{1,9},{2,10},{3,11},{4,12},{5,13},{6,14},{7,15},{8,0},{9,1},... | collective-permute-start | bytes 98312 | tf_op jit(solution)/shard_map/ppermute | solution.py:58
  25.1 5.5 %collective-permute-start.1 = (f32[2,64,128]{2,1,0:T(8,128)S(1)}, f32[2,64,128]{2,1,0:T(8,128)S(1)}, u32[]{:S(2)}, u32[]{:S(2)}) collective-permute-start(f32[2,64,128]{2,1,0:T(8,128)S(1)} %pad_maximum_fusion.1), channel_id=1, source_target_pairs={{0,2},{1,3},{2,0},{3,1},{4,6},{5,7},{6,4},{7,5},{8,10},{9,11},{10,... | collective-permute-start | bytes 196616 | tf_op jit(solution)/shard_map/ppermute | solution.py:58
  27.0 6.6 %collective-permute-start.2 = (f32[2,64,128]{2,1,0:T(8,128)S(1)}, f32[2,64,128]{2,1,0:T(8,128)S(1)}, u32[]{:S(2)}, u32[]{:S(2)}) collective-permute-start(f32[2,64,128]{2,1,0:T(8,128)S(1)} %pad_maximum_fusion.1), channel_id=1, source_target_pairs={{0,4},{1,5},{2,6},{3,7},{4,0},{5,1},{6,2},{7,3},{8,12},{9,13},{10,... | collective-permute-start | bytes 196616 | tf_op jit(solution)/shard_map/ppermute | solution.py:58
  30.6 5.5 %collective-permute-start.3 = (f32[2,64,128]{2,1,0:T(8,128)S(1)}, f32[2,64,128]{2,1,0:T(8,128)S(1)}, u32[]{:S(2)}, u32[]{:S(2)}) collective-permute-start(f32[2,64,128]{2,1,0:T(8,128)S(1)} %pad_maximum_fusion.1), channel_id=1, source_target_pairs={{0,6},{1,7},{2,4},{3,5},{4,2},{5,3},{6,0},{7,1},{8,14},{9,15},{10,... | collective-permute-start | bytes 196616 | tf_op jit(solution)/shard_map/ppermute | solution.py:58
  36.1 1.6 collective-permute-start.4
  40.9 11.6 %all-to-all-start.1 = ((f32[16,32,128]{2,1,0:T(8,128)}), f32[16,32,128]{2,1,0:T(8,128)S(1)}, u32[]{:S(2)}, u32[]{:S(2)}) async-start(f32[16,32,128]{2,1,0:T(8,128)} %transport.1), calls=%async_computation.1 | async-start | bytes 524288 | tf_op jit(solution)/shard_map/all_to_all | solution.py:34
  56.1 16.6 %all-to-all-start.2 = ((f32[16,88,128]{2,1,0:T(8,128)}), f32[16,88,128]{2,1,0:T(8,128)S(1)}, u32[]{:S(2)}, u32[]{:S(2)}) async-start(f32[16,88,128]{2,1,0:T(8,128)} %get-tuple-element.25), calls=%async_computation.2 | async-start | bytes 1441792 | tf_op jit(solution)/shard_map/all_to_all | solution.py:34
  89.0 7.9 %collective-permute-start.5 = (f32[8,512]{1,0:T(8,128)S(1)}, f32[8,512]{1,0:T(8,128)S(1)}, u32[]{:S(2)}, u32[]{:S(2)}) collective-permute-start(f32[8,512]{1,0:T(8,128)S(1)} %get-tuple-element.30), channel_id=1, source_target_pairs={{0,16},{16,32},{32,48},{48,64},{64,80},{80,96},{96,112},{112,0},{1... | collective-permute-start | bytes 49160 | tf_op jit(solution)/shard_map/ppermute | solution.py:578
  97.2 5.4 %collective-permute-start.6 = (f32[40,128]{1,0:T(8,128)S(1)}, f32[40,128]{1,0:T(8,128)S(1)}, u32[]{:S(2)}, u32[]{:S(2)}) collective-permute-start(f32[40,128]{1,0:T(8,128)S(1)} %pad_add_fusion), channel_id=1, source_target_pairs={{0,16},{1,17},{2,18},{3,19},{4,20},{5,21},{6,22},{7,23},{8,24},{9,... | collective-permute-start | bytes 61448 | tf_op jit(solution)/shard_map/ppermute | solution.py:58
  98.8 3.9 %collective-permute-start.7 = (f32[40,128]{1,0:T(8,128)S(1)}, f32[40,128]{1,0:T(8,128)S(1)}, u32[]{:S(2)}, u32[]{:S(2)}) collective-permute-start(f32[40,128]{1,0:T(8,128)S(1)} %pad_add_fusion), channel_id=1, source_target_pairs={{0,8},{1,9},{2,10},{3,11},{4,12},{5,13},{6,14},{7,15},{8,0},{9,1},... | collective-permute-start | bytes 61448 | tf_op jit(solution)/shard_map/ppermute | solution.py:58
  98.9 5.1 %collective-permute-start.8 = (f32[40,128]{1,0:T(8,128)S(1)}, f32[40,128]{1,0:T(8,128)S(1)}, u32[]{:S(2)}, u32[]{:S(2)}) collective-permute-start(f32[40,128]{1,0:T(8,128)S(1)} %pad_add_fusion), channel_id=1, source_target_pairs={{0,24},{1,25},{2,26},{3,27},{4,28},{5,29},{6,30},{7,31},{8,16},{9,... | collective-permute-start | bytes 61448 | tf_op jit(solution)/shard_map/ppermute | solution.py:58
  104.0 9.8 %collective-permute-start.10 = (f32[2,40,128]{2,1,0:T(8,128)S(1)}, f32[2,40,128]{2,1,0:T(8,128)S(1)}, u32[]{:S(2)}, u32[]{:S(2)}) collective-permute-start(f32[2,40,128]{2,1,0:T(8,128)S(1)} %pad_maximum_fusion.2), channel_id=1, source_target_pairs={{0,64},{1,65},{2,66},{3,67},{4,68},{5,69},{6,70},{7,71},{8,72},{9,... | collective-permute-start | bytes 122888 | tf_op jit(solution)/shard_map/ppermute | solution.py:58
  107.0 6.8 %collective-permute-start.11 = (f32[2,40,128]{2,1,0:T(8,128)S(1)}, f32[2,40,128]{2,1,0:T(8,128)S(1)}, u32[]{:S(2)}, u32[]{:S(2)}) collective-permute-start(f32[2,40,128]{2,1,0:T(8,128)S(1)} %pad_maximum_fusion.2), channel_id=1, source_target_pairs={{0,96},{1,97},{2,98},{3,99},{4,100},{5,101},{6,102},{7,103},{8,104... | collective-permute-start | bytes 122888 | tf_op jit(solution)/shard_map/ppermute | solution.py:58
  108.2 5.6 %collective-permute-start.9 = (f32[2,40,128]{2,1,0:T(8,128)S(1)}, f32[2,40,128]{2,1,0:T(8,128)S(1)}, u32[]{:S(2)}, u32[]{:S(2)}) collective-permute-start(f32[2,40,128]{2,1,0:T(8,128)S(1)} %pad_maximum_fusion.2), channel_id=1, source_target_pairs={{0,32},{1,33},{2,34},{3,35},{4,36},{5,37},{6,38},{7,39},{8,40},{9,... | collective-permute-start | bytes 122888 | tf_op jit(solution)/shard_map/ppermute | solution.py:58
  108.2 21.3 %all-to-all-start.4 = ((f32[8,256,128]{2,1,0:T(8,128)}), f32[8,256,128]{2,1,0:T(8,128)S(1)}, u32[]{:S(2)}, u32[]{:S(2)}) async-start(f32[8,256,128]{2,1,0:T(8,128)} %back.1), calls=%async_computation.4 | async-start | bytes 2097152 | tf_op jit(solution)/shard_map/all_to_all | solution.py:34
  113.8 9.5 %copy-start.3 = (f32[256,128]{1,0:T(8,128)S(1)}, f32[256,128]{1,0:T(8,128)}, u32[]{:S(2)}) copy-start(f32[256,128]{1,0:T(8,128)} %basis_ref.1) | copy-start | bytes 393220
  113.8 5.2 %collective-permute-start.12 = (f32[2,40,128]{2,1,0:T(8,128)S(1)}, f32[2,40,128]{2,1,0:T(8,128)S(1)}, u32[]{:S(2)}, u32[]{:S(2)}) collective-permute-start(f32[2,40,128]{2,1,0:T(8,128)S(1)} %get-tuple-element.53), channel_id=1, source_target_pairs={{0,2},{1,3},{2,0},{3,1},{4,6},{5,7},{6,4},{7,5},{8,10},{9,11},{10,... | collective-permute-start | bytes 122888 | tf_op jit(solution)/shard_map/ppermute | solution.py:58
  114.5 5.5 %collective-permute-start.13 = (f32[2,40,128]{2,1,0:T(8,128)S(1)}, f32[2,40,128]{2,1,0:T(8,128)S(1)}, u32[]{:S(2)}, u32[]{:S(2)}) collective-permute-start(f32[2,40,128]{2,1,0:T(8,128)S(1)} %get-tuple-element.53), channel_id=1, source_target_pairs={{0,4},{1,5},{2,6},{3,7},{4,0},{5,1},{6,2},{7,3},{8,12},{9,13},{10,... | collective-permute-start | bytes 122888 | tf_op jit(solution)/shard_map/ppermute | solution.py:58
  116.6 5.2 %collective-permute-start.14 = (f32[2,40,128]{2,1,0:T(8,128)S(1)}, f32[2,40,128]{2,1,0:T(8,128)S(1)}, u32[]{:S(2)}, u32[]{:S(2)}) collective-permute-start(f32[2,40,128]{2,1,0:T(8,128)S(1)} %get-tuple-element.53), channel_id=1, source_target_pairs={{0,6},{1,7},{2,4},{3,5},{4,2},{5,3},{6,0},{7,1},{8,14},{9,15},{10,... | collective-permute-start | bytes 122888 | tf_op jit(solution)/shard_map/ppermute | solution.py:58
  121.8 1.5 collective-permute-start.15
  130.2 1.3 collective-permute-start.16
  131.6 4.9 %collective-permute-start.17 = (f32[128,128]{1,0:T(8,128)S(1)}, f32[128,128]{1,0:T(8,128)S(1)}, u32[]{:S(2)}, u32[]{:S(2)}) collective-permute-start(f32[128,128]{1,0:T(8,128)S(1)} %add.444), channel_id=1, source_target_pairs={{0,2},{1,3},{2,0},{3,1},{4,6},{5,7},{6,4},{7,5},{8,10},{9,11},{10,... | collective-permute-start | bytes 196616 | tf_op jit(solution)/shard_map/ppermute | solution.py:58
  131.7 7.1 %collective-permute-start.18 = (f32[128,128]{1,0:T(8,128)S(1)}, f32[128,128]{1,0:T(8,128)S(1)}, u32[]{:S(2)}, u32[]{:S(2)}) collective-permute-start(f32[128,128]{1,0:T(8,128)S(1)} %add.444), channel_id=1, source_target_pairs={{0,4},{1,5},{2,6},{3,7},{4,0},{5,1},{6,2},{7,3},{8,12},{9,13},{10,... | collective-permute-start | bytes 196616 | tf_op jit(solution)/shard_map/ppermute | solution.py:58
  135.2 5.5 %collective-permute-start.19 = (f32[128,128]{1,0:T(8,128)S(1)}, f32[128,128]{1,0:T(8,128)S(1)}, u32[]{:S(2)}, u32[]{:S(2)}) collective-permute-start(f32[128,128]{1,0:T(8,128)S(1)} %add.444), channel_id=1, source_target_pairs={{0,6},{1,7},{2,4},{3,5},{4,2},{5,3},{6,0},{7,1},{8,14},{9,15},{10,... | collective-permute-start | bytes 196616 | tf_op jit(solution)/shard_map/ppermute | solution.py:58
  140.7 6.3 %collective-permute-start.20 = (f32[128,128]{1,0:T(8,128)S(1)}, f32[128,128]{1,0:T(8,128)S(1)}, u32[]{:S(2)}, u32[]{:S(2)}) collective-permute-start(f32[128,128]{1,0:T(8,128)S(1)} %add_add_fusion.2), channel_id=1, source_target_pairs={{0,8},{1,9},{2,10},{3,11},{4,12},{5,13},{6,14},{7,15},{8,0},{9,1},... | collective-permute-start | bytes 196616 | tf_op jit(solution)/shard_map/ppermute | solution.py:58
  142.8 7.2 %collective-permute-start.21 = (f32[128,128]{1,0:T(8,128)S(1)}, f32[128,128]{1,0:T(8,128)S(1)}, u32[]{:S(2)}, u32[]{:S(2)}) collective-permute-start(f32[128,128]{1,0:T(8,128)S(1)} %add_add_fusion.2), channel_id=1, source_target_pairs={{0,16},{1,17},{2,18},{3,19},{4,20},{5,21},{6,22},{7,23},{8,24},{9,... | collective-permute-start | bytes 196616 | tf_op jit(solution)/shard_map/ppermute | solution.py:58
  146.9 5.5 %collective-permute-start.22 = (f32[128,128]{1,0:T(8,128)S(1)}, f32[128,128]{1,0:T(8,128)S(1)}, u32[]{:S(2)}, u32[]{:S(2)}) collective-permute-start(f32[128,128]{1,0:T(8,128)S(1)} %add_add_fusion.2), channel_id=1, source_target_pairs={{0,24},{1,25},{2,26},{3,27},{4,28},{5,29},{6,30},{7,31},{8,16},{9,... | collective-permute-start | bytes 196616 | tf_op jit(solution)/shard_map/ppermute | solution.py:58
  152.4 4.8 %collective-permute-start.23 = (f32[128,128]{1,0:T(8,128)S(1)}, f32[128,128]{1,0:T(8,128)S(1)}, u32[]{:S(2)}, u32[]{:S(2)}) collective-permute-start(f32[128,128]{1,0:T(8,128)S(1)} %add_add_fusion.1), channel_id=1, source_target_pairs={{0,32},{1,33},{2,34},{3,35},{4,36},{5,37},{6,38},{7,39},{8,40},{9,... | collective-permute-start | bytes 196616 | tf_op jit(solution)/shard_map/ppermute | solution.py:58
  154.0 5.8 %collective-permute-start.24 = (f32[128,128]{1,0:T(8,128)S(1)}, f32[128,128]{1,0:T(8,128)S(1)}, u32[]{:S(2)}, u32[]{:S(2)}) collective-permute-start(f32[128,128]{1,0:T(8,128)S(1)} %add_add_fusion.1), channel_id=1, source_target_pairs={{0,64},{1,65},{2,66},{3,67},{4,68},{5,69},{6,70},{7,71},{8,72},{9,... | collective-permute-start | bytes 196616 | tf_op jit(solution)/shard_map/ppermute | solution.py:58
  156.7 5.5 %collective-permute-start.25 = (f32[128,128]{1,0:T(8,128)S(1)}, f32[128,128]{1,0:T(8,128)S(1)}, u32[]{:S(2)}, u32[]{:S(2)}) collective-permute-start(f32[128,128]{1,0:T(8,128)S(1)} %add_add_fusion.1), channel_id=1, source_target_pairs={{0,96},{1,97},{2,98},{3,99},{4,100},{5,101},{6,102},{7,103},{8,104... | collective-permute-start | bytes 196616 | tf_op jit(solution)/shard_map/ppermute | solution.py:58

commit v11 on v9

--- a/solution.py
+++ b/solution.py
@@ -499,12 +499,15 @@
         )(((slab + slabs - 1) % slabs).astype(jnp.int32)[None], v_basis, own_cells),
         "slab",
     )
-    k_slab = gather_relative(own_cells, "brick", BRICK_GROUPS)
+    k_part = gather_relative(own_cells, "brick", BRICK_GROUPS[:2])
     below, above = ((slab + shift) % slabs for shift in (slabs - 1, 1))
     k_below, k_above = (
         lax.dynamic_slice(nodes, (peer, rows, 0), (1, plane, rank)).reshape(k_coeffs[:1].shape)
         for peer in (below, above)
     )
+
+    k_part, nodes = lax.optimization_barrier((k_part, nodes))
+    k_slab = gather_more(k_part, "brick", BRICK_GROUPS[2:])
 
     across = velocities(brick * rows + jnp.arange(rows, dtype=jnp.int32))
     columns = [f(across[i]) for i in (1, 2) for f in (lambda v: jnp.maximum(v, 0.0), lambda v: jnp.minimum(v, 0.0))]

time: 163 us -> 160 us (0.982)
  starting transfers between devices: 61.8 us -> 56.7 us
  waiting for transfers between devices: 56.2 us -> 58.2 us
    ppermute x25, waiting for transfers between devices: 35.2 us -> 28.2 us  [from_peer(): return lax.ppermute(values, axis, [(i, i ^ mask) for i in range(peers)])]
    all_to_all x4, waiting for transfers between devices: 20.9 us -> 27.2 us  [exchange(): return lax.all_to_all(array, axis, 0, 0, tiled=True)]
    ppermute x1, waiting for transfers between devices: 0.01 us -> 2.83 us  [local(): chosen_below = lax.ppermute(chosen, 'slab', up)]
    ppermute x1, starting transfers between devices: 3.87 us -> 1.07 us  [local(): chosen_below = lax.ppermute(chosen, 'slab', up)]
  transfers between devices with their start and end apart: 30 -> 30, of which waited for: 20 -> 21; matrix products, arithmetic and copies ran while one was open for 1% -> 1% of each run, Pallas kernels for 7% -> 8%
where the time goes in v11:
time: 160 us
  waiting for transfers between devices  58.2 us (36%)
  starting transfers between devices  56.7 us (35%)
  Pallas kernels  25.1 us (16%)
  blocking collectives  14.2 us (9%)
  local copies, waits for them, and re-layouts  3.11 us (2%)
    ppermute x25, starting transfers between devices, from_peer(): return lax.ppermute(values, axis, [(i, i ^ mask) for i in range(peers)])  34.1 us
    ppermute x25, waiting for transfers between devices, from_peer(): return lax.ppermute(values, axis, [(i, i ^ mask) for i in range(peers)])  28.2 us
    all_to_all x4, waiting for transfers between devices, exchange(): return lax.all_to_all(array, axis, 0, 0, tiled=True)  27.2 us
    all_to_all x4, starting transfers between devices, exchange(): return lax.all_to_all(array, axis, 0, 0, tiled=True)  21.6 us
    all_to_all x1, blocking collectives, exchange(): return lax.all_to_all(array, axis, 0, 0, tiled=True)  14.2 us
    pallas_call x1, Pallas kernels, local(): pl.pallas_call(functools.partial(middle_kernel, lengths=lengths, time_ste...  6.2 us
    pallas_call x1, Pallas kernels, local(): pl.pallas_call(last_kernel, out_shape=(f32(rank, rank), f32(rows, rank)),...  4.49 us
    pallas_call x1, Pallas kernels, local(): pl.pallas_call(maxwell_kernel, out_shape=(f32(bricks, cells + 3 * height,...  3.68 us
  transfers between devices with their start and end apart: 30, of which 21 were waited for; matrix products, arithmetic and copies ran while one was open for 1% of the time, Pallas kernels for 8%

profile of v11, /device:TPU:0, one launch (start us, length us, event | category | flops | bytes accessed | tf_op | source)
XLA Modules:
  0.0 159.7 jit_solution(13736835300646726646)
XLA Ops:
  0.7 0.7 copy-done
  1.4 0.9 copy-done.2
  2.3 1.2 repeat.1
  3.5 7.0 %all-to-all-start = ((f32[8,288,128]{2,1,0:T(8,128)}), f32[8,288,128]{2,1,0:T(8,128)S(1)}, u32[]{:S(2)}, u32[]{:S(2)}) async-start(f32[8,288,128]{2,1,0:T(8,128)} %repeat.1), calls=%async_computation | async-start | bytes 2359296 | tf_op jit(solution)/shard_map/all_to_all | solution.py:34
  10.8 0.1 copy.24
  11.0 0.2 and_select_fusion.3
  11.3 0.1 slice_bitcast_fusion.4
  11.4 0.4 collective-permute-done
  11.8 1.9 %collective-permute-start.1 = (f32[2,64,128]{2,1,0:T(8,128)S(1)}, f32[2,64,128]{2,1,0:T(8,128)S(1)}, u32[]{:S(2)}, u32[]{:S(2)}) collective-permute-start(f32[2,64,128]{2,1,0:T(8,128)S(1)} %pad_maximum_fusion.1), channel_id=1, source_target_pairs={{0,2},{1,3},{2,0},{3,1},{4,6},{5,7},{6,4},{7,5},{8,10},{9,11},{10,... | collective-permute-start | bytes 196616 | tf_op jit(solution)/shard_map/ppermute | solution.py:58
  13.8 3.6 %collective-permute-start.2 = (f32[2,64,128]{2,1,0:T(8,128)S(1)}, f32[2,64,128]{2,1,0:T(8,128)S(1)}, u32[]{:S(2)}, u32[]{:S(2)}) collective-permute-start(f32[2,64,128]{2,1,0:T(8,128)S(1)} %pad_maximum_fusion.1), channel_id=1, source_target_pairs={{0,4},{1,5},{2,6},{3,7},{4,0},{5,1},{6,2},{7,3},{8,12},{9,13},{10,... | collective-permute-start | bytes 196616 | tf_op jit(solution)/shard_map/ppermute | solution.py:58
  17.4 3.5 %collective-permute-done.2 = f32[2,64,128]{2,1,0:T(8,128)S(1)} collective-permute-done((f32[2,64,128]{2,1,0:T(8,128)S(1)}, f32[2,64,128]{2,1,0:T(8,128)S(1)}, u32[]{:S(2)}, u32[]{:S(2)}) %collective-permute-start.2) | collective-permute-done | bytes 65568 | tf_op jit(solution)/shard_map/ppermute | solution.py:58
  20.9 1.9 %collective-permute-done.3 = f32[2,64,128]{2,1,0:T(8,128)S(1)} collective-permute-done((f32[2,64,128]{2,1,0:T(8,128)S(1)}, f32[2,64,128]{2,1,0:T(8,128)S(1)}, u32[]{:S(2)}, u32[]{:S(2)}) %collective-permute-start.3) | collective-permute-done | bytes 65568 | tf_op jit(solution)/shard_map/ppermute | solution.py:58
  22.8 6.4 %all-to-all-done.nodes_ref = f32[8,288,128]{2,1,0:T(8,128)S(1)} async-done(((f32[8,288,128]{2,1,0:T(8,128)}), f32[8,288,128]{2,1,0:T(8,128)S(1)}, u32[]{:S(2)}, u32[]{:S(2)}) %all-to-all-start) | async-done | bytes 1179680 | tf_op jit(solution)/shard_map/all_to_all | solution.py:34
  29.2 0.6 collective-permute-start.4
  29.8 0.3 minimum_reduce_fusion
  30.2 0.1 copy.25.columns_ref
  30.6 3.1 %transport.1 = f32[16,32,128]{2,1,0:T(8,128)} custom-call(f32[8,288,128]{2,1,0:T(8,128)S(1)} %all-to-all-done.nodes_ref, f32[256,8]{1,0:T(8,128)S(1)} %copy.25.columns_ref, f32[8,128]{1,0:T(8,128)S(1)} %broadcast_in_dim.18.speeds_ref.first_ref, f32[8,8,256]{2,1,0:T(8,128)S(1)} %stack.61.weights_ref), custom_call_target="tpu_custom_call" | custom-call | tf_op jit(solution)/shard_map/transport/pallas_call | solution.py:518
  33.7 6.3 %all-to-all-start.1 = ((f32[16,32,128]{2,1,0:T(8,128)}), f32[16,32,128]{2,1,0:T(8,128)S(1)}, u32[]{:S(2)}, u32[]{:S(2)}) async-start(f32[16,32,128]{2,1,0:T(8,128)} %transport.1), calls=%async_computation.1 | async-start | bytes 524288 | tf_op jit(solution)/shard_map/all_to_all | solution.py:34
  40.2 7.9 %all-to-all-done.1.integrals_ref = f32[16,32,128]{2,1,0:T(8,128)S(1)} async-done(((f32[16,32,128]{2,1,0:T(8,128)}), f32[16,32,128]{2,1,0:T(8,128)S(1)}, u32[]{:S(2)}, u32[]{:S(2)}) %all-to-all-start.1) | async-done | bytes 262176 | tf_op jit(solution)/shard_map/all_to_all | solution.py:34
  48.1 3.7 %maxwell.1 = (f32[16,88,128]{2,1,0:T(8,128)}, f32[1024,8]{1,0:T(8,128)S(1)}, f32[8,1024]{1,0:T(8,128)S(1)}, f32[8,128]{1,0:T(8,128)S(1)}) custom-call(s32[1]{0:T(128)} %bitcast.brick_ref, f32[16,64,128]{2,1,0:T(8,128)S(1)} %constant_dynamic-update-slice_fusion.5.cells_ref, f32[16,32,128]{2,1,0:T(8,128)S(1)} %all-to-all-done.1.integrals_ref, ...), custom_call_target="tpu_custom_call" | custom-call | tf_op jit(solution)/shard_map/maxwell/pallas_call | solution.py:524
  51.8 3.6 %all-to-all-start.2 = ((f32[16,88,128]{2,1,0:T(8,128)}), f32[16,88,128]{2,1,0:T(8,128)S(1)}, u32[]{:S(2)}, u32[]{:S(2)}) async-start(f32[16,88,128]{2,1,0:T(8,128)} %get-tuple-element.27), calls=%async_computation.2 | async-start | bytes 1441792 | tf_op jit(solution)/shard_map/all_to_all | solution.py:34
  55.5 12.9 %all-to-all-done.2.parts_ref = f32[16,88,128]{2,1,0:T(8,128)S(1)} async-done(((f32[16,88,128]{2,1,0:T(8,128)}), f32[16,88,128]{2,1,0:T(8,128)S(1)}, u32[]{:S(2)}, u32[]{:S(2)}) %all-to-all-start.2) | async-done | bytes 720928 | tf_op jit(solution)/shard_map/all_to_all | solution.py:34
  68.4 0.9 advance.1
  69.3 14.2 %all_to_all.25.parts_ref = f32[16,72,128]{2,1,0:T(8,128)S(1)} all-to-all(f32[16,72,128]{2,1,0:T(8,128)S(1)} %get-tuple-element.29), channel_id=1, replica_groups=mesh['slab'=8,'brick'=16] {'brick'}, dimensions={0} | all-to-all | bytes 1179648 | tf_op jit(solution)/shard_map/all_to_all | solution.py:34
  83.4 1.2 products.1
  84.6 1.1 collective-permute-start.5
  85.7 3.6 %back.1 = f32[8,256,128]{2,1,0:T(8,128)} custom-call(f32[16,72,128]{2,1,0:T(8,128)S(1)} %all_to_all.25.parts_ref, f32[1024,8]{1,0:T(8,128)S(1)} %get-tuple-element.34.line_ref, f32[8,1024]{1,0:T(8,128)S(1)} %get-tuple-element.35.state_ref, f32[256,2]{1,0:T(8,128)S(1)} %get-tuple-element.62.across_ref), custom_call_target="tpu_custom_call" | custom-call | tf_op jit(solution)/shard_map/back/pallas_call | solution.py:579
  89.4 2.8 %collective-permute-done.5 = f32[8,512]{1,0:T(8,128)S(1)} collective-permute-done((f32[8,512]{1,0:T(8,128)S(1)}, f32[8,512]{1,0:T(8,128)S(1)}, u32[]{:S(2)}, u32[]{:S(2)}) %collective-permute-start.5) | collective-permute-done | bytes 16416 | tf_op jit(solution)/shard_map/ppermute | solution.py:576
  92.3 0.2 fusion.31
  92.6 0.1 copy.27
  92.7 0.7 collective-permute-start.7
  93.4 3.5 %collective-permute-start.8 = (f32[40,128]{1,0:T(8,128)S(1)}, f32[40,128]{1,0:T(8,128)S(1)}, u32[]{:S(2)}, u32[]{:S(2)}) collective-permute-start(f32[40,128]{1,0:T(8,128)S(1)} %pad_add_fusion), channel_id=1, source_target_pairs={{0,24},{1,25},{2,26},{3,27},{4,28},{5,29},{6,30},{7,31},{8,16},{9,... | collective-permute-start | bytes 61448 | tf_op jit(solution)/shard_map/ppermute | solution.py:58
  96.9 1.0 collective-permute-done.6
  97.9 0.8 collective-permute-done.8
  98.7 1.4 collective-permute-start.10
  100.1 1.2 collective-permute-start.11
  101.3 1.0 collective-permute-start.9
  102.3 4.7 %all-to-all-start.4 = ((f32[8,256,128]{2,1,0:T(8,128)}), f32[8,256,128]{2,1,0:T(8,128)S(1)}, u32[]{:S(2)}, u32[]{:S(2)}) async-start(f32[8,256,128]{2,1,0:T(8,128)} %back.1), calls=%async_computation.4 | async-start | bytes 2097152 | tf_op jit(solution)/shard_map/all_to_all | solution.py:34
  107.1 0.3 slice_reduce_fusion
  107.4 0.1 copy.28.speeds_ref
  107.5 0.8 collective-permute-done.12
  108.3 0.6 collective-permute-start.13
  108.9 2.1 %collective-permute-start.14 = (f32[4,40,128]{2,1,0:T(8,128)S(1)}, f32[4,40,128]{2,1,0:T(8,128)S(1)}, u32[]{:S(2)}, u32[]{:S(2)}) collective-permute-start(f32[4,40,128]{2,1,0:T(8,128)S(1)} %pad_maximum_fusion), channel_id=1, source_target_pairs={{0,4},{1,5},{2,6},{3,7},{4,0},{5,1},{6,2},{7,3},{8,12},{9,13},{10,... | collective-permute-start | bytes 245768 | tf_op jit(solution)/shard_map/ppermute | solution.py:58
  110.9 2.1 %collective-permute-start.15 = (f32[4,40,128]{2,1,0:T(8,128)S(1)}, f32[4,40,128]{2,1,0:T(8,128)S(1)}, u32[]{:S(2)}, u32[]{:S(2)}) collective-permute-start(f32[4,40,128]{2,1,0:T(8,128)S(1)} %pad_maximum_fusion), channel_id=1, source_target_pairs={{0,6},{1,7},{2,4},{3,5},{4,2},{5,3},{6,0},{7,1},{8,14},{9,15},{10,... | collective-permute-start | bytes 245768 | tf_op jit(solution)/shard_map/ppermute | solution.py:58
  113.0 0.6 collective-permute-done.13
  113.6 1.7 %collective-permute-done.14 = f32[4,40,128]{2,1,0:T(8,128)S(1)} collective-permute-done((f32[4,40,128]{2,1,0:T(8,128)S(1)}, f32[4,40,128]{2,1,0:T(8,128)S(1)}, u32[]{:S(2)}, u32[]{:S(2)}) %collective-permute-start.14) | collective-permute-done | bytes 81952 | tf_op jit(solution)/shard_map/ppermute | solution.py:58
  115.3 1.7 %collective-permute-done.15 = f32[4,40,128]{2,1,0:T(8,128)S(1)} collective-permute-done((f32[4,40,128]{2,1,0:T(8,128)S(1)}, f32[4,40,128]{2,1,0:T(8,128)S(1)}, u32[]{:S(2)}, u32[]{:S(2)}) %collective-permute-start.15) | collective-permute-done | bytes 81952 | tf_op jit(solution)/shard_map/ppermute | solution.py:58
  116.9 6.2 %middle.1 = (f32[64,128]{1,0:T(8,128)}, f32[256,128]{1,0:T(8,128)S(1)}, f32[128,128]{1,0:T(8,128)S(1)}) custom-call(s32[1]{0:T(128)} %bitcast.brick_ref, f32[16,40,128]{2,1,0:T(8,128)S(1)} %constant_dynamic-update-slice_fusion.13.pieces_ref, f32[6,128,128]{2,1,0:T(8,128)S(1)} %get-tuple-element.37.transport_ref, f32[256,128]{1,0:T(8,128)S(1)} %copy-done.3, ...), custom_call_target="tpu_custom_call" | custom-call | tf_op jit(solution)/shard_map/middle/pallas_call | solution.py:595
  123.1 0.7 update.1
  124.0 1.2 collective-permute-done.16
  125.3 3.5 %collective-permute-start.18 = (f32[128,128]{1,0:T(8,128)S(1)}, f32[128,128]{1,0:T(8,128)S(1)}, u32[]{:S(2)}, u32[]{:S(2)}) collective-permute-start(f32[128,128]{1,0:T(8,128)S(1)} %add.428), channel_id=1, source_target_pairs={{0,4},{1,5},{2,6},{3,7},{4,0},{5,1},{6,2},{7,3},{8,12},{9,13},{10,... | collective-permute-start | bytes 196616 | tf_op jit(solution)/shard_map/ppermute | solution.py:58
  128.8 1.2 collective-permute-start.19
  130.1 2.3 %collective-permute-done.18 = f32[128,128]{1,0:T(8,128)S(1)} collective-permute-done((f32[128,128]{1,0:T(8,128)S(1)}, f32[128,128]{1,0:T(8,128)S(1)}, u32[]{:S(2)}, u32[]{:S(2)}) %collective-permute-start.18) | collective-permute-done | bytes 65568 | tf_op jit(solution)/shard_map/ppermute | solution.py:58
  132.4 1.9 %collective-permute-done.19 = f32[128,128]{1,0:T(8,128)S(1)} collective-permute-done((f32[128,128]{1,0:T(8,128)S(1)}, f32[128,128]{1,0:T(8,128)S(1)}, u32[]{:S(2)}, u32[]{:S(2)}) %collective-permute-start.19) | collective-permute-done | bytes 65568 | tf_op jit(solution)/shard_map/ppermute | solution.py:58
  134.3 1.5 collective-permute-start.20
  135.9 4.1 %collective-permute-start.21 = (f32[128,128]{1,0:T(8,128)S(1)}, f32[128,128]{1,0:T(8,128)S(1)}, u32[]{:S(2)}, u32[]{:S(2)}) collective-permute-start(f32[128,128]{1,0:T(8,128)S(1)} %add_add_fusion.2), channel_id=1, source_target_pairs={{0,16},{1,17},{2,18},{3,19},{4,20},{5,21},{6,22},{7,23},{8,24},{9,... | collective-permute-start | bytes 196616 | tf_op jit(solution)/shard_map/ppermute | solution.py:58
  140.0 3.0 %collective-permute-done.21 = f32[128,128]{1,0:T(8,128)S(1)} collective-permute-done((f32[128,128]{1,0:T(8,128)S(1)}, f32[128,128]{1,0:T(8,128)S(1)}, u32[]{:S(2)}, u32[]{:S(2)}) %collective-permute-start.21) | collective-permute-done | bytes 65568 | tf_op jit(solution)/shard_map/ppermute | solution.py:58
  143.0 2.4 %collective-permute-done.22 = f32[128,128]{1,0:T(8,128)S(1)} collective-permute-done((f32[128,128]{1,0:T(8,128)S(1)}, f32[128,128]{1,0:T(8,128)S(1)}, u32[]{:S(2)}, u32[]{:S(2)}) %collective-permute-start.22) | collective-permute-done | bytes 65568 | tf_op jit(solution)/shard_map/ppermute | solution.py:58
  145.5 1.5 collective-permute-start.23
  147.0 2.7 %collective-permute-start.24 = (f32[128,128]{1,0:T(8,128)S(1)}, f32[128,128]{1,0:T(8,128)S(1)}, u32[]{:S(2)}, u32[]{:S(2)}) collective-permute-start(f32[128,128]{1,0:T(8,128)S(1)} %add_add_fusion.1), channel_id=1, source_target_pairs={{0,64},{1,65},{2,66},{3,67},{4,68},{5,69},{6,70},{7,71},{8,72},{9,... | collective-permute-start | bytes 196616 | tf_op jit(solution)/shard_map/ppermute | solution.py:58
  149.7 0.6 collective-permute-start.25
  150.3 2.5 %collective-permute-done.24 = f32[128,128]{1,0:T(8,128)S(1)} collective-permute-done((f32[128,128]{1,0:T(8,128)S(1)}, f32[128,128]{1,0:T(8,128)S(1)}, u32[]{:S(2)}, u32[]{:S(2)}) %collective-permute-start.24) | collective-permute-done | bytes 65568 | tf_op jit(solution)/shard_map/ppermute | solution.py:58
  152.8 2.4 %collective-permute-done.25 = f32[128,128]{1,0:T(8,128)S(1)} collective-permute-done((f32[128,128]{1,0:T(8,128)S(1)}, f32[128,128]{1,0:T(8,128)S(1)}, u32[]{:S(2)}, u32[]{:S(2)}) %collective-permute-start.25) | collective-permute-done | bytes 65568 | tf_op jit(solution)/shard_map/ppermute | solution.py:58
  155.2 4.5 %last.1 = (f32[128,128]{1,0:T(8,128)}, f32[256,128]{1,0:T(8,128)}) custom-call(f32[128,128]{1,0:T(8,128)S(1)} %add_add_fusion.gram_ref, f32[256,128]{1,0:T(8,128)S(1)} %get-tuple-element.44.velocity_ref), custom_call_target="tpu_custom_call" | custom-call | tf_op jit(solution)/shard_map/last/pallas_call | solution.py:612
  (86 shorter events, 1.5 us)
Async XLA Ops:
  0.6 0.8 copy-start
  1.4 0.9 copy-start.2
  3.5 7.0 %copy-start.1 = (f32[2,2,16,128]{3,2,1,0:T(8,128)S(1)}, f32[2,2,16,128]{3,2,1,0:T(8,128)}, u32[]{:S(2)}) copy-start(f32[2,2,16,128]{3,2,1,0:T(8,128)} %param.2) | copy-start | bytes 98308
  3.5 25.7 %all-to-all-start = ((f32[8,288,128]{2,1,0:T(8,128)}), f32[8,288,128]{2,1,0:T(8,128)S(1)}, u32[]{:S(2)}, u32[]{:S(2)}) async-start(f32[8,288,128]{2,1,0:T(8,128)} %repeat.1), calls=%async_computation | async-start | bytes 2359296 | tf_op jit(solution)/shard_map/all_to_all | solution.py:34
  10.6 1.3 collective-permute-start
  11.8 5.5 %collective-permute-start.1 = (f32[2,64,128]{2,1,0:T(8,128)S(1)}, f32[2,64,128]{2,1,0:T(8,128)S(1)}, u32[]{:S(2)}, u32[]{:S(2)}) collective-permute-start(f32[2,64,128]{2,1,0:T(8,128)S(1)} %pad_maximum_fusion.1), channel_id=1, source_target_pairs={{0,2},{1,3},{2,0},{3,1},{4,6},{5,7},{6,4},{7,5},{8,10},{9,11},{10,... | collective-permute-start | bytes 196616 | tf_op jit(solution)/shard_map/ppermute | solution.py:58
  13.8 7.1 %collective-permute-start.2 = (f32[2,64,128]{2,1,0:T(8,128)S(1)}, f32[2,64,128]{2,1,0:T(8,128)S(1)}, u32[]{:S(2)}, u32[]{:S(2)}) collective-permute-start(f32[2,64,128]{2,1,0:T(8,128)S(1)} %pad_maximum_fusion.1), channel_id=1, source_target_pairs={{0,4},{1,5},{2,6},{3,7},{4,0},{5,1},{6,2},{7,3},{8,12},{9,13},{10,... | collective-permute-start | bytes 196616 | tf_op jit(solution)/shard_map/ppermute | solution.py:58
  17.3 5.5 %collective-permute-start.3 = (f32[2,64,128]{2,1,0:T(8,128)S(1)}, f32[2,64,128]{2,1,0:T(8,128)S(1)}, u32[]{:S(2)}, u32[]{:S(2)}) collective-permute-start(f32[2,64,128]{2,1,0:T(8,128)S(1)} %pad_maximum_fusion.1), channel_id=1, source_target_pairs={{0,6},{1,7},{2,4},{3,5},{4,2},{5,3},{6,0},{7,1},{8,14},{9,15},{10,... | collective-permute-start | bytes 196616 | tf_op jit(solution)/shard_map/ppermute | solution.py:58
  29.2 10.9 %collective-permute-start.4 = (f32[8,64,128]{2,1,0:T(8,128)S(1)}, f32[8,64,128]{2,1,0:T(8,128)S(1)}, u32[]{:S(2)}, u32[]{:S(2)}) collective-permute-start(f32[8,64,128]{2,1,0:T(8,128)S(1)} %constant_dynamic-update-slice_fusion), channel_id=1, source_target_pairs={{0,8},{1,9},{2,10},{3,11},{4,12},{5,13},{6,14},{7,15},{8,0},{9,1},... | collective-permute-start | bytes 786440 | tf_op jit(solution)/shard_map/ppermute | solution.py:58
  33.7 14.4 %all-to-all-start.1 = ((f32[16,32,128]{2,1,0:T(8,128)}), f32[16,32,128]{2,1,0:T(8,128)S(1)}, u32[]{:S(2)}, u32[]{:S(2)}) async-start(f32[16,32,128]{2,1,0:T(8,128)} %transport.1), calls=%async_computation.1 | async-start | bytes 524288 | tf_op jit(solution)/shard_map/all_to_all | solution.py:34
  51.8 16.6 %all-to-all-start.2 = ((f32[16,88,128]{2,1,0:T(8,128)}), f32[16,88,128]{2,1,0:T(8,128)S(1)}, u32[]{:S(2)}, u32[]{:S(2)}) async-start(f32[16,88,128]{2,1,0:T(8,128)} %get-tuple-element.27), calls=%async_computation.2 | async-start | bytes 1441792 | tf_op jit(solution)/shard_map/all_to_all | solution.py:34
  84.6 7.6 %collective-permute-start.5 = (f32[8,512]{1,0:T(8,128)S(1)}, f32[8,512]{1,0:T(8,128)S(1)}, u32[]{:S(2)}, u32[]{:S(2)}) collective-permute-start(f32[8,512]{1,0:T(8,128)S(1)} %get-tuple-element.32), channel_id=1, source_target_pairs={{0,16},{16,32},{32,48},{48,64},{64,80},{80,96},{96,112},{112,0},{1... | collective-permute-start | bytes 49160 | tf_op jit(solution)/shard_map/ppermute | solution.py:576
  92.5 5.4 %collective-permute-start.6 = (f32[40,128]{1,0:T(8,128)S(1)}, f32[40,128]{1,0:T(8,128)S(1)}, u32[]{:S(2)}, u32[]{:S(2)}) collective-permute-start(f32[40,128]{1,0:T(8,128)S(1)} %pad_add_fusion), channel_id=1, source_target_pairs={{0,16},{1,17},{2,18},{3,19},{4,20},{5,21},{6,22},{7,23},{8,24},{9,... | collective-permute-start | bytes 61448 | tf_op jit(solution)/shard_map/ppermute | solution.py:58
  92.7 5.1 %collective-permute-start.7 = (f32[40,128]{1,0:T(8,128)S(1)}, f32[40,128]{1,0:T(8,128)S(1)}, u32[]{:S(2)}, u32[]{:S(2)}) collective-permute-start(f32[40,128]{1,0:T(8,128)S(1)} %pad_add_fusion), channel_id=1, source_target_pairs={{0,8},{1,9},{2,10},{3,11},{4,12},{5,13},{6,14},{7,15},{8,0},{9,1},... | collective-permute-start | bytes 61448 | tf_op jit(solution)/shard_map/ppermute | solution.py:58
  93.4 5.3 %collective-permute-start.8 = (f32[40,128]{1,0:T(8,128)S(1)}, f32[40,128]{1,0:T(8,128)S(1)}, u32[]{:S(2)}, u32[]{:S(2)}) collective-permute-start(f32[40,128]{1,0:T(8,128)S(1)} %pad_add_fusion), channel_id=1, source_target_pairs={{0,24},{1,25},{2,26},{3,27},{4,28},{5,29},{6,30},{7,31},{8,16},{9,... | collective-permute-start | bytes 61448 | tf_op jit(solution)/shard_map/ppermute | solution.py:58
  98.7 8.3 %collective-permute-start.10 = (f32[2,40,128]{2,1,0:T(8,128)S(1)}, f32[2,40,128]{2,1,0:T(8,128)S(1)}, u32[]{:S(2)}, u32[]{:S(2)}) collective-permute-start(f32[2,40,128]{2,1,0:T(8,128)S(1)} %pad_maximum_fusion.2), channel_id=1, source_target_pairs={{0,64},{1,65},{2,66},{3,67},{4,68},{5,69},{6,70},{7,71},{8,72},{9,... | collective-permute-start | bytes 122888 | tf_op jit(solution)/shard_map/ppermute | solution.py:58
  100.1 6.9 %collective-permute-start.11 = (f32[2,40,128]{2,1,0:T(8,128)S(1)}, f32[2,40,128]{2,1,0:T(8,128)S(1)}, u32[]{:S(2)}, u32[]{:S(2)}) collective-permute-start(f32[2,40,128]{2,1,0:T(8,128)S(1)} %pad_maximum_fusion.2), channel_id=1, source_target_pairs={{0,96},{1,97},{2,98},{3,99},{4,100},{5,101},{6,102},{7,103},{8,104... | collective-permute-start | bytes 122888 | tf_op jit(solution)/shard_map/ppermute | solution.py:58
  101.3 5.7 %collective-permute-start.9 = (f32[2,40,128]{2,1,0:T(8,128)S(1)}, f32[2,40,128]{2,1,0:T(8,128)S(1)}, u32[]{:S(2)}, u32[]{:S(2)}) collective-permute-start(f32[2,40,128]{2,1,0:T(8,128)S(1)} %pad_maximum_fusion.2), channel_id=1, source_target_pairs={{0,32},{1,33},{2,34},{3,35},{4,36},{5,37},{6,38},{7,39},{8,40},{9,... | collective-permute-start | bytes 122888 | tf_op jit(solution)/shard_map/ppermute | solution.py:58
  102.3 20.9 %all-to-all-start.4 = ((f32[8,256,128]{2,1,0:T(8,128)}), f32[8,256,128]{2,1,0:T(8,128)S(1)}, u32[]{:S(2)}, u32[]{:S(2)}) async-start(f32[8,256,128]{2,1,0:T(8,128)} %back.1), calls=%async_computation.4 | async-start | bytes 2097152 | tf_op jit(solution)/shard_map/all_to_all | solution.py:34
  106.9 10.0 %copy-start.3 = (f32[256,128]{1,0:T(8,128)S(1)}, f32[256,128]{1,0:T(8,128)}, u32[]{:S(2)}) copy-start(f32[256,128]{1,0:T(8,128)} %basis_ref.1) | copy-start | bytes 393220
  107.0 1.3 collective-permute-start.12
  108.3 5.3 %collective-permute-start.13 = (f32[4,40,128]{2,1,0:T(8,128)S(1)}, f32[4,40,128]{2,1,0:T(8,128)S(1)}, u32[]{:S(2)}, u32[]{:S(2)}) collective-permute-start(f32[4,40,128]{2,1,0:T(8,128)S(1)} %pad_maximum_fusion), channel_id=1, source_target_pairs={{0,2},{1,3},{2,0},{3,1},{4,6},{5,7},{6,4},{7,5},{8,10},{9,11},{10,... | collective-permute-start | bytes 245768 | tf_op jit(solution)/shard_map/ppermute | solution.py:58
  108.9 6.4 %collective-permute-start.14 = (f32[4,40,128]{2,1,0:T(8,128)S(1)}, f32[4,40,128]{2,1,0:T(8,128)S(1)}, u32[]{:S(2)}, u32[]{:S(2)}) collective-permute-start(f32[4,40,128]{2,1,0:T(8,128)S(1)} %pad_maximum_fusion), channel_id=1, source_target_pairs={{0,4},{1,5},{2,6},{3,7},{4,0},{5,1},{6,2},{7,3},{8,12},{9,13},{10,... | collective-permute-start | bytes 245768 | tf_op jit(solution)/shard_map/ppermute | solution.py:58
  110.9 6.0 %collective-permute-start.15 = (f32[4,40,128]{2,1,0:T(8,128)S(1)}, f32[4,40,128]{2,1,0:T(8,128)S(1)}, u32[]{:S(2)}, u32[]{:S(2)}) collective-permute-start(f32[4,40,128]{2,1,0:T(8,128)S(1)} %pad_maximum_fusion), channel_id=1, source_target_pairs={{0,6},{1,7},{2,4},{3,5},{4,2},{5,3},{6,0},{7,1},{8,14},{9,15},{10,... | collective-permute-start | bytes 245768 | tf_op jit(solution)/shard_map/ppermute | solution.py:58
  123.9 1.3 collective-permute-start.16
  125.2 4.9 %collective-permute-start.17 = (f32[128,128]{1,0:T(8,128)S(1)}, f32[128,128]{1,0:T(8,128)S(1)}, u32[]{:S(2)}, u32[]{:S(2)}) collective-permute-start(f32[128,128]{1,0:T(8,128)S(1)} %add.428), channel_id=1, source_target_pairs={{0,2},{1,3},{2,0},{3,1},{4,6},{5,7},{6,4},{7,5},{8,10},{9,11},{10,... | collective-permute-start | bytes 196616 | tf_op jit(solution)/shard_map/ppermute | solution.py:58
  125.3 7.1 %collective-permute-start.18 = (f32[128,128]{1,0:T(8,128)S(1)}, f32[128,128]{1,0:T(8,128)S(1)}, u32[]{:S(2)}, u32[]{:S(2)}) collective-permute-start(f32[128,128]{1,0:T(8,128)S(1)} %add.428), channel_id=1, source_target_pairs={{0,4},{1,5},{2,6},{3,7},{4,0},{5,1},{6,2},{7,3},{8,12},{9,13},{10,... | collective-permute-start | bytes 196616 | tf_op jit(solution)/shard_map/ppermute | solution.py:58
  128.8 5.5 %collective-permute-start.19 = (f32[128,128]{1,0:T(8,128)S(1)}, f32[128,128]{1,0:T(8,128)S(1)}, u32[]{:S(2)}, u32[]{:S(2)}) collective-permute-start(f32[128,128]{1,0:T(8,128)S(1)} %add.428), channel_id=1, source_target_pairs={{0,6},{1,7},{2,4},{3,5},{4,2},{5,3},{6,0},{7,1},{8,14},{9,15},{10,... | collective-permute-start | bytes 196616 | tf_op jit(solution)/shard_map/ppermute | solution.py:58
  134.3 5.7 %collective-permute-start.20 = (f32[128,128]{1,0:T(8,128)S(1)}, f32[128,128]{1,0:T(8,128)S(1)}, u32[]{:S(2)}, u32[]{:S(2)}) collective-permute-start(f32[128,128]{1,0:T(8,128)S(1)} %add_add_fusion.2), channel_id=1, source_target_pairs={{0,8},{1,9},{2,10},{3,11},{4,12},{5,13},{6,14},{7,15},{8,0},{9,1},... | collective-permute-start | bytes 196616 | tf_op jit(solution)/shard_map/ppermute | solution.py:58
  135.9 7.2 %collective-permute-start.21 = (f32[128,128]{1,0:T(8,128)S(1)}, f32[128,128]{1,0:T(8,128)S(1)}, u32[]{:S(2)}, u32[]{:S(2)}) collective-permute-start(f32[128,128]{1,0:T(8,128)S(1)} %add_add_fusion.2), channel_id=1, source_target_pairs={{0,16},{1,17},{2,18},{3,19},{4,20},{5,21},{6,22},{7,23},{8,24},{9,... | collective-permute-start | bytes 196616 | tf_op jit(solution)/shard_map/ppermute | solution.py:58
  140.0 5.5 %collective-permute-start.22 = (f32[128,128]{1,0:T(8,128)S(1)}, f32[128,128]{1,0:T(8,128)S(1)}, u32[]{:S(2)}, u32[]{:S(2)}) collective-permute-start(f32[128,128]{1,0:T(8,128)S(1)} %add_add_fusion.2), channel_id=1, source_target_pairs={{0,24},{1,25},{2,26},{3,27},{4,28},{5,29},{6,30},{7,31},{8,16},{9,... | collective-permute-start | bytes 196616 | tf_op jit(solution)/shard_map/ppermute | solution.py:58
  145.5 4.8 %collective-permute-start.23 = (f32[128,128]{1,0:T(8,128)S(1)}, f32[128,128]{1,0:T(8,128)S(1)}, u32[]{:S(2)}, u32[]{:S(2)}) collective-permute-start(f32[128,128]{1,0:T(8,128)S(1)} %add_add_fusion.1), channel_id=1, source_target_pairs={{0,32},{1,33},{2,34},{3,35},{4,36},{5,37},{6,38},{7,39},{8,40},{9,... | collective-permute-start | bytes 196616 | tf_op jit(solution)/shard_map/ppermute | solution.py:58
  147.0 5.8 %collective-permute-start.24 = (f32[128,128]{1,0:T(8,128)S(1)}, f32[128,128]{1,0:T(8,128)S(1)}, u32[]{:S(2)}, u32[]{:S(2)}) collective-permute-start(f32[128,128]{1,0:T(8,128)S(1)} %add_add_fusion.1), channel_id=1, source_target_pairs={{0,64},{1,65},{2,66},{3,67},{4,68},{5,69},{6,70},{7,71},{8,72},{9,... | collective-permute-start | bytes 196616 | tf_op jit(solution)/shard_map/ppermute | solution.py:58
  149.7 5.5 %collective-permute-start.25 = (f32[128,128]{1,0:T(8,128)S(1)}, f32[128,128]{1,0:T(8,128)S(1)}, u32[]{:S(2)}, u32[]{:S(2)}) collective-permute-start(f32[128,128]{1,0:T(8,128)S(1)} %add_add_fusion.1), channel_id=1, source_target_pairs={{0,96},{1,97},{2,98},{3,99},{4,100},{5,101},{6,102},{7,103},{8,104... | collective-permute-start | bytes 196616 | tf_op jit(solution)/shard_map/ppermute | solution.py:58

commit v12 on v11

--- a/solution.py
+++ b/solution.py
@@ -78,12 +78,14 @@
 
 def gather_more(array, axis, groups):
     for masks in groups:
-        array = jnp.concatenate([array] + [from_peer(array, axis, mask) for mask in masks], axis=0)
+        far_first = masks[1:] + masks[:1]
+        peers = {mask: from_peer(array, axis, mask) for mask in far_first}
+        array = jnp.concatenate([array] + [peers[mask] for mask in masks], axis=0)
     return array
 
 
 BRICK_GROUPS = ((1,), (2, 4, 6), (8,))
-ALL_GROUPS = ((1,), (2, 4, 6), (8, 16, 24), (32, 64, 96))
+ALL_GROUPS = ((1,), (4, 6, 2), (16, 24, 8), (64, 96, 32))
 
 
 def three_parts(array):

time: 160 us -> 155 us (0.969)
  waiting for transfers between devices: 58.2 us -> 55.4 us
  starting transfers between devices: 56.7 us -> 54.5 us
    ppermute x25, waiting for transfers between devices: 28.2 us -> 25.4 us  [from_peer(): return lax.ppermute(values, axis, [(i, i ^ mask) for i in range(peers)])]
    ppermute x25, starting transfers between devices: 34.1 us -> 31.8 us  [from_peer(): return lax.ppermute(values, axis, [(i, i ^ mask) for i in range(peers)])]
  transfers between devices with their start and end apart: 30 -> 30, of which waited for: 21 -> 20; matrix products, arithmetic and copies ran while one was open for 1% -> 1% of each run, Pallas kernels for 8% -> 8%
where the time goes in v12:
time: 155 us
  waiting for transfers between devices  55.4 us (36%)
  starting transfers between devices  54.5 us (35%)
  Pallas kernels  25.1 us (16%)
  blocking collectives  14.2 us (9%)
  local copies, waits for them, and re-layouts  3.11 us (2%)
    ppermute x25, starting transfers between devices, from_peer(): return lax.ppermute(values, axis, [(i, i ^ mask) for i in range(peers)])  31.8 us
    all_to_all x4, waiting for transfers between devices, exchange(): return lax.all_to_all(array, axis, 0, 0, tiled=True)  27.2 us
    ppermute x25, waiting for transfers between devices, from_peer(): return lax.ppermute(values, axis, [(i, i ^ mask) for i in range(peers)])  25.4 us
    all_to_all x4, starting transfers between devices, exchange(): return lax.all_to_all(array, axis, 0, 0, tiled=True)  21.6 us
    all_to_all x1, blocking collectives, exchange(): return lax.all_to_all(array, axis, 0, 0, tiled=True)  14.2 us
    pallas_call x1, Pallas kernels, local(): pl.pallas_call(functools.partial(middle_kernel, lengths=lengths, time_ste...  6.2 us
    pallas_call x1, Pallas kernels, local(): pl.pallas_call(last_kernel, out_shape=(f32(rank, rank), f32(rows, rank)),...  4.5 us
    pallas_call x1, Pallas kernels, local(): pl.pallas_call(maxwell_kernel, out_shape=(f32(bricks, cells + 3 * height,...  3.68 us
  transfers between devices with their start and end apart: 30, of which 20 were waited for; matrix products, arithmetic and copies ran while one was open for 1% of the time, Pallas kernels for 8%

profile of v12, /device:TPU:0, one launch (start us, length us, event | category | flops | bytes accessed | tf_op | source)
XLA Modules:
  0.0 154.6 jit_solution(593612833909985238)
XLA Ops:
  0.7 0.7 copy-done
  1.4 0.9 copy-done.2
  2.3 1.2 repeat.1
  3.5 7.0 %all-to-all-start = ((f32[8,288,128]{2,1,0:T(8,128)}), f32[8,288,128]{2,1,0:T(8,128)S(1)}, u32[]{:S(2)}, u32[]{:S(2)}) async-start(f32[8,288,128]{2,1,0:T(8,128)} %repeat.1), calls=%async_computation | async-start | bytes 2359296 | tf_op jit(solution)/shard_map/all_to_all | solution.py:34
  10.8 0.1 copy.24
  11.0 0.2 and_select_fusion.3
  11.4 0.4 collective-permute-done
  11.8 1.9 %collective-permute-start.1 = (f32[2,64,128]{2,1,0:T(8,128)S(1)}, f32[2,64,128]{2,1,0:T(8,128)S(1)}, u32[]{:S(2)}, u32[]{:S(2)}) collective-permute-start(f32[2,64,128]{2,1,0:T(8,128)S(1)} %pad_maximum_fusion.1), channel_id=1, source_target_pairs={{0,2},{1,3},{2,0},{3,1},{4,6},{5,7},{6,4},{7,5},{8,10},{9,11},{10,... | collective-permute-start | bytes 196616 | tf_op jit(solution)/shard_map/ppermute | solution.py:58
  13.8 3.6 %collective-permute-start.2 = (f32[2,64,128]{2,1,0:T(8,128)S(1)}, f32[2,64,128]{2,1,0:T(8,128)S(1)}, u32[]{:S(2)}, u32[]{:S(2)}) collective-permute-start(f32[2,64,128]{2,1,0:T(8,128)S(1)} %pad_maximum_fusion.1), channel_id=1, source_target_pairs={{0,4},{1,5},{2,6},{3,7},{4,0},{5,1},{6,2},{7,3},{8,12},{9,13},{10,... | collective-permute-start | bytes 196616 | tf_op jit(solution)/shard_map/ppermute | solution.py:58
  17.4 3.5 %collective-permute-done.2 = f32[2,64,128]{2,1,0:T(8,128)S(1)} collective-permute-done((f32[2,64,128]{2,1,0:T(8,128)S(1)}, f32[2,64,128]{2,1,0:T(8,128)S(1)}, u32[]{:S(2)}, u32[]{:S(2)}) %collective-permute-start.2) | collective-permute-done | bytes 65568 | tf_op jit(solution)/shard_map/ppermute | solution.py:58
  20.9 1.9 %collective-permute-done.3 = f32[2,64,128]{2,1,0:T(8,128)S(1)} collective-permute-done((f32[2,64,128]{2,1,0:T(8,128)S(1)}, f32[2,64,128]{2,1,0:T(8,128)S(1)}, u32[]{:S(2)}, u32[]{:S(2)}) %collective-permute-start.3) | collective-permute-done | bytes 65568 | tf_op jit(solution)/shard_map/ppermute | solution.py:58
  22.8 6.4 %all-to-all-done.nodes_ref = f32[8,288,128]{2,1,0:T(8,128)S(1)} async-done(((f32[8,288,128]{2,1,0:T(8,128)}), f32[8,288,128]{2,1,0:T(8,128)S(1)}, u32[]{:S(2)}, u32[]{:S(2)}) %all-to-all-start) | async-done | bytes 1179680 | tf_op jit(solution)/shard_map/all_to_all | solution.py:34
  29.2 0.6 collective-permute-start.4
  29.8 0.3 minimum_reduce_fusion
  30.2 0.1 copy.25.columns_ref
  30.6 3.1 %transport.1 = f32[16,32,128]{2,1,0:T(8,128)} custom-call(f32[8,288,128]{2,1,0:T(8,128)S(1)} %all-to-all-done.nodes_ref, f32[256,8]{1,0:T(8,128)S(1)} %copy.25.columns_ref, f32[8,128]{1,0:T(8,128)S(1)} %broadcast_in_dim.18.speeds_ref.first_ref, f32[8,8,256]{2,1,0:T(8,128)S(1)} %stack.61.weights_ref), custom_call_target="tpu_custom_call" | custom-call | tf_op jit(solution)/shard_map/transport/pallas_call | solution.py:520
  33.7 6.3 %all-to-all-start.1 = ((f32[16,32,128]{2,1,0:T(8,128)}), f32[16,32,128]{2,1,0:T(8,128)S(1)}, u32[]{:S(2)}, u32[]{:S(2)}) async-start(f32[16,32,128]{2,1,0:T(8,128)} %transport.1), calls=%async_computation.1 | async-start | bytes 524288 | tf_op jit(solution)/shard_map/all_to_all | solution.py:34
  40.2 7.9 %all-to-all-done.1.integrals_ref = f32[16,32,128]{2,1,0:T(8,128)S(1)} async-done(((f32[16,32,128]{2,1,0:T(8,128)}), f32[16,32,128]{2,1,0:T(8,128)S(1)}, u32[]{:S(2)}, u32[]{:S(2)}) %all-to-all-start.1) | async-done | bytes 262176 | tf_op jit(solution)/shard_map/all_to_all | solution.py:34
  48.1 3.7 %maxwell.1 = (f32[16,88,128]{2,1,0:T(8,128)}, f32[1024,8]{1,0:T(8,128)S(1)}, f32[8,1024]{1,0:T(8,128)S(1)}, f32[8,128]{1,0:T(8,128)S(1)}) custom-call(s32[1]{0:T(128)} %bitcast.brick_ref, f32[16,64,128]{2,1,0:T(8,128)S(1)} %constant_dynamic-update-slice_fusion.5.cells_ref, f32[16,32,128]{2,1,0:T(8,128)S(1)} %all-to-all-done.1.integrals_ref, ...), custom_call_target="tpu_custom_call" | custom-call | tf_op jit(solution)/shard_map/maxwell/pallas_call | solution.py:526
  51.8 3.6 %all-to-all-start.2 = ((f32[16,88,128]{2,1,0:T(8,128)}), f32[16,88,128]{2,1,0:T(8,128)S(1)}, u32[]{:S(2)}, u32[]{:S(2)}) async-start(f32[16,88,128]{2,1,0:T(8,128)} %get-tuple-element.27), calls=%async_computation.2 | async-start | bytes 1441792 | tf_op jit(solution)/shard_map/all_to_all | solution.py:34
  55.5 12.9 %all-to-all-done.2.parts_ref = f32[16,88,128]{2,1,0:T(8,128)S(1)} async-done(((f32[16,88,128]{2,1,0:T(8,128)}), f32[16,88,128]{2,1,0:T(8,128)S(1)}, u32[]{:S(2)}, u32[]{:S(2)}) %all-to-all-start.2) | async-done | bytes 720928 | tf_op jit(solution)/shard_map/all_to_all | solution.py:34
  68.4 0.9 advance.1
  69.3 14.2 %all_to_all.25.parts_ref = f32[16,72,128]{2,1,0:T(8,128)S(1)} all-to-all(f32[16,72,128]{2,1,0:T(8,128)S(1)} %get-tuple-element.29), channel_id=1, replica_groups=mesh['slab'=8,'brick'=16] {'brick'}, dimensions={0} | all-to-all | bytes 1179648 | tf_op jit(solution)/shard_map/all_to_all | solution.py:34
  83.4 1.2 products.1
  84.6 1.1 collective-permute-start.5
  85.7 3.6 %back.1 = f32[8,256,128]{2,1,0:T(8,128)} custom-call(f32[16,72,128]{2,1,0:T(8,128)S(1)} %all_to_all.25.parts_ref, f32[1024,8]{1,0:T(8,128)S(1)} %get-tuple-element.34.line_ref, f32[8,1024]{1,0:T(8,128)S(1)} %get-tuple-element.35.state_ref, f32[256,2]{1,0:T(8,128)S(1)} %get-tuple-element.62.across_ref), custom_call_target="tpu_custom_call" | custom-call | tf_op jit(solution)/shard_map/back/pallas_call | solution.py:581
  89.4 2.8 %collective-permute-done.5 = f32[8,512]{1,0:T(8,128)S(1)} collective-permute-done((f32[8,512]{1,0:T(8,128)S(1)}, f32[8,512]{1,0:T(8,128)S(1)}, u32[]{:S(2)}, u32[]{:S(2)}) %collective-permute-start.5) | collective-permute-done | bytes 16416 | tf_op jit(solution)/shard_map/ppermute | solution.py:578
  92.3 0.2 fusion.31
  92.6 0.1 copy.27
  92.7 0.7 collective-permute-start.7
  93.4 3.5 %collective-permute-start.8 = (f32[40,128]{1,0:T(8,128)S(1)}, f32[40,128]{1,0:T(8,128)S(1)}, u32[]{:S(2)}, u32[]{:S(2)}) collective-permute-start(f32[40,128]{1,0:T(8,128)S(1)} %pad_add_fusion), channel_id=1, source_target_pairs={{0,24},{1,25},{2,26},{3,27},{4,28},{5,29},{6,30},{7,31},{8,16},{9,... | collective-permute-start | bytes 61448 | tf_op jit(solution)/shard_map/ppermute | solution.py:58
  96.9 1.0 collective-permute-done.6
  97.9 0.8 collective-permute-done.8
  98.7 1.4 collective-permute-start.10
  100.1 1.2 collective-permute-start.11
  101.3 1.0 collective-permute-start.9
  102.3 4.7 %all-to-all-start.4 = ((f32[8,256,128]{2,1,0:T(8,128)}), f32[8,256,128]{2,1,0:T(8,128)S(1)}, u32[]{:S(2)}, u32[]{:S(2)}) async-start(f32[8,256,128]{2,1,0:T(8,128)} %back.1), calls=%async_computation.4 | async-start | bytes 2097152 | tf_op jit(solution)/shard_map/all_to_all | solution.py:34
  107.1 0.3 slice_reduce_fusion
  107.4 0.1 copy.28.speeds_ref
  107.5 0.8 collective-permute-done.12
  108.3 0.6 collective-permute-start.13
  108.9 2.1 %collective-permute-start.14 = (f32[4,40,128]{2,1,0:T(8,128)S(1)}, f32[4,40,128]{2,1,0:T(8,128)S(1)}, u32[]{:S(2)}, u32[]{:S(2)}) collective-permute-start(f32[4,40,128]{2,1,0:T(8,128)S(1)} %pad_maximum_fusion), channel_id=1, source_target_pairs={{0,4},{1,5},{2,6},{3,7},{4,0},{5,1},{6,2},{7,3},{8,12},{9,13},{10,... | collective-permute-start | bytes 245768 | tf_op jit(solution)/shard_map/ppermute | solution.py:58
  110.9 2.1 %collective-permute-start.15 = (f32[4,40,128]{2,1,0:T(8,128)S(1)}, f32[4,40,128]{2,1,0:T(8,128)S(1)}, u32[]{:S(2)}, u32[]{:S(2)}) collective-permute-start(f32[4,40,128]{2,1,0:T(8,128)S(1)} %pad_maximum_fusion), channel_id=1, source_target_pairs={{0,6},{1,7},{2,4},{3,5},{4,2},{5,3},{6,0},{7,1},{8,14},{9,15},{10,... | collective-permute-start | bytes 245768 | tf_op jit(solution)/shard_map/ppermute | solution.py:58
  113.0 0.6 collective-permute-done.13
  113.6 1.7 %collective-permute-done.14 = f32[4,40,128]{2,1,0:T(8,128)S(1)} collective-permute-done((f32[4,40,128]{2,1,0:T(8,128)S(1)}, f32[4,40,128]{2,1,0:T(8,128)S(1)}, u32[]{:S(2)}, u32[]{:S(2)}) %collective-permute-start.14) | collective-permute-done | bytes 81952 | tf_op jit(solution)/shard_map/ppermute | solution.py:58
  115.3 1.7 %collective-permute-done.15 = f32[4,40,128]{2,1,0:T(8,128)S(1)} collective-permute-done((f32[4,40,128]{2,1,0:T(8,128)S(1)}, f32[4,40,128]{2,1,0:T(8,128)S(1)}, u32[]{:S(2)}, u32[]{:S(2)}) %collective-permute-start.15) | collective-permute-done | bytes 81952 | tf_op jit(solution)/shard_map/ppermute | solution.py:58
  116.9 6.2 %middle.1 = (f32[64,128]{1,0:T(8,128)}, f32[256,128]{1,0:T(8,128)S(1)}, f32[128,128]{1,0:T(8,128)S(1)}) custom-call(s32[1]{0:T(128)} %bitcast.brick_ref, f32[16,40,128]{2,1,0:T(8,128)S(1)} %constant_dynamic-update-slice_fusion.13.pieces_ref, f32[6,128,128]{2,1,0:T(8,128)S(1)} %get-tuple-element.37.transport_ref, f32[256,128]{1,0:T(8,128)S(1)} %copy-done.3, ...), custom_call_target="tpu_custom_call" | custom-call | tf_op jit(solution)/shard_map/middle/pallas_call | solution.py:597
  123.1 0.7 update.1
  124.0 1.2 collective-permute-done.16
  125.2 1.2 collective-permute-start.17
  126.5 1.5 collective-permute-start.18
  128.0 0.8 collective-permute-start.19
  128.8 2.3 %collective-permute-done.17 = f32[128,128]{1,0:T(8,128)S(1)} collective-permute-done((f32[128,128]{1,0:T(8,128)S(1)}, f32[128,128]{1,0:T(8,128)S(1)}, u32[]{:S(2)}, u32[]{:S(2)}) %collective-permute-start.17) | collective-permute-done | bytes 65568 | tf_op jit(solution)/shard_map/ppermute | solution.py:58
  131.1 1.2 collective-permute-done.18
  132.4 3.6 %collective-permute-start.20 = (f32[128,128]{1,0:T(8,128)S(1)}, f32[128,128]{1,0:T(8,128)S(1)}, u32[]{:S(2)}, u32[]{:S(2)}) collective-permute-start(f32[128,128]{1,0:T(8,128)S(1)} %add_add_fusion.2), channel_id=1, source_target_pairs={{0,16},{1,17},{2,18},{3,19},{4,20},{5,21},{6,22},{7,23},{8,24},{9,... | collective-permute-start | bytes 196616 | tf_op jit(solution)/shard_map/ppermute | solution.py:58
  136.0 0.8 collective-permute-start.21
  136.8 0.8 collective-permute-start.22
  137.5 0.8 collective-permute-done.20
  138.3 3.2 %collective-permute-done.21 = f32[128,128]{1,0:T(8,128)S(1)} collective-permute-done((f32[128,128]{1,0:T(8,128)S(1)}, f32[128,128]{1,0:T(8,128)S(1)}, u32[]{:S(2)}, u32[]{:S(2)}) %collective-permute-start.21) | collective-permute-done | bytes 65568 | tf_op jit(solution)/shard_map/ppermute | solution.py:58
  141.5 3.1 %collective-permute-start.23 = (f32[128,128]{1,0:T(8,128)S(1)}, f32[128,128]{1,0:T(8,128)S(1)}, u32[]{:S(2)}, u32[]{:S(2)}) collective-permute-start(f32[128,128]{1,0:T(8,128)S(1)} %add_add_fusion.1), channel_id=1, source_target_pairs={{0,64},{1,65},{2,66},{3,67},{4,68},{5,69},{6,70},{7,71},{8,72},{9,... | collective-permute-start | bytes 196616 | tf_op jit(solution)/shard_map/ppermute | solution.py:58
  144.6 1.2 collective-permute-start.24
  145.7 1.7 %collective-permute-done.23 = f32[128,128]{1,0:T(8,128)S(1)} collective-permute-done((f32[128,128]{1,0:T(8,128)S(1)}, f32[128,128]{1,0:T(8,128)S(1)}, u32[]{:S(2)}, u32[]{:S(2)}) %collective-permute-start.23) | collective-permute-done | bytes 65568 | tf_op jit(solution)/shard_map/ppermute | solution.py:58
  147.4 2.6 %collective-permute-done.24 = f32[128,128]{1,0:T(8,128)S(1)} collective-permute-done((f32[128,128]{1,0:T(8,128)S(1)}, f32[128,128]{1,0:T(8,128)S(1)}, u32[]{:S(2)}, u32[]{:S(2)}) %collective-permute-start.24) | collective-permute-done | bytes 65568 | tf_op jit(solution)/shard_map/ppermute | solution.py:58
  150.1 4.5 %last.1 = (f32[128,128]{1,0:T(8,128)}, f32[256,128]{1,0:T(8,128)}) custom-call(f32[128,128]{1,0:T(8,128)S(1)} %add_add_fusion.gram_ref, f32[256,128]{1,0:T(8,128)S(1)} %get-tuple-element.44.velocity_ref), custom_call_target="tpu_custom_call" | custom-call | tf_op jit(solution)/shard_map/last/pallas_call | solution.py:614
  (86 shorter events, 1.4 us)
Async XLA Ops:
  0.6 0.8 copy-start
  1.4 0.9 copy-start.2
  3.5 7.0 %copy-start.1 = (f32[2,2,16,128]{3,2,1,0:T(8,128)S(1)}, f32[2,2,16,128]{3,2,1,0:T(8,128)}, u32[]{:S(2)}) copy-start(f32[2,2,16,128]{3,2,1,0:T(8,128)} %param.2) | copy-start | bytes 98308
  3.5 25.7 %all-to-all-start = ((f32[8,288,128]{2,1,0:T(8,128)}), f32[8,288,128]{2,1,0:T(8,128)S(1)}, u32[]{:S(2)}, u32[]{:S(2)}) async-start(f32[8,288,128]{2,1,0:T(8,128)} %repeat.1), calls=%async_computation | async-start | bytes 2359296 | tf_op jit(solution)/shard_map/all_to_all | solution.py:34
  10.6 1.3 collective-permute-start
  11.8 5.5 %collective-permute-start.1 = (f32[2,64,128]{2,1,0:T(8,128)S(1)}, f32[2,64,128]{2,1,0:T(8,128)S(1)}, u32[]{:S(2)}, u32[]{:S(2)}) collective-permute-start(f32[2,64,128]{2,1,0:T(8,128)S(1)} %pad_maximum_fusion.1), channel_id=1, source_target_pairs={{0,2},{1,3},{2,0},{3,1},{4,6},{5,7},{6,4},{7,5},{8,10},{9,11},{10,... | collective-permute-start | bytes 196616 | tf_op jit(solution)/shard_map/ppermute | solution.py:58
  13.8 7.1 %collective-permute-start.2 = (f32[2,64,128]{2,1,0:T(8,128)S(1)}, f32[2,64,128]{2,1,0:T(8,128)S(1)}, u32[]{:S(2)}, u32[]{:S(2)}) collective-permute-start(f32[2,64,128]{2,1,0:T(8,128)S(1)} %pad_maximum_fusion.1), channel_id=1, source_target_pairs={{0,4},{1,5},{2,6},{3,7},{4,0},{5,1},{6,2},{7,3},{8,12},{9,13},{10,... | collective-permute-start | bytes 196616 | tf_op jit(solution)/shard_map/ppermute | solution.py:58
  17.3 5.5 %collective-permute-start.3 = (f32[2,64,128]{2,1,0:T(8,128)S(1)}, f32[2,64,128]{2,1,0:T(8,128)S(1)}, u32[]{:S(2)}, u32[]{:S(2)}) collective-permute-start(f32[2,64,128]{2,1,0:T(8,128)S(1)} %pad_maximum_fusion.1), channel_id=1, source_target_pairs={{0,6},{1,7},{2,4},{3,5},{4,2},{5,3},{6,0},{7,1},{8,14},{9,15},{10,... | collective-permute-start | bytes 196616 | tf_op jit(solution)/shard_map/ppermute | solution.py:58
  29.2 10.9 %collective-permute-start.4 = (f32[8,64,128]{2,1,0:T(8,128)S(1)}, f32[8,64,128]{2,1,0:T(8,128)S(1)}, u32[]{:S(2)}, u32[]{:S(2)}) collective-permute-start(f32[8,64,128]{2,1,0:T(8,128)S(1)} %constant_dynamic-update-slice_fusion), channel_id=1, source_target_pairs={{0,8},{1,9},{2,10},{3,11},{4,12},{5,13},{6,14},{7,15},{8,0},{9,1},... | collective-permute-start | bytes 786440 | tf_op jit(solution)/shard_map/ppermute | solution.py:58
  33.7 14.4 %all-to-all-start.1 = ((f32[16,32,128]{2,1,0:T(8,128)}), f32[16,32,128]{2,1,0:T(8,128)S(1)}, u32[]{:S(2)}, u32[]{:S(2)}) async-start(f32[16,32,128]{2,1,0:T(8,128)} %transport.1), calls=%async_computation.1 | async-start | bytes 524288 | tf_op jit(solution)/shard_map/all_to_all | solution.py:34
  51.8 16.6 %all-to-all-start.2 = ((f32[16,88,128]{2,1,0:T(8,128)}), f32[16,88,128]{2,1,0:T(8,128)S(1)}, u32[]{:S(2)}, u32[]{:S(2)}) async-start(f32[16,88,128]{2,1,0:T(8,128)} %get-tuple-element.27), calls=%async_computation.2 | async-start | bytes 1441792 | tf_op jit(solution)/shard_map/all_to_all | solution.py:34
  84.6 7.6 %collective-permute-start.5 = (f32[8,512]{1,0:T(8,128)S(1)}, f32[8,512]{1,0:T(8,128)S(1)}, u32[]{:S(2)}, u32[]{:S(2)}) collective-permute-start(f32[8,512]{1,0:T(8,128)S(1)} %get-tuple-element.32), channel_id=1, source_target_pairs={{0,16},{16,32},{32,48},{48,64},{64,80},{80,96},{96,112},{112,0},{1... | collective-permute-start | bytes 49160 | tf_op jit(solution)/shard_map/ppermute | solution.py:578
  92.5 5.4 %collective-permute-start.6 = (f32[40,128]{1,0:T(8,128)S(1)}, f32[40,128]{1,0:T(8,128)S(1)}, u32[]{:S(2)}, u32[]{:S(2)}) collective-permute-start(f32[40,128]{1,0:T(8,128)S(1)} %pad_add_fusion), channel_id=1, source_target_pairs={{0,16},{1,17},{2,18},{3,19},{4,20},{5,21},{6,22},{7,23},{8,24},{9,... | collective-permute-start | bytes 61448 | tf_op jit(solution)/shard_map/ppermute | solution.py:58
  92.7 5.1 %collective-permute-start.7 = (f32[40,128]{1,0:T(8,128)S(1)}, f32[40,128]{1,0:T(8,128)S(1)}, u32[]{:S(2)}, u32[]{:S(2)}) collective-permute-start(f32[40,128]{1,0:T(8,128)S(1)} %pad_add_fusion), channel_id=1, source_target_pairs={{0,8},{1,9},{2,10},{3,11},{4,12},{5,13},{6,14},{7,15},{8,0},{9,1},... | collective-permute-start | bytes 61448 | tf_op jit(solution)/shard_map/ppermute | solution.py:58
  93.4 5.3 %collective-permute-start.8 = (f32[40,128]{1,0:T(8,128)S(1)}, f32[40,128]{1,0:T(8,128)S(1)}, u32[]{:S(2)}, u32[]{:S(2)}) collective-permute-start(f32[40,128]{1,0:T(8,128)S(1)} %pad_add_fusion), channel_id=1, source_target_pairs={{0,24},{1,25},{2,26},{3,27},{4,28},{5,29},{6,30},{7,31},{8,16},{9,... | collective-permute-start | bytes 61448 | tf_op jit(solution)/shard_map/ppermute | solution.py:58
  98.7 8.3 %collective-permute-start.10 = (f32[2,40,128]{2,1,0:T(8,128)S(1)}, f32[2,40,128]{2,1,0:T(8,128)S(1)}, u32[]{:S(2)}, u32[]{:S(2)}) collective-permute-start(f32[2,40,128]{2,1,0:T(8,128)S(1)} %pad_maximum_fusion.2), channel_id=1, source_target_pairs={{0,64},{1,65},{2,66},{3,67},{4,68},{5,69},{6,70},{7,71},{8,72},{9,... | collective-permute-start | bytes 122888 | tf_op jit(solution)/shard_map/ppermute | solution.py:58
  100.1 6.9 %collective-permute-start.11 = (f32[2,40,128]{2,1,0:T(8,128)S(1)}, f32[2,40,128]{2,1,0:T(8,128)S(1)}, u32[]{:S(2)}, u32[]{:S(2)}) collective-permute-start(f32[2,40,128]{2,1,0:T(8,128)S(1)} %pad_maximum_fusion.2), channel_id=1, source_target_pairs={{0,96},{1,97},{2,98},{3,99},{4,100},{5,101},{6,102},{7,103},{8,104... | collective-permute-start | bytes 122888 | tf_op jit(solution)/shard_map/ppermute | solution.py:58
  101.3 5.7 %collective-permute-start.9 = (f32[2,40,128]{2,1,0:T(8,128)S(1)}, f32[2,40,128]{2,1,0:T(8,128)S(1)}, u32[]{:S(2)}, u32[]{:S(2)}) collective-permute-start(f32[2,40,128]{2,1,0:T(8,128)S(1)} %pad_maximum_fusion.2), channel_id=1, source_target_pairs={{0,32},{1,33},{2,34},{3,35},{4,36},{5,37},{6,38},{7,39},{8,40},{9,... | collective-permute-start | bytes 122888 | tf_op jit(solution)/shard_map/ppermute | solution.py:58
  102.3 20.9 %all-to-all-start.4 = ((f32[8,256,128]{2,1,0:T(8,128)}), f32[8,256,128]{2,1,0:T(8,128)S(1)}, u32[]{:S(2)}, u32[]{:S(2)}) async-start(f32[8,256,128]{2,1,0:T(8,128)} %back.1), calls=%async_computation.4 | async-start | bytes 2097152 | tf_op jit(solution)/shard_map/all_to_all | solution.py:34
  106.9 10.0 %copy-start.3 = (f32[256,128]{1,0:T(8,128)S(1)}, f32[256,128]{1,0:T(8,128)}, u32[]{:S(2)}) copy-start(f32[256,128]{1,0:T(8,128)} %basis_ref.1) | copy-start | bytes 393220
  107.0 1.3 collective-permute-start.12
  108.3 5.3 %collective-permute-start.13 = (f32[4,40,128]{2,1,0:T(8,128)S(1)}, f32[4,40,128]{2,1,0:T(8,128)S(1)}, u32[]{:S(2)}, u32[]{:S(2)}) collective-permute-start(f32[4,40,128]{2,1,0:T(8,128)S(1)} %pad_maximum_fusion), channel_id=1, source_target_pairs={{0,2},{1,3},{2,0},{3,1},{4,6},{5,7},{6,4},{7,5},{8,10},{9,11},{10,... | collective-permute-start | bytes 245768 | tf_op jit(solution)/shard_map/ppermute | solution.py:58
  108.9 6.4 %collective-permute-start.14 = (f32[4,40,128]{2,1,0:T(8,128)S(1)}, f32[4,40,128]{2,1,0:T(8,128)S(1)}, u32[]{:S(2)}, u32[]{:S(2)}) collective-permute-start(f32[4,40,128]{2,1,0:T(8,128)S(1)} %pad_maximum_fusion), channel_id=1, source_target_pairs={{0,4},{1,5},{2,6},{3,7},{4,0},{5,1},{6,2},{7,3},{8,12},{9,13},{10,... | collective-permute-start | bytes 245768 | tf_op jit(solution)/shard_map/ppermute | solution.py:58
  110.9 6.0 %collective-permute-start.15 = (f32[4,40,128]{2,1,0:T(8,128)S(1)}, f32[4,40,128]{2,1,0:T(8,128)S(1)}, u32[]{:S(2)}, u32[]{:S(2)}) collective-permute-start(f32[4,40,128]{2,1,0:T(8,128)S(1)} %pad_maximum_fusion), channel_id=1, source_target_pairs={{0,6},{1,7},{2,4},{3,5},{4,2},{5,3},{6,0},{7,1},{8,14},{9,15},{10,... | collective-permute-start | bytes 245768 | tf_op jit(solution)/shard_map/ppermute | solution.py:58
  123.9 1.3 collective-permute-start.16
  125.2 5.9 %collective-permute-start.17 = (f32[128,128]{1,0:T(8,128)S(1)}, f32[128,128]{1,0:T(8,128)S(1)}, u32[]{:S(2)}, u32[]{:S(2)}) collective-permute-start(f32[128,128]{1,0:T(8,128)S(1)} %add.428), channel_id=1, source_target_pairs={{0,4},{1,5},{2,6},{3,7},{4,0},{5,1},{6,2},{7,3},{8,12},{9,13},{10,... | collective-permute-start | bytes 196616 | tf_op jit(solution)/shard_map/ppermute | solution.py:58
  126.5 5.9 %collective-permute-start.18 = (f32[128,128]{1,0:T(8,128)S(1)}, f32[128,128]{1,0:T(8,128)S(1)}, u32[]{:S(2)}, u32[]{:S(2)}) collective-permute-start(f32[128,128]{1,0:T(8,128)S(1)} %add.428), channel_id=1, source_target_pairs={{0,6},{1,7},{2,4},{3,5},{4,2},{5,3},{6,0},{7,1},{8,14},{9,15},{10,... | collective-permute-start | bytes 196616 | tf_op jit(solution)/shard_map/ppermute | solution.py:58
  128.0 4.4 %collective-permute-start.19 = (f32[128,128]{1,0:T(8,128)S(1)}, f32[128,128]{1,0:T(8,128)S(1)}, u32[]{:S(2)}, u32[]{:S(2)}) collective-permute-start(f32[128,128]{1,0:T(8,128)S(1)} %add.428), channel_id=1, source_target_pairs={{0,2},{1,3},{2,0},{3,1},{4,6},{5,7},{6,4},{7,5},{8,10},{9,11},{10,... | collective-permute-start | bytes 196616 | tf_op jit(solution)/shard_map/ppermute | solution.py:58
  132.4 5.9 %collective-permute-start.20 = (f32[128,128]{1,0:T(8,128)S(1)}, f32[128,128]{1,0:T(8,128)S(1)}, u32[]{:S(2)}, u32[]{:S(2)}) collective-permute-start(f32[128,128]{1,0:T(8,128)S(1)} %add_add_fusion.2), channel_id=1, source_target_pairs={{0,16},{1,17},{2,18},{3,19},{4,20},{5,21},{6,22},{7,23},{8,24},{9,... | collective-permute-start | bytes 196616 | tf_op jit(solution)/shard_map/ppermute | solution.py:58
  136.0 5.5 %collective-permute-start.21 = (f32[128,128]{1,0:T(8,128)S(1)}, f32[128,128]{1,0:T(8,128)S(1)}, u32[]{:S(2)}, u32[]{:S(2)}) collective-permute-start(f32[128,128]{1,0:T(8,128)S(1)} %add_add_fusion.2), channel_id=1, source_target_pairs={{0,24},{1,25},{2,26},{3,27},{4,28},{5,29},{6,30},{7,31},{8,16},{9,... | collective-permute-start | bytes 196616 | tf_op jit(solution)/shard_map/ppermute | solution.py:58
  136.8 4.7 %collective-permute-start.22 = (f32[128,128]{1,0:T(8,128)S(1)}, f32[128,128]{1,0:T(8,128)S(1)}, u32[]{:S(2)}, u32[]{:S(2)}) collective-permute-start(f32[128,128]{1,0:T(8,128)S(1)} %add_add_fusion.2), channel_id=1, source_target_pairs={{0,8},{1,9},{2,10},{3,11},{4,12},{5,13},{6,14},{7,15},{8,0},{9,1},... | collective-permute-start | bytes 196616 | tf_op jit(solution)/shard_map/ppermute | solution.py:58
  141.5 5.9 %collective-permute-start.23 = (f32[128,128]{1,0:T(8,128)S(1)}, f32[128,128]{1,0:T(8,128)S(1)}, u32[]{:S(2)}, u32[]{:S(2)}) collective-permute-start(f32[128,128]{1,0:T(8,128)S(1)} %add_add_fusion.1), channel_id=1, source_target_pairs={{0,64},{1,65},{2,66},{3,67},{4,68},{5,69},{6,70},{7,71},{8,72},{9,... | collective-permute-start | bytes 196616 | tf_op jit(solution)/shard_map/ppermute | solution.py:58
  144.6 5.5 %collective-permute-start.24 = (f32[128,128]{1,0:T(8,128)S(1)}, f32[128,128]{1,0:T(8,128)S(1)}, u32[]{:S(2)}, u32[]{:S(2)}) collective-permute-start(f32[128,128]{1,0:T(8,128)S(1)} %add_add_fusion.1), channel_id=1, source_target_pairs={{0,96},{1,97},{2,98},{3,99},{4,100},{5,101},{6,102},{7,103},{8,104... | collective-permute-start | bytes 196616 | tf_op jit(solution)/shard_map/ppermute | solution.py:58
  145.7 4.3 %collective-permute-start.25 = (f32[128,128]{1,0:T(8,128)S(1)}, f32[128,128]{1,0:T(8,128)S(1)}, u32[]{:S(2)}, u32[]{:S(2)}) collective-permute-start(f32[128,128]{1,0:T(8,128)S(1)} %add_add_fusion.1), channel_id=1, source_target_pairs={{0,32},{1,33},{2,34},{3,35},{4,36},{5,37},{6,38},{7,39},{8,40},{9,... | collective-permute-start | bytes 196616 | tf_op jit(solution)/shard_map/ppermute | solution.py:58

commit v13 on v11

--- a/solution.py
+++ b/solution.py
@@ -83,7 +83,7 @@
 
 
 BRICK_GROUPS = ((1,), (2, 4, 6), (8,))
-ALL_GROUPS = ((1,), (2, 4, 6), (8, 16, 24), (32, 64, 96))
+ALL_GROUPS = ((1,), (4, 6, 2), (16, 24, 8), (64, 96, 32))
 
 
 def three_parts(array):
@@ -146,22 +146,31 @@
             work_ref[stop:, :] = work_ref[stop:, :] - update[stop:, :]
 
 
-def repeat_kernel(below_ref, source_ref, cells_ref, out_ref, sems):
+def repeat_kernel(below_ref, source_ref, cells_ref, out_ref, nodes_ref, planes_ref, sems):
     rows = source_ref.shape[0]
     plane = out_ref.shape[1] - rows
     last = cells_ref.shape[0] - plane
-    copies = []
-    for i in range(out_ref.shape[0]):
+    groups = out_ref.shape[0]
+    fetch_nodes = pltpu.make_async_copy(source_ref, nodes_ref, sems.at[0, groups])
+    fetch_planes = pltpu.make_async_copy(cells_ref, planes_ref, sems.at[1, groups])
+    fetch_nodes.start()
+    fetch_planes.start()
+    to_nodes, to_planes = [], []
+    for i in range(groups):
         start = pl.multiple_of(jnp.where(below_ref[0] == i, 0, last), 8)
-        copies.append(pltpu.make_async_copy(source_ref, out_ref.at[i, :rows], sems.at[0, i]))
-        copies.append(
+        to_nodes.append(pltpu.make_async_copy(nodes_ref, out_ref.at[i, :rows], sems.at[0, i]))
+        to_planes.append(
             pltpu.make_async_copy(
-                cells_ref.at[pl.ds(start, plane)], out_ref.at[i, rows:], sems.at[1, i]
+                planes_ref.at[pl.ds(start, plane)], out_ref.at[i, rows:], sems.at[1, i]
             )
         )
-    for copy in copies:
+    fetch_nodes.wait()
+    for copy in to_nodes:
         copy.start()
-    for copy in copies:
+    fetch_planes.wait()
+    for copy in to_planes:
+        copy.start()
+    for copy in to_nodes + to_planes:
         copy.wait()
 
 
@@ -395,7 +404,9 @@
     rows = basis_ref.shape[0]
     height = rank // bricks
     masks = [j ^ brick_ref[0] for j in range(bricks)]
-    slots = [((m >> 1) & 3) * 4 + (m & 1) * 2 + (m >> 3) for m in masks]
+    depths = [(m >> 1) & 3 for m in masks]
+    depths = [jnp.where(depth == 0, 0, (depth + 1) % 3 + 1) for depth in depths]
+    slots = [depth * 4 + (m & 1) * 2 + (m >> 3) for depth, m in zip(depths, masks)]
 
     def piece(ref, i):
         if ref is transport_ref:
@@ -432,18 +443,35 @@
     velocity_ref[...] = now - time_step * drift_sum - COLLIDE * now
 
 
-def update_kernel(back_ref, velocity_ref, inverse_ref, updated_ref, gram_ref, *, weight_x):
+def update_kernel(back_ref, velocity_ref, inverse_ref, updated_ref, packed_ref, *, weight_x):
     back = back_ref[0]
     for i in range(1, back_ref.shape[0]):
         back = back + back_ref[i]
     back_proj = contract(back * weight_x, inverse_ref[...], 1, 1)
     updated = velocity_ref[...] + COLLIDE * back_proj
     updated_ref[...] = updated
-    gram_ref[...] = contract(updated, updated, 0, 0) * WEIGHT_V
-
-
-def last_kernel(gram_ref, velocity_ref, coupling_ref, basis_ref, work_ref, upper_ref, inverse_ref):
-    factor_into(gram_ref[...], work_ref, upper_ref, inverse_ref)
+    gram = contract(updated, updated, 0, 0) * WEIGHT_V
+    half = gram.shape[0] // 2
+    row = lax.broadcasted_iota(jnp.int32, (half, 2 * half), 0)
+    col = lax.broadcasted_iota(jnp.int32, (half, 2 * half), 1)
+    second = pltpu.roll(gram[half:], half, 1)
+    diagonal = jnp.sum(jnp.where(row == col, second, 0.0), axis=0, keepdims=True)
+    packed_ref[:half, :] = jnp.where(col < row, second, gram[:half])
+    packed_ref[half:, :] = jnp.broadcast_to(diagonal, (8, 2 * half))
+
+
+def last_kernel(packed_ref, velocity_ref, coupling_ref, basis_ref, work_ref, upper_ref, inverse_ref):
+    half = packed_ref.shape[1] // 2
+    packed = packed_ref[:half, :]
+    row = lax.broadcasted_iota(jnp.int32, (half, 2 * half), 0)
+    col = lax.broadcasted_iota(jnp.int32, (half, 2 * half), 1)
+    turned = jnp.concatenate([packed, jnp.zeros_like(packed)], axis=0).T[:half]
+    second = jnp.where(col < row, packed, turned)
+    second = jnp.where(col == row, packed_ref[half : half + 1, :], second)
+    gram = jnp.concatenate(
+        [jnp.where(col >= row, packed, turned), pltpu.roll(second, half, 1)], axis=0
+    )
+    factor_into(gram, work_ref, upper_ref, inverse_ref)
     coupling_ref[...] = upper_ref[...].T
     basis_ref[...] = contract(velocity_ref[...], inverse_ref[...], 1, 1)
 
@@ -491,9 +519,13 @@
         pl.pallas_call(
             repeat_kernel,
             out_shape=f32(slabs, rows + plane, rank),
-            in_specs=vector_specs + [whole] * 2,
+            in_specs=vector_specs + [pl.BlockSpec(memory_space=pltpu.HBM)] * 2,
             out_specs=pl.BlockSpec(memory_space=pl.ANY),
-            scratch_shapes=[pltpu.SemaphoreType.DMA((2, slabs))],
+            scratch_shapes=[
+                pltpu.VMEM((rows, rank), jnp.float32),
+                pltpu.VMEM((cells, rank), jnp.float32),
+                pltpu.SemaphoreType.DMA((2, slabs + 1)),
+            ],
             name="repeat",
             compiler_params=pltpu.CompilerParams(vmem_limit_bytes=VMEM_BYTES),
         )(((slab + slabs - 1) % slabs).astype(jnp.int32)[None], v_basis, own_cells),
@@ -589,7 +621,7 @@
     lower_x, upper_x, cross_x = (from_peer(pieces, both, mask) for mask in (8, 16, 24))
     reduced = jnp.stack([pieces + upper_x, lower_x + cross_x])
     reduced = sum_over(reduced, both, ((32, 64, 96),))
-    reduced = gather_more(reduced, both, ((1,), (2, 4, 6)))
+    reduced = gather_more(reduced, both, ((1,), (4, 6, 2)))
 
     speeds = jnp.stack(list(own_velocity) + [jnp.zeros_like(ones)] * 5, axis=1)
     basis_new, velocity_part, inverse = pl.pallas_call(
@@ -604,7 +636,7 @@
     )(brick_id, reduced, transport, v_basis, advanced, speeds)
     velocity_new, gram_part = pl.pallas_call(
         functools.partial(update_kernel, weight_x=weight_x),
-        out_shape=(f32(rows, rank), f32(rank, rank)),
+        out_shape=(f32(rows, rank), f32(rank // 2 + 8, rank)),
         name="update",
         compiler_params=pltpu.CompilerParams(vmem_limit_bytes=VMEM_BYTES),
     )(fourth, velocity_part, inverse)

time: 160 us -> 154 us (0.963)
  starting transfers between devices: 56.7 us -> 53.1 us
  waiting for transfers between devices: 58.2 us -> 54.9 us
    ppermute x25, starting transfers between devices: 34.1 us -> 30.5 us  [from_peer(): return lax.ppermute(values, axis, [(i, i ^ mask) for i in range(peers)])]
    ppermute x25, waiting for transfers between devices: 28.2 us -> 24.9 us  [from_peer(): return lax.ppermute(values, axis, [(i, i ^ mask) for i in range(peers)])]
  transfers between devices with their start and end apart: 30 -> 30, of which waited for: 21 -> 20; matrix products, arithmetic and copies ran while one was open for 1% -> 1% of each run, Pallas kernels for 8% -> 8%
where the time goes in v13:
time: 154 us; the launch traced here: 153 us
  waiting for transfers between devices  54.9 us (36%)
  starting transfers between devices  53.1 us (34%)
  Pallas kernels  25.5 us (17%)
  blocking collectives  14.2 us (9%)
  local copies, waits for them, and re-layouts  3.11 us (2%)
    ppermute x25, starting transfers between devices, from_peer(): return lax.ppermute(values, axis, [(i, i ^ mask) for i in range(peers)])  30.5 us
    all_to_all x4, waiting for transfers between devices, exchange(): return lax.all_to_all(array, axis, 0, 0, tiled=True)  27.2 us
    ppermute x25, waiting for transfers between devices, from_peer(): return lax.ppermute(values, axis, [(i, i ^ mask) for i in range(peers)])  24.9 us
    all_to_all x4, starting transfers between devices, exchange(): return lax.all_to_all(array, axis, 0, 0, tiled=True)  21.6 us
    all_to_all x1, blocking collectives, exchange(): return lax.all_to_all(array, axis, 0, 0, tiled=True)  14.2 us
    pallas_call x1, Pallas kernels, local(): pl.pallas_call(functools.partial(middle_kernel, lengths=lengths, time_ste...  6.21 us
    pallas_call x1, Pallas kernels, local(): pl.pallas_call(last_kernel, out_shape=(f32(rank, rank), f32(rows, rank)),...  4.63 us
    pallas_call x1, Pallas kernels, local(): pl.pallas_call(maxwell_kernel, out_shape=(f32(bricks, cells + 3 * height,...  3.68 us
  transfers between devices with their start and end apart: 30, of which 20 were waited for; matrix products, arithmetic and copies ran while one was open for 1% of the time, Pallas kernels for 8%

profile of v13, /device:TPU:0, one launch (start us, length us, event | category | flops | bytes accessed | tf_op | source)
XLA Modules:
  0.0 153.2 jit_solution(4308962151379714482)
XLA Ops:
  0.7 0.7 copy-done
  1.4 0.9 copy-done.2
  2.3 1.4 repeat.1
  3.7 7.0 %all-to-all-start = ((f32[8,288,128]{2,1,0:T(8,128)}), f32[8,288,128]{2,1,0:T(8,128)S(1)}, u32[]{:S(2)}, u32[]{:S(2)}) async-start(f32[8,288,128]{2,1,0:T(8,128)} %repeat.1), calls=%async_computation | async-start | bytes 2359296 | tf_op jit(solution)/shard_map/all_to_all | solution.py:34
  11.0 0.1 copy.24
  11.2 0.2 and_select_fusion.3
  11.6 0.4 collective-permute-done
  12.0 1.9 %collective-permute-start.1 = (f32[2,64,128]{2,1,0:T(8,128)S(1)}, f32[2,64,128]{2,1,0:T(8,128)S(1)}, u32[]{:S(2)}, u32[]{:S(2)}) collective-permute-start(f32[2,64,128]{2,1,0:T(8,128)S(1)} %pad_maximum_fusion.1), channel_id=1, source_target_pairs={{0,2},{1,3},{2,0},{3,1},{4,6},{5,7},{6,4},{7,5},{8,10},{9,11},{10,... | collective-permute-start | bytes 196616 | tf_op jit(solution)/shard_map/ppermute | solution.py:58
  14.0 3.6 %collective-permute-start.2 = (f32[2,64,128]{2,1,0:T(8,128)S(1)}, f32[2,64,128]{2,1,0:T(8,128)S(1)}, u32[]{:S(2)}, u32[]{:S(2)}) collective-permute-start(f32[2,64,128]{2,1,0:T(8,128)S(1)} %pad_maximum_fusion.1), channel_id=1, source_target_pairs={{0,4},{1,5},{2,6},{3,7},{4,0},{5,1},{6,2},{7,3},{8,12},{9,13},{10,... | collective-permute-start | bytes 196616 | tf_op jit(solution)/shard_map/ppermute | solution.py:58
  17.6 3.5 %collective-permute-done.2 = f32[2,64,128]{2,1,0:T(8,128)S(1)} collective-permute-done((f32[2,64,128]{2,1,0:T(8,128)S(1)}, f32[2,64,128]{2,1,0:T(8,128)S(1)}, u32[]{:S(2)}, u32[]{:S(2)}) %collective-permute-start.2) | collective-permute-done | bytes 65568 | tf_op jit(solution)/shard_map/ppermute | solution.py:58
  21.1 1.9 %collective-permute-done.3 = f32[2,64,128]{2,1,0:T(8,128)S(1)} collective-permute-done((f32[2,64,128]{2,1,0:T(8,128)S(1)}, f32[2,64,128]{2,1,0:T(8,128)S(1)}, u32[]{:S(2)}, u32[]{:S(2)}) %collective-permute-start.3) | collective-permute-done | bytes 65568 | tf_op jit(solution)/shard_map/ppermute | solution.py:58
  23.0 6.4 %all-to-all-done.nodes_ref = f32[8,288,128]{2,1,0:T(8,128)S(1)} async-done(((f32[8,288,128]{2,1,0:T(8,128)}), f32[8,288,128]{2,1,0:T(8,128)S(1)}, u32[]{:S(2)}, u32[]{:S(2)}) %all-to-all-start) | async-done | bytes 1179680 | tf_op jit(solution)/shard_map/all_to_all | solution.py:34
  29.4 0.6 collective-permute-start.4
  30.0 0.3 minimum_reduce_fusion
  30.4 0.1 copy.25.columns_ref
  30.8 3.1 %transport.1 = f32[16,32,128]{2,1,0:T(8,128)} custom-call(f32[8,288,128]{2,1,0:T(8,128)S(1)} %all-to-all-done.nodes_ref, f32[256,8]{1,0:T(8,128)S(1)} %copy.25.columns_ref, f32[8,128]{1,0:T(8,128)S(1)} %broadcast_in_dim.18.speeds_ref.first_ref, f32[8,8,256]{2,1,0:T(8,128)S(1)} %stack.61.weights_ref), custom_call_target="tpu_custom_call" | custom-call | tf_op jit(solution)/shard_map/transport/pallas_call | solution.py:550
  33.9 6.3 %all-to-all-start.1 = ((f32[16,32,128]{2,1,0:T(8,128)}), f32[16,32,128]{2,1,0:T(8,128)S(1)}, u32[]{:S(2)}, u32[]{:S(2)}) async-start(f32[16,32,128]{2,1,0:T(8,128)} %transport.1), calls=%async_computation.1 | async-start | bytes 524288 | tf_op jit(solution)/shard_map/all_to_all | solution.py:34
  40.3 7.9 %all-to-all-done.1.integrals_ref = f32[16,32,128]{2,1,0:T(8,128)S(1)} async-done(((f32[16,32,128]{2,1,0:T(8,128)}), f32[16,32,128]{2,1,0:T(8,128)S(1)}, u32[]{:S(2)}, u32[]{:S(2)}) %all-to-all-start.1) | async-done | bytes 262176 | tf_op jit(solution)/shard_map/all_to_all | solution.py:34
  48.3 3.7 %maxwell.1 = (f32[16,88,128]{2,1,0:T(8,128)}, f32[1024,8]{1,0:T(8,128)S(1)}, f32[8,1024]{1,0:T(8,128)S(1)}, f32[8,128]{1,0:T(8,128)S(1)}) custom-call(s32[1]{0:T(128)} %bitcast.brick_ref, f32[16,64,128]{2,1,0:T(8,128)S(1)} %constant_dynamic-update-slice_fusion.5.cells_ref, f32[16,32,128]{2,1,0:T(8,128)S(1)} %all-to-all-done.1.integrals_ref, ...), custom_call_target="tpu_custom_call" | custom-call | tf_op jit(solution)/shard_map/maxwell/pallas_call | solution.py:556
  51.9 3.6 %all-to-all-start.2 = ((f32[16,88,128]{2,1,0:T(8,128)}), f32[16,88,128]{2,1,0:T(8,128)S(1)}, u32[]{:S(2)}, u32[]{:S(2)}) async-start(f32[16,88,128]{2,1,0:T(8,128)} %get-tuple-element.27), calls=%async_computation.2 | async-start | bytes 1441792 | tf_op jit(solution)/shard_map/all_to_all | solution.py:34
  55.7 12.9 %all-to-all-done.2.parts_ref = f32[16,88,128]{2,1,0:T(8,128)S(1)} async-done(((f32[16,88,128]{2,1,0:T(8,128)}), f32[16,88,128]{2,1,0:T(8,128)S(1)}, u32[]{:S(2)}, u32[]{:S(2)}) %all-to-all-start.2) | async-done | bytes 720928 | tf_op jit(solution)/shard_map/all_to_all | solution.py:34
  68.6 0.9 advance.1
  69.5 14.2 %all_to_all.25.parts_ref = f32[16,72,128]{2,1,0:T(8,128)S(1)} all-to-all(f32[16,72,128]{2,1,0:T(8,128)S(1)} %get-tuple-element.29), channel_id=1, replica_groups=mesh['slab'=8,'brick'=16] {'brick'}, dimensions={0} | all-to-all | bytes 1179648 | tf_op jit(solution)/shard_map/all_to_all | solution.py:34
  83.6 1.2 products.1
  84.8 1.1 collective-permute-start.5
  85.9 3.6 %back.1 = f32[8,256,128]{2,1,0:T(8,128)} custom-call(f32[16,72,128]{2,1,0:T(8,128)S(1)} %all_to_all.25.parts_ref, f32[1024,8]{1,0:T(8,128)S(1)} %get-tuple-element.34.line_ref, f32[8,1024]{1,0:T(8,128)S(1)} %get-tuple-element.35.state_ref, f32[256,2]{1,0:T(8,128)S(1)} %get-tuple-element.62.across_ref), custom_call_target="tpu_custom_call" | custom-call | tf_op jit(solution)/shard_map/back/pallas_call | solution.py:611
  89.6 2.8 %collective-permute-done.5 = f32[8,512]{1,0:T(8,128)S(1)} collective-permute-done((f32[8,512]{1,0:T(8,128)S(1)}, f32[8,512]{1,0:T(8,128)S(1)}, u32[]{:S(2)}, u32[]{:S(2)}) %collective-permute-start.5) | collective-permute-done | bytes 16416 | tf_op jit(solution)/shard_map/ppermute | solution.py:608
  92.4 0.2 fusion.31
  92.8 0.1 copy.27
  92.9 0.7 collective-permute-start.7
  93.6 3.5 %collective-permute-start.8 = (f32[40,128]{1,0:T(8,128)S(1)}, f32[40,128]{1,0:T(8,128)S(1)}, u32[]{:S(2)}, u32[]{:S(2)}) collective-permute-start(f32[40,128]{1,0:T(8,128)S(1)} %pad_add_fusion), channel_id=1, source_target_pairs={{0,24},{1,25},{2,26},{3,27},{4,28},{5,29},{6,30},{7,31},{8,16},{9,... | collective-permute-start | bytes 61448 | tf_op jit(solution)/shard_map/ppermute | solution.py:58
  97.1 1.0 collective-permute-done.6
  98.1 0.8 collective-permute-done.8
  98.9 1.4 collective-permute-start.10
  100.3 1.2 collective-permute-start.11
  101.5 1.0 collective-permute-start.9
  102.4 4.7 %all-to-all-start.4 = ((f32[8,256,128]{2,1,0:T(8,128)}), f32[8,256,128]{2,1,0:T(8,128)S(1)}, u32[]{:S(2)}, u32[]{:S(2)}) async-start(f32[8,256,128]{2,1,0:T(8,128)} %back.1), calls=%async_computation.4 | async-start | bytes 2097152 | tf_op jit(solution)/shard_map/all_to_all | solution.py:34
  107.3 0.3 slice_reduce_fusion
  107.6 0.1 copy.28.speeds_ref
  107.7 0.8 collective-permute-done.12
  108.5 1.3 collective-permute-start.13
  109.8 1.9 %collective-permute-start.14 = (f32[4,40,128]{2,1,0:T(8,128)S(1)}, f32[4,40,128]{2,1,0:T(8,128)S(1)}, u32[]{:S(2)}, u32[]{:S(2)}) collective-permute-start(f32[4,40,128]{2,1,0:T(8,128)S(1)} %pad_maximum_fusion), channel_id=1, source_target_pairs={{0,6},{1,7},{2,4},{3,5},{4,2},{5,3},{6,0},{7,1},{8,14},{9,15},{10,... | collective-permute-start | bytes 245768 | tf_op jit(solution)/shard_map/ppermute | solution.py:58
  111.7 0.3 collective-permute-start.15
  112.0 2.6 %collective-permute-done.13 = f32[4,40,128]{2,1,0:T(8,128)S(1)} collective-permute-done((f32[4,40,128]{2,1,0:T(8,128)S(1)}, f32[4,40,128]{2,1,0:T(8,128)S(1)}, u32[]{:S(2)}, u32[]{:S(2)}) %collective-permute-start.13) | collective-permute-done | bytes 81952 | tf_op jit(solution)/shard_map/ppermute | solution.py:58
  114.6 1.6 %collective-permute-done.14 = f32[4,40,128]{2,1,0:T(8,128)S(1)} collective-permute-done((f32[4,40,128]{2,1,0:T(8,128)S(1)}, f32[4,40,128]{2,1,0:T(8,128)S(1)}, u32[]{:S(2)}, u32[]{:S(2)}) %collective-permute-start.14) | collective-permute-done | bytes 81952 | tf_op jit(solution)/shard_map/ppermute | solution.py:58
  116.3 6.2 %middle.1 = (f32[64,128]{1,0:T(8,128)}, f32[256,128]{1,0:T(8,128)S(1)}, f32[128,128]{1,0:T(8,128)S(1)}) custom-call(s32[1]{0:T(128)} %bitcast.brick_ref, f32[16,40,128]{2,1,0:T(8,128)S(1)} %constant_dynamic-update-slice_fusion.13.pieces_ref, f32[6,128,128]{2,1,0:T(8,128)S(1)} %get-tuple-element.37.transport_ref, f32[256,128]{1,0:T(8,128)S(1)} %copy-done.3, ...), custom_call_target="tpu_custom_call" | custom-call | tf_op jit(solution)/shard_map/middle/pallas_call | solution.py:627
  122.5 0.8 update.1
  123.4 1.2 collective-permute-done.16
  124.6 1.3 collective-permute-start.17
  126.0 1.6 %collective-permute-start.18 = (f32[72,128]{1,0:T(8,128)S(1)}, f32[72,128]{1,0:T(8,128)S(1)}, u32[]{:S(2)}, u32[]{:S(2)}) collective-permute-start(f32[72,128]{1,0:T(8,128)S(1)} %add.428), channel_id=1, source_target_pairs={{0,6},{1,7},{2,4},{3,5},{4,2},{5,3},{6,0},{7,1},{8,14},{9,15},{10,... | collective-permute-start | bytes 110600 | tf_op jit(solution)/shard_map/ppermute | solution.py:58
  127.5 0.6 collective-permute-start.19
  128.1 2.1 %collective-permute-done.17 = f32[72,128]{1,0:T(8,128)S(1)} collective-permute-done((f32[72,128]{1,0:T(8,128)S(1)}, f32[72,128]{1,0:T(8,128)S(1)}, u32[]{:S(2)}, u32[]{:S(2)}) %collective-permute-start.17) | collective-permute-done | bytes 36896 | tf_op jit(solution)/shard_map/ppermute | solution.py:58
  130.2 0.9 collective-permute-done.18
  131.1 0.4 collective-permute-done.19
  131.5 3.6 %collective-permute-start.20 = (f32[72,128]{1,0:T(8,128)S(1)}, f32[72,128]{1,0:T(8,128)S(1)}, u32[]{:S(2)}, u32[]{:S(2)}) collective-permute-start(f32[72,128]{1,0:T(8,128)S(1)} %add_add_fusion.3), channel_id=1, source_target_pairs={{0,16},{1,17},{2,18},{3,19},{4,20},{5,21},{6,22},{7,23},{8,24},{9,... | collective-permute-start | bytes 110600 | tf_op jit(solution)/shard_map/ppermute | solution.py:58
  135.1 0.8 collective-permute-start.21
  135.9 0.8 collective-permute-start.22
  136.6 0.4 collective-permute-done.20
  137.1 3.2 %collective-permute-done.21 = f32[72,128]{1,0:T(8,128)S(1)} collective-permute-done((f32[72,128]{1,0:T(8,128)S(1)}, f32[72,128]{1,0:T(8,128)S(1)}, u32[]{:S(2)}, u32[]{:S(2)}) %collective-permute-start.21) | collective-permute-done | bytes 36896 | tf_op jit(solution)/shard_map/ppermute | solution.py:58
  140.3 3.1 %collective-permute-start.23 = (f32[72,128]{1,0:T(8,128)S(1)}, f32[72,128]{1,0:T(8,128)S(1)}, u32[]{:S(2)}, u32[]{:S(2)}) collective-permute-start(f32[72,128]{1,0:T(8,128)S(1)} %add_add_fusion.2), channel_id=1, source_target_pairs={{0,64},{1,65},{2,66},{3,67},{4,68},{5,69},{6,70},{7,71},{8,72},{9,... | collective-permute-start | bytes 110600 | tf_op jit(solution)/shard_map/ppermute | solution.py:58
  143.4 1.2 collective-permute-start.24
  144.5 1.6 %collective-permute-done.23 = f32[72,128]{1,0:T(8,128)S(1)} collective-permute-done((f32[72,128]{1,0:T(8,128)S(1)}, f32[72,128]{1,0:T(8,128)S(1)}, u32[]{:S(2)}, u32[]{:S(2)}) %collective-permute-start.23) | collective-permute-done | bytes 36896 | tf_op jit(solution)/shard_map/ppermute | solution.py:58
  146.1 2.4 %collective-permute-done.24 = f32[72,128]{1,0:T(8,128)S(1)} collective-permute-done((f32[72,128]{1,0:T(8,128)S(1)}, f32[72,128]{1,0:T(8,128)S(1)}, u32[]{:S(2)}, u32[]{:S(2)}) %collective-permute-start.24) | collective-permute-done | bytes 36896 | tf_op jit(solution)/shard_map/ppermute | solution.py:58
  148.5 4.6 %last.1 = (f32[128,128]{1,0:T(8,128)}, f32[256,128]{1,0:T(8,128)}) custom-call(f32[72,128]{1,0:T(8,128)S(1)} %add_add_fusion.1.packed_ref, f32[256,128]{1,0:T(8,128)S(1)} %get-tuple-element.44.velocity_ref), custom_call_target="tpu_custom_call" | custom-call | tf_op jit(solution)/shard_map/last/pallas_call | solution.py:644
  (86 shorter events, 1.4 us)
Async XLA Ops:
  0.6 0.8 copy-start
  1.4 0.9 copy-start.2
  3.7 7.0 %copy-start.1 = (f32[2,2,16,128]{3,2,1,0:T(8,128)S(1)}, f32[2,2,16,128]{3,2,1,0:T(8,128)}, u32[]{:S(2)}) copy-start(f32[2,2,16,128]{3,2,1,0:T(8,128)} %param.2) | copy-start | bytes 98308
  3.7 25.7 %all-to-all-start = ((f32[8,288,128]{2,1,0:T(8,128)}), f32[8,288,128]{2,1,0:T(8,128)S(1)}, u32[]{:S(2)}, u32[]{:S(2)}) async-start(f32[8,288,128]{2,1,0:T(8,128)} %repeat.1), calls=%async_computation | async-start | bytes 2359296 | tf_op jit(solution)/shard_map/all_to_all | solution.py:34
  10.7 1.3 collective-permute-start
  12.0 5.5 %collective-permute-start.1 = (f32[2,64,128]{2,1,0:T(8,128)S(1)}, f32[2,64,128]{2,1,0:T(8,128)S(1)}, u32[]{:S(2)}, u32[]{:S(2)}) collective-permute-start(f32[2,64,128]{2,1,0:T(8,128)S(1)} %pad_maximum_fusion.1), channel_id=1, source_target_pairs={{0,2},{1,3},{2,0},{3,1},{4,6},{5,7},{6,4},{7,5},{8,10},{9,11},{10,... | collective-permute-start | bytes 196616 | tf_op jit(solution)/shard_map/ppermute | solution.py:58
  14.0 7.1 %collective-permute-start.2 = (f32[2,64,128]{2,1,0:T(8,128)S(1)}, f32[2,64,128]{2,1,0:T(8,128)S(1)}, u32[]{:S(2)}, u32[]{:S(2)}) collective-permute-start(f32[2,64,128]{2,1,0:T(8,128)S(1)} %pad_maximum_fusion.1), channel_id=1, source_target_pairs={{0,4},{1,5},{2,6},{3,7},{4,0},{5,1},{6,2},{7,3},{8,12},{9,13},{10,... | collective-permute-start | bytes 196616 | tf_op jit(solution)/shard_map/ppermute | solution.py:58
  17.5 5.5 %collective-permute-start.3 = (f32[2,64,128]{2,1,0:T(8,128)S(1)}, f32[2,64,128]{2,1,0:T(8,128)S(1)}, u32[]{:S(2)}, u32[]{:S(2)}) collective-permute-start(f32[2,64,128]{2,1,0:T(8,128)S(1)} %pad_maximum_fusion.1), channel_id=1, source_target_pairs={{0,6},{1,7},{2,4},{3,5},{4,2},{5,3},{6,0},{7,1},{8,14},{9,15},{10,... | collective-permute-start | bytes 196616 | tf_op jit(solution)/shard_map/ppermute | solution.py:58
  29.4 10.9 %collective-permute-start.4 = (f32[8,64,128]{2,1,0:T(8,128)S(1)}, f32[8,64,128]{2,1,0:T(8,128)S(1)}, u32[]{:S(2)}, u32[]{:S(2)}) collective-permute-start(f32[8,64,128]{2,1,0:T(8,128)S(1)} %constant_dynamic-update-slice_fusion), channel_id=1, source_target_pairs={{0,8},{1,9},{2,10},{3,11},{4,12},{5,13},{6,14},{7,15},{8,0},{9,1},... | collective-permute-start | bytes 786440 | tf_op jit(solution)/shard_map/ppermute | solution.py:58
  33.9 14.3 %all-to-all-start.1 = ((f32[16,32,128]{2,1,0:T(8,128)}), f32[16,32,128]{2,1,0:T(8,128)S(1)}, u32[]{:S(2)}, u32[]{:S(2)}) async-start(f32[16,32,128]{2,1,0:T(8,128)} %transport.1), calls=%async_computation.1 | async-start | bytes 524288 | tf_op jit(solution)/shard_map/all_to_all | solution.py:34
  51.9 16.6 %all-to-all-start.2 = ((f32[16,88,128]{2,1,0:T(8,128)}), f32[16,88,128]{2,1,0:T(8,128)S(1)}, u32[]{:S(2)}, u32[]{:S(2)}) async-start(f32[16,88,128]{2,1,0:T(8,128)} %get-tuple-element.27), calls=%async_computation.2 | async-start | bytes 1441792 | tf_op jit(solution)/shard_map/all_to_all | solution.py:34
  84.8 7.6 %collective-permute-start.5 = (f32[8,512]{1,0:T(8,128)S(1)}, f32[8,512]{1,0:T(8,128)S(1)}, u32[]{:S(2)}, u32[]{:S(2)}) collective-permute-start(f32[8,512]{1,0:T(8,128)S(1)} %get-tuple-element.32), channel_id=1, source_target_pairs={{0,16},{16,32},{32,48},{48,64},{64,80},{80,96},{96,112},{112,0},{1... | collective-permute-start | bytes 49160 | tf_op jit(solution)/shard_map/ppermute | solution.py:608
  92.7 5.4 %collective-permute-start.6 = (f32[40,128]{1,0:T(8,128)S(1)}, f32[40,128]{1,0:T(8,128)S(1)}, u32[]{:S(2)}, u32[]{:S(2)}) collective-permute-start(f32[40,128]{1,0:T(8,128)S(1)} %pad_add_fusion), channel_id=1, source_target_pairs={{0,16},{1,17},{2,18},{3,19},{4,20},{5,21},{6,22},{7,23},{8,24},{9,... | collective-permute-start | bytes 61448 | tf_op jit(solution)/shard_map/ppermute | solution.py:58
  92.9 5.1 %collective-permute-start.7 = (f32[40,128]{1,0:T(8,128)S(1)}, f32[40,128]{1,0:T(8,128)S(1)}, u32[]{:S(2)}, u32[]{:S(2)}) collective-permute-start(f32[40,128]{1,0:T(8,128)S(1)} %pad_add_fusion), channel_id=1, source_target_pairs={{0,8},{1,9},{2,10},{3,11},{4,12},{5,13},{6,14},{7,15},{8,0},{9,1},... | collective-permute-start | bytes 61448 | tf_op jit(solution)/shard_map/ppermute | solution.py:58
  93.6 5.3 %collective-permute-start.8 = (f32[40,128]{1,0:T(8,128)S(1)}, f32[40,128]{1,0:T(8,128)S(1)}, u32[]{:S(2)}, u32[]{:S(2)}) collective-permute-start(f32[40,128]{1,0:T(8,128)S(1)} %pad_add_fusion), channel_id=1, source_target_pairs={{0,24},{1,25},{2,26},{3,27},{4,28},{5,29},{6,30},{7,31},{8,16},{9,... | collective-permute-start | bytes 61448 | tf_op jit(solution)/shard_map/ppermute | solution.py:58
  98.9 8.3 %collective-permute-start.10 = (f32[2,40,128]{2,1,0:T(8,128)S(1)}, f32[2,40,128]{2,1,0:T(8,128)S(1)}, u32[]{:S(2)}, u32[]{:S(2)}) collective-permute-start(f32[2,40,128]{2,1,0:T(8,128)S(1)} %pad_maximum_fusion.2), channel_id=1, source_target_pairs={{0,64},{1,65},{2,66},{3,67},{4,68},{5,69},{6,70},{7,71},{8,72},{9,... | collective-permute-start | bytes 122888 | tf_op jit(solution)/shard_map/ppermute | solution.py:58
  100.3 6.9 %collective-permute-start.11 = (f32[2,40,128]{2,1,0:T(8,128)S(1)}, f32[2,40,128]{2,1,0:T(8,128)S(1)}, u32[]{:S(2)}, u32[]{:S(2)}) collective-permute-start(f32[2,40,128]{2,1,0:T(8,128)S(1)} %pad_maximum_fusion.2), channel_id=1, source_target_pairs={{0,96},{1,97},{2,98},{3,99},{4,100},{5,101},{6,102},{7,103},{8,104... | collective-permute-start | bytes 122888 | tf_op jit(solution)/shard_map/ppermute | solution.py:58
  101.5 5.7 %collective-permute-start.9 = (f32[2,40,128]{2,1,0:T(8,128)S(1)}, f32[2,40,128]{2,1,0:T(8,128)S(1)}, u32[]{:S(2)}, u32[]{:S(2)}) collective-permute-start(f32[2,40,128]{2,1,0:T(8,128)S(1)} %pad_maximum_fusion.2), channel_id=1, source_target_pairs={{0,32},{1,33},{2,34},{3,35},{4,36},{5,37},{6,38},{7,39},{8,40},{9,... | collective-permute-start | bytes 122888 | tf_op jit(solution)/shard_map/ppermute | solution.py:58
  102.4 20.1 %all-to-all-start.4 = ((f32[8,256,128]{2,1,0:T(8,128)}), f32[8,256,128]{2,1,0:T(8,128)S(1)}, u32[]{:S(2)}, u32[]{:S(2)}) async-start(f32[8,256,128]{2,1,0:T(8,128)} %back.1), calls=%async_computation.4 | async-start | bytes 2097152 | tf_op jit(solution)/shard_map/all_to_all | solution.py:34
  107.1 9.2 %copy-start.3 = (f32[256,128]{1,0:T(8,128)S(1)}, f32[256,128]{1,0:T(8,128)}, u32[]{:S(2)}) copy-start(f32[256,128]{1,0:T(8,128)} %basis_ref.1) | copy-start | bytes 393220
  107.2 1.3 collective-permute-start.12
  108.5 6.1 %collective-permute-start.13 = (f32[4,40,128]{2,1,0:T(8,128)S(1)}, f32[4,40,128]{2,1,0:T(8,128)S(1)}, u32[]{:S(2)}, u32[]{:S(2)}) collective-permute-start(f32[4,40,128]{2,1,0:T(8,128)S(1)} %pad_maximum_fusion), channel_id=1, source_target_pairs={{0,4},{1,5},{2,6},{3,7},{4,0},{5,1},{6,2},{7,3},{8,12},{9,13},{10,... | collective-permute-start | bytes 245768 | tf_op jit(solution)/shard_map/ppermute | solution.py:58
  109.8 6.4 %collective-permute-start.14 = (f32[4,40,128]{2,1,0:T(8,128)S(1)}, f32[4,40,128]{2,1,0:T(8,128)S(1)}, u32[]{:S(2)}, u32[]{:S(2)}) collective-permute-start(f32[4,40,128]{2,1,0:T(8,128)S(1)} %pad_maximum_fusion), channel_id=1, source_target_pairs={{0,6},{1,7},{2,4},{3,5},{4,2},{5,3},{6,0},{7,1},{8,14},{9,15},{10,... | collective-permute-start | bytes 245768 | tf_op jit(solution)/shard_map/ppermute | solution.py:58
  111.7 4.5 %collective-permute-start.15 = (f32[4,40,128]{2,1,0:T(8,128)S(1)}, f32[4,40,128]{2,1,0:T(8,128)S(1)}, u32[]{:S(2)}, u32[]{:S(2)}) collective-permute-start(f32[4,40,128]{2,1,0:T(8,128)S(1)} %pad_maximum_fusion), channel_id=1, source_target_pairs={{0,2},{1,3},{2,0},{3,1},{4,6},{5,7},{6,4},{7,5},{8,10},{9,11},{10,... | collective-permute-start | bytes 245768 | tf_op jit(solution)/shard_map/ppermute | solution.py:58
  123.3 1.3 collective-permute-start.16
  124.6 5.6 %collective-permute-start.17 = (f32[72,128]{1,0:T(8,128)S(1)}, f32[72,128]{1,0:T(8,128)S(1)}, u32[]{:S(2)}, u32[]{:S(2)}) collective-permute-start(f32[72,128]{1,0:T(8,128)S(1)} %add.428), channel_id=1, source_target_pairs={{0,4},{1,5},{2,6},{3,7},{4,0},{5,1},{6,2},{7,3},{8,12},{9,13},{10,... | collective-permute-start | bytes 110600 | tf_op jit(solution)/shard_map/ppermute | solution.py:58
  126.0 5.2 %collective-permute-start.18 = (f32[72,128]{1,0:T(8,128)S(1)}, f32[72,128]{1,0:T(8,128)S(1)}, u32[]{:S(2)}, u32[]{:S(2)}) collective-permute-start(f32[72,128]{1,0:T(8,128)S(1)} %add.428), channel_id=1, source_target_pairs={{0,6},{1,7},{2,4},{3,5},{4,2},{5,3},{6,0},{7,1},{8,14},{9,15},{10,... | collective-permute-start | bytes 110600 | tf_op jit(solution)/shard_map/ppermute | solution.py:58
  127.5 4.0 %collective-permute-start.19 = (f32[72,128]{1,0:T(8,128)S(1)}, f32[72,128]{1,0:T(8,128)S(1)}, u32[]{:S(2)}, u32[]{:S(2)}) collective-permute-start(f32[72,128]{1,0:T(8,128)S(1)} %add.428), channel_id=1, source_target_pairs={{0,2},{1,3},{2,0},{3,1},{4,6},{5,7},{6,4},{7,5},{8,10},{9,11},{10,... | collective-permute-start | bytes 110600 | tf_op jit(solution)/shard_map/ppermute | solution.py:58
  131.5 5.5 %collective-permute-start.20 = (f32[72,128]{1,0:T(8,128)S(1)}, f32[72,128]{1,0:T(8,128)S(1)}, u32[]{:S(2)}, u32[]{:S(2)}) collective-permute-start(f32[72,128]{1,0:T(8,128)S(1)} %add_add_fusion.3), channel_id=1, source_target_pairs={{0,16},{1,17},{2,18},{3,19},{4,20},{5,21},{6,22},{7,23},{8,24},{9,... | collective-permute-start | bytes 110600 | tf_op jit(solution)/shard_map/ppermute | solution.py:58
  135.1 5.2 %collective-permute-start.21 = (f32[72,128]{1,0:T(8,128)S(1)}, f32[72,128]{1,0:T(8,128)S(1)}, u32[]{:S(2)}, u32[]{:S(2)}) collective-permute-start(f32[72,128]{1,0:T(8,128)S(1)} %add_add_fusion.3), channel_id=1, source_target_pairs={{0,24},{1,25},{2,26},{3,27},{4,28},{5,29},{6,30},{7,31},{8,16},{9,... | collective-permute-start | bytes 110600 | tf_op jit(solution)/shard_map/ppermute | solution.py:58
  135.9 4.4 %collective-permute-start.22 = (f32[72,128]{1,0:T(8,128)S(1)}, f32[72,128]{1,0:T(8,128)S(1)}, u32[]{:S(2)}, u32[]{:S(2)}) collective-permute-start(f32[72,128]{1,0:T(8,128)S(1)} %add_add_fusion.3), channel_id=1, source_target_pairs={{0,8},{1,9},{2,10},{3,11},{4,12},{5,13},{6,14},{7,15},{8,0},{9,1},... | collective-permute-start | bytes 110600 | tf_op jit(solution)/shard_map/ppermute | solution.py:58
  140.3 5.8 %collective-permute-start.23 = (f32[72,128]{1,0:T(8,128)S(1)}, f32[72,128]{1,0:T(8,128)S(1)}, u32[]{:S(2)}, u32[]{:S(2)}) collective-permute-start(f32[72,128]{1,0:T(8,128)S(1)} %add_add_fusion.2), channel_id=1, source_target_pairs={{0,64},{1,65},{2,66},{3,67},{4,68},{5,69},{6,70},{7,71},{8,72},{9,... | collective-permute-start | bytes 110600 | tf_op jit(solution)/shard_map/ppermute | solution.py:58
  143.4 5.2 %collective-permute-start.24 = (f32[72,128]{1,0:T(8,128)S(1)}, f32[72,128]{1,0:T(8,128)S(1)}, u32[]{:S(2)}, u32[]{:S(2)}) collective-permute-start(f32[72,128]{1,0:T(8,128)S(1)} %add_add_fusion.2), channel_id=1, source_target_pairs={{0,96},{1,97},{2,98},{3,99},{4,100},{5,101},{6,102},{7,103},{8,104... | collective-permute-start | bytes 110600 | tf_op jit(solution)/shard_map/ppermute | solution.py:58
  144.5 4.0 %collective-permute-start.25 = (f32[72,128]{1,0:T(8,128)S(1)}, f32[72,128]{1,0:T(8,128)S(1)}, u32[]{:S(2)}, u32[]{:S(2)}) collective-permute-start(f32[72,128]{1,0:T(8,128)S(1)} %add_add_fusion.2), channel_id=1, source_target_pairs={{0,32},{1,33},{2,34},{3,35},{4,36},{5,37},{6,38},{7,39},{8,40},{9,... | collective-permute-start | bytes 110600 | tf_op jit(solution)/shard_map/ppermute | solution.py:58

commit v14 on v11

--- a/solution.py
+++ b/solution.py
@@ -83,7 +83,7 @@
 
 
 BRICK_GROUPS = ((1,), (2, 4, 6), (8,))
-ALL_GROUPS = ((1,), (2, 4, 6), (8, 16, 24), (32, 64, 96))
+ALL_GROUPS = ((1,), (4, 2, 6), (16, 8, 24), (64, 32, 96))
 
 
 def three_parts(array):
@@ -395,7 +395,7 @@
     rows = basis_ref.shape[0]
     height = rank // bricks
     masks = [j ^ brick_ref[0] for j in range(bricks)]
-    slots = [((m >> 1) & 3) * 4 + (m & 1) * 2 + (m >> 3) for m in masks]
+    slots = [((m >> 1) & 1) * 8 + ((m >> 2) & 1) * 4 + (m & 1) * 2 + (m >> 3) for m in masks]
 
     def piece(ref, i):
         if ref is transport_ref:
@@ -432,18 +432,35 @@
     velocity_ref[...] = now - time_step * drift_sum - COLLIDE * now
 
 
-def update_kernel(back_ref, velocity_ref, inverse_ref, updated_ref, gram_ref, *, weight_x):
+def update_kernel(back_ref, velocity_ref, inverse_ref, updated_ref, packed_ref, *, weight_x):
     back = back_ref[0]
     for i in range(1, back_ref.shape[0]):
         back = back + back_ref[i]
     back_proj = contract(back * weight_x, inverse_ref[...], 1, 1)
     updated = velocity_ref[...] + COLLIDE * back_proj
     updated_ref[...] = updated
-    gram_ref[...] = contract(updated, updated, 0, 0) * WEIGHT_V
-
-
-def last_kernel(gram_ref, velocity_ref, coupling_ref, basis_ref, work_ref, upper_ref, inverse_ref):
-    factor_into(gram_ref[...], work_ref, upper_ref, inverse_ref)
+    gram = contract(updated, updated, 0, 0) * WEIGHT_V
+    half = gram.shape[0] // 2
+    row = lax.broadcasted_iota(jnp.int32, (half, 2 * half), 0)
+    col = lax.broadcasted_iota(jnp.int32, (half, 2 * half), 1)
+    second = pltpu.roll(gram[half:], half, 1)
+    diagonal = jnp.sum(jnp.where(row == col, second, 0.0), axis=0, keepdims=True)
+    packed_ref[:half, :] = jnp.where(col < row, second, gram[:half])
+    packed_ref[half:, :] = jnp.broadcast_to(diagonal, (8, 2 * half))
+
+
+def last_kernel(packed_ref, velocity_ref, coupling_ref, basis_ref, work_ref, upper_ref, inverse_ref):
+    half = packed_ref.shape[1] // 2
+    packed = packed_ref[:half, :]
+    row = lax.broadcasted_iota(jnp.int32, (half, 2 * half), 0)
+    col = lax.broadcasted_iota(jnp.int32, (half, 2 * half), 1)
+    turned = jnp.concatenate([packed, jnp.zeros_like(packed)], axis=0).T[:half]
+    second = jnp.where(col < row, packed, turned)
+    second = jnp.where(col == row, packed_ref[half : half + 1, :], second)
+    gram = jnp.concatenate(
+        [jnp.where(col >= row, packed, turned), pltpu.roll(second, half, 1)], axis=0
+    )
+    factor_into(gram, work_ref, upper_ref, inverse_ref)
     coupling_ref[...] = upper_ref[...].T
     basis_ref[...] = contract(velocity_ref[...], inverse_ref[...], 1, 1)
 
@@ -588,8 +605,8 @@
     both = ("slab", "brick")
     lower_x, upper_x, cross_x = (from_peer(pieces, both, mask) for mask in (8, 16, 24))
     reduced = jnp.stack([pieces + upper_x, lower_x + cross_x])
-    reduced = sum_over(reduced, both, ((32, 64, 96),))
-    reduced = gather_more(reduced, both, ((1,), (2, 4, 6)))
+    reduced = sum_over(reduced, both, ((96, 64, 32),))
+    reduced = gather_more(reduced, both, ((1,), (4, 2, 6)))
 
     speeds = jnp.stack(list(own_velocity) + [jnp.zeros_like(ones)] * 5, axis=1)
     basis_new, velocity_part, inverse = pl.pallas_call(
@@ -604,7 +621,7 @@
     )(brick_id, reduced, transport, v_basis, advanced, speeds)
     velocity_new, gram_part = pl.pallas_call(
         functools.partial(update_kernel, weight_x=weight_x),
-        out_shape=(f32(rows, rank), f32(rank, rank)),
+        out_shape=(f32(rows, rank), f32(rank // 2 + 8, rank)),
         name="update",
         compiler_params=pltpu.CompilerParams(vmem_limit_bytes=VMEM_BYTES),
     )(fourth, velocity_part, inverse)

time: 160 us -> 157 us (0.981)
  starting transfers between devices: 56.7 us -> 53.9 us
    ppermute x25, starting transfers between devices: 34.1 us -> 32 us  [from_peer(): return lax.ppermute(values, axis, [(i, i ^ mask) for i in range(peers)])]
  transfers between devices with their start and end apart: 30 -> 30, of which waited for: 21 -> 22; matrix products, arithmetic and copies ran while one was open for 1% -> 1% of each run, Pallas kernels for 8% -> 8%
where the time goes in v14:
time: 157 us; the launch traced here: 156 us
  waiting for transfers between devices  57.2 us (36%)
  starting transfers between devices  53.9 us (34%)
  Pallas kernels  25.3 us (16%)
  blocking collectives  14.2 us (9%)
  local copies, waits for them, and re-layouts  3.11 us (2%)
    ppermute x25, starting transfers between devices, from_peer(): return lax.ppermute(values, axis, [(i, i ^ mask) for i in range(peers)])  32 us
    all_to_all x4, waiting for transfers between devices, exchange(): return lax.all_to_all(array, axis, 0, 0, tiled=True)  27.2 us
    ppermute x25, waiting for transfers between devices, from_peer(): return lax.ppermute(values, axis, [(i, i ^ mask) for i in range(peers)])  27.1 us
    all_to_all x4, starting transfers between devices, exchange(): return lax.all_to_all(array, axis, 0, 0, tiled=True)  20.9 us
    all_to_all x1, blocking collectives, exchange(): return lax.all_to_all(array, axis, 0, 0, tiled=True)  14.2 us
    pallas_call x1, Pallas kernels, local(): pl.pallas_call(functools.partial(middle_kernel, lengths=lengths, time_ste...  6.2 us
    pallas_call x1, Pallas kernels, local(): pl.pallas_call(last_kernel, out_shape=(f32(rank, rank), f32(rows, rank)),...  4.63 us
    pallas_call x1, Pallas kernels, local(): pl.pallas_call(maxwell_kernel, out_shape=(f32(bricks, cells + 3 * height,...  3.68 us
  transfers between devices with their start and end apart: 30, of which 22 were waited for; matrix products, arithmetic and copies ran while one was open for 1% of the time, Pallas kernels for 8%

profile of v14, /device:TPU:0, one launch (start us, length us, event | category | flops | bytes accessed | tf_op | source)
XLA Modules:
  0.0 155.9 jit_solution(765239644468832831)
XLA Ops:
  0.7 0.7 copy-done
  1.4 0.9 copy-done.2
  2.3 1.2 repeat.1
  3.5 7.0 %all-to-all-start = ((f32[8,288,128]{2,1,0:T(8,128)}), f32[8,288,128]{2,1,0:T(8,128)S(1)}, u32[]{:S(2)}, u32[]{:S(2)}) async-start(f32[8,288,128]{2,1,0:T(8,128)} %repeat.1), calls=%async_computation | async-start | bytes 2359296 | tf_op jit(solution)/shard_map/all_to_all | solution.py:34
  10.8 0.1 copy.24
  11.0 0.2 and_select_fusion.3
  11.4 0.4 collective-permute-done
  11.8 1.9 %collective-permute-start.1 = (f32[2,64,128]{2,1,0:T(8,128)S(1)}, f32[2,64,128]{2,1,0:T(8,128)S(1)}, u32[]{:S(2)}, u32[]{:S(2)}) collective-permute-start(f32[2,64,128]{2,1,0:T(8,128)S(1)} %pad_maximum_fusion.1), channel_id=1, source_target_pairs={{0,2},{1,3},{2,0},{3,1},{4,6},{5,7},{6,4},{7,5},{8,10},{9,11},{10,... | collective-permute-start | bytes 196616 | tf_op jit(solution)/shard_map/ppermute | solution.py:58
  13.8 3.6 %collective-permute-start.2 = (f32[2,64,128]{2,1,0:T(8,128)S(1)}, f32[2,64,128]{2,1,0:T(8,128)S(1)}, u32[]{:S(2)}, u32[]{:S(2)}) collective-permute-start(f32[2,64,128]{2,1,0:T(8,128)S(1)} %pad_maximum_fusion.1), channel_id=1, source_target_pairs={{0,4},{1,5},{2,6},{3,7},{4,0},{5,1},{6,2},{7,3},{8,12},{9,13},{10,... | collective-permute-start | bytes 196616 | tf_op jit(solution)/shard_map/ppermute | solution.py:58
  17.4 3.5 %collective-permute-done.2 = f32[2,64,128]{2,1,0:T(8,128)S(1)} collective-permute-done((f32[2,64,128]{2,1,0:T(8,128)S(1)}, f32[2,64,128]{2,1,0:T(8,128)S(1)}, u32[]{:S(2)}, u32[]{:S(2)}) %collective-permute-start.2) | collective-permute-done | bytes 65568 | tf_op jit(solution)/shard_map/ppermute | solution.py:58
  20.9 1.9 %collective-permute-done.3 = f32[2,64,128]{2,1,0:T(8,128)S(1)} collective-permute-done((f32[2,64,128]{2,1,0:T(8,128)S(1)}, f32[2,64,128]{2,1,0:T(8,128)S(1)}, u32[]{:S(2)}, u32[]{:S(2)}) %collective-permute-start.3) | collective-permute-done | bytes 65568 | tf_op jit(solution)/shard_map/ppermute | solution.py:58
  22.8 6.4 %all-to-all-done.nodes_ref = f32[8,288,128]{2,1,0:T(8,128)S(1)} async-done(((f32[8,288,128]{2,1,0:T(8,128)}), f32[8,288,128]{2,1,0:T(8,128)S(1)}, u32[]{:S(2)}, u32[]{:S(2)}) %all-to-all-start) | async-done | bytes 1179680 | tf_op jit(solution)/shard_map/all_to_all | solution.py:34
  29.2 0.6 collective-permute-start.4
  29.8 0.3 minimum_reduce_fusion
  30.6 3.1 %transport.1 = f32[16,32,128]{2,1,0:T(8,128)} custom-call(f32[8,288,128]{2,1,0:T(8,128)S(1)} %all-to-all-done.nodes_ref, f32[256,8]{1,0:T(8,128)S(1)} %copy.25.columns_ref, f32[8,128]{1,0:T(8,128)S(1)} %broadcast_in_dim.18.speeds_ref.first_ref, f32[8,8,256]{2,1,0:T(8,128)S(1)} %stack.61.weights_ref), custom_call_target="tpu_custom_call" | custom-call | tf_op jit(solution)/shard_map/transport/pallas_call | solution.py:535
  33.7 6.3 %all-to-all-start.1 = ((f32[16,32,128]{2,1,0:T(8,128)}), f32[16,32,128]{2,1,0:T(8,128)S(1)}, u32[]{:S(2)}, u32[]{:S(2)}) async-start(f32[16,32,128]{2,1,0:T(8,128)} %transport.1), calls=%async_computation.1 | async-start | bytes 524288 | tf_op jit(solution)/shard_map/all_to_all | solution.py:34
  40.2 7.9 %all-to-all-done.1.integrals_ref = f32[16,32,128]{2,1,0:T(8,128)S(1)} async-done(((f32[16,32,128]{2,1,0:T(8,128)}), f32[16,32,128]{2,1,0:T(8,128)S(1)}, u32[]{:S(2)}, u32[]{:S(2)}) %all-to-all-start.1) | async-done | bytes 262176 | tf_op jit(solution)/shard_map/all_to_all | solution.py:34
  48.1 3.7 %maxwell.1 = (f32[16,88,128]{2,1,0:T(8,128)}, f32[1024,8]{1,0:T(8,128)S(1)}, f32[8,1024]{1,0:T(8,128)S(1)}, f32[8,128]{1,0:T(8,128)S(1)}) custom-call(s32[1]{0:T(128)} %bitcast.brick_ref, f32[16,64,128]{2,1,0:T(8,128)S(1)} %constant_dynamic-update-slice_fusion.5.cells_ref, f32[16,32,128]{2,1,0:T(8,128)S(1)} %all-to-all-done.1.integrals_ref, ...), custom_call_target="tpu_custom_call" | custom-call | tf_op jit(solution)/shard_map/maxwell/pallas_call | solution.py:541
  51.8 3.6 %all-to-all-start.2 = ((f32[16,88,128]{2,1,0:T(8,128)}), f32[16,88,128]{2,1,0:T(8,128)S(1)}, u32[]{:S(2)}, u32[]{:S(2)}) async-start(f32[16,88,128]{2,1,0:T(8,128)} %get-tuple-element.27), calls=%async_computation.2 | async-start | bytes 1441792 | tf_op jit(solution)/shard_map/all_to_all | solution.py:34
  55.5 12.9 %all-to-all-done.2.parts_ref = f32[16,88,128]{2,1,0:T(8,128)S(1)} async-done(((f32[16,88,128]{2,1,0:T(8,128)}), f32[16,88,128]{2,1,0:T(8,128)S(1)}, u32[]{:S(2)}, u32[]{:S(2)}) %all-to-all-start.2) | async-done | bytes 720928 | tf_op jit(solution)/shard_map/all_to_all | solution.py:34
  68.4 0.9 advance.1
  69.3 14.2 %all_to_all.25.parts_ref = f32[16,72,128]{2,1,0:T(8,128)S(1)} all-to-all(f32[16,72,128]{2,1,0:T(8,128)S(1)} %get-tuple-element.29), channel_id=1, replica_groups=mesh['slab'=8,'brick'=16] {'brick'}, dimensions={0} | all-to-all | bytes 1179648 | tf_op jit(solution)/shard_map/all_to_all | solution.py:34
  83.4 1.2 products.1
  84.6 1.1 collective-permute-start.5
  85.7 3.6 %back.1 = f32[8,256,128]{2,1,0:T(8,128)} custom-call(f32[16,72,128]{2,1,0:T(8,128)S(1)} %all_to_all.25.parts_ref, f32[1024,8]{1,0:T(8,128)S(1)} %get-tuple-element.34.line_ref, f32[8,1024]{1,0:T(8,128)S(1)} %get-tuple-element.35.state_ref, f32[256,2]{1,0:T(8,128)S(1)} %get-tuple-element.62.across_ref), custom_call_target="tpu_custom_call" | custom-call | tf_op jit(solution)/shard_map/back/pallas_call | solution.py:596
  89.4 2.8 %collective-permute-done.5 = f32[8,512]{1,0:T(8,128)S(1)} collective-permute-done((f32[8,512]{1,0:T(8,128)S(1)}, f32[8,512]{1,0:T(8,128)S(1)}, u32[]{:S(2)}, u32[]{:S(2)}) %collective-permute-start.5) | collective-permute-done | bytes 16416 | tf_op jit(solution)/shard_map/ppermute | solution.py:593
  92.3 0.2 fusion.31
  92.6 0.1 copy.27
  92.7 0.7 collective-permute-start.7
  93.4 3.5 %collective-permute-start.8 = (f32[40,128]{1,0:T(8,128)S(1)}, f32[40,128]{1,0:T(8,128)S(1)}, u32[]{:S(2)}, u32[]{:S(2)}) collective-permute-start(f32[40,128]{1,0:T(8,128)S(1)} %pad_add_fusion), channel_id=1, source_target_pairs={{0,24},{1,25},{2,26},{3,27},{4,28},{5,29},{6,30},{7,31},{8,16},{9,... | collective-permute-start | bytes 61448 | tf_op jit(solution)/shard_map/ppermute | solution.py:58
  96.9 1.0 collective-permute-done.6
  97.9 0.8 collective-permute-done.8
  98.7 1.4 collective-permute-start.10
  100.1 1.8 %collective-permute-start.11 = (f32[2,40,128]{2,1,0:T(8,128)S(1)}, f32[2,40,128]{2,1,0:T(8,128)S(1)}, u32[]{:S(2)}, u32[]{:S(2)}) collective-permute-start(f32[2,40,128]{2,1,0:T(8,128)S(1)} %pad_maximum_fusion.2), channel_id=1, source_target_pairs={{0,32},{1,33},{2,34},{3,35},{4,36},{5,37},{6,38},{7,39},{8,40},{9,... | collective-permute-start | bytes 122888 | tf_op jit(solution)/shard_map/ppermute | solution.py:58
  101.9 1.0 collective-permute-start.9
  102.9 3.9 %all-to-all-start.4 = ((f32[8,256,128]{2,1,0:T(8,128)}), f32[8,256,128]{2,1,0:T(8,128)S(1)}, u32[]{:S(2)}, u32[]{:S(2)}) async-start(f32[8,256,128]{2,1,0:T(8,128)} %back.1), calls=%async_computation.4 | async-start | bytes 2097152 | tf_op jit(solution)/shard_map/all_to_all | solution.py:34
  106.8 0.3 collective-permute-done.9
  107.2 0.3 slice_reduce_fusion
  107.7 0.8 collective-permute-done.12
  108.4 1.3 collective-permute-start.13
  109.8 0.7 collective-permute-start.14
  110.5 2.1 %collective-permute-start.15 = (f32[4,40,128]{2,1,0:T(8,128)S(1)}, f32[4,40,128]{2,1,0:T(8,128)S(1)}, u32[]{:S(2)}, u32[]{:S(2)}) collective-permute-start(f32[4,40,128]{2,1,0:T(8,128)S(1)} %pad_maximum_fusion), channel_id=1, source_target_pairs={{0,6},{1,7},{2,4},{3,5},{4,2},{5,3},{6,0},{7,1},{8,14},{9,15},{10,... | collective-permute-start | bytes 245768 | tf_op jit(solution)/shard_map/ppermute | solution.py:58
  112.5 2.7 %collective-permute-done.13 = f32[4,40,128]{2,1,0:T(8,128)S(1)} collective-permute-done((f32[4,40,128]{2,1,0:T(8,128)S(1)}, f32[4,40,128]{2,1,0:T(8,128)S(1)}, u32[]{:S(2)}, u32[]{:S(2)}) %collective-permute-start.13) | collective-permute-done | bytes 81952 | tf_op jit(solution)/shard_map/ppermute | solution.py:58
  115.3 1.0 collective-permute-done.15
  116.3 6.2 %middle.1 = (f32[64,128]{1,0:T(8,128)}, f32[256,128]{1,0:T(8,128)S(1)}, f32[128,128]{1,0:T(8,128)S(1)}) custom-call(s32[1]{0:T(128)} %bitcast.brick_ref, f32[16,40,128]{2,1,0:T(8,128)S(1)} %constant_dynamic-update-slice_fusion.13.pieces_ref, f32[6,128,128]{2,1,0:T(8,128)S(1)} %get-tuple-element.37.transport_ref, f32[256,128]{1,0:T(8,128)S(1)} %copy-done.3, ...), custom_call_target="tpu_custom_call" | custom-call | tf_op jit(solution)/shard_map/middle/pallas_call | solution.py:612
  122.5 0.8 update.1
  123.4 1.2 collective-permute-done.16
  124.6 1.4 collective-permute-start.17
  126.0 1.3 collective-permute-start.18
  127.4 1.4 collective-permute-start.19
  128.7 1.7 %collective-permute-done.17 = f32[72,128]{1,0:T(8,128)S(1)} collective-permute-done((f32[72,128]{1,0:T(8,128)S(1)}, f32[72,128]{1,0:T(8,128)S(1)}, u32[]{:S(2)}, u32[]{:S(2)}) %collective-permute-start.17) | collective-permute-done | bytes 36896 | tf_op jit(solution)/shard_map/ppermute | solution.py:58
  130.5 2.1 %collective-permute-done.19 = f32[72,128]{1,0:T(8,128)S(1)} collective-permute-done((f32[72,128]{1,0:T(8,128)S(1)}, f32[72,128]{1,0:T(8,128)S(1)}, u32[]{:S(2)}, u32[]{:S(2)}) %collective-permute-start.19) | collective-permute-done | bytes 36896 | tf_op jit(solution)/shard_map/ppermute | solution.py:58
  132.5 3.3 %collective-permute-start.20 = (f32[72,128]{1,0:T(8,128)S(1)}, f32[72,128]{1,0:T(8,128)S(1)}, u32[]{:S(2)}, u32[]{:S(2)}) collective-permute-start(f32[72,128]{1,0:T(8,128)S(1)} %add_add_fusion.3), channel_id=1, source_target_pairs={{0,16},{1,17},{2,18},{3,19},{4,20},{5,21},{6,22},{7,23},{8,24},{9,... | collective-permute-start | bytes 110600 | tf_op jit(solution)/shard_map/ppermute | solution.py:58
  135.9 1.4 collective-permute-start.21
  137.3 0.8 collective-permute-done.20
  138.1 1.8 %collective-permute-done.21 = f32[72,128]{1,0:T(8,128)S(1)} collective-permute-done((f32[72,128]{1,0:T(8,128)S(1)}, f32[72,128]{1,0:T(8,128)S(1)}, u32[]{:S(2)}, u32[]{:S(2)}) %collective-permute-start.21) | collective-permute-done | bytes 36896 | tf_op jit(solution)/shard_map/ppermute | solution.py:58
  139.8 2.7 %collective-permute-done.22 = f32[72,128]{1,0:T(8,128)S(1)} collective-permute-done((f32[72,128]{1,0:T(8,128)S(1)}, f32[72,128]{1,0:T(8,128)S(1)}, u32[]{:S(2)}, u32[]{:S(2)}) %collective-permute-start.22) | collective-permute-done | bytes 36896 | tf_op jit(solution)/shard_map/ppermute | solution.py:58
  142.5 3.0 %collective-permute-start.23 = (f32[72,128]{1,0:T(8,128)S(1)}, f32[72,128]{1,0:T(8,128)S(1)}, u32[]{:S(2)}, u32[]{:S(2)}) collective-permute-start(f32[72,128]{1,0:T(8,128)S(1)} %add_add_fusion.2), channel_id=1, source_target_pairs={{0,64},{1,65},{2,66},{3,67},{4,68},{5,69},{6,70},{7,71},{8,72},{9,... | collective-permute-start | bytes 110600 | tf_op jit(solution)/shard_map/ppermute | solution.py:58
  145.6 0.6 collective-permute-start.24
  146.1 0.6 collective-permute-start.25
  146.7 1.3 collective-permute-done.23
  148.1 1.5 collective-permute-done.24
  149.5 1.8 %collective-permute-done.25 = f32[72,128]{1,0:T(8,128)S(1)} collective-permute-done((f32[72,128]{1,0:T(8,128)S(1)}, f32[72,128]{1,0:T(8,128)S(1)}, u32[]{:S(2)}, u32[]{:S(2)}) %collective-permute-start.25) | collective-permute-done | bytes 36896 | tf_op jit(solution)/shard_map/ppermute | solution.py:58
  151.3 4.6 %last.1 = (f32[128,128]{1,0:T(8,128)}, f32[256,128]{1,0:T(8,128)}) custom-call(f32[72,128]{1,0:T(8,128)S(1)} %add_add_fusion.1.packed_ref, f32[256,128]{1,0:T(8,128)S(1)} %get-tuple-element.44.velocity_ref), custom_call_target="tpu_custom_call" | custom-call | tf_op jit(solution)/shard_map/last/pallas_call | solution.py:629
  (86 shorter events, 1.6 us)
Async XLA Ops:
  0.6 0.8 copy-start
  1.4 0.9 copy-start.2
  3.5 7.0 %copy-start.1 = (f32[2,2,16,128]{3,2,1,0:T(8,128)S(1)}, f32[2,2,16,128]{3,2,1,0:T(8,128)}, u32[]{:S(2)}) copy-start(f32[2,2,16,128]{3,2,1,0:T(8,128)} %param.2) | copy-start | bytes 98308
  3.5 25.7 %all-to-all-start = ((f32[8,288,128]{2,1,0:T(8,128)}), f32[8,288,128]{2,1,0:T(8,128)S(1)}, u32[]{:S(2)}, u32[]{:S(2)}) async-start(f32[8,288,128]{2,1,0:T(8,128)} %repeat.1), calls=%async_computation | async-start | bytes 2359296 | tf_op jit(solution)/shard_map/all_to_all | solution.py:34
  10.6 1.3 collective-permute-start
  11.8 5.5 %collective-permute-start.1 = (f32[2,64,128]{2,1,0:T(8,128)S(1)}, f32[2,64,128]{2,1,0:T(8,128)S(1)}, u32[]{:S(2)}, u32[]{:S(2)}) collective-permute-start(f32[2,64,128]{2,1,0:T(8,128)S(1)} %pad_maximum_fusion.1), channel_id=1, source_target_pairs={{0,2},{1,3},{2,0},{3,1},{4,6},{5,7},{6,4},{7,5},{8,10},{9,11},{10,... | collective-permute-start | bytes 196616 | tf_op jit(solution)/shard_map/ppermute | solution.py:58
  13.8 7.1 %collective-permute-start.2 = (f32[2,64,128]{2,1,0:T(8,128)S(1)}, f32[2,64,128]{2,1,0:T(8,128)S(1)}, u32[]{:S(2)}, u32[]{:S(2)}) collective-permute-start(f32[2,64,128]{2,1,0:T(8,128)S(1)} %pad_maximum_fusion.1), channel_id=1, source_target_pairs={{0,4},{1,5},{2,6},{3,7},{4,0},{5,1},{6,2},{7,3},{8,12},{9,13},{10,... | collective-permute-start | bytes 196616 | tf_op jit(solution)/shard_map/ppermute | solution.py:58
  17.3 5.5 %collective-permute-start.3 = (f32[2,64,128]{2,1,0:T(8,128)S(1)}, f32[2,64,128]{2,1,0:T(8,128)S(1)}, u32[]{:S(2)}, u32[]{:S(2)}) collective-permute-start(f32[2,64,128]{2,1,0:T(8,128)S(1)} %pad_maximum_fusion.1), channel_id=1, source_target_pairs={{0,6},{1,7},{2,4},{3,5},{4,2},{5,3},{6,0},{7,1},{8,14},{9,15},{10,... | collective-permute-start | bytes 196616 | tf_op jit(solution)/shard_map/ppermute | solution.py:58
  29.2 10.9 %collective-permute-start.4 = (f32[8,64,128]{2,1,0:T(8,128)S(1)}, f32[8,64,128]{2,1,0:T(8,128)S(1)}, u32[]{:S(2)}, u32[]{:S(2)}) collective-permute-start(f32[8,64,128]{2,1,0:T(8,128)S(1)} %constant_dynamic-update-slice_fusion), channel_id=1, source_target_pairs={{0,8},{1,9},{2,10},{3,11},{4,12},{5,13},{6,14},{7,15},{8,0},{9,1},... | collective-permute-start | bytes 786440 | tf_op jit(solution)/shard_map/ppermute | solution.py:58
  33.7 14.4 %all-to-all-start.1 = ((f32[16,32,128]{2,1,0:T(8,128)}), f32[16,32,128]{2,1,0:T(8,128)S(1)}, u32[]{:S(2)}, u32[]{:S(2)}) async-start(f32[16,32,128]{2,1,0:T(8,128)} %transport.1), calls=%async_computation.1 | async-start | bytes 524288 | tf_op jit(solution)/shard_map/all_to_all | solution.py:34
  51.8 16.6 %all-to-all-start.2 = ((f32[16,88,128]{2,1,0:T(8,128)}), f32[16,88,128]{2,1,0:T(8,128)S(1)}, u32[]{:S(2)}, u32[]{:S(2)}) async-start(f32[16,88,128]{2,1,0:T(8,128)} %get-tuple-element.27), calls=%async_computation.2 | async-start | bytes 1441792 | tf_op jit(solution)/shard_map/all_to_all | solution.py:34
  84.6 7.6 %collective-permute-start.5 = (f32[8,512]{1,0:T(8,128)S(1)}, f32[8,512]{1,0:T(8,128)S(1)}, u32[]{:S(2)}, u32[]{:S(2)}) collective-permute-start(f32[8,512]{1,0:T(8,128)S(1)} %get-tuple-element.32), channel_id=1, source_target_pairs={{0,16},{16,32},{32,48},{48,64},{64,80},{80,96},{96,112},{112,0},{1... | collective-permute-start | bytes 49160 | tf_op jit(solution)/shard_map/ppermute | solution.py:593
  92.5 5.4 %collective-permute-start.6 = (f32[40,128]{1,0:T(8,128)S(1)}, f32[40,128]{1,0:T(8,128)S(1)}, u32[]{:S(2)}, u32[]{:S(2)}) collective-permute-start(f32[40,128]{1,0:T(8,128)S(1)} %pad_add_fusion), channel_id=1, source_target_pairs={{0,16},{1,17},{2,18},{3,19},{4,20},{5,21},{6,22},{7,23},{8,24},{9,... | collective-permute-start | bytes 61448 | tf_op jit(solution)/shard_map/ppermute | solution.py:58
  92.7 5.1 %collective-permute-start.7 = (f32[40,128]{1,0:T(8,128)S(1)}, f32[40,128]{1,0:T(8,128)S(1)}, u32[]{:S(2)}, u32[]{:S(2)}) collective-permute-start(f32[40,128]{1,0:T(8,128)S(1)} %pad_add_fusion), channel_id=1, source_target_pairs={{0,8},{1,9},{2,10},{3,11},{4,12},{5,13},{6,14},{7,15},{8,0},{9,1},... | collective-permute-start | bytes 61448 | tf_op jit(solution)/shard_map/ppermute | solution.py:58
  93.4 5.3 %collective-permute-start.8 = (f32[40,128]{1,0:T(8,128)S(1)}, f32[40,128]{1,0:T(8,128)S(1)}, u32[]{:S(2)}, u32[]{:S(2)}) collective-permute-start(f32[40,128]{1,0:T(8,128)S(1)} %pad_add_fusion), channel_id=1, source_target_pairs={{0,24},{1,25},{2,26},{3,27},{4,28},{5,29},{6,30},{7,31},{8,16},{9,... | collective-permute-start | bytes 61448 | tf_op jit(solution)/shard_map/ppermute | solution.py:58
  98.7 8.1 %collective-permute-start.10 = (f32[2,40,128]{2,1,0:T(8,128)S(1)}, f32[2,40,128]{2,1,0:T(8,128)S(1)}, u32[]{:S(2)}, u32[]{:S(2)}) collective-permute-start(f32[2,40,128]{2,1,0:T(8,128)S(1)} %pad_maximum_fusion.2), channel_id=1, source_target_pairs={{0,64},{1,65},{2,66},{3,67},{4,68},{5,69},{6,70},{7,71},{8,72},{9,... | collective-permute-start | bytes 122888 | tf_op jit(solution)/shard_map/ppermute | solution.py:58
  100.1 6.7 %collective-permute-start.11 = (f32[2,40,128]{2,1,0:T(8,128)S(1)}, f32[2,40,128]{2,1,0:T(8,128)S(1)}, u32[]{:S(2)}, u32[]{:S(2)}) collective-permute-start(f32[2,40,128]{2,1,0:T(8,128)S(1)} %pad_maximum_fusion.2), channel_id=1, source_target_pairs={{0,32},{1,33},{2,34},{3,35},{4,36},{5,37},{6,38},{7,39},{8,40},{9,... | collective-permute-start | bytes 122888 | tf_op jit(solution)/shard_map/ppermute | solution.py:58
  101.9 5.2 %collective-permute-start.9 = (f32[2,40,128]{2,1,0:T(8,128)S(1)}, f32[2,40,128]{2,1,0:T(8,128)S(1)}, u32[]{:S(2)}, u32[]{:S(2)}) collective-permute-start(f32[2,40,128]{2,1,0:T(8,128)S(1)} %pad_maximum_fusion.2), channel_id=1, source_target_pairs={{0,96},{1,97},{2,98},{3,99},{4,100},{5,101},{6,102},{7,103},{8,104... | collective-permute-start | bytes 122888 | tf_op jit(solution)/shard_map/ppermute | solution.py:58
  102.9 19.7 %all-to-all-start.4 = ((f32[8,256,128]{2,1,0:T(8,128)}), f32[8,256,128]{2,1,0:T(8,128)S(1)}, u32[]{:S(2)}, u32[]{:S(2)}) async-start(f32[8,256,128]{2,1,0:T(8,128)} %back.1), calls=%async_computation.4 | async-start | bytes 2097152 | tf_op jit(solution)/shard_map/all_to_all | solution.py:34
  106.8 9.5 %copy-start.3 = (f32[256,128]{1,0:T(8,128)S(1)}, f32[256,128]{1,0:T(8,128)}, u32[]{:S(2)}) copy-start(f32[256,128]{1,0:T(8,128)} %basis_ref.1) | copy-start | bytes 393220
  107.1 1.3 collective-permute-start.12
  108.4 6.8 %collective-permute-start.13 = (f32[4,40,128]{2,1,0:T(8,128)S(1)}, f32[4,40,128]{2,1,0:T(8,128)S(1)}, u32[]{:S(2)}, u32[]{:S(2)}) collective-permute-start(f32[4,40,128]{2,1,0:T(8,128)S(1)} %pad_maximum_fusion), channel_id=1, source_target_pairs={{0,4},{1,5},{2,6},{3,7},{4,0},{5,1},{6,2},{7,3},{8,12},{9,13},{10,... | collective-permute-start | bytes 245768 | tf_op jit(solution)/shard_map/ppermute | solution.py:58
  109.8 5.5 %collective-permute-start.14 = (f32[4,40,128]{2,1,0:T(8,128)S(1)}, f32[4,40,128]{2,1,0:T(8,128)S(1)}, u32[]{:S(2)}, u32[]{:S(2)}) collective-permute-start(f32[4,40,128]{2,1,0:T(8,128)S(1)} %pad_maximum_fusion), channel_id=1, source_target_pairs={{0,2},{1,3},{2,0},{3,1},{4,6},{5,7},{6,4},{7,5},{8,10},{9,11},{10,... | collective-permute-start | bytes 245768 | tf_op jit(solution)/shard_map/ppermute | solution.py:58
  110.5 5.8 %collective-permute-start.15 = (f32[4,40,128]{2,1,0:T(8,128)S(1)}, f32[4,40,128]{2,1,0:T(8,128)S(1)}, u32[]{:S(2)}, u32[]{:S(2)}) collective-permute-start(f32[4,40,128]{2,1,0:T(8,128)S(1)} %pad_maximum_fusion), channel_id=1, source_target_pairs={{0,6},{1,7},{2,4},{3,5},{4,2},{5,3},{6,0},{7,1},{8,14},{9,15},{10,... | collective-permute-start | bytes 245768 | tf_op jit(solution)/shard_map/ppermute | solution.py:58
  123.3 1.3 collective-permute-start.16
  124.6 5.8 %collective-permute-start.17 = (f32[72,128]{1,0:T(8,128)S(1)}, f32[72,128]{1,0:T(8,128)S(1)}, u32[]{:S(2)}, u32[]{:S(2)}) collective-permute-start(f32[72,128]{1,0:T(8,128)S(1)} %add.428), channel_id=1, source_target_pairs={{0,4},{1,5},{2,6},{3,7},{4,0},{5,1},{6,2},{7,3},{8,12},{9,13},{10,... | collective-permute-start | bytes 110600 | tf_op jit(solution)/shard_map/ppermute | solution.py:58
  126.0 4.4 %collective-permute-start.18 = (f32[72,128]{1,0:T(8,128)S(1)}, f32[72,128]{1,0:T(8,128)S(1)}, u32[]{:S(2)}, u32[]{:S(2)}) collective-permute-start(f32[72,128]{1,0:T(8,128)S(1)} %add.428), channel_id=1, source_target_pairs={{0,2},{1,3},{2,0},{3,1},{4,6},{5,7},{6,4},{7,5},{8,10},{9,11},{10,... | collective-permute-start | bytes 110600 | tf_op jit(solution)/shard_map/ppermute | solution.py:58
  127.4 5.2 %collective-permute-start.19 = (f32[72,128]{1,0:T(8,128)S(1)}, f32[72,128]{1,0:T(8,128)S(1)}, u32[]{:S(2)}, u32[]{:S(2)}) collective-permute-start(f32[72,128]{1,0:T(8,128)S(1)} %add.428), channel_id=1, source_target_pairs={{0,6},{1,7},{2,4},{3,5},{4,2},{5,3},{6,0},{7,1},{8,14},{9,15},{10,... | collective-permute-start | bytes 110600 | tf_op jit(solution)/shard_map/ppermute | solution.py:58
  132.5 5.5 %collective-permute-start.20 = (f32[72,128]{1,0:T(8,128)S(1)}, f32[72,128]{1,0:T(8,128)S(1)}, u32[]{:S(2)}, u32[]{:S(2)}) collective-permute-start(f32[72,128]{1,0:T(8,128)S(1)} %add_add_fusion.3), channel_id=1, source_target_pairs={{0,16},{1,17},{2,18},{3,19},{4,20},{5,21},{6,22},{7,23},{8,24},{9,... | collective-permute-start | bytes 110600 | tf_op jit(solution)/shard_map/ppermute | solution.py:58
  135.9 4.0 %collective-permute-start.21 = (f32[72,128]{1,0:T(8,128)S(1)}, f32[72,128]{1,0:T(8,128)S(1)}, u32[]{:S(2)}, u32[]{:S(2)}) collective-permute-start(f32[72,128]{1,0:T(8,128)S(1)} %add_add_fusion.3), channel_id=1, source_target_pairs={{0,8},{1,9},{2,10},{3,11},{4,12},{5,13},{6,14},{7,15},{8,0},{9,1},... | collective-permute-start | bytes 110600 | tf_op jit(solution)/shard_map/ppermute | solution.py:58
  137.3 5.2 %collective-permute-start.22 = (f32[72,128]{1,0:T(8,128)S(1)}, f32[72,128]{1,0:T(8,128)S(1)}, u32[]{:S(2)}, u32[]{:S(2)}) collective-permute-start(f32[72,128]{1,0:T(8,128)S(1)} %add_add_fusion.3), channel_id=1, source_target_pairs={{0,24},{1,25},{2,26},{3,27},{4,28},{5,29},{6,30},{7,31},{8,16},{9,... | collective-permute-start | bytes 110600 | tf_op jit(solution)/shard_map/ppermute | solution.py:58
  142.5 5.5 %collective-permute-start.23 = (f32[72,128]{1,0:T(8,128)S(1)}, f32[72,128]{1,0:T(8,128)S(1)}, u32[]{:S(2)}, u32[]{:S(2)}) collective-permute-start(f32[72,128]{1,0:T(8,128)S(1)} %add_add_fusion.2), channel_id=1, source_target_pairs={{0,64},{1,65},{2,66},{3,67},{4,68},{5,69},{6,70},{7,71},{8,72},{9,... | collective-permute-start | bytes 110600 | tf_op jit(solution)/shard_map/ppermute | solution.py:58
  145.6 4.0 %collective-permute-start.24 = (f32[72,128]{1,0:T(8,128)S(1)}, f32[72,128]{1,0:T(8,128)S(1)}, u32[]{:S(2)}, u32[]{:S(2)}) collective-permute-start(f32[72,128]{1,0:T(8,128)S(1)} %add_add_fusion.2), channel_id=1, source_target_pairs={{0,32},{1,33},{2,34},{3,35},{4,36},{5,37},{6,38},{7,39},{8,40},{9,... | collective-permute-start | bytes 110600 | tf_op jit(solution)/shard_map/ppermute | solution.py:58
  146.1 5.2 %collective-permute-start.25 = (f32[72,128]{1,0:T(8,128)S(1)}, f32[72,128]{1,0:T(8,128)S(1)}, u32[]{:S(2)}, u32[]{:S(2)}) collective-permute-start(f32[72,128]{1,0:T(8,128)S(1)} %add_add_fusion.2), channel_id=1, source_target_pairs={{0,96},{1,97},{2,98},{3,99},{4,100},{5,101},{6,102},{7,103},{8,104... | collective-permute-start | bytes 110600 | tf_op jit(solution)/shard_map/ppermute | solution.py:58

commit v15 on v14

--- a/solution.py
+++ b/solution.py
@@ -83,7 +83,7 @@
 
 
 BRICK_GROUPS = ((1,), (2, 4, 6), (8,))
-ALL_GROUPS = ((1,), (4, 2, 6), (16, 8, 24), (64, 32, 96))
+ALL_GROUPS = ((1,), (4, 6, 2), (16, 24, 8), (64, 96, 32))
 
 
 def three_parts(array):

time: 157 us -> 154 us (0.981)
  waiting for transfers between devices: 57.2 us -> 55 us
    ppermute x25, waiting for transfers between devices: 27.1 us -> 24.9 us  [from_peer(): return lax.ppermute(values, axis, [(i, i ^ mask) for i in range(peers)])]
  transfers between devices with their start and end apart: 30 -> 30, of which waited for: 22 -> 21; matrix products, arithmetic and copies ran while one was open for 1% -> 1% of each run, Pallas kernels for 8% -> 8%
where the time goes in v15:
time: 154 us; the launch traced here: 153 us
  waiting for transfers between devices  55 us (36%)
  starting transfers between devices  53.3 us (35%)
  Pallas kernels  25.3 us (16%)
  blocking collectives  14.2 us (9%)
  local copies, waits for them, and re-layouts  3.11 us (2%)
    ppermute x25, starting transfers between devices, from_peer(): return lax.ppermute(values, axis, [(i, i ^ mask) for i in range(peers)])  31.3 us
    all_to_all x4, waiting for transfers between devices, exchange(): return lax.all_to_all(array, axis, 0, 0, tiled=True)  27.2 us
    ppermute x25, waiting for transfers between devices, from_peer(): return lax.ppermute(values, axis, [(i, i ^ mask) for i in range(peers)])  24.9 us
    all_to_all x4, starting transfers between devices, exchange(): return lax.all_to_all(array, axis, 0, 0, tiled=True)  20.9 us
    all_to_all x1, blocking collectives, exchange(): return lax.all_to_all(array, axis, 0, 0, tiled=True)  14.2 us
    pallas_call x1, Pallas kernels, local(): pl.pallas_call(functools.partial(middle_kernel, lengths=lengths, time_ste...  6.2 us
    pallas_call x1, Pallas kernels, local(): pl.pallas_call(last_kernel, out_shape=(f32(rank, rank), f32(rows, rank)),...  4.63 us
    pallas_call x1, Pallas kernels, local(): pl.pallas_call(maxwell_kernel, out_shape=(f32(bricks, cells + 3 * height,...  3.68 us
  transfers between devices with their start and end apart: 30, of which 21 were waited for; matrix products, arithmetic and copies ran while one was open for 1% of the time, Pallas kernels for 8%

profile of v15, /device:TPU:0, one launch (start us, length us, event | category | flops | bytes accessed | tf_op | source)
XLA Modules:
  0.0 153.1 jit_solution(4510106969209821551)
XLA Ops:
  0.7 0.7 copy-done
  1.4 0.9 copy-done.2
  2.3 1.2 repeat.1
  3.5 7.0 %all-to-all-start = ((f32[8,288,128]{2,1,0:T(8,128)}), f32[8,288,128]{2,1,0:T(8,128)S(1)}, u32[]{:S(2)}, u32[]{:S(2)}) async-start(f32[8,288,128]{2,1,0:T(8,128)} %repeat.1), calls=%async_computation | async-start | bytes 2359296 | tf_op jit(solution)/shard_map/all_to_all | solution.py:34
  10.8 0.1 copy.24
  11.0 0.2 and_select_fusion.3
  11.4 0.4 collective-permute-done
  11.8 1.9 %collective-permute-start.1 = (f32[2,64,128]{2,1,0:T(8,128)S(1)}, f32[2,64,128]{2,1,0:T(8,128)S(1)}, u32[]{:S(2)}, u32[]{:S(2)}) collective-permute-start(f32[2,64,128]{2,1,0:T(8,128)S(1)} %pad_maximum_fusion.1), channel_id=1, source_target_pairs={{0,2},{1,3},{2,0},{3,1},{4,6},{5,7},{6,4},{7,5},{8,10},{9,11},{10,... | collective-permute-start | bytes 196616 | tf_op jit(solution)/shard_map/ppermute | solution.py:58
  13.8 3.6 %collective-permute-start.2 = (f32[2,64,128]{2,1,0:T(8,128)S(1)}, f32[2,64,128]{2,1,0:T(8,128)S(1)}, u32[]{:S(2)}, u32[]{:S(2)}) collective-permute-start(f32[2,64,128]{2,1,0:T(8,128)S(1)} %pad_maximum_fusion.1), channel_id=1, source_target_pairs={{0,4},{1,5},{2,6},{3,7},{4,0},{5,1},{6,2},{7,3},{8,12},{9,13},{10,... | collective-permute-start | bytes 196616 | tf_op jit(solution)/shard_map/ppermute | solution.py:58
  17.4 3.5 %collective-permute-done.2 = f32[2,64,128]{2,1,0:T(8,128)S(1)} collective-permute-done((f32[2,64,128]{2,1,0:T(8,128)S(1)}, f32[2,64,128]{2,1,0:T(8,128)S(1)}, u32[]{:S(2)}, u32[]{:S(2)}) %collective-permute-start.2) | collective-permute-done | bytes 65568 | tf_op jit(solution)/shard_map/ppermute | solution.py:58
  20.9 1.9 %collective-permute-done.3 = f32[2,64,128]{2,1,0:T(8,128)S(1)} collective-permute-done((f32[2,64,128]{2,1,0:T(8,128)S(1)}, f32[2,64,128]{2,1,0:T(8,128)S(1)}, u32[]{:S(2)}, u32[]{:S(2)}) %collective-permute-start.3) | collective-permute-done | bytes 65568 | tf_op jit(solution)/shard_map/ppermute | solution.py:58
  22.8 6.4 %all-to-all-done.nodes_ref = f32[8,288,128]{2,1,0:T(8,128)S(1)} async-done(((f32[8,288,128]{2,1,0:T(8,128)}), f32[8,288,128]{2,1,0:T(8,128)S(1)}, u32[]{:S(2)}, u32[]{:S(2)}) %all-to-all-start) | async-done | bytes 1179680 | tf_op jit(solution)/shard_map/all_to_all | solution.py:34
  29.2 0.6 collective-permute-start.4
  29.8 0.3 minimum_reduce_fusion
  30.6 3.1 %transport.1 = f32[16,32,128]{2,1,0:T(8,128)} custom-call(f32[8,288,128]{2,1,0:T(8,128)S(1)} %all-to-all-done.nodes_ref, f32[256,8]{1,0:T(8,128)S(1)} %copy.25.columns_ref, f32[8,128]{1,0:T(8,128)S(1)} %broadcast_in_dim.18.speeds_ref.first_ref, f32[8,8,256]{2,1,0:T(8,128)S(1)} %stack.61.weights_ref), custom_call_target="tpu_custom_call" | custom-call | tf_op jit(solution)/shard_map/transport/pallas_call | solution.py:535
  33.7 6.3 %all-to-all-start.1 = ((f32[16,32,128]{2,1,0:T(8,128)}), f32[16,32,128]{2,1,0:T(8,128)S(1)}, u32[]{:S(2)}, u32[]{:S(2)}) async-start(f32[16,32,128]{2,1,0:T(8,128)} %transport.1), calls=%async_computation.1 | async-start | bytes 524288 | tf_op jit(solution)/shard_map/all_to_all | solution.py:34
  40.2 7.9 %all-to-all-done.1.integrals_ref = f32[16,32,128]{2,1,0:T(8,128)S(1)} async-done(((f32[16,32,128]{2,1,0:T(8,128)}), f32[16,32,128]{2,1,0:T(8,128)S(1)}, u32[]{:S(2)}, u32[]{:S(2)}) %all-to-all-start.1) | async-done | bytes 262176 | tf_op jit(solution)/shard_map/all_to_all | solution.py:34
  48.1 3.7 %maxwell.1 = (f32[16,88,128]{2,1,0:T(8,128)}, f32[1024,8]{1,0:T(8,128)S(1)}, f32[8,1024]{1,0:T(8,128)S(1)}, f32[8,128]{1,0:T(8,128)S(1)}) custom-call(s32[1]{0:T(128)} %bitcast.brick_ref, f32[16,64,128]{2,1,0:T(8,128)S(1)} %constant_dynamic-update-slice_fusion.5.cells_ref, f32[16,32,128]{2,1,0:T(8,128)S(1)} %all-to-all-done.1.integrals_ref, ...), custom_call_target="tpu_custom_call" | custom-call | tf_op jit(solution)/shard_map/maxwell/pallas_call | solution.py:541
  51.8 3.6 %all-to-all-start.2 = ((f32[16,88,128]{2,1,0:T(8,128)}), f32[16,88,128]{2,1,0:T(8,128)S(1)}, u32[]{:S(2)}, u32[]{:S(2)}) async-start(f32[16,88,128]{2,1,0:T(8,128)} %get-tuple-element.27), calls=%async_computation.2 | async-start | bytes 1441792 | tf_op jit(solution)/shard_map/all_to_all | solution.py:34
  55.5 12.9 %all-to-all-done.2.parts_ref = f32[16,88,128]{2,1,0:T(8,128)S(1)} async-done(((f32[16,88,128]{2,1,0:T(8,128)}), f32[16,88,128]{2,1,0:T(8,128)S(1)}, u32[]{:S(2)}, u32[]{:S(2)}) %all-to-all-start.2) | async-done | bytes 720928 | tf_op jit(solution)/shard_map/all_to_all | solution.py:34
  68.4 0.9 advance.1
  69.3 14.2 %all_to_all.25.parts_ref = f32[16,72,128]{2,1,0:T(8,128)S(1)} all-to-all(f32[16,72,128]{2,1,0:T(8,128)S(1)} %get-tuple-element.29), channel_id=1, replica_groups=mesh['slab'=8,'brick'=16] {'brick'}, dimensions={0} | all-to-all | bytes 1179648 | tf_op jit(solution)/shard_map/all_to_all | solution.py:34
  83.4 1.2 products.1
  84.6 1.1 collective-permute-start.5
  85.7 3.6 %back.1 = f32[8,256,128]{2,1,0:T(8,128)} custom-call(f32[16,72,128]{2,1,0:T(8,128)S(1)} %all_to_all.25.parts_ref, f32[1024,8]{1,0:T(8,128)S(1)} %get-tuple-element.34.line_ref, f32[8,1024]{1,0:T(8,128)S(1)} %get-tuple-element.35.state_ref, f32[256,2]{1,0:T(8,128)S(1)} %get-tuple-element.62.across_ref), custom_call_target="tpu_custom_call" | custom-call | tf_op jit(solution)/shard_map/back/pallas_call | solution.py:596
  89.4 2.8 %collective-permute-done.5 = f32[8,512]{1,0:T(8,128)S(1)} collective-permute-done((f32[8,512]{1,0:T(8,128)S(1)}, f32[8,512]{1,0:T(8,128)S(1)}, u32[]{:S(2)}, u32[]{:S(2)}) %collective-permute-start.5) | collective-permute-done | bytes 16416 | tf_op jit(solution)/shard_map/ppermute | solution.py:593
  92.3 0.2 fusion.31
  92.6 0.1 copy.27
  92.7 0.7 collective-permute-start.7
  93.4 3.5 %collective-permute-start.8 = (f32[40,128]{1,0:T(8,128)S(1)}, f32[40,128]{1,0:T(8,128)S(1)}, u32[]{:S(2)}, u32[]{:S(2)}) collective-permute-start(f32[40,128]{1,0:T(8,128)S(1)} %pad_add_fusion), channel_id=1, source_target_pairs={{0,24},{1,25},{2,26},{3,27},{4,28},{5,29},{6,30},{7,31},{8,16},{9,... | collective-permute-start | bytes 61448 | tf_op jit(solution)/shard_map/ppermute | solution.py:58
  96.9 1.0 collective-permute-done.6
  97.9 0.8 collective-permute-done.8
  98.7 1.4 collective-permute-start.10
  100.1 1.8 %collective-permute-start.11 = (f32[2,40,128]{2,1,0:T(8,128)S(1)}, f32[2,40,128]{2,1,0:T(8,128)S(1)}, u32[]{:S(2)}, u32[]{:S(2)}) collective-permute-start(f32[2,40,128]{2,1,0:T(8,128)S(1)} %pad_maximum_fusion.2), channel_id=1, source_target_pairs={{0,32},{1,33},{2,34},{3,35},{4,36},{5,37},{6,38},{7,39},{8,40},{9,... | collective-permute-start | bytes 122888 | tf_op jit(solution)/shard_map/ppermute | solution.py:58
  101.9 1.0 collective-permute-start.9
  102.9 3.9 %all-to-all-start.4 = ((f32[8,256,128]{2,1,0:T(8,128)}), f32[8,256,128]{2,1,0:T(8,128)S(1)}, u32[]{:S(2)}, u32[]{:S(2)}) async-start(f32[8,256,128]{2,1,0:T(8,128)} %back.1), calls=%async_computation.4 | async-start | bytes 2097152 | tf_op jit(solution)/shard_map/all_to_all | solution.py:34
  106.8 0.3 collective-permute-done.9
  107.2 0.3 slice_reduce_fusion
  107.5 0.1 copy.28.speeds_ref
  107.7 0.8 collective-permute-done.12
  108.4 1.3 collective-permute-start.13
  109.8 0.7 collective-permute-start.14
  110.5 2.1 %collective-permute-start.15 = (f32[4,40,128]{2,1,0:T(8,128)S(1)}, f32[4,40,128]{2,1,0:T(8,128)S(1)}, u32[]{:S(2)}, u32[]{:S(2)}) collective-permute-start(f32[4,40,128]{2,1,0:T(8,128)S(1)} %pad_maximum_fusion), channel_id=1, source_target_pairs={{0,6},{1,7},{2,4},{3,5},{4,2},{5,3},{6,0},{7,1},{8,14},{9,15},{10,... | collective-permute-start | bytes 245768 | tf_op jit(solution)/shard_map/ppermute | solution.py:58
  112.5 2.7 %collective-permute-done.13 = f32[4,40,128]{2,1,0:T(8,128)S(1)} collective-permute-done((f32[4,40,128]{2,1,0:T(8,128)S(1)}, f32[4,40,128]{2,1,0:T(8,128)S(1)}, u32[]{:S(2)}, u32[]{:S(2)}) %collective-permute-start.13) | collective-permute-done | bytes 81952 | tf_op jit(solution)/shard_map/ppermute | solution.py:58
  115.3 1.0 collective-permute-done.15
  116.3 6.2 %middle.1 = (f32[64,128]{1,0:T(8,128)}, f32[256,128]{1,0:T(8,128)S(1)}, f32[128,128]{1,0:T(8,128)S(1)}) custom-call(s32[1]{0:T(128)} %bitcast.brick_ref, f32[16,40,128]{2,1,0:T(8,128)S(1)} %constant_dynamic-update-slice_fusion.13.pieces_ref, f32[6,128,128]{2,1,0:T(8,128)S(1)} %get-tuple-element.37.transport_ref, f32[256,128]{1,0:T(8,128)S(1)} %copy-done.3, ...), custom_call_target="tpu_custom_call" | custom-call | tf_op jit(solution)/shard_map/middle/pallas_call | solution.py:612
  122.5 0.8 update.1
  123.4 1.2 collective-permute-done.16
  124.6 1.4 collective-permute-start.17
  126.0 1.7 %collective-permute-start.18 = (f32[72,128]{1,0:T(8,128)S(1)}, f32[72,128]{1,0:T(8,128)S(1)}, u32[]{:S(2)}, u32[]{:S(2)}) collective-permute-start(f32[72,128]{1,0:T(8,128)S(1)} %add.428), channel_id=1, source_target_pairs={{0,6},{1,7},{2,4},{3,5},{4,2},{5,3},{6,0},{7,1},{8,14},{9,15},{10,... | collective-permute-start | bytes 110600 | tf_op jit(solution)/shard_map/ppermute | solution.py:58
  127.8 0.4 collective-permute-start.19
  128.1 2.0 %collective-permute-done.17 = f32[72,128]{1,0:T(8,128)S(1)} collective-permute-done((f32[72,128]{1,0:T(8,128)S(1)}, f32[72,128]{1,0:T(8,128)S(1)}, u32[]{:S(2)}, u32[]{:S(2)}) %collective-permute-start.17) | collective-permute-done | bytes 36896 | tf_op jit(solution)/shard_map/ppermute | solution.py:58
  130.1 1.1 collective-permute-done.18
  131.2 0.5 collective-permute-done.19
  131.7 3.3 %collective-permute-start.20 = (f32[72,128]{1,0:T(8,128)S(1)}, f32[72,128]{1,0:T(8,128)S(1)}, u32[]{:S(2)}, u32[]{:S(2)}) collective-permute-start(f32[72,128]{1,0:T(8,128)S(1)} %add_add_fusion.3), channel_id=1, source_target_pairs={{0,16},{1,17},{2,18},{3,19},{4,20},{5,21},{6,22},{7,23},{8,24},{9,... | collective-permute-start | bytes 110600 | tf_op jit(solution)/shard_map/ppermute | solution.py:58
  135.1 0.7 collective-permute-start.21
  135.7 0.8 collective-permute-start.22
  136.5 0.8 collective-permute-done.20
  137.3 3.0 %collective-permute-done.21 = f32[72,128]{1,0:T(8,128)S(1)} collective-permute-done((f32[72,128]{1,0:T(8,128)S(1)}, f32[72,128]{1,0:T(8,128)S(1)}, u32[]{:S(2)}, u32[]{:S(2)}) %collective-permute-start.21) | collective-permute-done | bytes 36896 | tf_op jit(solution)/shard_map/ppermute | solution.py:58
  140.3 3.0 %collective-permute-start.23 = (f32[72,128]{1,0:T(8,128)S(1)}, f32[72,128]{1,0:T(8,128)S(1)}, u32[]{:S(2)}, u32[]{:S(2)}) collective-permute-start(f32[72,128]{1,0:T(8,128)S(1)} %add_add_fusion.2), channel_id=1, source_target_pairs={{0,64},{1,65},{2,66},{3,67},{4,68},{5,69},{6,70},{7,71},{8,72},{9,... | collective-permute-start | bytes 110600 | tf_op jit(solution)/shard_map/ppermute | solution.py:58
  143.3 1.2 collective-permute-start.24
  144.5 1.6 %collective-permute-done.23 = f32[72,128]{1,0:T(8,128)S(1)} collective-permute-done((f32[72,128]{1,0:T(8,128)S(1)}, f32[72,128]{1,0:T(8,128)S(1)}, u32[]{:S(2)}, u32[]{:S(2)}) %collective-permute-start.23) | collective-permute-done | bytes 36896 | tf_op jit(solution)/shard_map/ppermute | solution.py:58
  146.0 2.4 %collective-permute-done.24 = f32[72,128]{1,0:T(8,128)S(1)} collective-permute-done((f32[72,128]{1,0:T(8,128)S(1)}, f32[72,128]{1,0:T(8,128)S(1)}, u32[]{:S(2)}, u32[]{:S(2)}) %collective-permute-start.24) | collective-permute-done | bytes 36896 | tf_op jit(solution)/shard_map/ppermute | solution.py:58
  148.5 4.6 %last.1 = (f32[128,128]{1,0:T(8,128)}, f32[256,128]{1,0:T(8,128)}) custom-call(f32[72,128]{1,0:T(8,128)S(1)} %add_add_fusion.1.packed_ref, f32[256,128]{1,0:T(8,128)S(1)} %get-tuple-element.44.velocity_ref), custom_call_target="tpu_custom_call" | custom-call | tf_op jit(solution)/shard_map/last/pallas_call | solution.py:629
  (86 shorter events, 1.5 us)
Async XLA Ops:
  0.6 0.8 copy-start
  1.4 0.9 copy-start.2
  3.5 7.0 %copy-start.1 = (f32[2,2,16,128]{3,2,1,0:T(8,128)S(1)}, f32[2,2,16,128]{3,2,1,0:T(8,128)}, u32[]{:S(2)}) copy-start(f32[2,2,16,128]{3,2,1,0:T(8,128)} %param.2) | copy-start | bytes 98308
  3.5 25.7 %all-to-all-start = ((f32[8,288,128]{2,1,0:T(8,128)}), f32[8,288,128]{2,1,0:T(8,128)S(1)}, u32[]{:S(2)}, u32[]{:S(2)}) async-start(f32[8,288,128]{2,1,0:T(8,128)} %repeat.1), calls=%async_computation | async-start | bytes 2359296 | tf_op jit(solution)/shard_map/all_to_all | solution.py:34
  10.6 1.3 collective-permute-start
  11.8 5.5 %collective-permute-start.1 = (f32[2,64,128]{2,1,0:T(8,128)S(1)}, f32[2,64,128]{2,1,0:T(8,128)S(1)}, u32[]{:S(2)}, u32[]{:S(2)}) collective-permute-start(f32[2,64,128]{2,1,0:T(8,128)S(1)} %pad_maximum_fusion.1), channel_id=1, source_target_pairs={{0,2},{1,3},{2,0},{3,1},{4,6},{5,7},{6,4},{7,5},{8,10},{9,11},{10,... | collective-permute-start | bytes 196616 | tf_op jit(solution)/shard_map/ppermute | solution.py:58
  13.8 7.1 %collective-permute-start.2 = (f32[2,64,128]{2,1,0:T(8,128)S(1)}, f32[2,64,128]{2,1,0:T(8,128)S(1)}, u32[]{:S(2)}, u32[]{:S(2)}) collective-permute-start(f32[2,64,128]{2,1,0:T(8,128)S(1)} %pad_maximum_fusion.1), channel_id=1, source_target_pairs={{0,4},{1,5},{2,6},{3,7},{4,0},{5,1},{6,2},{7,3},{8,12},{9,13},{10,... | collective-permute-start | bytes 196616 | tf_op jit(solution)/shard_map/ppermute | solution.py:58
  17.3 5.5 %collective-permute-start.3 = (f32[2,64,128]{2,1,0:T(8,128)S(1)}, f32[2,64,128]{2,1,0:T(8,128)S(1)}, u32[]{:S(2)}, u32[]{:S(2)}) collective-permute-start(f32[2,64,128]{2,1,0:T(8,128)S(1)} %pad_maximum_fusion.1), channel_id=1, source_target_pairs={{0,6},{1,7},{2,4},{3,5},{4,2},{5,3},{6,0},{7,1},{8,14},{9,15},{10,... | collective-permute-start | bytes 196616 | tf_op jit(solution)/shard_map/ppermute | solution.py:58
  29.2 10.9 %collective-permute-start.4 = (f32[8,64,128]{2,1,0:T(8,128)S(1)}, f32[8,64,128]{2,1,0:T(8,128)S(1)}, u32[]{:S(2)}, u32[]{:S(2)}) collective-permute-start(f32[8,64,128]{2,1,0:T(8,128)S(1)} %constant_dynamic-update-slice_fusion), channel_id=1, source_target_pairs={{0,8},{1,9},{2,10},{3,11},{4,12},{5,13},{6,14},{7,15},{8,0},{9,1},... | collective-permute-start | bytes 786440 | tf_op jit(solution)/shard_map/ppermute | solution.py:58
  33.7 14.4 %all-to-all-start.1 = ((f32[16,32,128]{2,1,0:T(8,128)}), f32[16,32,128]{2,1,0:T(8,128)S(1)}, u32[]{:S(2)}, u32[]{:S(2)}) async-start(f32[16,32,128]{2,1,0:T(8,128)} %transport.1), calls=%async_computation.1 | async-start | bytes 524288 | tf_op jit(solution)/shard_map/all_to_all | solution.py:34
  51.8 16.6 %all-to-all-start.2 = ((f32[16,88,128]{2,1,0:T(8,128)}), f32[16,88,128]{2,1,0:T(8,128)S(1)}, u32[]{:S(2)}, u32[]{:S(2)}) async-start(f32[16,88,128]{2,1,0:T(8,128)} %get-tuple-element.27), calls=%async_computation.2 | async-start | bytes 1441792 | tf_op jit(solution)/shard_map/all_to_all | solution.py:34
  84.6 7.6 %collective-permute-start.5 = (f32[8,512]{1,0:T(8,128)S(1)}, f32[8,512]{1,0:T(8,128)S(1)}, u32[]{:S(2)}, u32[]{:S(2)}) collective-permute-start(f32[8,512]{1,0:T(8,128)S(1)} %get-tuple-element.32), channel_id=1, source_target_pairs={{0,16},{16,32},{32,48},{48,64},{64,80},{80,96},{96,112},{112,0},{1... | collective-permute-start | bytes 49160 | tf_op jit(solution)/shard_map/ppermute | solution.py:593
  92.5 5.4 %collective-permute-start.6 = (f32[40,128]{1,0:T(8,128)S(1)}, f32[40,128]{1,0:T(8,128)S(1)}, u32[]{:S(2)}, u32[]{:S(2)}) collective-permute-start(f32[40,128]{1,0:T(8,128)S(1)} %pad_add_fusion), channel_id=1, source_target_pairs={{0,16},{1,17},{2,18},{3,19},{4,20},{5,21},{6,22},{7,23},{8,24},{9,... | collective-permute-start | bytes 61448 | tf_op jit(solution)/shard_map/ppermute | solution.py:58
  92.7 5.1 %collective-permute-start.7 = (f32[40,128]{1,0:T(8,128)S(1)}, f32[40,128]{1,0:T(8,128)S(1)}, u32[]{:S(2)}, u32[]{:S(2)}) collective-permute-start(f32[40,128]{1,0:T(8,128)S(1)} %pad_add_fusion), channel_id=1, source_target_pairs={{0,8},{1,9},{2,10},{3,11},{4,12},{5,13},{6,14},{7,15},{8,0},{9,1},... | collective-permute-start | bytes 61448 | tf_op jit(solution)/shard_map/ppermute | solution.py:58
  93.4 5.3 %collective-permute-start.8 = (f32[40,128]{1,0:T(8,128)S(1)}, f32[40,128]{1,0:T(8,128)S(1)}, u32[]{:S(2)}, u32[]{:S(2)}) collective-permute-start(f32[40,128]{1,0:T(8,128)S(1)} %pad_add_fusion), channel_id=1, source_target_pairs={{0,24},{1,25},{2,26},{3,27},{4,28},{5,29},{6,30},{7,31},{8,16},{9,... | collective-permute-start | bytes 61448 | tf_op jit(solution)/shard_map/ppermute | solution.py:58
  98.7 8.1 %collective-permute-start.10 = (f32[2,40,128]{2,1,0:T(8,128)S(1)}, f32[2,40,128]{2,1,0:T(8,128)S(1)}, u32[]{:S(2)}, u32[]{:S(2)}) collective-permute-start(f32[2,40,128]{2,1,0:T(8,128)S(1)} %pad_maximum_fusion.2), channel_id=1, source_target_pairs={{0,64},{1,65},{2,66},{3,67},{4,68},{5,69},{6,70},{7,71},{8,72},{9,... | collective-permute-start | bytes 122888 | tf_op jit(solution)/shard_map/ppermute | solution.py:58
  100.1 6.7 %collective-permute-start.11 = (f32[2,40,128]{2,1,0:T(8,128)S(1)}, f32[2,40,128]{2,1,0:T(8,128)S(1)}, u32[]{:S(2)}, u32[]{:S(2)}) collective-permute-start(f32[2,40,128]{2,1,0:T(8,128)S(1)} %pad_maximum_fusion.2), channel_id=1, source_target_pairs={{0,32},{1,33},{2,34},{3,35},{4,36},{5,37},{6,38},{7,39},{8,40},{9,... | collective-permute-start | bytes 122888 | tf_op jit(solution)/shard_map/ppermute | solution.py:58
  101.9 5.2 %collective-permute-start.9 = (f32[2,40,128]{2,1,0:T(8,128)S(1)}, f32[2,40,128]{2,1,0:T(8,128)S(1)}, u32[]{:S(2)}, u32[]{:S(2)}) collective-permute-start(f32[2,40,128]{2,1,0:T(8,128)S(1)} %pad_maximum_fusion.2), channel_id=1, source_target_pairs={{0,96},{1,97},{2,98},{3,99},{4,100},{5,101},{6,102},{7,103},{8,104... | collective-permute-start | bytes 122888 | tf_op jit(solution)/shard_map/ppermute | solution.py:58
  102.9 19.7 %all-to-all-start.4 = ((f32[8,256,128]{2,1,0:T(8,128)}), f32[8,256,128]{2,1,0:T(8,128)S(1)}, u32[]{:S(2)}, u32[]{:S(2)}) async-start(f32[8,256,128]{2,1,0:T(8,128)} %back.1), calls=%async_computation.4 | async-start | bytes 2097152 | tf_op jit(solution)/shard_map/all_to_all | solution.py:34
  106.8 9.5 %copy-start.3 = (f32[256,128]{1,0:T(8,128)S(1)}, f32[256,128]{1,0:T(8,128)}, u32[]{:S(2)}) copy-start(f32[256,128]{1,0:T(8,128)} %basis_ref.1) | copy-start | bytes 393220
  107.1 1.3 collective-permute-start.12
  108.4 6.8 %collective-permute-start.13 = (f32[4,40,128]{2,1,0:T(8,128)S(1)}, f32[4,40,128]{2,1,0:T(8,128)S(1)}, u32[]{:S(2)}, u32[]{:S(2)}) collective-permute-start(f32[4,40,128]{2,1,0:T(8,128)S(1)} %pad_maximum_fusion), channel_id=1, source_target_pairs={{0,4},{1,5},{2,6},{3,7},{4,0},{5,1},{6,2},{7,3},{8,12},{9,13},{10,... | collective-permute-start | bytes 245768 | tf_op jit(solution)/shard_map/ppermute | solution.py:58
  109.8 5.5 %collective-permute-start.14 = (f32[4,40,128]{2,1,0:T(8,128)S(1)}, f32[4,40,128]{2,1,0:T(8,128)S(1)}, u32[]{:S(2)}, u32[]{:S(2)}) collective-permute-start(f32[4,40,128]{2,1,0:T(8,128)S(1)} %pad_maximum_fusion), channel_id=1, source_target_pairs={{0,2},{1,3},{2,0},{3,1},{4,6},{5,7},{6,4},{7,5},{8,10},{9,11},{10,... | collective-permute-start | bytes 245768 | tf_op jit(solution)/shard_map/ppermute | solution.py:58
  110.5 5.8 %collective-permute-start.15 = (f32[4,40,128]{2,1,0:T(8,128)S(1)}, f32[4,40,128]{2,1,0:T(8,128)S(1)}, u32[]{:S(2)}, u32[]{:S(2)}) collective-permute-start(f32[4,40,128]{2,1,0:T(8,128)S(1)} %pad_maximum_fusion), channel_id=1, source_target_pairs={{0,6},{1,7},{2,4},{3,5},{4,2},{5,3},{6,0},{7,1},{8,14},{9,15},{10,... | collective-permute-start | bytes 245768 | tf_op jit(solution)/shard_map/ppermute | solution.py:58
  123.3 1.3 collective-permute-start.16
  124.6 5.5 %collective-permute-start.17 = (f32[72,128]{1,0:T(8,128)S(1)}, f32[72,128]{1,0:T(8,128)S(1)}, u32[]{:S(2)}, u32[]{:S(2)}) collective-permute-start(f32[72,128]{1,0:T(8,128)S(1)} %add.428), channel_id=1, source_target_pairs={{0,4},{1,5},{2,6},{3,7},{4,0},{5,1},{6,2},{7,3},{8,12},{9,13},{10,... | collective-permute-start | bytes 110600 | tf_op jit(solution)/shard_map/ppermute | solution.py:58
  126.0 5.2 %collective-permute-start.18 = (f32[72,128]{1,0:T(8,128)S(1)}, f32[72,128]{1,0:T(8,128)S(1)}, u32[]{:S(2)}, u32[]{:S(2)}) collective-permute-start(f32[72,128]{1,0:T(8,128)S(1)} %add.428), channel_id=1, source_target_pairs={{0,6},{1,7},{2,4},{3,5},{4,2},{5,3},{6,0},{7,1},{8,14},{9,15},{10,... | collective-permute-start | bytes 110600 | tf_op jit(solution)/shard_map/ppermute | solution.py:58
  127.8 4.0 %collective-permute-start.19 = (f32[72,128]{1,0:T(8,128)S(1)}, f32[72,128]{1,0:T(8,128)S(1)}, u32[]{:S(2)}, u32[]{:S(2)}) collective-permute-start(f32[72,128]{1,0:T(8,128)S(1)} %add.428), channel_id=1, source_target_pairs={{0,2},{1,3},{2,0},{3,1},{4,6},{5,7},{6,4},{7,5},{8,10},{9,11},{10,... | collective-permute-start | bytes 110600 | tf_op jit(solution)/shard_map/ppermute | solution.py:58
  131.7 5.5 %collective-permute-start.20 = (f32[72,128]{1,0:T(8,128)S(1)}, f32[72,128]{1,0:T(8,128)S(1)}, u32[]{:S(2)}, u32[]{:S(2)}) collective-permute-start(f32[72,128]{1,0:T(8,128)S(1)} %add_add_fusion.3), channel_id=1, source_target_pairs={{0,16},{1,17},{2,18},{3,19},{4,20},{5,21},{6,22},{7,23},{8,24},{9,... | collective-permute-start | bytes 110600 | tf_op jit(solution)/shard_map/ppermute | solution.py:58
  135.1 5.2 %collective-permute-start.21 = (f32[72,128]{1,0:T(8,128)S(1)}, f32[72,128]{1,0:T(8,128)S(1)}, u32[]{:S(2)}, u32[]{:S(2)}) collective-permute-start(f32[72,128]{1,0:T(8,128)S(1)} %add_add_fusion.3), channel_id=1, source_target_pairs={{0,24},{1,25},{2,26},{3,27},{4,28},{5,29},{6,30},{7,31},{8,16},{9,... | collective-permute-start | bytes 110600 | tf_op jit(solution)/shard_map/ppermute | solution.py:58
  135.7 4.5 %collective-permute-start.22 = (f32[72,128]{1,0:T(8,128)S(1)}, f32[72,128]{1,0:T(8,128)S(1)}, u32[]{:S(2)}, u32[]{:S(2)}) collective-permute-start(f32[72,128]{1,0:T(8,128)S(1)} %add_add_fusion.3), channel_id=1, source_target_pairs={{0,8},{1,9},{2,10},{3,11},{4,12},{5,13},{6,14},{7,15},{8,0},{9,1},... | collective-permute-start | bytes 110600 | tf_op jit(solution)/shard_map/ppermute | solution.py:58
  140.3 5.8 %collective-permute-start.23 = (f32[72,128]{1,0:T(8,128)S(1)}, f32[72,128]{1,0:T(8,128)S(1)}, u32[]{:S(2)}, u32[]{:S(2)}) collective-permute-start(f32[72,128]{1,0:T(8,128)S(1)} %add_add_fusion.2), channel_id=1, source_target_pairs={{0,64},{1,65},{2,66},{3,67},{4,68},{5,69},{6,70},{7,71},{8,72},{9,... | collective-permute-start | bytes 110600 | tf_op jit(solution)/shard_map/ppermute | solution.py:58
  143.3 5.2 %collective-permute-start.24 = (f32[72,128]{1,0:T(8,128)S(1)}, f32[72,128]{1,0:T(8,128)S(1)}, u32[]{:S(2)}, u32[]{:S(2)}) collective-permute-start(f32[72,128]{1,0:T(8,128)S(1)} %add_add_fusion.2), channel_id=1, source_target_pairs={{0,96},{1,97},{2,98},{3,99},{4,100},{5,101},{6,102},{7,103},{8,104... | collective-permute-start | bytes 110600 | tf_op jit(solution)/shard_map/ppermute | solution.py:58
  144.5 4.0 %collective-permute-start.25 = (f32[72,128]{1,0:T(8,128)S(1)}, f32[72,128]{1,0:T(8,128)S(1)}, u32[]{:S(2)}, u32[]{:S(2)}) collective-permute-start(f32[72,128]{1,0:T(8,128)S(1)} %add_add_fusion.2), channel_id=1, source_target_pairs={{0,32},{1,33},{2,34},{3,35},{4,36},{5,37},{6,38},{7,39},{8,40},{9,... | collective-permute-start | bytes 110600 | tf_op jit(solution)/shard_map/ppermute | solution.py:58
